TPU v7x, 32 devices: a whole 2x2x4 slice. The times are simulated.
32 devices in a mesh: seq: 16 (over z, x, core), head: 2 (over y).
Axes of the slice: x: 2, y: 2, z: 4, core: 2. Of those that a mesh axis runs over, the one named last changes fastest.
Arguments:
- tokens: bfloat16 [8, 2048, 1024], P(None, 'seq'), may hold values from -6 to 6
- cotangent: bfloat16 [8, 2048, 1024], P(None, 'seq'), may hold values from -6 to 6
- domain_ids: int32 [8], replicated, may hold values from 0 to 3, as said below
- block_order: int32 [16], replicated, may hold values from 0 to 15, each once
- headwise: float32 [1024, 160], P('seq', 'head'), may hold values from -0.375 to 0.375
- headwise_mean: float32 [1024, 160], P('seq', 'head'), may hold values from -320 to 320
- headwise_square: float32 [1024, 160], P('seq', 'head'), may hold values from 6815.744 to 108953.6
- shared_factors: float32 [1024, 640], P('seq'), may hold values from -0.1875 to 0.1875
- shared_factors_mean: float32 [1024, 640], P('seq'), may hold values from -320 to 320
- shared_factors_square: float32 [1024, 640], P('seq'), may hold values from 6815.744 to 108953.6
- out_weight: float32 [1024, 1024], P('head', 'seq'), may hold values from -1 to 1
- out_weight_mean: float32 [1024, 1024], P('head', 'seq'), may hold values from -8 to 8
- out_weight_square: float32 [1024, 1024], P('head', 'seq'), may hold values from 4.25984 to 68.15744
- gate_up: float32 [2, 1024, 2816], P(None, 'seq', 'head'), may hold values from -0.1875 to 0.1875
- gate_up_mean: float32 [2, 1024, 2816], P(None, 'seq', 'head'), may hold values from -16 to 16
- gate_up_square: float32 [2, 1024, 2816], P(None, 'seq', 'head'), may hold values from 13.80352 to 220.7744
- down_weight: float32 [2816, 1024], P('head', 'seq'), may hold values from -0.109375 to 0.109375
- down_weight_mean: float32 [2816, 1024], P('head', 'seq'), may hold values from -24 to 24
- down_weight_square: float32 [2816, 1024], P('head', 'seq'), may hold values from 38.33856 to 613.5808
- norm_gains: float32 [2, 1024], P(None, 'seq'), may hold values from 0.5 to 1.5
- norm_gains_mean: float32 [2, 1024], P(None, 'seq'), may hold values from -112 to 112
- norm_gains_square: float32 [2, 1024], P(None, 'seq'), may hold values from 665.6 to 10649.6
Outputs:
- layer_output: bfloat16 [8, 2048, 1024], P(None, 'seq')
- input_grad: float32 [8, 2048, 1024], P(None, 'seq')
- headwise_new: float32 [1024, 160], P('seq', 'head')
- headwise_mean_new: float32 [1024, 160], P('seq', 'head')
- headwise_square_new: float32 [1024, 160], P('seq', 'head')
- shared_factors_new: float32 [1024, 640], P('seq')
- shared_factors_mean_new: float32 [1024, 640], P('seq')
- shared_factors_square_new: float32 [1024, 640], P('seq')
- out_weight_new: float32 [1024, 1024], P('head', 'seq')
- out_weight_mean_new: float32 [1024, 1024], P('head', 'seq')
- out_weight_square_new: float32 [1024, 1024], P('head', 'seq')
- gate_up_new: float32 [2, 1024, 2816], P(None, 'seq', 'head')
- gate_up_mean_new: float32 [2, 1024, 2816], P(None, 'seq', 'head')
- gate_up_square_new: float32 [2, 1024, 2816], P(None, 'seq', 'head')
- down_weight_new: float32 [2816, 1024], P('head', 'seq')
- down_weight_mean_new: float32 [2816, 1024], P('head', 'seq')
- down_weight_square_new: float32 [2816, 1024], P('head', 'seq')
- norm_gains_new: float32 [2, 1024], P(None, 'seq')
- norm_gains_mean_new: float32 [2, 1024], P(None, 'seq')
- norm_gains_square_new: float32 [2, 1024], P(None, 'seq')
Inputs may be any that keep to these rules, and one draw needn't show every extreme that they name: Each value appears once; index r of seq holds rows r * 128 to (r + 1) * 128 - 1 of every sequence, which stand at block block_order[r] of positions. `domain_ids`: sequences with equal ids share a domain; some sequence has id 0 and another has id 4 - 1.
All inputs are finite; a program needn't handle non-finite values.
Results may differ from a plain program's by a relative error of at most 0.025.
The roundings to bfloat16 on the way count: a program that leaves them out, or rounds other values in their place, can miss the bound.
Values may be sent and summed in bfloat16 or wider, within the bound.
No kernel may reach another device: no remote copies, remote signals or barrier semaphores. Data moves between devices by JAX's collectives and lax.ppermute only.
A program may use at most 192 MiB of HBM per device.

v0:
```python
import jax
import jax.numpy as jnp
from jax import lax
from jax.sharding import PartitionSpec as P

D = 1024
H = 16
DH = 64
RQ = 6
RK = 2
FF = 2816
STEP = 10


EPSILON = 1e-05
BETA_ONE = 0.9
BETA_TWO = 0.95
ADAM_EPS = 1e-08
DECAY = 0.1
NEGATIVE = -1e30
MAXIMAL_PRECISE = lax.Precision.HIGHEST


def passed_along(block, axis, distance):
    devices = range(lax.axis_size(axis))
    route = [((i - distance) % len(devices), i) for i in devices]
    return lax.ppermute(block, axis, route)


def table_pick(table, where_at):
    spots = jnp.arange(table.shape[0], dtype=jnp.int32)
    return jnp.sum(jnp.where(spots == where_at, table, 0))


def rope_tables(positions):
    half_dim = DH // 2
    frequency = 10000.0 ** (-(2.0 * jnp.arange(half_dim, dtype=jnp.float32)) / DH)
    angles = positions.astype(jnp.float32)[:, None] * frequency[None, :]
    return (jnp.cos(angles), jnp.sin(angles))


def rotate(factor, cos_rows, sin_rows):
    half_dim = factor.shape[-1] // 2
    first_half = factor[..., :half_dim]
    second_half = factor[..., half_dim:]
    cos_wide = cos_rows[:, None, :]
    sin_wide = sin_rows[:, None, :]
    return jnp.concatenate(
        [
            first_half * cos_wide - second_half * sin_wide,
            second_half * cos_wide + first_half * sin_wide,
        ],
        axis=-1,
    )


def unrotate(grad_rows, cos_rows, sin_rows):
    half_dim = grad_rows.shape[-1] // 2
    first_half = grad_rows[..., :half_dim]
    second_half = grad_rows[..., half_dim:]
    cos_wide = cos_rows[:, None, :]
    sin_wide = sin_rows[:, None, :]
    return jnp.concatenate(
        [
            first_half * cos_wide + second_half * sin_wide,
            second_half * cos_wide - first_half * sin_wide,
        ],
        axis=-1,
    )


def normalize(row_data):
    inverse = lax.rsqrt(jnp.mean(row_data * row_data, -1, keepdims=True) + EPSILON)
    return (row_data * inverse, inverse)


def norm_back(normed_grad, gain_row, hat_rows, inverse):
    hat_grad = normed_grad * gain_row
    return inverse * (hat_grad - hat_rows * jnp.mean(hat_grad * hat_rows, -1, keepdims=True))


def adam_update(master, mean_old, square_old, gradient, rate):
    mean_new = BETA_ONE * mean_old + (1.0 - BETA_ONE) * gradient
    square_new = BETA_TWO * square_old + (1.0 - BETA_TWO) * gradient * gradient
    mean_hat = mean_new / (1.0 - BETA_ONE**STEP)
    square_hat = square_new / (1.0 - BETA_TWO**STEP)
    master_new = master - rate * (mean_hat / (jnp.sqrt(square_hat) + ADAM_EPS) + DECAY * master)
    return (master_new, mean_new, square_new)


def step_rates():
    return (
        2.5 * (D // 4) ** (-0.5),
        2.5 * D ** (-0.5),
        2.5 * (H * DH // 32) ** (-0.5),
        2.5 * D ** (-0.5),
        2.5 * FF ** (-0.5),
        0.5,
    )


def on_device(
    tokens,
    cotangent,
    domain_ids,
    block_order,
    headwise,
    headwise_mean,
    headwise_square,
    shared_factors,
    shared_factors_mean,
    shared_factors_square,
    out_weight,
    out_weight_mean,
    out_weight_square,
    gate_up,
    gate_up_mean,
    gate_up_square,
    down_weight,
    down_weight_mean,
    down_weight_square,
    norm_gains,
    norm_gains_mean,
    norm_gains_square,
):
    cycle_size = lax.axis_size("seq")
    cycle_pos = lax.axis_index("seq")
    copies = (
        lax.all_gather(headwise.astype(jnp.bfloat16), "seq", axis=0, tiled=True),
        lax.all_gather(shared_factors.astype(jnp.bfloat16), "seq", axis=0, tiled=True),
        lax.all_gather(out_weight.astype(jnp.bfloat16), "seq", axis=1, tiled=True),
        lax.all_gather(gate_up.astype(jnp.bfloat16), "seq", axis=1, tiled=True),
        lax.all_gather(down_weight.astype(jnp.bfloat16), "seq", axis=1, tiled=True),
        lax.all_gather(norm_gains.astype(jnp.bfloat16), "seq", axis=1, tiled=True),
    )
    w_heads, w_shared, w_out, w_gate, w_down, gains_low = copies
    gain_first = gains_low[0].astype(jnp.float32)
    gain_second = gains_low[1].astype(jnp.float32)
    seq_count, block_len, model_width = tokens.shape
    head_count = w_out.shape[0] // DH
    rank_all = RQ + 2 * RK
    scale = DH ** (-0.5)
    own_block = table_pick(block_order, cycle_pos)
    offsets = jnp.arange(block_len, dtype=jnp.int32)
    query_pos = own_block * block_len + offsets
    cos_rows, sin_rows = rope_tables(query_pos)
    token_rows_broad = tokens.astype(jnp.float32)
    first_hat, first_inverse = normalize(token_rows_broad)
    first_normalized = (first_hat * gain_first).astype(jnp.bfloat16)
    head_factor_piece = jnp.dot(first_normalized, w_heads, preferred_element_type=jnp.float32)
    head_factor_piece = head_factor_piece.reshape(seq_count, block_len, head_count, rank_all)
    shared_factor_piece = jnp.dot(first_normalized, w_shared, preferred_element_type=jnp.float32)
    shared_factor_piece = shared_factor_piece.reshape(seq_count, block_len, rank_all, DH)
    a_query = head_factor_piece[..., :RQ]
    a_key = head_factor_piece[..., RQ : RQ + RK]
    a_value = head_factor_piece[..., RQ + RK :]
    b_query = rotate(shared_factor_piece[:, :, :RQ], cos_rows, sin_rows)
    b_key = rotate(shared_factor_piece[:, :, RQ : RQ + RK], cos_rows, sin_rows)
    b_value = shared_factor_piece[:, :, RQ + RK :]
    query_low = (
        jnp.einsum("schr,scre->sche", a_query, b_query, precision=MAXIMAL_PRECISE) / RQ
    ).astype(jnp.bfloat16)
    key_low = (jnp.einsum("schr,scre->sche", a_key, b_key, precision=MAXIMAL_PRECISE) / RK).astype(
        jnp.bfloat16
    )
    value_low = (
        jnp.einsum("schr,scre->sche", a_value, b_value, precision=MAXIMAL_PRECISE) / RK
    ).astype(jnp.bfloat16)

    def block_scores(key_rows, key_block):
        raw_scores = jnp.einsum(
            "sqhe,skhe->shqk", query_low, key_rows, preferred_element_type=jnp.float32
        )
        key_pos = key_block * block_len + offsets
        allowed = key_pos[None, :] <= query_pos[:, None]
        return (raw_scores * scale, allowed)

    def absorb(state, key_rows, value_rows, key_block):
        best, total, accum = state
        scores, allowed = block_scores(key_rows, key_block)
        masked = jnp.where(allowed, scores, NEGATIVE)
        best_new = jnp.maximum(best, jnp.max(masked, axis=-1))
        probs = jnp.where(allowed, jnp.exp(scores - best_new[..., None]), 0.0)
        factor = jnp.exp(best - best_new)
        total_new = total * factor + jnp.sum(probs, axis=-1)
        accum_new = accum * factor[..., None] + jnp.einsum(
            "shqk,skhe->shqe", probs, value_rows.astype(jnp.float32), precision=MAXIMAL_PRECISE
        )
        return (best_new, total_new, accum_new)

    def visit(state, key_rows, value_rows, key_block):
        return absorb(state, key_rows, value_rows, key_block)

    start_state = (
        jnp.full((seq_count, head_count, block_len), NEGATIVE, jnp.float32),
        jnp.zeros((seq_count, head_count, block_len), jnp.float32),
        jnp.zeros((seq_count, head_count, block_len, DH), jnp.float32),
    )
    start_state = visit(start_state, key_low, value_low, own_block)

    def forward_turn(cycle_step, loop_state):
        state, key_cur, value_cur = loop_state
        key_cur, value_cur = passed_along((key_cur, value_cur), "seq", 1)
        key_block = table_pick(block_order, jnp.mod(cycle_pos - cycle_step, cycle_size))
        state = visit(state, key_cur, value_cur, key_block)
        return (state, key_cur, value_cur)

    final_state, key_last, value_last = lax.fori_loop(
        1, cycle_size, forward_turn, (start_state, key_low, value_low)
    )
    best, total, accum = final_state
    log_sum = best + jnp.log(total)
    heads_wide = (accum / total[..., None]).transpose(0, 2, 1, 3)
    heads_low = heads_wide.astype(jnp.bfloat16).reshape(seq_count, block_len, head_count * DH)
    attn_part = jnp.dot(heads_low, w_out, preferred_element_type=jnp.float32)
    attn_total = lax.psum(attn_part, "head")
    middle_activation = token_rows_broad + attn_total
    second_hat, second_inverse = normalize(middle_activation)
    second_normalized = (second_hat * gain_second).astype(jnp.bfloat16)
    gate_both = jnp.einsum(
        "scd,gdf->gscf", second_normalized, w_gate, preferred_element_type=jnp.float32
    )
    gate_row_values = gate_both[0]
    up_rows = gate_both[1]
    sigmoid_gate = jax.nn.sigmoid(gate_row_values)
    silu_gate = gate_row_values * sigmoid_gate
    hidden_low = (silu_gate * up_rows).astype(jnp.bfloat16)
    ffn_part = jnp.dot(hidden_low, w_down, preferred_element_type=jnp.float32)
    ffn_total = lax.psum(ffn_part.astype(jnp.bfloat16), "head").astype(jnp.float32)
    layer_output = (middle_activation + ffn_total).astype(jnp.bfloat16)
    same_domain = (domain_ids[:, None] == domain_ids[None, :]).astype(jnp.float32)
    seq_weight = 1.0 / jnp.sum(same_domain, axis=1)
    out_grad = cotangent.astype(jnp.float32) * seq_weight[:, None, None]
    out_low = out_grad.astype(jnp.bfloat16)
    down_grad = jnp.einsum("scf,scd->fd", hidden_low, out_low, preferred_element_type=jnp.float32)
    hidden_grad = jnp.einsum("scd,fd->scf", out_low, w_down, preferred_element_type=jnp.float32)
    up_grad = hidden_grad * silu_gate
    gate_grad = (
        hidden_grad * up_rows * (sigmoid_gate * (1.0 + gate_row_values * (1.0 - sigmoid_gate)))
    )
    gu_low = jnp.stack([gate_grad, up_grad]).astype(jnp.bfloat16)
    gate_up_grad = jnp.einsum(
        "scd,gscf->gdf", second_normalized, gu_low, preferred_element_type=jnp.float32
    )
    second_part = jnp.einsum("gscf,gdf->scd", gu_low, w_gate, preferred_element_type=jnp.float32)
    second_grad = lax.psum(second_part.astype(jnp.bfloat16), "head").astype(jnp.float32)
    second_gain_grad = jnp.sum(second_grad * second_hat, axis=(0, 1))
    middle_grad = out_grad + norm_back(second_grad, gain_second, second_hat, second_inverse)
    middle_low = middle_grad.astype(jnp.bfloat16)
    out_weight_grad = jnp.einsum(
        "sce,scd->ed", heads_low, middle_low, preferred_element_type=jnp.float32
    )
    heads_grad = jnp.einsum("scd,ed->sce", middle_low, w_out, preferred_element_type=jnp.float32)
    heads_grad_low = heads_grad.astype(jnp.bfloat16).reshape(seq_count, block_len, head_count, DH)
    heads_grad_wide = heads_grad_low.astype(jnp.float32)
    delta = jnp.sum(heads_grad_wide * heads_wide, axis=-1).transpose(0, 2, 1)

    def back_block(key_rows, value_rows, key_block):
        scores, allowed = block_scores(key_rows, key_block)
        probs = jnp.where(allowed, jnp.exp(scores - log_sum[..., None]), 0.0)
        prob_grad = jnp.einsum(
            "sqhe,skhe->shqk", heads_grad_low, value_rows, preferred_element_type=jnp.float32
        )
        score_grad = (probs * (prob_grad - delta[..., None]) * scale).astype(jnp.bfloat16)
        query_part = jnp.einsum(
            "shqk,skhe->sqhe", score_grad, key_rows, preferred_element_type=jnp.float32
        )
        key_part = jnp.einsum(
            "shqk,sqhe->skhe", score_grad, query_low, preferred_element_type=jnp.float32
        )
        value_part = jnp.einsum(
            "shqk,sqhe->skhe", probs, heads_grad_wide, precision=MAXIMAL_PRECISE
        )
        return (query_part, key_part, value_part)

    zero_rows = jnp.zeros((seq_count, block_len, head_count, DH), jnp.float32)

    def visit_back(key_rows, value_rows, key_block):
        return back_block(key_rows, value_rows, key_block)

    def again_turn(cycle_step, loop_state):
        query_acc, key_cur, value_cur, key_acc, value_acc = loop_state
        key_block = table_pick(block_order, jnp.mod(cycle_pos - cycle_step, cycle_size))
        query_part, key_part, value_part = visit_back(key_cur, value_cur, key_block)
        key_cur, value_cur = passed_along((key_cur, value_cur), "seq", 1)
        key_acc, value_acc = passed_along((key_acc + key_part, value_acc + value_part), "seq", 1)
        return (query_acc + query_part, key_cur, value_cur, key_acc, value_acc)

    query_grad, key_back, value_back, key_grad, value_grad = lax.fori_loop(
        0, cycle_size, again_turn, (zero_rows, key_low, value_low, zero_rows, zero_rows)
    )
    a_query_grad = (
        jnp.einsum("sche,scre->schr", query_grad, b_query, precision=MAXIMAL_PRECISE) / RQ
    )
    b_query_grad = unrotate(
        jnp.einsum("sche,schr->scre", query_grad, a_query, precision=MAXIMAL_PRECISE) / RQ,
        cos_rows,
        sin_rows,
    )
    a_key_grad = jnp.einsum("sche,scre->schr", key_grad, b_key, precision=MAXIMAL_PRECISE) / RK
    b_key_grad = unrotate(
        jnp.einsum("sche,schr->scre", key_grad, a_key, precision=MAXIMAL_PRECISE) / RK,
        cos_rows,
        sin_rows,
    )
    a_value_grad = (
        jnp.einsum("sche,scre->schr", value_grad, b_value, precision=MAXIMAL_PRECISE) / RK
    )
    b_value_grad = (
        jnp.einsum("sche,schr->scre", value_grad, a_value, precision=MAXIMAL_PRECISE) / RK
    )
    head_grad = jnp.concatenate([a_query_grad, a_key_grad, a_value_grad], axis=-1)
    head_grad_low = head_grad.reshape(seq_count, block_len, head_count * rank_all).astype(
        jnp.bfloat16
    )
    shared_grad_part = jnp.concatenate([b_query_grad, b_key_grad, b_value_grad], axis=2)
    shared_grad_part = shared_grad_part.reshape(seq_count, block_len, rank_all * DH)
    first_part = jnp.einsum(
        "scj,dj->scd", head_grad_low, w_heads, preferred_element_type=jnp.float32
    )
    first_sum, shared_grad = (
        lax.psum(first_part.astype(jnp.bfloat16), "head").astype(jnp.float32),
        lax.psum(shared_grad_part.astype(jnp.bfloat16), "head").astype(jnp.float32),
    )
    shared_grad_low = shared_grad.astype(jnp.bfloat16)
    first_grad = first_sum + jnp.einsum(
        "scj,dj->scd", shared_grad_low, w_shared, preferred_element_type=jnp.float32
    )
    headwise_grad = jnp.einsum(
        "scd,scj->dj", first_normalized, head_grad_low, preferred_element_type=jnp.float32
    )
    shared_weight_grad = jnp.einsum(
        "scd,scj->dj", first_normalized, shared_grad_low, preferred_element_type=jnp.float32
    )
    first_gain_grad = jnp.sum(first_grad * first_hat, axis=(0, 1))
    input_grad = middle_grad + norm_back(first_grad, gain_first, first_hat, first_inverse)
    gains_grad = jnp.stack([first_gain_grad, second_gain_grad])
    summed = (
        lax.psum_scatter(
            headwise_grad.astype(jnp.bfloat16), "seq", scatter_dimension=0, tiled=True
        ).astype(jnp.float32),
        lax.psum_scatter(
            shared_weight_grad.astype(jnp.bfloat16), "seq", scatter_dimension=0, tiled=True
        ).astype(jnp.float32),
        lax.psum_scatter(
            out_weight_grad.astype(jnp.bfloat16), "seq", scatter_dimension=1, tiled=True
        ).astype(jnp.float32),
        lax.psum_scatter(
            gate_up_grad.astype(jnp.bfloat16), "seq", scatter_dimension=1, tiled=True
        ).astype(jnp.float32),
        lax.psum_scatter(
            down_grad.astype(jnp.bfloat16), "seq", scatter_dimension=1, tiled=True
        ).astype(jnp.float32),
        lax.psum_scatter(
            gains_grad.astype(jnp.bfloat16), "seq", scatter_dimension=1, tiled=True
        ).astype(jnp.float32),
    )
    rates = step_rates()
    heads_new = adam_update(headwise, headwise_mean, headwise_square, summed[0], rates[0])
    shared_new = adam_update(
        shared_factors, shared_factors_mean, shared_factors_square, summed[1], rates[1]
    )
    out_new = adam_update(out_weight, out_weight_mean, out_weight_square, summed[2], rates[2])
    gate_new = adam_update(gate_up, gate_up_mean, gate_up_square, summed[3], rates[3])
    down_new = adam_update(down_weight, down_weight_mean, down_weight_square, summed[4], rates[4])
    gains_new = adam_update(norm_gains, norm_gains_mean, norm_gains_square, summed[5], rates[5])
    return (
        layer_output,
        input_grad,
        heads_new[0],
        heads_new[1],
        heads_new[2],
        shared_new[0],
        shared_new[1],
        shared_new[2],
        out_new[0],
        out_new[1],
        out_new[2],
        gate_new[0],
        gate_new[1],
        gate_new[2],
        down_new[0],
        down_new[1],
        down_new[2],
        gains_new[0],
        gains_new[1],
        gains_new[2],
    )


def solution(mesh):
    return jax.shard_map(
        on_device,
        mesh=mesh,
        in_specs=(
            P(None, "seq", None),
            P(None, "seq", None),
            P(),
            P(),
            P("seq", "head"),
            P("seq", "head"),
            P("seq", "head"),
            P("seq", None),
            P("seq", None),
            P("seq", None),
            P("head", "seq"),
            P("head", "seq"),
            P("head", "seq"),
            P(None, "seq", "head"),
            P(None, "seq", "head"),
            P(None, "seq", "head"),
            P("head", "seq"),
            P("head", "seq"),
            P("head", "seq"),
            P(None, "seq"),
            P(None, "seq"),
            P(None, "seq"),
        ),
        out_specs=(
            P(None, "seq", None),
            P(None, "seq", None),
            P("seq", "head"),
            P("seq", "head"),
            P("seq", "head"),
            P("seq", None),
            P("seq", None),
            P("seq", None),
            P("head", "seq"),
            P("head", "seq"),
            P("head", "seq"),
            P(None, "seq", "head"),
            P(None, "seq", "head"),
            P(None, "seq", "head"),
            P("head", "seq"),
            P("head", "seq"),
            P("head", "seq"),
            P(None, "seq"),
            P(None, "seq"),
            P(None, "seq"),
        ),
        check_vma=False,
    )
```

profile of v0, /device:TPU:1, one launch (start us, length us, event | category | flops | bytes accessed | tf_op | source)
XLA Modules:
  0.0 3016.2 jit_solution(12486487730127264492)
XLA Ops:
  11.2 22.9 all-gather
  37.7 18.4 all_gather.19
  144.9 507.4 %while.48 = (s32[]{:T(128)}, f32[8,8,128]{2,1,0:T(8,128)S(1)}, f32[8,8,128]{2,1,0:T(8,128)S(1)}, f32[8,8,128,64]{2,3,1,0:T(8,128)S(1)}, bf16[8,128,8,64]{1,3,2,0...) while((s32[]{:T(128)}, f32[8,8,128]{2,1,0:T(8,128)S(1)}, ...), condition=%wide.region_8.9_spmd.clone, body=%wide.region_4.8_spmd.clone.sunk | while | flops 951091520 | bytes 33098160 | solution.py:208
  311.7 12.0 collective-permute-done
  345.0 13.8 collective-permute-done
  378.4 15.6 collective-permute-done
  411.8 17.4 collective-permute-done
  445.1 19.2 collective-permute-done
  478.5 21.0 collective-permute-done
  513.3 21.3 collective-permute-done
  548.4 21.3 collective-permute-done
  583.6 21.3 collective-permute-done
  618.8 21.3 collective-permute-done
  662.5 120.8 %all-reduce.7.cloned.1.call-done = f32[8,128,1024]{2,1,0:T(8,128)} async-done(((f32[8,128,1024]{2,1,0:T(8,128)}), f32[8,128,1024]{2,1,0:T(8,128)}) %all-reduce.7.cloned.1.call-update) | async-done | bytes 4194320 | tf_op jit(solution)/shard_map/psum | solution.py:216
  788.8 56.6 %all-gather.10.cloned.1.call-done = bf16[2,1024,1408]{2,1,0:T(8,128)(2,1)} async-done(((bf16[2,64,1408]{2,1,0:T(8,128)(2,1)}), bf16[2,1024,1408]{2,1,0:T(8,128)(2,1)}) %all-gather.10.cloned.1.call-update) | async-done | bytes 5767184 | tf_op jit(solution)/shard_map/all_gather | solution.py:132
  845.4 12.5 convolution_bitcast_fusion
  857.9 32.8 %all-gather.12.cloned.1.call-done = bf16[1408,1024]{0,1:T(8,128)(2,1)} async-done(((bf16[1408,64]{0,1:T(8,128)(2,1)}), bf16[1408,1024]{0,1:T(8,128)(2,1)}) %all-gather.12.cloned.1.call-update) | async-done | bytes 2883600 | tf_op jit(solution)/shard_map/all_gather | solution.py:133
  911.1 61.1 %all-reduce.9.cloned.1.call-done = bf16[8,128,1024]{2,1,0:T(8,128)(2,1)} async-done(((bf16[8,128,1024]{2,1,0:T(8,128)(2,1)}), bf16[8,128,1024]{2,1,0:T(8,128)(2,1)}) %all-reduce.9.cloned.1.call-update) | async-done | bytes 2097168 | tf_op jit(solution)/shard_map/psum | solution.py:246
  994.2 1344.8 %while.49 = (s32[]{:T(128)}, f32[8,128,8,64]{1,3,2,0:T(8,128)}, bf16[8,128,8,64]{1,3,2,0:T(8,128)(2,1)}, bf16[8,128,8,64]{1,3,2,0:T(8,128)(2,1)S(1)}, f32[8,128,...) while((s32[]{:T(128)}, f32[8,128,8,64]{1,3,2,0:T(8,128)}, ...), condition=%wide.region_18.19_spmd.clone, body=%wide.region_16.18_spmd.clone.sunk | while | flops 1354776832 | bytes 90327680 | solution.py:289
  1022.7 43.8 %collective-permute-done.2 = bf16[8,128,8,64]{1,3,2,0:T(8,128)(2,1)} collective-permute-done((bf16[8,128,8,64]{1,3,2,0:T(8,128)(2,1)S(1)}, bf16[8,128,8,64]{1,3,2,0:T(8,128)(2,1)}, u32[]{:S(2)}, u32[]{:S(2)}) %collective-permute-start.2) | collective-permute-done | bytes 1048608 | tf_op jit(solution)/shard_map/while/body/eval_jaxpr/ppermute | solution.py:27
  1066.5 11.3 collective-permute-done.3
  1108.3 42.3 %collective-permute-done.2 = bf16[8,128,8,64]{1,3,2,0:T(8,128)(2,1)} collective-permute-done((bf16[8,128,8,64]{1,3,2,0:T(8,128)(2,1)S(1)}, bf16[8,128,8,64]{1,3,2,0:T(8,128)(2,1)}, u32[]{:S(2)}, u32[]{:S(2)}) %collective-permute-start.2) | collective-permute-done | bytes 1048608 | tf_op jit(solution)/shard_map/while/body/eval_jaxpr/ppermute | solution.py:27
  1150.6 11.3 collective-permute-done.3
  1193.3 41.4 %collective-permute-done.2 = bf16[8,128,8,64]{1,3,2,0:T(8,128)(2,1)} collective-permute-done((bf16[8,128,8,64]{1,3,2,0:T(8,128)(2,1)S(1)}, bf16[8,128,8,64]{1,3,2,0:T(8,128)(2,1)}, u32[]{:S(2)}, u32[]{:S(2)}) %collective-permute-start.2) | collective-permute-done | bytes 1048608 | tf_op jit(solution)/shard_map/while/body/eval_jaxpr/ppermute | solution.py:27
  1234.6 11.3 collective-permute-done.3
  1278.2 40.5 %collective-permute-done.2 = bf16[8,128,8,64]{1,3,2,0:T(8,128)(2,1)} collective-permute-done((bf16[8,128,8,64]{1,3,2,0:T(8,128)(2,1)S(1)}, bf16[8,128,8,64]{1,3,2,0:T(8,128)(2,1)}, u32[]{:S(2)}, u32[]{:S(2)}) %collective-permute-start.2) | collective-permute-done | bytes 1048608 | tf_op jit(solution)/shard_map/while/body/eval_jaxpr/ppermute | solution.py:27
  1318.7 11.3 collective-permute-done.3
  1363.2 39.6 %collective-permute-done.2 = bf16[8,128,8,64]{1,3,2,0:T(8,128)(2,1)} collective-permute-done((bf16[8,128,8,64]{1,3,2,0:T(8,128)(2,1)S(1)}, bf16[8,128,8,64]{1,3,2,0:T(8,128)(2,1)}, u32[]{:S(2)}, u32[]{:S(2)}) %collective-permute-start.2) | collective-permute-done | bytes 1048608 | tf_op jit(solution)/shard_map/while/body/eval_jaxpr/ppermute | solution.py:27
  1402.8 11.3 collective-permute-done.3
  1448.2 38.7 %collective-permute-done.2 = bf16[8,128,8,64]{1,3,2,0:T(8,128)(2,1)} collective-permute-done((bf16[8,128,8,64]{1,3,2,0:T(8,128)(2,1)S(1)}, bf16[8,128,8,64]{1,3,2,0:T(8,128)(2,1)}, u32[]{:S(2)}, u32[]{:S(2)}) %collective-permute-start.2) | collective-permute-done | bytes 1048608 | tf_op jit(solution)/shard_map/while/body/eval_jaxpr/ppermute | solution.py:27
  1486.9 11.3 collective-permute-done.3
  1533.2 37.8 %collective-permute-done.2 = bf16[8,128,8,64]{1,3,2,0:T(8,128)(2,1)} collective-permute-done((bf16[8,128,8,64]{1,3,2,0:T(8,128)(2,1)S(1)}, bf16[8,128,8,64]{1,3,2,0:T(8,128)(2,1)}, u32[]{:S(2)}, u32[]{:S(2)}) %collective-permute-start.2) | collective-permute-done | bytes 1048608 | tf_op jit(solution)/shard_map/while/body/eval_jaxpr/ppermute | solution.py:27
  1571.0 11.3 collective-permute-done.3
  1618.2 36.9 %collective-permute-done.2 = bf16[8,128,8,64]{1,3,2,0:T(8,128)(2,1)} collective-permute-done((bf16[8,128,8,64]{1,3,2,0:T(8,128)(2,1)S(1)}, bf16[8,128,8,64]{1,3,2,0:T(8,128)(2,1)}, u32[]{:S(2)}, u32[]{:S(2)}) %collective-permute-start.2) | collective-permute-done | bytes 1048608 | tf_op jit(solution)/shard_map/while/body/eval_jaxpr/ppermute | solution.py:27
  1655.0 11.3 collective-permute-done.3
  1703.1 36.0 %collective-permute-done.2 = bf16[8,128,8,64]{1,3,2,0:T(8,128)(2,1)} collective-permute-done((bf16[8,128,8,64]{1,3,2,0:T(8,128)(2,1)S(1)}, bf16[8,128,8,64]{1,3,2,0:T(8,128)(2,1)}, u32[]{:S(2)}, u32[]{:S(2)}) %collective-permute-start.2) | collective-permute-done | bytes 1048608 | tf_op jit(solution)/shard_map/while/body/eval_jaxpr/ppermute | solution.py:27
  1739.1 11.3 collective-permute-done.3
  1788.1 35.1 %collective-permute-done.2 = bf16[8,128,8,64]{1,3,2,0:T(8,128)(2,1)} collective-permute-done((bf16[8,128,8,64]{1,3,2,0:T(8,128)(2,1)S(1)}, bf16[8,128,8,64]{1,3,2,0:T(8,128)(2,1)}, u32[]{:S(2)}, u32[]{:S(2)}) %collective-permute-start.2) | collective-permute-done | bytes 1048608 | tf_op jit(solution)/shard_map/while/body/eval_jaxpr/ppermute | solution.py:27
  1823.2 11.3 collective-permute-done.3
  1873.1 34.2 %collective-permute-done.2 = bf16[8,128,8,64]{1,3,2,0:T(8,128)(2,1)} collective-permute-done((bf16[8,128,8,64]{1,3,2,0:T(8,128)(2,1)S(1)}, bf16[8,128,8,64]{1,3,2,0:T(8,128)(2,1)}, u32[]{:S(2)}, u32[]{:S(2)}) %collective-permute-start.2) | collective-permute-done | bytes 1048608 | tf_op jit(solution)/shard_map/while/body/eval_jaxpr/ppermute | solution.py:27
  1907.3 11.3 collective-permute-done.3
  1958.1 33.3 %collective-permute-done.2 = bf16[8,128,8,64]{1,3,2,0:T(8,128)(2,1)} collective-permute-done((bf16[8,128,8,64]{1,3,2,0:T(8,128)(2,1)S(1)}, bf16[8,128,8,64]{1,3,2,0:T(8,128)(2,1)}, u32[]{:S(2)}, u32[]{:S(2)}) %collective-permute-start.2) | collective-permute-done | bytes 1048608 | tf_op jit(solution)/shard_map/while/body/eval_jaxpr/ppermute | solution.py:27
  1991.4 11.3 collective-permute-done.3
  2043.1 32.4 %collective-permute-done.2 = bf16[8,128,8,64]{1,3,2,0:T(8,128)(2,1)} collective-permute-done((bf16[8,128,8,64]{1,3,2,0:T(8,128)(2,1)S(1)}, bf16[8,128,8,64]{1,3,2,0:T(8,128)(2,1)}, u32[]{:S(2)}, u32[]{:S(2)}) %collective-permute-start.2) | collective-permute-done | bytes 1048608 | tf_op jit(solution)/shard_map/while/body/eval_jaxpr/ppermute | solution.py:27
  2075.5 11.3 collective-permute-done.3
  2128.0 31.5 %collective-permute-done.2 = bf16[8,128,8,64]{1,3,2,0:T(8,128)(2,1)} collective-permute-done((bf16[8,128,8,64]{1,3,2,0:T(8,128)(2,1)S(1)}, bf16[8,128,8,64]{1,3,2,0:T(8,128)(2,1)}, u32[]{:S(2)}, u32[]{:S(2)}) %collective-permute-start.2) | collective-permute-done | bytes 1048608 | tf_op jit(solution)/shard_map/while/body/eval_jaxpr/ppermute | solution.py:27
  2159.5 11.3 collective-permute-done.3
  2193.7 10.9 collective-permute-start.5
  2213.0 30.6 %collective-permute-done.2 = bf16[8,128,8,64]{1,3,2,0:T(8,128)(2,1)} collective-permute-done((bf16[8,128,8,64]{1,3,2,0:T(8,128)(2,1)S(1)}, bf16[8,128,8,64]{1,3,2,0:T(8,128)(2,1)}, u32[]{:S(2)}, u32[]{:S(2)}) %collective-permute-start.2) | collective-permute-done | bytes 1048608 | tf_op jit(solution)/shard_map/while/body/eval_jaxpr/ppermute | solution.py:27
  2243.6 11.3 collective-permute-done.3
  2277.8 11.8 collective-permute-start.5
  2298.0 29.7 collective-permute-done.2
  2327.7 11.3 collective-permute-done.3
  2355.9 11.1 convolution_multiply_fusion.5
  2371.4 13.7 convolution_multiply_fusion.1
  2390.2 11.8 fusion.35
  2402.1 15.1 copy.304
  2450.2 10.7 convolution_multiply_fusion
  2486.6 134.4 %all-reduce.11.cloned.1.call-done = bf16[2,1024,1408]{2,0,1:T(2,128)(2,1)} async-done(((bf16[2,1024,1408]{2,0,1:T(2,128)(2,1)}), bf16[2,1024,1408]{2,0,1:T(2,128)(2,1)}) %all-reduce.11.cloned.1.call-update) | async-done | bytes 5767184
  2625.0 55.5 %reduce-scatter.12.cloned.1.call-done = bf16[512,64]{0,1:T(8,128)(2,1)} async-done(((bf16[512,1024]{0,1:T(8,128)(2,1)}), bf16[512,64]{0,1:T(8,128)(2,1)}) %reduce-scatter.12.cloned.1.call-update) | async-done | bytes 65552 | tf_op jit(solution)/shard_map/reduce_scatter | solution.py:345
  2682.4 138.2 %all-reduce.13.cloned.1.call-done = (bf16[8,128,1024]{2,1,0:T(8,128)(2,1)}, bf16[8,128,1024]{2,1,0:T(8,128)(2,1)}, bf16[8,128,640]{2,1,0:T(8,128)(2,1)}) async-done(((bf16[8,128,1024]{2,1,0:T(8,128)(2,1)}, bf16[8,128,1024]{2,1,0:T(8,128)(2,1)}, bf16[8,128,640]{2,1,0:T(8,128)(2,1)}), (bf16[8,128,1024]{2,1,0:T(8,128)(2,1)}, bf16[8,128,1024]{2,1,0:T(8,128)(2,1)}, ...) | async-done | bytes 5505040 | tf_op jit(solution)/shard_map/psum | solution.py:229
  2832.8 55.2 %reduce-scatter.14.cloned.1.call-done = bf16[1408,64]{0,1:T(8,128)(2,1)} async-done(((bf16[1408,1024]{0,1:T(8,128)(2,1)}), bf16[1408,64]{0,1:T(8,128)(2,1)}) %reduce-scatter.14.cloned.1.call-update) | async-done | bytes 180240 | tf_op jit(solution)/shard_map/reduce_scatter | solution.py:351
  2898.8 47.2 %reduce-scatter.16.cloned.1.call-done = bf16[64,2]{1,0:T(8,128)(2,1)} async-done(((bf16[1024,2]{1,0:T(8,128)(2,1)}), bf16[64,2]{1,0:T(8,128)(2,1)}) %reduce-scatter.16.cloned.1.call-update) | async-done | bytes 272
  2947.4 60.1 %reduce-scatter.10.cloned.1.call-done = bf16[64,640]{1,0:T(8,128)(2,1)} async-done(((bf16[1024,640]{1,0:T(8,128)(2,1)}), bf16[64,640]{1,0:T(8,128)(2,1)}) %reduce-scatter.10.cloned.1.call-update) | async-done | bytes 81936 | tf_op jit(solution)/shard_map/reduce_scatter | solution.py:342
  (833 shorter events, 1127.0 us)
Async XLA Ops:
  7.2 59.0 %all-gather.6.cloned.1.call-start = ((), (), s32[]{:S(2)}) async-start(), calls=%async_computation.5 | async-start | bytes 1392640 | tf_op jit(solution)/shard_map/all_gather | solution.py:130
  8.8 644.8 %all-gather.8.cloned.1.call-start = ((), (), s32[]{:S(2)}) async-start(), calls=%async_computation.6 | async-start | bytes 1114112 | tf_op jit(solution)/shard_map/all_gather | solution.py:131
  10.5 772.9 %all-reduce.7.cloned.1.call-start = ((), (), s32[]{:S(2)}) async-start(), calls=%async_computation.7 | async-start | bytes 8388608 | tf_op jit(solution)/shard_map/psum | solution.py:216
  658.6 186.8 %all-gather.10.cloned.1.call-start = ((), (), s32[]{:S(2)}) async-start(), calls=%async_computation.8 | async-start | bytes 6127616 | tf_op jit(solution)/shard_map/all_gather | solution.py:132
  660.5 230.2 %all-gather.12.cloned.1.call-start = ((), (), s32[]{:S(2)}) async-start(), calls=%async_computation.9 | async-start | bytes 3063808 | tf_op jit(solution)/shard_map/all_gather | solution.py:133
  662.3 309.9 %all-reduce.9.cloned.1.call-start = ((), (), s32[]{:S(2)}) async-start(), calls=%async_computation.10 | async-start | bytes 4194304 | tf_op jit(solution)/shard_map/psum | solution.py:246
  911.0 1574.1 %reduce-scatter.8.cloned.1.call-start = ((), (), s32[]{:S(2)}) async-start(), calls=%async_computation.11 | async-start | bytes 278528 | tf_op jit(solution)/shard_map/reduce_scatter | solution.py:339
  1007.7 70.2 %collective-permute-start.4 = (f32[8,128,8,64]{1,3,2,0:T(8,128)}, f32[8,128,8,64]{1,3,2,0:T(8,128)}, u32[]{:S(2)}, u32[]{:S(2)}) collective-permute-start(f32[8,128,8,64]{1,3,2,0:T(8,128)} %bitcast_add_fusion.7), channel_id=1, source_target_pairs={{30,0},{0,2},{2,4},{4,6},{6,8},{8,10},{10,12},{12,14},{14,16},{16,... | collective-permute-start | bytes 6291464 | tf_op jit(solution)/shard_map/while/body/eval_jaxpr/ppermute | solution.py:27
  1016.6 61.2 %collective-permute-start.5 = (f32[8,128,8,64]{1,3,2,0:T(8,128)}, f32[8,128,8,64]{1,3,2,0:T(8,128)}, u32[]{:S(2)}, u32[]{:S(2)}) collective-permute-start(f32[8,128,8,64]{1,3,2,0:T(8,128)} %bitcast_add_fusion.8), channel_id=1, source_target_pairs={{30,0},{0,2},{2,4},{4,6},{6,8},{8,10},{10,12},{12,14},{14,16},{16,... | collective-permute-start | bytes 6291464 | tf_op jit(solution)/shard_map/while/body/eval_jaxpr/ppermute | solution.py:27
  1016.6 49.9 %collective-permute-start.2 = (bf16[8,128,8,64]{1,3,2,0:T(8,128)(2,1)S(1)}, bf16[8,128,8,64]{1,3,2,0:T(8,128)(2,1)}, u32[]{:S(2)}, u32[]{:S(2)}) collective-permute-start(bf16[8,128,8,64]{1,3,2,0:T(8,128)(2,1)S(1)} %copy.368), channel_id=1, source_target_pairs={{30,0},{0,2},{2,4},{4,6},{6,8},{8,10},{10,12},{12,14},{14,16},{16,... | collective-permute-start | bytes 3145736 | tf_op jit(solution)/shard_map/while/body/eval_jaxpr/ppermute | solution.py:27
  1018.2 59.6 %collective-permute-start.3 = (bf16[8,128,8,64]{1,3,2,0:T(8,128)(2,1)}, bf16[8,128,8,64]{1,3,2,0:T(8,128)(2,1)S(1)}, u32[]{:S(2)}, u32[]{:S(2)}) collective-permute-start(bf16[8,128,8,64]{1,3,2,0:T(8,128)(2,1)} %copy.369), channel_id=1, source_target_pairs={{30,0},{0,2},{2,4},{4,6},{6,8},{8,10},{10,12},{12,14},{14,16},{16,... | collective-permute-start | bytes 3145736 | tf_op jit(solution)/shard_map/while/body/eval_jaxpr/ppermute | solution.py:27
  1091.3 70.6 %collective-permute-start.4 = (f32[8,128,8,64]{1,3,2,0:T(8,128)}, f32[8,128,8,64]{1,3,2,0:T(8,128)}, u32[]{:S(2)}, u32[]{:S(2)}) collective-permute-start(f32[8,128,8,64]{1,3,2,0:T(8,128)} %bitcast_add_fusion.7), channel_id=1, source_target_pairs={{30,0},{0,2},{2,4},{4,6},{6,8},{8,10},{10,12},{12,14},{14,16},{16,... | collective-permute-start | bytes 6291464 | tf_op jit(solution)/shard_map/while/body/eval_jaxpr/ppermute | solution.py:27
  1100.7 61.2 %collective-permute-start.5 = (f32[8,128,8,64]{1,3,2,0:T(8,128)}, f32[8,128,8,64]{1,3,2,0:T(8,128)}, u32[]{:S(2)}, u32[]{:S(2)}) collective-permute-start(f32[8,128,8,64]{1,3,2,0:T(8,128)} %bitcast_add_fusion.8), channel_id=1, source_target_pairs={{30,0},{0,2},{2,4},{4,6},{6,8},{8,10},{10,12},{12,14},{14,16},{16,... | collective-permute-start | bytes 6291464 | tf_op jit(solution)/shard_map/while/body/eval_jaxpr/ppermute | solution.py:27
  1100.7 49.9 %collective-permute-start.2 = (bf16[8,128,8,64]{1,3,2,0:T(8,128)(2,1)S(1)}, bf16[8,128,8,64]{1,3,2,0:T(8,128)(2,1)}, u32[]{:S(2)}, u32[]{:S(2)}) collective-permute-start(bf16[8,128,8,64]{1,3,2,0:T(8,128)(2,1)S(1)} %copy.368), channel_id=1, source_target_pairs={{30,0},{0,2},{2,4},{4,6},{6,8},{8,10},{10,12},{12,14},{14,16},{16,... | collective-permute-start | bytes 3145736 | tf_op jit(solution)/shard_map/while/body/eval_jaxpr/ppermute | solution.py:27
  1103.2 58.7 %collective-permute-start.3 = (bf16[8,128,8,64]{1,3,2,0:T(8,128)(2,1)}, bf16[8,128,8,64]{1,3,2,0:T(8,128)(2,1)S(1)}, u32[]{:S(2)}, u32[]{:S(2)}) collective-permute-start(bf16[8,128,8,64]{1,3,2,0:T(8,128)(2,1)} %copy.369), channel_id=1, source_target_pairs={{30,0},{0,2},{2,4},{4,6},{6,8},{8,10},{10,12},{12,14},{14,16},{16,... | collective-permute-start | bytes 3145736 | tf_op jit(solution)/shard_map/while/body/eval_jaxpr/ppermute | solution.py:27
  1175.4 70.6 %collective-permute-start.4 = (f32[8,128,8,64]{1,3,2,0:T(8,128)}, f32[8,128,8,64]{1,3,2,0:T(8,128)}, u32[]{:S(2)}, u32[]{:S(2)}) collective-permute-start(f32[8,128,8,64]{1,3,2,0:T(8,128)} %bitcast_add_fusion.7), channel_id=1, source_target_pairs={{30,0},{0,2},{2,4},{4,6},{6,8},{8,10},{10,12},{12,14},{14,16},{16,... | collective-permute-start | bytes 6291464 | tf_op jit(solution)/shard_map/while/body/eval_jaxpr/ppermute | solution.py:27
  1184.8 61.2 %collective-permute-start.5 = (f32[8,128,8,64]{1,3,2,0:T(8,128)}, f32[8,128,8,64]{1,3,2,0:T(8,128)}, u32[]{:S(2)}, u32[]{:S(2)}) collective-permute-start(f32[8,128,8,64]{1,3,2,0:T(8,128)} %bitcast_add_fusion.8), channel_id=1, source_target_pairs={{30,0},{0,2},{2,4},{4,6},{6,8},{8,10},{10,12},{12,14},{14,16},{16,... | collective-permute-start | bytes 6291464 | tf_op jit(solution)/shard_map/while/body/eval_jaxpr/ppermute | solution.py:27
  1184.9 49.8 %collective-permute-start.2 = (bf16[8,128,8,64]{1,3,2,0:T(8,128)(2,1)S(1)}, bf16[8,128,8,64]{1,3,2,0:T(8,128)(2,1)}, u32[]{:S(2)}, u32[]{:S(2)}) collective-permute-start(bf16[8,128,8,64]{1,3,2,0:T(8,128)(2,1)S(1)} %copy.368), channel_id=1, source_target_pairs={{30,0},{0,2},{2,4},{4,6},{6,8},{8,10},{10,12},{12,14},{14,16},{16,... | collective-permute-start | bytes 3145736 | tf_op jit(solution)/shard_map/while/body/eval_jaxpr/ppermute | solution.py:27
  1188.2 57.8 %collective-permute-start.3 = (bf16[8,128,8,64]{1,3,2,0:T(8,128)(2,1)}, bf16[8,128,8,64]{1,3,2,0:T(8,128)(2,1)S(1)}, u32[]{:S(2)}, u32[]{:S(2)}) collective-permute-start(bf16[8,128,8,64]{1,3,2,0:T(8,128)(2,1)} %copy.369), channel_id=1, source_target_pairs={{30,0},{0,2},{2,4},{4,6},{6,8},{8,10},{10,12},{12,14},{14,16},{16,... | collective-permute-start | bytes 3145736 | tf_op jit(solution)/shard_map/while/body/eval_jaxpr/ppermute | solution.py:27
  1259.5 70.6 %collective-permute-start.4 = (f32[8,128,8,64]{1,3,2,0:T(8,128)}, f32[8,128,8,64]{1,3,2,0:T(8,128)}, u32[]{:S(2)}, u32[]{:S(2)}) collective-permute-start(f32[8,128,8,64]{1,3,2,0:T(8,128)} %bitcast_add_fusion.7), channel_id=1, source_target_pairs={{30,0},{0,2},{2,4},{4,6},{6,8},{8,10},{10,12},{12,14},{14,16},{16,... | collective-permute-start | bytes 6291464 | tf_op jit(solution)/shard_map/while/body/eval_jaxpr/ppermute | solution.py:27
  1268.8 61.2 %collective-permute-start.5 = (f32[8,128,8,64]{1,3,2,0:T(8,128)}, f32[8,128,8,64]{1,3,2,0:T(8,128)}, u32[]{:S(2)}, u32[]{:S(2)}) collective-permute-start(f32[8,128,8,64]{1,3,2,0:T(8,128)} %bitcast_add_fusion.8), channel_id=1, source_target_pairs={{30,0},{0,2},{2,4},{4,6},{6,8},{8,10},{10,12},{12,14},{14,16},{16,... | collective-permute-start | bytes 6291464 | tf_op jit(solution)/shard_map/while/body/eval_jaxpr/ppermute | solution.py:27
  1269.9 48.9 %collective-permute-start.2 = (bf16[8,128,8,64]{1,3,2,0:T(8,128)(2,1)S(1)}, bf16[8,128,8,64]{1,3,2,0:T(8,128)(2,1)}, u32[]{:S(2)}, u32[]{:S(2)}) collective-permute-start(bf16[8,128,8,64]{1,3,2,0:T(8,128)(2,1)S(1)} %copy.368), channel_id=1, source_target_pairs={{30,0},{0,2},{2,4},{4,6},{6,8},{8,10},{10,12},{12,14},{14,16},{16,... | collective-permute-start | bytes 3145736 | tf_op jit(solution)/shard_map/while/body/eval_jaxpr/ppermute | solution.py:27
  1273.1 56.9 %collective-permute-start.3 = (bf16[8,128,8,64]{1,3,2,0:T(8,128)(2,1)}, bf16[8,128,8,64]{1,3,2,0:T(8,128)(2,1)S(1)}, u32[]{:S(2)}, u32[]{:S(2)}) collective-permute-start(bf16[8,128,8,64]{1,3,2,0:T(8,128)(2,1)} %copy.369), channel_id=1, source_target_pairs={{30,0},{0,2},{2,4},{4,6},{6,8},{8,10},{10,12},{12,14},{14,16},{16,... | collective-permute-start | bytes 3145736 | tf_op jit(solution)/shard_map/while/body/eval_jaxpr/ppermute | solution.py:27
  1343.5 70.6 %collective-permute-start.4 = (f32[8,128,8,64]{1,3,2,0:T(8,128)}, f32[8,128,8,64]{1,3,2,0:T(8,128)}, u32[]{:S(2)}, u32[]{:S(2)}) collective-permute-start(f32[8,128,8,64]{1,3,2,0:T(8,128)} %bitcast_add_fusion.7), channel_id=1, source_target_pairs={{30,0},{0,2},{2,4},{4,6},{6,8},{8,10},{10,12},{12,14},{14,16},{16,... | collective-permute-start | bytes 6291464 | tf_op jit(solution)/shard_map/while/body/eval_jaxpr/ppermute | solution.py:27
  1352.9 61.2 %collective-permute-start.5 = (f32[8,128,8,64]{1,3,2,0:T(8,128)}, f32[8,128,8,64]{1,3,2,0:T(8,128)}, u32[]{:S(2)}, u32[]{:S(2)}) collective-permute-start(f32[8,128,8,64]{1,3,2,0:T(8,128)} %bitcast_add_fusion.8), channel_id=1, source_target_pairs={{30,0},{0,2},{2,4},{4,6},{6,8},{8,10},{10,12},{12,14},{14,16},{16,... | collective-permute-start | bytes 6291464 | tf_op jit(solution)/shard_map/while/body/eval_jaxpr/ppermute | solution.py:27
  1354.8 48.0 %collective-permute-start.2 = (bf16[8,128,8,64]{1,3,2,0:T(8,128)(2,1)S(1)}, bf16[8,128,8,64]{1,3,2,0:T(8,128)(2,1)}, u32[]{:S(2)}, u32[]{:S(2)}) collective-permute-start(bf16[8,128,8,64]{1,3,2,0:T(8,128)(2,1)S(1)} %copy.368), channel_id=1, source_target_pairs={{30,0},{0,2},{2,4},{4,6},{6,8},{8,10},{10,12},{12,14},{14,16},{16,... | collective-permute-start | bytes 3145736 | tf_op jit(solution)/shard_map/while/body/eval_jaxpr/ppermute | solution.py:27
  1358.1 56.0 %collective-permute-start.3 = (bf16[8,128,8,64]{1,3,2,0:T(8,128)(2,1)}, bf16[8,128,8,64]{1,3,2,0:T(8,128)(2,1)S(1)}, u32[]{:S(2)}, u32[]{:S(2)}) collective-permute-start(bf16[8,128,8,64]{1,3,2,0:T(8,128)(2,1)} %copy.369), channel_id=1, source_target_pairs={{30,0},{0,2},{2,4},{4,6},{6,8},{8,10},{10,12},{12,14},{14,16},{16,... | collective-permute-start | bytes 3145736 | tf_op jit(solution)/shard_map/while/body/eval_jaxpr/ppermute | solution.py:27
  1427.6 70.6 %collective-permute-start.4 = (f32[8,128,8,64]{1,3,2,0:T(8,128)}, f32[8,128,8,64]{1,3,2,0:T(8,128)}, u32[]{:S(2)}, u32[]{:S(2)}) collective-permute-start(f32[8,128,8,64]{1,3,2,0:T(8,128)} %bitcast_add_fusion.7), channel_id=1, source_target_pairs={{30,0},{0,2},{2,4},{4,6},{6,8},{8,10},{10,12},{12,14},{14,16},{16,... | collective-permute-start | bytes 6291464 | tf_op jit(solution)/shard_map/while/body/eval_jaxpr/ppermute | solution.py:27
  1437.0 61.2 %collective-permute-start.5 = (f32[8,128,8,64]{1,3,2,0:T(8,128)}, f32[8,128,8,64]{1,3,2,0:T(8,128)}, u32[]{:S(2)}, u32[]{:S(2)}) collective-permute-start(f32[8,128,8,64]{1,3,2,0:T(8,128)} %bitcast_add_fusion.8), channel_id=1, source_target_pairs={{30,0},{0,2},{2,4},{4,6},{6,8},{8,10},{10,12},{12,14},{14,16},{16,... | collective-permute-start | bytes 6291464 | tf_op jit(solution)/shard_map/while/body/eval_jaxpr/ppermute | solution.py:27
  1443.1 55.1 %collective-permute-start.3 = (bf16[8,128,8,64]{1,3,2,0:T(8,128)(2,1)}, bf16[8,128,8,64]{1,3,2,0:T(8,128)(2,1)S(1)}, u32[]{:S(2)}, u32[]{:S(2)}) collective-permute-start(bf16[8,128,8,64]{1,3,2,0:T(8,128)(2,1)} %copy.369), channel_id=1, source_target_pairs={{30,0},{0,2},{2,4},{4,6},{6,8},{8,10},{10,12},{12,14},{14,16},{16,... | collective-permute-start | bytes 3145736 | tf_op jit(solution)/shard_map/while/body/eval_jaxpr/ppermute | solution.py:27
  1511.7 70.6 %collective-permute-start.4 = (f32[8,128,8,64]{1,3,2,0:T(8,128)}, f32[8,128,8,64]{1,3,2,0:T(8,128)}, u32[]{:S(2)}, u32[]{:S(2)}) collective-permute-start(f32[8,128,8,64]{1,3,2,0:T(8,128)} %bitcast_add_fusion.7), channel_id=1, source_target_pairs={{30,0},{0,2},{2,4},{4,6},{6,8},{8,10},{10,12},{12,14},{14,16},{16,... | collective-permute-start | bytes 6291464 | tf_op jit(solution)/shard_map/while/body/eval_jaxpr/ppermute | solution.py:27
  1521.1 61.2 %collective-permute-start.5 = (f32[8,128,8,64]{1,3,2,0:T(8,128)}, f32[8,128,8,64]{1,3,2,0:T(8,128)}, u32[]{:S(2)}, u32[]{:S(2)}) collective-permute-start(f32[8,128,8,64]{1,3,2,0:T(8,128)} %bitcast_add_fusion.8), channel_id=1, source_target_pairs={{30,0},{0,2},{2,4},{4,6},{6,8},{8,10},{10,12},{12,14},{14,16},{16,... | collective-permute-start | bytes 6291464 | tf_op jit(solution)/shard_map/while/body/eval_jaxpr/ppermute | solution.py:27
  1528.1 54.2 %collective-permute-start.3 = (bf16[8,128,8,64]{1,3,2,0:T(8,128)(2,1)}, bf16[8,128,8,64]{1,3,2,0:T(8,128)(2,1)S(1)}, u32[]{:S(2)}, u32[]{:S(2)}) collective-permute-start(bf16[8,128,8,64]{1,3,2,0:T(8,128)(2,1)} %copy.369), channel_id=1, source_target_pairs={{30,0},{0,2},{2,4},{4,6},{6,8},{8,10},{10,12},{12,14},{14,16},{16,... | collective-permute-start | bytes 3145736 | tf_op jit(solution)/shard_map/while/body/eval_jaxpr/ppermute | solution.py:27
  1595.8 70.6 %collective-permute-start.4 = (f32[8,128,8,64]{1,3,2,0:T(8,128)}, f32[8,128,8,64]{1,3,2,0:T(8,128)}, u32[]{:S(2)}, u32[]{:S(2)}) collective-permute-start(f32[8,128,8,64]{1,3,2,0:T(8,128)} %bitcast_add_fusion.7), channel_id=1, source_target_pairs={{30,0},{0,2},{2,4},{4,6},{6,8},{8,10},{10,12},{12,14},{14,16},{16,... | collective-permute-start | bytes 6291464 | tf_op jit(solution)/shard_map/while/body/eval_jaxpr/ppermute | solution.py:27
  1605.2 61.2 %collective-permute-start.5 = (f32[8,128,8,64]{1,3,2,0:T(8,128)}, f32[8,128,8,64]{1,3,2,0:T(8,128)}, u32[]{:S(2)}, u32[]{:S(2)}) collective-permute-start(f32[8,128,8,64]{1,3,2,0:T(8,128)} %bitcast_add_fusion.8), channel_id=1, source_target_pairs={{30,0},{0,2},{2,4},{4,6},{6,8},{8,10},{10,12},{12,14},{14,16},{16,... | collective-permute-start | bytes 6291464 | tf_op jit(solution)/shard_map/while/body/eval_jaxpr/ppermute | solution.py:27
  1613.1 53.3 %collective-permute-start.3 = (bf16[8,128,8,64]{1,3,2,0:T(8,128)(2,1)}, bf16[8,128,8,64]{1,3,2,0:T(8,128)(2,1)S(1)}, u32[]{:S(2)}, u32[]{:S(2)}) collective-permute-start(bf16[8,128,8,64]{1,3,2,0:T(8,128)(2,1)} %copy.369), channel_id=1, source_target_pairs={{30,0},{0,2},{2,4},{4,6},{6,8},{8,10},{10,12},{12,14},{14,16},{16,... | collective-permute-start | bytes 3145736 | tf_op jit(solution)/shard_map/while/body/eval_jaxpr/ppermute | solution.py:27
  1679.9 70.6 %collective-permute-start.4 = (f32[8,128,8,64]{1,3,2,0:T(8,128)}, f32[8,128,8,64]{1,3,2,0:T(8,128)}, u32[]{:S(2)}, u32[]{:S(2)}) collective-permute-start(f32[8,128,8,64]{1,3,2,0:T(8,128)} %bitcast_add_fusion.7), channel_id=1, source_target_pairs={{30,0},{0,2},{2,4},{4,6},{6,8},{8,10},{10,12},{12,14},{14,16},{16,... | collective-permute-start | bytes 6291464 | tf_op jit(solution)/shard_map/while/body/eval_jaxpr/ppermute | solution.py:27
  1689.2 61.2 %collective-permute-start.5 = (f32[8,128,8,64]{1,3,2,0:T(8,128)}, f32[8,128,8,64]{1,3,2,0:T(8,128)}, u32[]{:S(2)}, u32[]{:S(2)}) collective-permute-start(f32[8,128,8,64]{1,3,2,0:T(8,128)} %bitcast_add_fusion.8), channel_id=1, source_target_pairs={{30,0},{0,2},{2,4},{4,6},{6,8},{8,10},{10,12},{12,14},{14,16},{16,... | collective-permute-start | bytes 6291464 | tf_op jit(solution)/shard_map/while/body/eval_jaxpr/ppermute | solution.py:27
  1698.0 52.4 %collective-permute-start.3 = (bf16[8,128,8,64]{1,3,2,0:T(8,128)(2,1)}, bf16[8,128,8,64]{1,3,2,0:T(8,128)(2,1)S(1)}, u32[]{:S(2)}, u32[]{:S(2)}) collective-permute-start(bf16[8,128,8,64]{1,3,2,0:T(8,128)(2,1)} %copy.369), channel_id=1, source_target_pairs={{30,0},{0,2},{2,4},{4,6},{6,8},{8,10},{10,12},{12,14},{14,16},{16,... | collective-permute-start | bytes 3145736 | tf_op jit(solution)/shard_map/while/body/eval_jaxpr/ppermute | solution.py:27
  1763.9 70.6 %collective-permute-start.4 = (f32[8,128,8,64]{1,3,2,0:T(8,128)}, f32[8,128,8,64]{1,3,2,0:T(8,128)}, u32[]{:S(2)}, u32[]{:S(2)}) collective-permute-start(f32[8,128,8,64]{1,3,2,0:T(8,128)} %bitcast_add_fusion.7), channel_id=1, source_target_pairs={{30,0},{0,2},{2,4},{4,6},{6,8},{8,10},{10,12},{12,14},{14,16},{16,... | collective-permute-start | bytes 6291464 | tf_op jit(solution)/shard_map/while/body/eval_jaxpr/ppermute | solution.py:27
  1773.3 61.2 %collective-permute-start.5 = (f32[8,128,8,64]{1,3,2,0:T(8,128)}, f32[8,128,8,64]{1,3,2,0:T(8,128)}, u32[]{:S(2)}, u32[]{:S(2)}) collective-permute-start(f32[8,128,8,64]{1,3,2,0:T(8,128)} %bitcast_add_fusion.8), channel_id=1, source_target_pairs={{30,0},{0,2},{2,4},{4,6},{6,8},{8,10},{10,12},{12,14},{14,16},{16,... | collective-permute-start | bytes 6291464 | tf_op jit(solution)/shard_map/while/body/eval_jaxpr/ppermute | solution.py:27
  1783.0 51.5 %collective-permute-start.3 = (bf16[8,128,8,64]{1,3,2,0:T(8,128)(2,1)}, bf16[8,128,8,64]{1,3,2,0:T(8,128)(2,1)S(1)}, u32[]{:S(2)}, u32[]{:S(2)}) collective-permute-start(bf16[8,128,8,64]{1,3,2,0:T(8,128)(2,1)} %copy.369), channel_id=1, source_target_pairs={{30,0},{0,2},{2,4},{4,6},{6,8},{8,10},{10,12},{12,14},{14,16},{16,... | collective-permute-start | bytes 3145736 | tf_op jit(solution)/shard_map/while/body/eval_jaxpr/ppermute | solution.py:27
  1848.0 70.6 %collective-permute-start.4 = (f32[8,128,8,64]{1,3,2,0:T(8,128)}, f32[8,128,8,64]{1,3,2,0:T(8,128)}, u32[]{:S(2)}, u32[]{:S(2)}) collective-permute-start(f32[8,128,8,64]{1,3,2,0:T(8,128)} %bitcast_add_fusion.7), channel_id=1, source_target_pairs={{30,0},{0,2},{2,4},{4,6},{6,8},{8,10},{10,12},{12,14},{14,16},{16,... | collective-permute-start | bytes 6291464 | tf_op jit(solution)/shard_map/while/body/eval_jaxpr/ppermute | solution.py:27
  1857.4 61.2 %collective-permute-start.5 = (f32[8,128,8,64]{1,3,2,0:T(8,128)}, f32[8,128,8,64]{1,3,2,0:T(8,128)}, u32[]{:S(2)}, u32[]{:S(2)}) collective-permute-start(f32[8,128,8,64]{1,3,2,0:T(8,128)} %bitcast_add_fusion.8), channel_id=1, source_target_pairs={{30,0},{0,2},{2,4},{4,6},{6,8},{8,10},{10,12},{12,14},{14,16},{16,... | collective-permute-start | bytes 6291464 | tf_op jit(solution)/shard_map/while/body/eval_jaxpr/ppermute | solution.py:27
  1868.0 50.6 %collective-permute-start.3 = (bf16[8,128,8,64]{1,3,2,0:T(8,128)(2,1)}, bf16[8,128,8,64]{1,3,2,0:T(8,128)(2,1)S(1)}, u32[]{:S(2)}, u32[]{:S(2)}) collective-permute-start(bf16[8,128,8,64]{1,3,2,0:T(8,128)(2,1)} %copy.369), channel_id=1, source_target_pairs={{30,0},{0,2},{2,4},{4,6},{6,8},{8,10},{10,12},{12,14},{14,16},{16,... | collective-permute-start | bytes 3145736 | tf_op jit(solution)/shard_map/while/body/eval_jaxpr/ppermute | solution.py:27
  1932.1 70.6 %collective-permute-start.4 = (f32[8,128,8,64]{1,3,2,0:T(8,128)}, f32[8,128,8,64]{1,3,2,0:T(8,128)}, u32[]{:S(2)}, u32[]{:S(2)}) collective-permute-start(f32[8,128,8,64]{1,3,2,0:T(8,128)} %bitcast_add_fusion.7), channel_id=1, source_target_pairs={{30,0},{0,2},{2,4},{4,6},{6,8},{8,10},{10,12},{12,14},{14,16},{16,... | collective-permute-start | bytes 6291464 | tf_op jit(solution)/shard_map/while/body/eval_jaxpr/ppermute | solution.py:27
  1941.5 61.2 %collective-permute-start.5 = (f32[8,128,8,64]{1,3,2,0:T(8,128)}, f32[8,128,8,64]{1,3,2,0:T(8,128)}, u32[]{:S(2)}, u32[]{:S(2)}) collective-permute-start(f32[8,128,8,64]{1,3,2,0:T(8,128)} %bitcast_add_fusion.8), channel_id=1, source_target_pairs={{30,0},{0,2},{2,4},{4,6},{6,8},{8,10},{10,12},{12,14},{14,16},{16,... | collective-permute-start | bytes 6291464 | tf_op jit(solution)/shard_map/while/body/eval_jaxpr/ppermute | solution.py:27
  1953.0 49.7 %collective-permute-start.3 = (bf16[8,128,8,64]{1,3,2,0:T(8,128)(2,1)}, bf16[8,128,8,64]{1,3,2,0:T(8,128)(2,1)S(1)}, u32[]{:S(2)}, u32[]{:S(2)}) collective-permute-start(bf16[8,128,8,64]{1,3,2,0:T(8,128)(2,1)} %copy.369), channel_id=1, source_target_pairs={{30,0},{0,2},{2,4},{4,6},{6,8},{8,10},{10,12},{12,14},{14,16},{16,... | collective-permute-start | bytes 3145736 | tf_op jit(solution)/shard_map/while/body/eval_jaxpr/ppermute | solution.py:27
  2016.2 70.6 %collective-permute-start.4 = (f32[8,128,8,64]{1,3,2,0:T(8,128)}, f32[8,128,8,64]{1,3,2,0:T(8,128)}, u32[]{:S(2)}, u32[]{:S(2)}) collective-permute-start(f32[8,128,8,64]{1,3,2,0:T(8,128)} %bitcast_add_fusion.7), channel_id=1, source_target_pairs={{30,0},{0,2},{2,4},{4,6},{6,8},{8,10},{10,12},{12,14},{14,16},{16,... | collective-permute-start | bytes 6291464 | tf_op jit(solution)/shard_map/while/body/eval_jaxpr/ppermute | solution.py:27
  2025.6 61.2 %collective-permute-start.5 = (f32[8,128,8,64]{1,3,2,0:T(8,128)}, f32[8,128,8,64]{1,3,2,0:T(8,128)}, u32[]{:S(2)}, u32[]{:S(2)}) collective-permute-start(f32[8,128,8,64]{1,3,2,0:T(8,128)} %bitcast_add_fusion.8), channel_id=1, source_target_pairs={{30,0},{0,2},{2,4},{4,6},{6,8},{8,10},{10,12},{12,14},{14,16},{16,... | collective-permute-start | bytes 6291464 | tf_op jit(solution)/shard_map/while/body/eval_jaxpr/ppermute | solution.py:27
  2038.0 48.8 %collective-permute-start.3 = (bf16[8,128,8,64]{1,3,2,0:T(8,128)(2,1)}, bf16[8,128,8,64]{1,3,2,0:T(8,128)(2,1)S(1)}, u32[]{:S(2)}, u32[]{:S(2)}) collective-permute-start(bf16[8,128,8,64]{1,3,2,0:T(8,128)(2,1)} %copy.369), channel_id=1, source_target_pairs={{30,0},{0,2},{2,4},{4,6},{6,8},{8,10},{10,12},{12,14},{14,16},{16,... | collective-permute-start | bytes 3145736 | tf_op jit(solution)/shard_map/while/body/eval_jaxpr/ppermute | solution.py:27
  2100.3 70.6 %collective-permute-start.4 = (f32[8,128,8,64]{1,3,2,0:T(8,128)}, f32[8,128,8,64]{1,3,2,0:T(8,128)}, u32[]{:S(2)}, u32[]{:S(2)}) collective-permute-start(f32[8,128,8,64]{1,3,2,0:T(8,128)} %bitcast_add_fusion.7), channel_id=1, source_target_pairs={{30,0},{0,2},{2,4},{4,6},{6,8},{8,10},{10,12},{12,14},{14,16},{16,... | collective-permute-start | bytes 6291464 | tf_op jit(solution)/shard_map/while/body/eval_jaxpr/ppermute | solution.py:27
  2109.7 61.2 %collective-permute-start.5 = (f32[8,128,8,64]{1,3,2,0:T(8,128)}, f32[8,128,8,64]{1,3,2,0:T(8,128)}, u32[]{:S(2)}, u32[]{:S(2)}) collective-permute-start(f32[8,128,8,64]{1,3,2,0:T(8,128)} %bitcast_add_fusion.8), channel_id=1, source_target_pairs={{30,0},{0,2},{2,4},{4,6},{6,8},{8,10},{10,12},{12,14},{14,16},{16,... | collective-permute-start | bytes 6291464 | tf_op jit(solution)/shard_map/while/body/eval_jaxpr/ppermute | solution.py:27
  2122.9 47.9 %collective-permute-start.3 = (bf16[8,128,8,64]{1,3,2,0:T(8,128)(2,1)}, bf16[8,128,8,64]{1,3,2,0:T(8,128)(2,1)S(1)}, u32[]{:S(2)}, u32[]{:S(2)}) collective-permute-start(bf16[8,128,8,64]{1,3,2,0:T(8,128)(2,1)} %copy.369), channel_id=1, source_target_pairs={{30,0},{0,2},{2,4},{4,6},{6,8},{8,10},{10,12},{12,14},{14,16},{16,... | collective-permute-start | bytes 3145736 | tf_op jit(solution)/shard_map/while/body/eval_jaxpr/ppermute | solution.py:27
  2184.3 70.6 %collective-permute-start.4 = (f32[8,128,8,64]{1,3,2,0:T(8,128)}, f32[8,128,8,64]{1,3,2,0:T(8,128)}, u32[]{:S(2)}, u32[]{:S(2)}) collective-permute-start(f32[8,128,8,64]{1,3,2,0:T(8,128)} %bitcast_add_fusion.7), channel_id=1, source_target_pairs={{30,0},{0,2},{2,4},{4,6},{6,8},{8,10},{10,12},{12,14},{14,16},{16,... | collective-permute-start | bytes 6291464 | tf_op jit(solution)/shard_map/while/body/eval_jaxpr/ppermute | solution.py:27
  2193.7 61.2 %collective-permute-start.5 = (f32[8,128,8,64]{1,3,2,0:T(8,128)}, f32[8,128,8,64]{1,3,2,0:T(8,128)}, u32[]{:S(2)}, u32[]{:S(2)}) collective-permute-start(f32[8,128,8,64]{1,3,2,0:T(8,128)} %bitcast_add_fusion.8), channel_id=1, source_target_pairs={{30,0},{0,2},{2,4},{4,6},{6,8},{8,10},{10,12},{12,14},{14,16},{16,... | collective-permute-start | bytes 6291464 | tf_op jit(solution)/shard_map/while/body/eval_jaxpr/ppermute | solution.py:27
  2268.4 70.6 %collective-permute-start.4 = (f32[8,128,8,64]{1,3,2,0:T(8,128)}, f32[8,128,8,64]{1,3,2,0:T(8,128)}, u32[]{:S(2)}, u32[]{:S(2)}) collective-permute-start(f32[8,128,8,64]{1,3,2,0:T(8,128)} %bitcast_add_fusion.7), channel_id=1, source_target_pairs={{30,0},{0,2},{2,4},{4,6},{6,8},{8,10},{10,12},{12,14},{14,16},{16,... | collective-permute-start | bytes 6291464 | tf_op jit(solution)/shard_map/while/body/eval_jaxpr/ppermute | solution.py:27
  2277.8 61.2 %collective-permute-start.5 = (f32[8,128,8,64]{1,3,2,0:T(8,128)}, f32[8,128,8,64]{1,3,2,0:T(8,128)}, u32[]{:S(2)}, u32[]{:S(2)}) collective-permute-start(f32[8,128,8,64]{1,3,2,0:T(8,128)} %bitcast_add_fusion.8), channel_id=1, source_target_pairs={{30,0},{0,2},{2,4},{4,6},{6,8},{8,10},{10,12},{12,14},{14,16},{16,... | collective-permute-start | bytes 6291464 | tf_op jit(solution)/shard_map/while/body/eval_jaxpr/ppermute | solution.py:27
  2390.2 230.8 %all-reduce.11.cloned.1.call-start = ((), (), s32[]{:S(2)}) async-start(), calls=%async_computation.16 | async-start | bytes 11534336
  2417.2 263.3 %reduce-scatter.12.cloned.1.call-start = ((), (), s32[]{:S(2)}) async-start(), calls=%async_computation.13 | async-start | bytes 1114112 | tf_op jit(solution)/shard_map/reduce_scatter | solution.py:345
  2442.1 378.5 %all-reduce.13.cloned.1.call-start = ((), (), s32[]{:S(2)}) async-start(), calls=%async_computation.17 | async-start | bytes 11010048 | tf_op jit(solution)/shard_map/psum | solution.py:229
  2475.8 412.1 %reduce-scatter.14.cloned.1.call-start = ((), (), s32[]{:S(2)}) async-start(), calls=%async_computation.14 | async-start | bytes 3063808 | tf_op jit(solution)/shard_map/reduce_scatter | solution.py:351
  2483.8 462.2 %reduce-scatter.16.cloned.1.call-start = ((), (), s32[]{:S(2)}) async-start(), calls=%async_computation.15 | async-start | bytes 278528
  2828.2 179.3 %reduce-scatter.10.cloned.1.call-start = ((), (), s32[]{:S(2)}) async-start(), calls=%async_computation.12 | async-start | bytes 1392640 | tf_op jit(solution)/shard_map/reduce_scatter | solution.py:342
  (148 other events, 2999.2 us)
Sparse Core Ops, SparseCore 0:
  10.9 41.6 all-gather.5
  55.3 36.7 all-gather.7
  658.7 124.6 all-reduce.6
  786.1 59.2 all-gather.9
  848.1 42.5 all-gather.11
  911.1 61.0 all-reduce.8
  2390.3 93.6 reduce-scatter.7
  2487.7 133.1 all-reduce.10
  2624.6 55.8 reduce-scatter.11
  2683.5 136.9 all-reduce.12
  2824.3 63.5 reduce-scatter.13
  2891.3 54.6 reduce-scatter.15
  2949.6 57.8 reduce-scatter.9
where the time goes:
time: 3030 us; the launch traced here: 3020 us
  waiting for transfers between devices  1790 us (59%)
  matrix products  612 us (20%)
  local copies, waits for them, and re-layouts  216 us (7%)
  starting transfers between devices  207 us (7%)
  other arithmetic  107 us (4%)
  blocking collectives  41.3 us (1%)
    ppermute x94, waiting for transfers between devices, passed_along(): return lax.ppermute(block, axis, route)  1030 us
    ppermute x94, starting transfers between devices, passed_along(): return lax.ppermute(block, axis, route)  206 us
    unnamed x15, waiting for transfers between devices  182 us
    psum x1, waiting for transfers between devices, on_device(): lax.psum(ffn_part.astype(jnp.bfloat16), 'head').astype(jnp.float32)  138 us
    while x173, local copies, waits for them, and re-layouts  125 us
    psum x1, waiting for transfers between devices, on_device(): attn_total = lax.psum(attn_part, 'head')  121 us
    dot_general x16, matrix products, back_block(): jnp.einsum('shqk,sqhe->skhe', probs, heads_grad_wide, precision=MAXIMAL_P...  112 us
    dot_general x16, matrix products, back_block(): jnp.einsum('shqk,skhe->sqhe', score_grad, key_rows, preferred_element_typ...  80.6 us
  transfers between devices with their start and end apart: 107, of which 64 were waited for; matrix products, arithmetic and copies ran while one was open for 21% of the time, Pallas kernels for 0%

commit v1 on v0

v1 whole, which is shorter than its diff:
```python
import functools

import jax
import jax.numpy as jnp
from jax import lax
from jax.experimental import pallas as pl
from jax.experimental.pallas import tpu as pltpu
from jax.sharding import Mesh
from jax.sharding import PartitionSpec as P

D = 1024
H = 16
DH = 64
RQ = 6
RK = 2
RA = RQ + 2 * RK
FF = 2816
STEP = 10
HB = 4

EPSILON = 1e-05
BETA_ONE = 0.9
BETA_TWO = 0.95
ADAM_EPS = 1e-08
DECAY = 0.1
NEGATIVE = -1e30
SCALE = DH ** (-0.5)
BF = jnp.bfloat16
F32 = jnp.float32
SEQ = ("a", "b", "c")


def rope_tables(positions):
    half_dim = DH // 2
    frequency = 10000.0 ** (-(2.0 * jnp.arange(half_dim, dtype=F32)) / DH)
    angles = frequency[:, None] * positions.astype(F32)[None, :]
    return (jnp.cos(angles), jnp.sin(angles))


def normalize(row_data):
    inverse = lax.rsqrt(jnp.mean(row_data * row_data, -1, keepdims=True) + EPSILON)
    return (row_data * inverse, inverse)


def norm_back(normed_grad, gain_row, hat_rows, inverse):
    hat_grad = normed_grad * gain_row
    return inverse * (hat_grad - hat_rows * jnp.mean(hat_grad * hat_rows, -1, keepdims=True))


def adam_update(master, mean_old, square_old, gradient, rate):
    mean_new = BETA_ONE * mean_old + (1.0 - BETA_ONE) * gradient
    square_new = BETA_TWO * square_old + (1.0 - BETA_TWO) * gradient * gradient
    mean_hat = mean_new / (1.0 - BETA_ONE**STEP)
    square_hat = square_new / (1.0 - BETA_TWO**STEP)
    master_new = master - rate * (mean_hat / (jnp.sqrt(square_hat) + ADAM_EPS) + DECAY * master)
    return (master_new, mean_new, square_new)


def step_rates():
    return (
        2.5 * (D // 4) ** (-0.5),
        2.5 * D ** (-0.5),
        2.5 * (H * DH // 32) ** (-0.5),
        2.5 * D ** (-0.5),
        2.5 * FF ** (-0.5),
        0.5,
    )


def rotated(pair, cos_t, sin_t):
    u = pair[: DH // 2]
    w = pair[DH // 2 :]
    return jnp.concatenate([u * cos_t - w * sin_t, w * cos_t + u * sin_t], axis=0)


def unrotated(pair, cos_t, sin_t):
    u = pair[: DH // 2]
    w = pair[DH // 2 :]
    return jnp.concatenate([u * cos_t + w * sin_t, w * cos_t - u * sin_t], axis=0)


def prologue_body(f_ref, cos_ref, sin_ref, q_ref, fac_ref):
    cos_t = cos_ref[...]
    sin_t = sin_ref[...]
    base = H * RA
    bq = [
        rotated(f_ref[0, base + r * DH : base + (r + 1) * DH, :], cos_t, sin_t) for r in range(RQ)
    ]
    for pair in range(H // 2):
        parts = []
        for h in (2 * pair, 2 * pair + 1):
            acc = f_ref[0, h * RA : h * RA + 1, :] * bq[0]
            for r in range(1, RQ):
                acc = acc + f_ref[0, h * RA + r : h * RA + r + 1, :] * bq[r]
            parts.append(acc)
        both = jnp.concatenate(parts, axis=0) / RQ
        rows = jnp.transpose(both).astype(BF) * SCALE
        q_ref[0, :, pair * 2 * DH : (pair + 1) * 2 * DH] = rows.astype(BF)
    for r in range(RK):
        at = base + (RQ + r) * DH
        fac_ref[0, r * 2 * DH : r * 2 * DH + DH, :] = rotated(
            f_ref[0, at : at + DH, :], cos_t, sin_t
        ).astype(BF)
        at = base + (RQ + RK + r) * DH
        fac_ref[0, r * 2 * DH + DH : (r + 1) * 2 * DH, :] = f_ref[0, at : at + DH, :].astype(BF)
    rows = [f_ref[0, h * RA + RQ : (h + 1) * RA, :] for h in range(H)]
    fac_ref[0, RK * 2 * DH :, :] = (jnp.concatenate(rows, axis=0) * (1.0 / RK)).astype(BF)


FAC = RK * 2 * DH + 2 * RK * H


def prologue(factors, cos_t, sin_t):
    count, width, block = factors.shape
    return pl.pallas_call(
        prologue_body,
        grid=(count,),
        in_specs=[
            pl.BlockSpec((1, width, block), lambda s: (s, 0, 0)),
            pl.BlockSpec((DH // 2, block), lambda s: (0, 0)),
            pl.BlockSpec((DH // 2, block), lambda s: (0, 0)),
        ],
        out_specs=[
            pl.BlockSpec((1, block, H * DH), lambda s: (s, 0, 0)),
            pl.BlockSpec((1, FAC, block), lambda s: (s, 0, 0)),
        ],
        out_shape=[
            jax.ShapeDtypeStruct((count, block, H * DH), BF),
            jax.ShapeDtypeStruct((count, FAC, block), BF),
        ],
        name="factor_prologue",
    )(factors, cos_t, sin_t)


def epilogue_body(dq_ref, df_ref, f_ref, cos_ref, sin_ref, g_ref):
    cos_t = cos_ref[...]
    sin_t = sin_ref[...]
    base = H * RA
    bq = [
        rotated(f_ref[0, base + r * DH : base + (r + 1) * DH, :], cos_t, sin_t) for r in range(RQ)
    ]
    sums = [None] * RQ
    rows = []
    wide = RK * 2 * DH
    for pair in range(H // 2):
        both = jnp.transpose(dq_ref[0, :, pair * 2 * DH : (pair + 1) * 2 * DH])
        for k in range(2):
            h = 2 * pair + k
            dq = both[k * DH : (k + 1) * DH] * (1.0 / RQ)
            for r in range(RQ):
                rows.append(jnp.sum(dq * bq[r], axis=0, keepdims=True))
                term = f_ref[0, h * RA + r : h * RA + r + 1, :] * dq
                sums[r] = term if sums[r] is None else sums[r] + term
            rows.append(df_ref[0, wide + h * 2 * RK : wide + (h + 1) * 2 * RK, :].astype(F32))
    g_ref[0, :base, :] = jnp.concatenate(rows, axis=0).astype(BF)
    for r in range(RQ):
        g_ref[0, base + r * DH : base + (r + 1) * DH, :] = unrotated(sums[r], cos_t, sin_t).astype(BF)
    for r in range(RK):
        at = base + (RQ + r) * DH
        part = df_ref[0, r * 2 * DH : (r + 1) * 2 * DH, :].astype(F32)
        g_ref[0, at : at + DH, :] = unrotated(part[:DH], cos_t, sin_t).astype(BF)
        at = base + (RQ + RK + r) * DH
        g_ref[0, at : at + DH, :] = part[DH:].astype(BF)


def epilogue(query_grad, factor_grad, factors, cos_t, sin_t):
    count, width, block = factors.shape
    return pl.pallas_call(
        epilogue_body,
        grid=(count,),
        in_specs=[
            pl.BlockSpec((1, block, H * DH), lambda s: (s, 0, 0)),
            pl.BlockSpec((1, FAC, block), lambda s: (s, 0, 0)),
            pl.BlockSpec((1, width, block), lambda s: (s, 0, 0)),
            pl.BlockSpec((DH // 2, block), lambda s: (0, 0)),
            pl.BlockSpec((DH // 2, block), lambda s: (0, 0)),
        ],
        out_specs=pl.BlockSpec((1, width, block), lambda s: (s, 0, 0)),
        out_shape=jax.ShapeDtypeStruct((count, width, block), BF),
        name="factor_epilogue",
    )(query_grad, factor_grad, factors, cos_t, sin_t)


def keys_values(a_rows, b_rows, h):
    a = a_rows[4 * h : 4 * h + 4]
    key_t = a[0:1] * b_rows[:DH] + a[1:2] * b_rows[2 * DH : 3 * DH]
    value_t = a[2:3] * b_rows[DH : 2 * DH] + a[3:4] * b_rows[3 * DH :]
    return key_t.astype(BF), value_t.astype(BF)


NT = (((1,), (1,)), ((), ()))
TN = (((0,), (0,)), ((), ()))


def forward_body(q_ref, b_ref, a_ref, kpos_ref, qpos_ref, o_ref, lse_ref):
    allowed = kpos_ref[...] <= qpos_ref[...]
    b_rows = b_ref[0].astype(F32)
    a_rows = a_ref[0].astype(F32)
    outs = []
    stats = []
    for h in range(HB):
        key_t, value_t = keys_values(a_rows, b_rows, h)
        scores = jnp.dot(q_ref[0, :, h * DH : (h + 1) * DH], key_t, preferred_element_type=F32)
        scores = jnp.where(allowed, scores, NEGATIVE)
        best = jnp.max(scores, axis=1, keepdims=True)
        probs = jnp.exp(scores - best)
        total = jnp.sum(probs, axis=1, keepdims=True)
        part = lax.dot_general(probs.astype(BF), value_t, NT, preferred_element_type=F32)
        outs.append(part / total)
        stats.append(best + jnp.log(total))
    o_ref[0] = jnp.concatenate(outs, axis=1)
    lse_ref[0, 0] = jnp.concatenate(stats, axis=1)


def attention_forward(query, gathered, key_pos, query_pos):
    count, block, width = query.shape
    length = gathered.shape[2]
    wide = RK * 2 * DH
    return pl.pallas_call(
        forward_body,
        grid=(count, H // HB),
        in_specs=[
            pl.BlockSpec((1, block, HB * DH), lambda s, g: (s, 0, g)),
            pl.BlockSpec((1, wide, length), lambda s, g: (s, 0, 0)),
            pl.BlockSpec((1, 4 * HB, length), lambda s, g: (s, wide // (4 * HB) + g, 0)),
            pl.BlockSpec((1, length), lambda s, g: (0, 0)),
            pl.BlockSpec((block, 1), lambda s, g: (0, 0)),
        ],
        out_specs=[
            pl.BlockSpec((1, block, HB * DH), lambda s, g: (s, 0, g)),
            pl.BlockSpec((1, 1, block, HB), lambda s, g: (s, g, 0, 0)),
        ],
        out_shape=[
            jax.ShapeDtypeStruct((count, block, width), F32),
            jax.ShapeDtypeStruct((count, H // HB, block, HB), F32),
        ],
        name="attention_forward",
    )(query, gathered, gathered, key_pos, query_pos)


def backward_body(
    q_ref, do_ref, o_ref, lse_ref, b_ref, a_ref, kpos_ref, qpos_ref, dq_ref, db_ref, da_ref, acc_ref
):
    group = pl.program_id(1)

    @pl.when(group == 0)
    def _():
        acc_ref[...] = jnp.zeros_like(acc_ref)

    allowed = kpos_ref[...] <= qpos_ref[...]
    b_rows = b_ref[0].astype(F32)
    a_rows = a_ref[0].astype(F32)
    lse = lse_ref[0, 0]
    dqs = []
    rows = []
    for h in range(HB):
        key_t, value_t = keys_values(a_rows, b_rows, h)
        q = q_ref[0, :, h * DH : (h + 1) * DH]
        do = do_ref[0, :, h * DH : (h + 1) * DH]
        delta = jnp.sum(do.astype(F32) * o_ref[0, :, h * DH : (h + 1) * DH], axis=1, keepdims=True)
        scores = jnp.dot(q, key_t, preferred_element_type=F32)
        probs = jnp.exp(jnp.where(allowed, scores - lse[:, h : h + 1], NEGATIVE))
        prob_grad = jnp.dot(do, value_t, preferred_element_type=F32)
        score_grad = (probs * (prob_grad - delta)).astype(BF)
        dqs.append(lax.dot_general(score_grad, key_t, NT, preferred_element_type=F32) * SCALE)
        dk = lax.dot_general(q, score_grad, TN, preferred_element_type=F32)
        dv = lax.dot_general(do, probs.astype(BF), TN, preferred_element_type=F32)
        a = a_rows[4 * h : 4 * h + 4]
        acc_ref[:DH] += a[0:1] * dk
        acc_ref[DH : 2 * DH] += a[2:3] * dv
        acc_ref[2 * DH : 3 * DH] += a[1:2] * dk
        acc_ref[3 * DH :] += a[3:4] * dv
        rows.append(jnp.sum(dk * b_rows[:DH], axis=0, keepdims=True))
        rows.append(jnp.sum(dk * b_rows[2 * DH : 3 * DH], axis=0, keepdims=True))
        rows.append(jnp.sum(dv * b_rows[DH : 2 * DH], axis=0, keepdims=True))
        rows.append(jnp.sum(dv * b_rows[3 * DH :], axis=0, keepdims=True))
    dq_ref[0] = jnp.concatenate(dqs, axis=1)
    da_ref[0] = (jnp.concatenate(rows, axis=0) * (1.0 / RK)).astype(BF)

    @pl.when(group == pl.num_programs(1) - 1)
    def _():
        db_ref[0] = acc_ref[...].astype(BF)


def attention_backward(query, heads_grad, heads_wide, lse, gathered, key_pos, query_pos):
    count, block, width = query.shape
    length = gathered.shape[2]
    wide = RK * 2 * DH
    return pl.pallas_call(
        backward_body,
        grid=(count, H // HB),
        in_specs=[
            pl.BlockSpec((1, block, HB * DH), lambda s, g: (s, 0, g)),
            pl.BlockSpec((1, block, HB * DH), lambda s, g: (s, 0, g)),
            pl.BlockSpec((1, block, HB * DH), lambda s, g: (s, 0, g)),
            pl.BlockSpec((1, 1, block, HB), lambda s, g: (s, g, 0, 0)),
            pl.BlockSpec((1, wide, length), lambda s, g: (s, 0, 0)),
            pl.BlockSpec((1, 4 * HB, length), lambda s, g: (s, wide // (4 * HB) + g, 0)),
            pl.BlockSpec((1, length), lambda s, g: (0, 0)),
            pl.BlockSpec((block, 1), lambda s, g: (0, 0)),
        ],
        out_specs=[
            pl.BlockSpec((1, block, HB * DH), lambda s, g: (s, 0, g)),
            pl.BlockSpec((1, wide, length), lambda s, g: (s, 0, 0)),
            pl.BlockSpec((1, 4 * HB, length), lambda s, g: (s, g, 0)),
        ],
        out_shape=[
            jax.ShapeDtypeStruct((count, block, width), F32),
            jax.ShapeDtypeStruct((count, wide, length), BF),
            jax.ShapeDtypeStruct((count, 4 * H, length), BF),
        ],
        scratch_shapes=[pltpu.VMEM((wide, length), F32)],
        name="attention_backward",
    )(query, heads_grad, heads_wide, lse, gathered, gathered, key_pos, query_pos)


def swap(block, axis):
    return lax.ppermute(block, axis, [(0, 1), (1, 0)])


def turn_core_head(block):
    return lax.ppermute(block, ("c", "h"), [(0, 0), (1, 2), (2, 1), (3, 3)])


def sum_over_head(block, n_head):
    if n_head == 2:
        return block + swap(block, "h")
    return lax.psum(block, "h")


def share_over_head(block, n_head):
    if n_head == 2:
        other = swap(block, "h")
        mine = lax.axis_index("h") == 0
        first = jnp.where(mine, block, other)
        second = jnp.where(mine, other, block)
        return jnp.concatenate([first, second], axis=0)
    return lax.all_gather(block, "h", axis=0, tiled=True)


def on_device(
    tokens,
    cotangent,
    domain_ids,
    block_order,
    headwise,
    headwise_mean,
    headwise_square,
    shared_factors,
    shared_factors_mean,
    shared_factors_square,
    out_weight,
    out_weight_mean,
    out_weight_square,
    gate_up,
    gate_up_mean,
    gate_up_square,
    down_weight,
    down_weight_mean,
    down_weight_square,
    norm_gains,
    norm_gains_mean,
    norm_gains_square,
):
    n_head = lax.axis_size("h")
    n_seq = lax.axis_size(SEQ)
    paired = n_head == 2
    seq_at = lax.axis_index(SEQ)
    head_at = lax.axis_index("h")
    seq_all, block_len, _ = tokens.shape
    count = seq_all // n_head
    rows = D // n_seq
    o_cols = H * DH // n_head
    h_cols = H * RA // n_head
    s_cols = RA * DH // n_head
    f_cols = FF // n_head

    out_t = out_weight.T.astype(BF)
    shared_part = lax.dynamic_slice_in_dim(shared_factors, head_at * s_cols, s_cols, 1).astype(BF)
    small = jnp.concatenate(
        [out_t, headwise.astype(BF), shared_part, norm_gains.T.astype(BF)], axis=1
    )
    small_all = lax.all_gather(small, SEQ + ("h",), axis=0)
    small_all = small_all.reshape(n_seq, n_head, rows, small.shape[1]).transpose(0, 2, 1, 3)
    small_all = small_all.reshape(D, n_head, small.shape[1])
    w_out_t = small_all[:, :, :o_cols].reshape(D, H * DH)
    w_heads = small_all[:, :, o_cols : o_cols + h_cols].reshape(D, H * RA)
    w_shared = small_all[:, :, o_cols + h_cols : o_cols + h_cols + s_cols].reshape(D, RA * DH)
    w_factors = jnp.concatenate([w_heads, w_shared], axis=1)
    gains_low = small_all[:, 0, o_cols + h_cols + s_cols :].T.astype(F32)
    gain_first = gains_low[0]
    gain_second = gains_low[1]

    wide_part = jnp.concatenate(
        [gate_up[0].astype(BF), gate_up[1].astype(BF), down_weight.T.astype(BF)], axis=1
    )
    if paired:
        wide_part = turn_core_head(wide_part)
        wide_all = lax.all_gather(wide_part, ("a", "b", "h"), axis=0, tiled=True)
        w_gate = wide_all[:, :f_cols]
        w_up = wide_all[:, f_cols : 2 * f_cols]
        w_down_t = wide_all[:, 2 * f_cols :]
    else:
        wide_all = lax.all_gather(wide_part, SEQ + ("h",), axis=0)
        wide_all = wide_all.reshape(n_seq, n_head, rows, 3, f_cols).transpose(3, 0, 2, 1, 4)
        wide_all = wide_all.reshape(3, D, FF)
        w_gate, w_up, w_down_t = wide_all[0], wide_all[1], wide_all[2]

    spots = jnp.arange(n_seq, dtype=jnp.int32)
    own_block = jnp.sum(jnp.where(spots == seq_at, block_order, 0))
    offsets = jnp.arange(block_len, dtype=jnp.int32)
    query_pos = own_block * block_len + offsets
    key_pos = (block_order[:, None] * block_len + offsets[None, :]).reshape(1, n_seq * block_len)
    cos_t, sin_t = rope_tables(query_pos)

    tok = lax.dynamic_slice_in_dim(tokens, head_at * count, count, 0).astype(F32)
    cot = lax.dynamic_slice_in_dim(cotangent, head_at * count, count, 0).astype(F32)
    same_domain = (domain_ids[:, None] == domain_ids[None, :]).astype(F32)
    seq_weight = lax.dynamic_slice_in_dim(1.0 / jnp.sum(same_domain, axis=1), head_at * count, count, 0)
    out_grad = cot * seq_weight[:, None, None]
    out_low = out_grad.astype(BF)

    first_hat, first_inverse = normalize(tok)
    first_normalized = (first_hat * gain_first).astype(BF)
    factors = jnp.einsum("scd,dj->sjc", first_normalized, w_factors, preferred_element_type=F32)
    query, own_factors = prologue(factors, cos_t, sin_t)
    gathered = lax.all_gather(own_factors, SEQ, axis=2, tiled=True)
    heads_wide, lse = attention_forward(query, gathered, key_pos, query_pos[:, None])
    heads_low = heads_wide.astype(BF)
    attn = jnp.einsum("sce,de->scd", heads_low, w_out_t, preferred_element_type=F32)
    middle = tok + attn
    second_hat, second_inverse = normalize(middle)
    second_normalized = (second_hat * gain_second).astype(BF)

    tokens_own = count * block_len

    def both_cores(block):
        flat = block.reshape(tokens_own, D)
        if paired:
            return jnp.concatenate([flat, swap(flat, "c")], axis=0)
        return flat

    def own_sum(partial):
        if paired:
            partial = partial[:tokens_own] + swap(partial[tokens_own:].astype(BF), "c").astype(F32)
        return partial.reshape(count, block_len, D)

    x_low = both_cores(second_normalized)
    y_low = both_cores(out_low)
    gate = jnp.dot(x_low, w_gate, preferred_element_type=F32)
    up = jnp.dot(x_low, w_up, preferred_element_type=F32)
    sigmoid_gate = jax.nn.sigmoid(gate)
    silu_gate = gate * sigmoid_gate
    hidden_low = (silu_gate * up).astype(BF)
    ffn = own_sum(jnp.einsum("tf,df->td", hidden_low, w_down_t, preferred_element_type=F32))
    layer_output = share_over_head((middle + ffn).astype(BF), n_head)

    hidden_grad = jnp.dot(y_low, w_down_t, preferred_element_type=F32)
    up_grad = (hidden_grad * silu_gate).astype(BF)
    gate_grad = (
        hidden_grad * up * (sigmoid_gate * (1.0 + gate * (1.0 - sigmoid_gate)))
    ).astype(BF)
    down_t_grad = jnp.einsum("td,tf->df", y_low, hidden_low, preferred_element_type=F32)
    gate_w_grad = jnp.einsum("td,tf->df", x_low, gate_grad, preferred_element_type=F32)
    up_w_grad = jnp.einsum("td,tf->df", x_low, up_grad, preferred_element_type=F32)
    second_part = jnp.einsum("tf,df->td", gate_grad, w_gate, preferred_element_type=F32)
    second_part = second_part + jnp.einsum("tf,df->td", up_grad, w_up, preferred_element_type=F32)
    second_grad = own_sum(second_part)

    wide_grad = jnp.concatenate(
        [gate_w_grad.astype(BF), up_w_grad.astype(BF), down_t_grad.astype(BF)], axis=1
    )
    if paired:
        wide_sum = lax.psum_scatter(wide_grad, ("a", "b", "h"), scatter_dimension=0, tiled=True)
        wide_sum = turn_core_head(wide_sum).astype(F32).reshape(rows, 3, f_cols)
    else:
        wide_sum = lax.psum_scatter(wide_grad, SEQ, scatter_dimension=0, tiled=True)
        wide_sum = lax.psum(wide_sum, "h").reshape(rows, 3, n_head, f_cols)
        wide_sum = lax.dynamic_index_in_dim(wide_sum, head_at, 2, keepdims=False).astype(F32)

    second_gain_grad = jnp.sum(second_grad * second_hat, axis=(0, 1))
    middle_grad = out_grad + norm_back(second_grad, gain_second, second_hat, second_inverse)
    middle_low = middle_grad.astype(BF)
    out_t_grad = jnp.einsum("scd,sce->de", middle_low, heads_low, preferred_element_type=F32)
    heads_grad = jnp.einsum("scd,de->sce", middle_low, w_out_t, preferred_element_type=F32).astype(BF)

    query_grad, b_grad, a_grad = attention_backward(
        query, heads_grad, heads_wide, lse, gathered, key_pos, query_pos[:, None]
    )
    factor_grad = jnp.concatenate([b_grad, a_grad], axis=1)
    factor_grad = factor_grad.reshape(count, FAC, n_seq, block_len).transpose(2, 0, 1, 3)
    own_grad = lax.psum_scatter(factor_grad, SEQ, scatter_dimension=0, tiled=True)
    own_grad = own_grad.reshape(count, FAC, block_len)
    joint_grad = epilogue(query_grad, own_grad, factors, cos_t, sin_t)

    first_grad = jnp.einsum("sjc,dj->scd", joint_grad, w_factors, preferred_element_type=F32)
    factors_w_grad = jnp.einsum(
        "scd,sjc->dj", first_normalized, joint_grad, preferred_element_type=F32
    )
    first_gain_grad = jnp.sum(first_grad * first_hat, axis=(0, 1))
    input_grad = middle_grad + norm_back(first_grad, gain_first, first_hat, first_inverse)
    input_grad = share_over_head(input_grad.astype(BF), n_head).astype(F32)

    small_grad = jnp.concatenate(
        [
            out_t_grad.astype(BF),
            factors_w_grad.astype(BF),
            first_gain_grad[:, None].astype(BF),
            second_gain_grad[:, None].astype(BF),
        ],
        axis=1,
    )
    small_sum = lax.psum_scatter(small_grad, SEQ, scatter_dimension=0, tiled=True)
    small_sum = sum_over_head(small_sum, n_head).astype(F32)
    out_sum = lax.dynamic_slice_in_dim(small_sum, head_at * o_cols, o_cols, 1).T
    heads_sum = lax.dynamic_slice_in_dim(small_sum, H * DH + head_at * h_cols, h_cols, 1)
    shared_sum = small_sum[:, H * DH + H * RA : H * DH + H * RA + RA * DH]
    gains_sum = small_sum[:, H * DH + H * RA + RA * DH :].T
    gate_up_sum = jnp.stack([wide_sum[:, 0], wide_sum[:, 1]])
    down_sum = wide_sum[:, 2].T

    rates = step_rates()
    heads_new = adam_update(headwise, headwise_mean, headwise_square, heads_sum, rates[0])
    shared_new = adam_update(
        shared_factors, shared_factors_mean, shared_factors_square, shared_sum, rates[1]
    )
    out_new = adam_update(out_weight, out_weight_mean, out_weight_square, out_sum, rates[2])
    gate_new = adam_update(gate_up, gate_up_mean, gate_up_square, gate_up_sum, rates[3])
    down_new = adam_update(down_weight, down_weight_mean, down_weight_square, down_sum, rates[4])
    gains_new = adam_update(norm_gains, norm_gains_mean, norm_gains_square, gains_sum, rates[5])
    return (
        layer_output,
        input_grad,
        *heads_new,
        *shared_new,
        *out_new,
        *gate_new,
        *down_new,
        *gains_new,
    )


def solution(mesh):
    n_seq = mesh.shape["seq"]
    n_head = mesh.shape["head"]
    inner = max(1, n_seq // 8)
    fine = Mesh(mesh.devices.reshape(n_seq // 2 // inner, inner, 2, n_head), ("a", "b", "c", "h"))
    token = P(None, SEQ, None)
    heads = P(SEQ, "h")
    shared = P(SEQ, None)
    turned = P("h", SEQ)
    gates = P(None, SEQ, "h")
    gains = P(None, SEQ)
    weights = sum(([spec] * 3 for spec in (heads, shared, turned, gates, turned, gains)), [])
    return jax.shard_map(
        on_device,
        mesh=fine,
        in_specs=(token, token, P(), P(), *weights),
        out_specs=(token, token, *weights),
        check_vma=False,
    )
```

time: 3030 us -> 767 us (0.25)
  waiting for transfers between devices: 1790 us -> 454 us
  matrix products: 612 us -> 72.7 us
  starting transfers between devices: 207 us -> 14.5 us
  local copies, waits for them, and re-layouts: 216 us -> 49.1 us
  Pallas kernels: 0 us -> 112 us
  other arithmetic: 107 us -> 41.5 us
  blocking collectives: 41.3 us -> 0 us
    ppermute x94 -> x9, waiting for transfers between devices: 1030 us -> 30.6 us  [the longest x7 19.8 us: swap(): return lax.ppermute(block, axis, [(0, 1), (1, 0)])]
    dot_general x136 -> x15, matrix products: 612 us -> 72.7 us  [the longest x1 9.77 us: on_device(): gate = jnp.dot(x_low, w_gate, preferred_element_type=F32)]
    psum x3 -> x0, waiting for transfers between devices: 320 us -> none  [the longest x1 138 us: on_device(): lax.psum(ffn_part.astype(jnp.bfloat16), 'head').astype(jnp.float32)]
    ppermute x94 -> x9, starting transfers between devices: 206 us -> 14 us  [the longest x2 8.6 us: turn_core_head(): return lax.ppermute(block, ('c', 'h'), [(0, 0), (1, 2), (2, 1), (3, 3)])]
    unnamed x15 -> x6, waiting for transfers between devices: 182 us -> 0.1 us
    while x176 -> x0, local copies, waits for them, and re-layouts: 136 us -> none
    pallas_call x0 -> x4, Pallas kernels: none -> 112 us  [the longest x1 63.2 us: attention_backward(): pl.pallas_call(backward_body, grid=(count, H // HB), in_specs=[pl.BlockSp...]
    reduce_scatter x4 -> x3, waiting for transfers between devices: 171 us -> 256 us  [the longest x1 164 us: on_device(): lax.psum_scatter(wide_grad, ('a', 'b', 'h'), scatter_dimension=0, tiled=T...]
  transfers between devices with their start and end apart: 107 -> 15, of which waited for: 64 -> 11; matrix products, arithmetic and copies ran while one was open for 21% -> 9% of each run, Pallas kernels for 0% -> 5%
where the time goes in v1:
time: 767 us; the launch traced here: 760 us
  waiting for transfers between devices  454 us (59%)
  Pallas kernels  112 us (15%)
  matrix products  72.7 us (9%)
  local copies, waits for them, and re-layouts  49.1 us (6%)
  other arithmetic  41.5 us (5%)
  between operations  15.9 us (2%)
  starting transfers between devices  14.5 us (2%)
    reduce_scatter x1, waiting for transfers between devices, on_device(): lax.psum_scatter(wide_grad, ('a', 'b', 'h'), scatter_dimension=0, tiled=T...  164 us
    all_gather x1, waiting for transfers between devices, on_device(): wide_all = lax.all_gather(wide_part, ('a', 'b', 'h'), axis=0, tiled=True)  70.6 us
    reduce_scatter x1, waiting for transfers between devices, on_device(): lax.psum_scatter(factor_grad, SEQ, scatter_dimension=0, tiled=True)  69.1 us
    pallas_call x1, Pallas kernels, attention_backward(): pl.pallas_call(backward_body, grid=(count, H // HB), in_specs=[pl.BlockSp...  63.2 us
    all_gather x1, waiting for transfers between devices, on_device(): small_all = lax.all_gather(small, SEQ + ('h',), axis=0)  60 us
    pallas_call x1, Pallas kernels, attention_forward(): pl.pallas_call(forward_body, grid=(count, H // HB), in_specs=[pl.BlockSpe...  39.3 us
    all_gather x1, waiting for transfers between devices, on_device(): gathered = lax.all_gather(own_factors, SEQ, axis=2, tiled=True)  36.4 us
    reduce_scatter x1, waiting for transfers between devices, on_device(): lax.psum_scatter(small_grad, SEQ, scatter_dimension=0, tiled=True)  23.2 us
  transfers between devices with their start and end apart: 15, of which 11 were waited for; matrix products, arithmetic and copies ran while one was open for 9% of the time, Pallas kernels for 5%

profile of v1, /device:TPU:1, one launch (start us, length us, event | category | flops | bytes accessed | tf_op | source)
XLA Modules:
  0.0 759.8 jit_solution(7526150900117006181)
XLA Ops:
  7.2 0.9 convert_bitcast_fusion.2
  9.7 1.0 dynamic-slice_convert_fusion
  11.5 1.3 broadcast_multiply_fusion.5
  13.5 1.5 fusion.24
  15.8 60.0 %all-gather.9.cloned.1.call-done = bf16[2048,914]{1,0:T(8,128)(2,1)} async-done(((bf16[64,914]{1,0:T(8,128)(2,1)}), bf16[2048,914]{1,0:T(8,128)(2,1)}) %all-gather.9.cloned.1.call-update) | async-done | bytes 3743760 | tf_op jit(solution)/shard_map/all_gather | solution.py:383
  75.8 2.6 copy.211
  78.6 0.8 slice.85
  79.6 0.9 copy-done
  81.9 0.8 copy-done.10
  82.9 3.5 convolution_bitcast_fusion.f_ref
  86.4 4.2 factor_prologue.1
  90.9 3.4 collective-permute-start.1
  94.2 7.8 %collective-permute-done.1 = bf16[64,4224]{1,0:T(8,128)(2,1)S(1)} collective-permute-done((bf16[64,4224]{1,0:T(8,128)(2,1)S(1)}, bf16[64,4224]{1,0:T(8,128)(2,1)S(1)}, u32[]{:S(2)}, u32[]{:S(2)}) %collective-permute-start.1) | collective-permute-done | bytes 540704 | tf_op jit(solution)/shard_map/ppermute | solution.py:322
  102.1 0.8 copy-done.15
  103.2 1.4 fusion.25
  106.0 1.7 slice.88
  107.7 2.2 copy.214
  109.9 3.2 reshape.193
  113.1 36.4 %all-gather.5.cloned.1.call-done.b_ref.a_ref = bf16[4,320,2048]{2,1,0:T(8,128)(2,1)} async-done(((bf16[4,320,128]{2,1,0:T(8,128)(2,1)}), bf16[4,320,2048]{2,1,0:T(8,128)(2,1)}) %all-gather.5.cloned.1.call-update) | async-done | bytes 5242896 | tf_op jit(solution)/shard_map/all_gather | solution.py:427
  149.5 39.3 %attention_forward.1 = (f32[4,128,1024]{2,1,0:T(8,128)}, f32[4,4,128,4]{3,2,1,0:T(8,128)}) custom-call(bf16[4,128,1024]{2,1,0:T(8,128)(2,1)} %get-tuple-element.27.q_ref, bf16[4,320,2048]{2,1,0:T(8,128)(2,1)} %all-gather.5.cloned.1.call-done.b_ref.a_ref, bf16[4,320,2048]{2,1,0:T(8,128)(2,1)} %all-gather.5.cloned.1.call-done.b_ref.a_ref, ...), custom_call_target="tpu_custom_call" | custom-call | tf_op jit(solution)/shard_map/attention_forward/pallas_call | solution.py:219
  188.8 3.9 multiply_reduce_fusion.2
  193.3 70.6 %all-gather.7.cloned.1.call-done = bf16[1024,4224]{1,0:T(8,128)(2,1)} async-done(((bf16[64,4224]{1,0:T(8,128)(2,1)}), bf16[1024,4224]{1,0:T(8,128)(2,1)}) %all-gather.7.cloned.1.call-update) | async-done | bytes 8650768 | tf_op jit(solution)/shard_map/all_gather | solution.py:399
  263.9 6.0 fusion.5
  270.0 6.4 fusion.11
  276.4 9.8 %multiply_convert_fusion.1 = (bf16[1024,1408]{1,0:T(8,128)(2,1)S(1)}, bf16[1024,1408]{1,0:T(8,128)(2,1)}, bf16[1024,1408]{1,0:T(8,128)(2,1)}) fusion(f32[1024,1408]{1,0:T(8,128)S(1)} %fusion.5, f32[1024,1408]{1,0:T(8,128)} %fusion.11, bf16[1024,4224]{1,0:T(8,128)(2,1)S(1)} %copy-done.33, bf16[512,1024]{1,0:T(8,128)(2,1)} %collective-permute-done, ...), kind=kOutput, calls=%fused_computation.2 | convolution fusion | flops 2978611200 | bytes 25165824 | tf_op jit(solution)/shard_map/dot_general | solution.py:450
  286.2 6.3 fusion.9
  292.5 3.4 fusion.26
  296.1 2.3 collective-permute-start.5
  298.4 3.4 fusion.7
  303.2 1.5 collective-permute-done.2
  306.7 2.3 convolution_convert_fusion.3.do_ref
  309.0 63.2 %attention_backward.1 = (f32[4,128,1024]{2,1,0:T(8,128)}, bf16[4,256,2048]{2,1,0:T(8,128)(2,1)}, bf16[4,64,2048]{2,1,0:T(8,128)(2,1)}) custom-call(bf16[4,128,1024]{2,1,0:T(8,128)(2,1)} %get-tuple-element.27.q_ref, bf16[4,128,1024]{2,1,0:T(8,128)(2,1)} %convolution_convert_fusion.3.do_ref, f32[4,128,1024]{2,1,0:T(8,128)} %get-tuple-element.29.o_ref, ...), custom_call_target="tpu_custom_call" | custom-call | tf_op jit(solution)/shard_map/attention_backward/pallas_call | solution.py:289
  372.2 6.3 bitcast_bitcast_fusion
  378.6 1.5 copy-done.2
  380.1 4.2 bitcast_convert_fusion
  384.3 69.1 %reduce-scatter.6.cloned.1.call-done = bf16[1,4,320,128]{3,2,1,0:T(8,128)(2,1)} async-done(((bf16[16,4,320,128]{3,2,1,0:T(8,128)(2,1)}), bf16[1,4,320,128]{3,2,1,0:T(8,128)(2,1)}) %reduce-scatter.6.cloned.1.call-update) | async-done | bytes 327696 | tf_op jit(solution)/shard_map/reduce_scatter | solution.py:492
  453.4 5.4 factor_epilogue.1
  458.8 3.9 bitcast_convert_fusion.1
  462.7 2.8 fusion.23
  465.5 17.9 %concatenate.38 = bf16[1024,1826]{0,1:T(8,128)(2,1)} concatenate(bf16[1024,1024]{0,1:T(8,128)(2,1)} %bitcast_convert_fusion, bf16[1024,800]{0,1:T(8,128)(2,1)} %bitcast_convert_fusion.1, bf16[1024,1]{0,1:T(2,128)(2,1)S(1)} %convert_element_type.182, bf16[1024,1]{0,1:T(2,128)(2,1)S(1)} %convert_element_type.184), dimensions={1} | concatenate | bytes 7479296 | tf_op jit(solution)/shard_map/concatenate | solution.py:504
  483.5 6.1 copy.240
  489.9 6.1 convolution_convert_fusion.1
  496.0 5.2 convolution_convert_fusion.2
  501.2 5.5 convolution_convert_fusion
  506.6 3.8 pad_maximum_fusion
  510.5 1.4 collective-permute-start.3
  511.9 3.5 fusion.22
  515.8 17.5 %collective-permute-done.3 = bf16[4,128,1024]{2,1,0:T(8,128)(2,1)} collective-permute-done((bf16[4,128,1024]{2,1,0:T(8,128)(2,1)S(1)}, bf16[4,128,1024]{2,1,0:T(8,128)(2,1)}, u32[]{:S(2)}, u32[]{:S(2)}) %collective-permute-start.3) | collective-permute-done | bytes 1048608 | tf_op jit(solution)/shard_map/ppermute | solution.py:318
  533.3 1.4 broadcast_select_fusion.3
  534.7 1.5 pad_maximum_fusion.2
  536.2 23.2 %reduce-scatter.10.cloned.1.call-done = bf16[64,1826]{1,0:T(8,128)(2,1)} async-done(((bf16[1024,1826]{1,0:T(8,128)(2,1)}), bf16[64,1826]{1,0:T(8,128)(2,1)}) %reduce-scatter.10.cloned.1.call-update) | async-done | bytes 233744 | tf_op jit(solution)/shard_map/reduce_scatter | solution.py:513
  559.4 1.2 collective-permute-start.7
  560.5 1.4 broadcast_select_fusion.1
  562.0 2.3 maximum_convert_fusion
  566.1 163.9 %reduce-scatter.8.cloned.1.call-done = bf16[64,4224]{1,0:T(8,128)(2,1)} async-done(((bf16[1024,4224]{1,0:T(8,128)(2,1)}), bf16[64,4224]{1,0:T(8,128)(2,1)}) %reduce-scatter.8.cloned.1.call-update) | async-done | bytes 540688 | tf_op jit(solution)/shard_map/reduce_scatter | solution.py:474
  730.1 5.2 collective-permute-start.8
  737.3 0.9 multiply_subtract_fusion.3
  738.2 1.0 multiply_subtract_fusion.2
  739.2 3.0 collective-permute-done.8
  743.5 5.1 multiply_subtract_fusion
  748.6 0.9 copy.233
  749.5 0.9 copy.234
  750.4 0.9 copy.235
  751.3 1.1 multiply_subtract_fusion.1
  (147 shorter events, 16.9 us)
Async XLA Ops:
  7.2 68.6 %all-gather.9.cloned.1.call-start = ((), (), s32[]{:S(2)}) async-start(), calls=%async_computation.7 | async-start | bytes 4325376 | tf_op jit(solution)/shard_map/all_gather | solution.py:383
  11.5 138.0 %all-gather.5.cloned.1.call-start = ((), (), s32[]{:S(2)}) async-start(), calls=%async_computation.3 | async-start | bytes 5570560 | tf_op jit(solution)/shard_map/all_gather | solution.py:427
  78.5 2.0 copy-start
  81.7 1.1 copy-start.10
  81.9 0.9 copy-start.19
  86.4 4.3 copy-start.3
  86.4 4.4 copy-start.9
  90.6 12.3 %copy-start.34 = (s32[8]{0:T(128)S(1)}, s32[8]{0:T(128)}, u32[]{:S(2)}) copy-start(s32[8]{0:T(128)} %param.24) | copy-start | bytes 100
  90.6 12.6 %copy-start.6 = (bf16[8,128,1024]{2,1,0:T(8,128)(2,1)S(1)}, bf16[8,128,1024]{2,1,0:T(8,128)(2,1)}, u32[]{:S(2)}) copy-start(bf16[8,128,1024]{2,1,0:T(8,128)(2,1)} %param.23) | copy-start | bytes 6291460
  90.6 173.3 %all-gather.7.cloned.1.call-start = ((), (), s32[]{:S(2)}) async-start(), calls=%async_computation.4 | async-start | bytes 9191424 | tf_op jit(solution)/shard_map/all_gather | solution.py:399
  90.9 11.2 %collective-permute-start.1 = (bf16[64,4224]{1,0:T(8,128)(2,1)S(1)}, bf16[64,4224]{1,0:T(8,128)(2,1)S(1)}, u32[]{:S(2)}, u32[]{:S(2)}) collective-permute-start(bf16[64,4224]{1,0:T(8,128)(2,1)S(1)} %pad_maximum_fusion.7), channel_id=1, source_target_pairs={{0,0},{1,2},{2,1},{3,3},{4,4},{5,6},{6,5},{7,7},{8,8},{9,10},{10,9... | collective-permute-start | bytes 1622024 | tf_op jit(solution)/shard_map/ppermute | solution.py:322
  102.1 0.8 copy-start.15
  102.9 350.5 %reduce-scatter.6.cloned.1.call-start = ((), (), s32[]{:S(2)}) async-start(), calls=%async_computation.5 | async-start | bytes 5570560 | tf_op jit(solution)/shard_map/reduce_scatter | solution.py:492
  104.7 88.7 %collective-permute-start.4 = (bf16[512,1024]{1,0:T(8,128)(2,1)}, bf16[512,1024]{1,0:T(8,128)(2,1)}, u32[]{:S(2)}, u32[]{:S(2)}) collective-permute-start(bf16[512,1024]{1,0:T(8,128)(2,1)} %bitcast.19), channel_id=1, source_target_pairs={{0,2},{2,0},{1,3},{3,1},{4,6},{6,4},{5,7},{7,5},{8,10},{10,8},{9,1... | collective-permute-start | bytes 3145736 | tf_op jit(solution)/shard_map/ppermute | solution.py:318
  193.0 83.4 %copy-start.12 = (bf16[4,128,1024]{2,1,0:T(8,128)(2,1)}, bf16[4,128,1024]{2,1,0:T(8,128)(2,1)S(1)}, u32[]{:S(2)}) copy-start(bf16[4,128,1024]{2,1,0:T(8,128)(2,1)S(1)} %multiply_convert_fusion.3) | copy-start | bytes 3145732
  193.0 77.0 %collective-permute-start = (bf16[512,1024]{1,0:T(8,128)(2,1)S(1)}, bf16[512,1024]{1,0:T(8,128)(2,1)}, u32[]{:S(2)}, u32[]{:S(2)}) collective-permute-start(bf16[512,1024]{1,0:T(8,128)(2,1)S(1)} %bitcast.98), channel_id=1, source_target_pairs={{0,2},{2,0},{1,3},{3,1},{4,6},{6,4},{5,7},{7,5},{8,10},{10,8},{9,1... | collective-permute-start | bytes 3145736 | tf_op jit(solution)/shard_map/ppermute | solution.py:318
  263.9 6.0 copy-start.33
  286.2 6.3 copy-start.35
  292.5 5.9 copy-start.37
  296.1 6.0 collective-permute-start.5
  302.0 2.7 collective-permute-start.2
  303.2 1.9 copy-start.7
  305.1 1.6 copy-start.8
  305.9 3.1 copy-start.1
  378.5 1.6 copy-start.2
  378.5 180.9 %reduce-scatter.10.cloned.1.call-start = ((), (), s32[]{:S(2)}) async-start(), calls=%async_computation.8 | async-start | bytes 4177920 | tf_op jit(solution)/shard_map/reduce_scatter | solution.py:513
  458.8 4.0 copy-start.5
  458.8 4.0 copy-start.11
  458.8 4.0 copy-start.14
  458.8 4.0 copy-start.20
  489.6 240.5 %reduce-scatter.8.cloned.1.call-start = ((), (), s32[]{:S(2)}) async-start(), calls=%async_computation.6 | async-start | bytes 9191424 | tf_op jit(solution)/shard_map/reduce_scatter | solution.py:474
  489.9 6.1 copy-start.13
  489.9 6.1 copy-start.36
  496.0 5.2 copy-start.38
  510.5 22.8 %collective-permute-start.3 = (bf16[4,128,1024]{2,1,0:T(8,128)(2,1)S(1)}, bf16[4,128,1024]{2,1,0:T(8,128)(2,1)}, u32[]{:S(2)}, u32[]{:S(2)}) collective-permute-start(bf16[4,128,1024]{2,1,0:T(8,128)(2,1)S(1)} %get-tuple-element.185), channel_id=1, source_target_pairs={{0,1},{1,0},{2,3},{3,2},{4,5},{5,4},{6,7},{7,6},{8,9},{9,8},{10,11... | collective-permute-start | bytes 3145736 | tf_op jit(solution)/shard_map/ppermute | solution.py:318
  511.9 3.6 copy-start.30
  511.9 3.7 copy-start.31
  511.9 3.8 copy-start.32
  515.3 45.2 %collective-permute-start.6 = (bf16[4,128,1024]{2,1,0:T(8,128)(2,1)}, bf16[4,128,1024]{2,1,0:T(8,128)(2,1)S(1)}, u32[]{:S(2)}, u32[]{:S(2)}) collective-permute-start(bf16[4,128,1024]{2,1,0:T(8,128)(2,1)} %fusion.22), channel_id=1, source_target_pairs={{0,1},{1,0},{2,3},{3,2},{4,5},{5,4},{6,7},{7,6},{8,9},{9,8},{10,11... | collective-permute-start | bytes 3145736 | tf_op jit(solution)/shard_map/ppermute | solution.py:318
  559.4 5.7 collective-permute-start.7
  561.9 3.2 copy-start.22
  561.9 3.4 copy-start.27
  561.9 3.4 copy-start.28
  561.9 3.4 copy-start.29
  562.0 175.3 %copy-start.16 = (f32[512,64]{0,1:T(8,128)S(1)}, f32[512,64]{0,1:T(8,128)}, u32[]{:S(2)}) copy-start(f32[512,64]{0,1:T(8,128)} %param.32) | copy-start | bytes 393220
  562.0 175.3 %copy-start.25 = (f32[512,64]{0,1:T(8,128)S(1)}, f32[512,64]{0,1:T(8,128)}, u32[]{:S(2)}) copy-start(f32[512,64]{0,1:T(8,128)} %param.33) | copy-start | bytes 393220
  562.0 175.3 %copy-start.26 = (f32[512,64]{0,1:T(8,128)S(1)}, f32[512,64]{0,1:T(8,128)}, u32[]{:S(2)}) copy-start(f32[512,64]{0,1:T(8,128)} %param.34) | copy-start | bytes 393220
  564.3 173.9 %copy-start.21 = (f32[64,640]{1,0:T(8,128)S(1)}, f32[64,640]{1,0:T(8,128)}, u32[]{:S(2)}) copy-start(f32[64,640]{1,0:T(8,128)} %param.29) | copy-start | bytes 491524
  564.3 173.9 %copy-start.23 = (f32[64,640]{1,0:T(8,128)S(1)}, f32[64,640]{1,0:T(8,128)}, u32[]{:S(2)}) copy-start(f32[64,640]{1,0:T(8,128)} %param.30) | copy-start | bytes 491524
  564.3 173.9 %copy-start.24 = (f32[64,640]{1,0:T(8,128)S(1)}, f32[64,640]{1,0:T(8,128)}, u32[]{:S(2)}) copy-start(f32[64,640]{1,0:T(8,128)} %param.31) | copy-start | bytes 491524
  730.1 12.2 %collective-permute-start.8 = (bf16[64,4224]{1,0:T(8,128)(2,1)}, bf16[64,4224]{1,0:T(8,128)(2,1)S(1)}, u32[]{:S(2)}, u32[]{:S(2)}) collective-permute-start(bf16[64,4224]{1,0:T(8,128)(2,1)} %reduce-scatter.8.cloned.1.call-done), channel_id=1, source_target_pairs={{0,0},{1,2},{2,1},{3,3},{4,4},{5,6},{6,5},{7,7},{8,8},{9,10},{10,9... | collective-permute-start | bytes 1622024 | tf_op jit(solution)/shard_map/ppermute | solution.py:322
  739.2 4.3 copy-start.4
  748.6 2.7 copy-start.17
  748.6 2.7 copy-start.18
Sparse Core Ops, SparseCore 0:
  11.6 64.1 all-gather.8
  90.7 58.7 all-gather.4
  152.9 111.0 all-gather.6
  378.6 74.7 reduce-scatter.5
  489.7 69.6 reduce-scatter.9
  564.9 165.1 reduce-scatter.7

commit v2 on v1

--- a/solution.py
+++ b/solution.py
@@ -239,9 +239,11 @@
 
 
 def backward_body(
-    q_ref, do_ref, o_ref, lse_ref, b_ref, a_ref, kpos_ref, qpos_ref, dq_ref, db_ref, da_ref, acc_ref
+    q_ref, do_ref, o_ref, lse_ref, b_ref, a_ref, kpos_ref, qpos_ref, dq_ref, *refs
 ):
+    piece_refs, acc_ref = refs[:-1], refs[-1]
     group = pl.program_id(1)
+    wide = RK * 2 * DH
 
     @pl.when(group == 0)
     def _():
@@ -275,17 +277,28 @@
         rows.append(jnp.sum(dv * b_rows[DH : 2 * DH], axis=0, keepdims=True))
         rows.append(jnp.sum(dv * b_rows[3 * DH :], axis=0, keepdims=True))
     dq_ref[0] = jnp.concatenate(dqs, axis=1)
-    da_ref[0] = (jnp.concatenate(rows, axis=0) * (1.0 / RK)).astype(BF)
+    a_grad = (jnp.concatenate(rows, axis=0) * (1.0 / RK)).astype(BF)
+    block = piece_refs[0].shape[3]
+    depth = piece_refs[0].shape[0]
+    at = pl.multiple_of(wide + group * 4 * HB, 4 * HB)
+    for i, ref in enumerate(piece_refs):
+        for m in range(depth):
+            lanes = (i * depth + m) * block
+            ref[m, 0, pl.ds(at, 4 * HB), :] = a_grad[:, lanes : lanes + block]
 
     @pl.when(group == pl.num_programs(1) - 1)
     def _():
-        db_ref[0] = acc_ref[...].astype(BF)
-
-
-def attention_backward(query, heads_grad, heads_wide, lse, gathered, key_pos, query_pos):
+        for i, ref in enumerate(piece_refs):
+            for m in range(depth):
+                lanes = (i * depth + m) * block
+                ref[m, 0, :wide, :] = acc_ref[:, lanes : lanes + block].astype(BF)
+
+
+def attention_backward(query, heads_grad, heads_wide, lse, gathered, key_pos, query_pos, depth):
     count, block, width = query.shape
     length = gathered.shape[2]
     wide = RK * 2 * DH
+    pieces = length // (depth * block)
     return pl.pallas_call(
         backward_body,
         grid=(count, H // HB),
@@ -299,16 +312,10 @@
             pl.BlockSpec((1, length), lambda s, g: (0, 0)),
             pl.BlockSpec((block, 1), lambda s, g: (0, 0)),
         ],
-        out_specs=[
-            pl.BlockSpec((1, block, HB * DH), lambda s, g: (s, 0, g)),
-            pl.BlockSpec((1, wide, length), lambda s, g: (s, 0, 0)),
-            pl.BlockSpec((1, 4 * HB, length), lambda s, g: (s, g, 0)),
-        ],
-        out_shape=[
-            jax.ShapeDtypeStruct((count, block, width), F32),
-            jax.ShapeDtypeStruct((count, wide, length), BF),
-            jax.ShapeDtypeStruct((count, 4 * H, length), BF),
-        ],
+        out_specs=[pl.BlockSpec((1, block, HB * DH), lambda s, g: (s, 0, g))]
+        + [pl.BlockSpec((depth, 1, FAC, block), lambda s, g: (0, s, 0, 0))] * pieces,
+        out_shape=[jax.ShapeDtypeStruct((count, block, width), F32)]
+        + [jax.ShapeDtypeStruct((depth, count, FAC, block), BF)] * pieces,
         scratch_shapes=[pltpu.VMEM((wide, length), F32)],
         name="attention_backward",
     )(query, heads_grad, heads_wide, lse, gathered, gathered, key_pos, query_pos)
@@ -320,12 +327,165 @@
 
 def turn_core_head(block):
     return lax.ppermute(block, ("c", "h"), [(0, 0), (1, 2), (2, 1), (3, 3)])
+
+
+def from_ahead(block, axis, distance):
+    size = lax.axis_size(axis)
+    return lax.ppermute(block, axis, [((i + distance) % size, i) for i in range(size)])
+
+
+def to_ahead(block, axis, distance):
+    size = lax.axis_size(axis)
+    return lax.ppermute(block, axis, [(i, (i + distance) % size) for i in range(size)])
+
+
+def ordered_gather(block, axis):
+    size = lax.axis_size(axis)
+    spot = lax.axis_index(axis)
+    if size == 2:
+        other = swap(block, axis)
+        mine = spot == 0
+        return jnp.stack([jnp.where(mine, block, other), jnp.where(mine, other, block)])
+    parts = [block] + [from_ahead(block, axis, m) for m in range(1, size)]
+    twice = jnp.stack(parts + parts[:-1])
+    return lax.dynamic_slice_in_dim(twice, jnp.mod(size - spot, size), size, 0)
+
+
+def ordered_scatter(block, axis, dim):
+    size = lax.axis_size(axis)
+    spot = lax.axis_index(axis)
+
+    def part(m):
+        return lax.dynamic_index_in_dim(block, jnp.mod(spot + m, size), dim, keepdims=False)
+
+    total = part(0).astype(F32)
+    for m in range(1, size):
+        total = total + to_ahead(part(m), axis, m).astype(F32)
+    return total.astype(BF)
+
+
+def gather_blocks(block):
+    order = {}
+    for ma in range(lax.axis_size("a")):
+        at_a = from_ahead(block, "a", ma) if ma else block
+        for mb in range(lax.axis_size("b")):
+            at_b = from_ahead(at_a, "b", mb) if mb else at_a
+            order[0, mb, ma] = at_b
+            order[1, mb, ma] = swap(at_b, "c")
+    return [order[key] for key in sorted(order)]
+
+
+def blocks_ahead():
+    na, nb = lax.axis_size("a"), lax.axis_size("b")
+    at = [lax.axis_index(name) for name in SEQ]
+    spots = []
+    for mc in range(2):
+        for mb in range(nb):
+            for ma in range(na):
+                a = jnp.mod(at[0] + ma, na)
+                b = jnp.mod(at[1] + mb, nb)
+                spots.append((a * nb + b) * 2 + jnp.mod(at[2] + mc, 2))
+    return jnp.stack(spots)
+
+
+def scatter_blocks(pieces):
+    na, nb = lax.axis_size("a"), lax.axis_size("b")
+    after_core = []
+    for mb in range(nb):
+        other = swap(pieces[nb + mb], "c")
+        after_core.append((pieces[mb].astype(F32) + other.astype(F32)).astype(BF))
+    moved = [to_ahead(after_core[mb], "b", mb) for mb in range(1, nb)]
+    total = None
+    for ma in range(na):
+        part = after_core[0][ma].astype(F32)
+        for block in moved:
+            part = part + block[ma].astype(F32)
+        if ma:
+            part = to_ahead(part.astype(BF), "a", ma).astype(F32)
+        total = part if total is None else total + part
+    return total
+
+
+def place_body(at_ref, t1, r1, t2, r2, out_ref, sems):
+    depth = t1.shape[1]
+    copies = []
+    for m in range(depth):
+        z = lax.rem(at_ref[0] + m, depth)
+        for i in range(2):
+            for j in range(2):
+                x = lax.rem(at_ref[1] + i, 2)
+                y = lax.rem(at_ref[2] + j, 2)
+                first = (r1 if j else t1).at[i, m]
+                second = (r2 if i else t2).at[j, m]
+                copies.append((first, out_ref.at[z, x, y, 0]))
+                copies.append((second, out_ref.at[z, x, y, 1]))
+    copies = [pltpu.make_async_copy(a, b, sems.at[n]) for n, (a, b) in enumerate(copies)]
+    for copy in copies:
+        copy.start()
+    for copy in copies:
+        copy.wait()
+
+
+def place(t1, r1, t2, r2):
+    _, depth, part, cols = t1.shape
+    at = jnp.stack([lax.axis_index(name) for name in ("a", "b", "h")]).astype(jnp.int32)
+    out = pl.pallas_call(
+        place_body,
+        grid_spec=pltpu.PrefetchScalarGridSpec(
+            num_scalar_prefetch=1,
+            grid=(1,),
+            in_specs=[pl.BlockSpec(memory_space=pl.ANY)] * 4,
+            out_specs=pl.BlockSpec(memory_space=pl.ANY),
+            scratch_shapes=[pltpu.SemaphoreType.DMA((8 * depth,))],
+        ),
+        out_shape=jax.ShapeDtypeStruct((depth, 2, 2, 2, part, cols), t1.dtype),
+        name="place_rows",
+    )(at, t1, r1, t2, r2)
+    return out.reshape(depth * 8 * part, cols)
+
+
+def bulk_gather(block):
+    part = block.shape[0] // 2
+    parts = [block] + [from_ahead(block, "a", m) for m in range(1, lax.axis_size("a"))]
+    low = jnp.stack([p[:part] for p in parts])
+    high = jnp.stack([p[part:] for p in parts])
+    t1 = jnp.stack([low, swap(low, "b")])
+    t2 = jnp.stack([high, swap(high, "h")])
+    return place(t1, swap(t1, "h"), t2, swap(t2, "b"))
+
+
+def bulk_scatter(grad):
+    na = lax.axis_size("a")
+    part = grad.shape[0] // (8 * na)
+    cols = grad.shape[1]
+    a, b, h = (lax.axis_index(name) for name in ("a", "b", "h"))
+    grad = grad.reshape(na, 2, 2, 2, part, cols)
+
+    def take(block, spot, dim):
+        return lax.dynamic_index_in_dim(block, spot, dim, keepdims=False)
+
+    def fold(block, axis, spot, dim):
+        other = swap(take(block, 1 - spot, dim), axis)
+        return (take(block, spot, dim).astype(F32) + other.astype(F32)).astype(BF)
+
+    low = fold(fold(grad[:, :, :, 0], "h", h, 2), "b", b, 1)
+    high = fold(fold(grad[:, :, :, 1], "b", b, 1), "h", h, 1)
+    both = jnp.concatenate([low, high], axis=1)
+    total = take(both, a, 0).astype(F32)
+    for m in range(1, na):
+        total = total + to_ahead(take(both, jnp.mod(a + m, na), 0), "a", m).astype(F32)
+    return turn_core_head(total.astype(BF)).astype(F32)
 
 
 def sum_over_head(block, n_head):
     if n_head == 2:
         return block + swap(block, "h")
     return lax.psum(block, "h")
+
+
+def in_core_order(own, other, axis):
+    first = lax.axis_index("c") == 0
+    return jnp.concatenate([jnp.where(first, own, other), jnp.where(first, other, own)], axis=axis)
 
 
 def share_over_head(block, n_head):
@@ -364,7 +524,7 @@
 ):
     n_head = lax.axis_size("h")
     n_seq = lax.axis_size(SEQ)
-    paired = n_head == 2
+    paired = n_head == 2 and lax.axis_size("b") == 2
     seq_at = lax.axis_index(SEQ)
     head_at = lax.axis_index("h")
     seq_all, block_len, _ = tokens.shape
@@ -375,42 +535,45 @@
     s_cols = RA * DH // n_head
     f_cols = FF // n_head
 
-    out_t = out_weight.T.astype(BF)
-    shared_part = lax.dynamic_slice_in_dim(shared_factors, head_at * s_cols, s_cols, 1).astype(BF)
-    small = jnp.concatenate(
-        [out_t, headwise.astype(BF), shared_part, norm_gains.T.astype(BF)], axis=1
-    )
-    small_all = lax.all_gather(small, SEQ + ("h",), axis=0)
-    small_all = small_all.reshape(n_seq, n_head, rows, small.shape[1]).transpose(0, 2, 1, 3)
-    small_all = small_all.reshape(D, n_head, small.shape[1])
-    w_out_t = small_all[:, :, :o_cols].reshape(D, H * DH)
-    w_heads = small_all[:, :, o_cols : o_cols + h_cols].reshape(D, H * RA)
-    w_shared = small_all[:, :, o_cols + h_cols : o_cols + h_cols + s_cols].reshape(D, RA * DH)
+    shared_part = lax.dynamic_slice_in_dim(shared_factors, head_at * s_cols, s_cols, 1)
+    small = jnp.concatenate([headwise, shared_part, norm_gains.T], axis=1).astype(BF)
+    for name in ("a", "b", "c"):
+        small = ordered_gather(small, name)
+    if paired:
+        small = ordered_gather(small, "h")
+    else:
+        small = lax.all_gather(small, "h", axis=0)
+    small = small.transpose(3, 2, 1, 4, 0, 5).reshape(D, n_head, h_cols + s_cols + 2)
+    w_heads = small[:, :, :h_cols].reshape(D, H * RA)
+    w_shared = small[:, :, h_cols : h_cols + s_cols].reshape(D, RA * DH)
     w_factors = jnp.concatenate([w_heads, w_shared], axis=1)
-    gains_low = small_all[:, 0, o_cols + h_cols + s_cols :].T.astype(F32)
+    gains_low = small[:, 0, h_cols + s_cols :].T.astype(F32)
     gain_first = gains_low[0]
     gain_second = gains_low[1]
 
-    wide_part = jnp.concatenate(
-        [gate_up[0].astype(BF), gate_up[1].astype(BF), down_weight.T.astype(BF)], axis=1
-    )
+    wide_parts = [
+        part.astype(BF) for part in (out_weight.T, gate_up[0], gate_up[1], down_weight.T)
+    ]
     if paired:
-        wide_part = turn_core_head(wide_part)
-        wide_all = lax.all_gather(wide_part, ("a", "b", "h"), axis=0, tiled=True)
-        w_gate = wide_all[:, :f_cols]
-        w_up = wide_all[:, f_cols : 2 * f_cols]
-        w_down_t = wide_all[:, 2 * f_cols :]
+        wide_parts = [turn_core_head(part) for part in wide_parts]
+        own_out, w_gate, w_up, w_down_t = [bulk_gather(part) for part in wide_parts]
+        w_out_t = in_core_order(own_out, swap(own_out, "c"), 1)
     else:
+        wide_part = jnp.concatenate(wide_parts, axis=1)
         wide_all = lax.all_gather(wide_part, SEQ + ("h",), axis=0)
-        wide_all = wide_all.reshape(n_seq, n_head, rows, 3, f_cols).transpose(3, 0, 2, 1, 4)
-        wide_all = wide_all.reshape(3, D, FF)
+        wide_all = wide_all.reshape(n_seq, n_head, rows, 3 * f_cols + o_cols)
+        w_out_t = wide_all[..., :o_cols].transpose(0, 2, 1, 3).reshape(D, H * DH)
+        wide_all = wide_all[..., o_cols:].reshape(n_seq, n_head, rows, 3, f_cols)
+        wide_all = wide_all.transpose(3, 0, 2, 1, 4).reshape(3, D, FF)
         w_gate, w_up, w_down_t = wide_all[0], wide_all[1], wide_all[2]
 
     spots = jnp.arange(n_seq, dtype=jnp.int32)
     own_block = jnp.sum(jnp.where(spots == seq_at, block_order, 0))
     offsets = jnp.arange(block_len, dtype=jnp.int32)
     query_pos = own_block * block_len + offsets
-    key_pos = (block_order[:, None] * block_len + offsets[None, :]).reshape(1, n_seq * block_len)
+    ahead = blocks_ahead()
+    ahead_block = jnp.sum(jnp.where(spots[None, :] == ahead[:, None], block_order[None, :], 0), axis=1)
+    key_pos = (ahead_block[:, None] * block_len + offsets[None, :]).reshape(1, n_seq * block_len)
     cos_t, sin_t = rope_tables(query_pos)
 
     tok = lax.dynamic_slice_in_dim(tokens, head_at * count, count, 0).astype(F32)
@@ -424,8 +587,14 @@
     first_normalized = (first_hat * gain_first).astype(BF)
     factors = jnp.einsum("scd,dj->sjc", first_normalized, w_factors, preferred_element_type=F32)
     query, own_factors = prologue(factors, cos_t, sin_t)
-    gathered = lax.all_gather(own_factors, SEQ, axis=2, tiled=True)
-    heads_wide, lse = attention_forward(query, gathered, key_pos, query_pos[:, None])
+    half = max(1, count // 2)
+    groups = [slice(at, at + half) for at in range(0, count, half)]
+    gathered = [jnp.concatenate(gather_blocks(own_factors[g]), axis=2) for g in groups]
+    forward = [
+        attention_forward(query[g], keys, key_pos, query_pos[:, None])
+        for g, keys in zip(groups, gathered)
+    ]
+    heads_wide = jnp.concatenate([part[0] for part in forward], axis=0)
     heads_low = heads_wide.astype(BF)
     attn = jnp.einsum("sce,de->scd", heads_low, w_out_t, preferred_element_type=F32)
     middle = tok + attn
@@ -467,31 +636,52 @@
     second_part = second_part + jnp.einsum("tf,df->td", up_grad, w_up, preferred_element_type=F32)
     second_grad = own_sum(second_part)
 
-    wide_grad = jnp.concatenate(
-        [gate_w_grad.astype(BF), up_w_grad.astype(BF), down_t_grad.astype(BF)], axis=1
-    )
-    if paired:
-        wide_sum = lax.psum_scatter(wide_grad, ("a", "b", "h"), scatter_dimension=0, tiled=True)
-        wide_sum = turn_core_head(wide_sum).astype(F32).reshape(rows, 3, f_cols)
-    else:
-        wide_sum = lax.psum_scatter(wide_grad, SEQ, scatter_dimension=0, tiled=True)
-        wide_sum = lax.psum(wide_sum, "h").reshape(rows, 3, n_head, f_cols)
-        wide_sum = lax.dynamic_index_in_dim(wide_sum, head_at, 2, keepdims=False).astype(F32)
-
     second_gain_grad = jnp.sum(second_grad * second_hat, axis=(0, 1))
     middle_grad = out_grad + norm_back(second_grad, gain_second, second_hat, second_inverse)
     middle_low = middle_grad.astype(BF)
-    out_t_grad = jnp.einsum("scd,sce->de", middle_low, heads_low, preferred_element_type=F32)
     heads_grad = jnp.einsum("scd,de->sce", middle_low, w_out_t, preferred_element_type=F32).astype(BF)
 
-    query_grad, b_grad, a_grad = attention_backward(
-        query, heads_grad, heads_wide, lse, gathered, key_pos, query_pos[:, None]
-    )
-    factor_grad = jnp.concatenate([b_grad, a_grad], axis=1)
-    factor_grad = factor_grad.reshape(count, FAC, n_seq, block_len).transpose(2, 0, 1, 3)
-    own_grad = lax.psum_scatter(factor_grad, SEQ, scatter_dimension=0, tiled=True)
-    own_grad = own_grad.reshape(count, FAC, block_len)
-    joint_grad = epilogue(query_grad, own_grad, factors, cos_t, sin_t)
+    def out_grad_of(columns):
+        return jnp.einsum("scd,sce->de", middle_low, columns, preferred_element_type=F32)
+
+    if paired:
+        core_at = lax.axis_index("c")
+        mine = lax.dynamic_slice_in_dim(heads_low, core_at * o_cols, o_cols, 2)
+        theirs = lax.dynamic_slice_in_dim(heads_low, (1 - core_at) * o_cols, o_cols, 2)
+        sent = swap(out_grad_of(theirs).astype(BF), "c")
+        out_t_grad = out_grad_of(mine) + sent.astype(F32)
+    else:
+        out_t_grad = out_grad_of(heads_low)
+    wide_grads = [
+        grad.astype(BF) for grad in (down_t_grad, gate_w_grad, up_w_grad, out_t_grad)
+    ]
+    wide_grads, heads_grad = lax.optimization_barrier((wide_grads, heads_grad))
+    if paired:
+        down_sum, gate_sum, up_sum, out_sum = [bulk_scatter(grad) for grad in wide_grads]
+    else:
+        wide_sum = jnp.concatenate(wide_grads, axis=1)
+        wide_sum = lax.psum_scatter(wide_sum, SEQ, scatter_dimension=0, tiled=True)
+        wide_sum = lax.psum(wide_sum, "h").astype(F32)
+        out_sum = lax.dynamic_slice_in_dim(wide_sum, 3 * FF + head_at * o_cols, o_cols, 1)
+        wide_sum = wide_sum[:, : 3 * FF].reshape(rows, 3, n_head, f_cols)
+        wide_sum = lax.dynamic_index_in_dim(wide_sum, head_at, 2, keepdims=False)
+        down_sum, gate_sum, up_sum = wide_sum[:, 0], wide_sum[:, 1], wide_sum[:, 2]
+
+    joint = []
+    for at, g in enumerate(groups):
+        query_grad, *pieces = attention_backward(
+            query[g],
+            heads_grad[g],
+            forward[at][0],
+            forward[at][1],
+            gathered[at],
+            key_pos,
+            query_pos[:, None],
+            lax.axis_size("a"),
+        )
+        own_grad = scatter_blocks(pieces)
+        joint.append(epilogue(query_grad, own_grad, factors[g], cos_t, sin_t))
+    joint_grad = jnp.concatenate(joint, axis=0)
 
     first_grad = jnp.einsum("sjc,dj->scd", joint_grad, w_factors, preferred_element_type=F32)
     factors_w_grad = jnp.einsum(
@@ -501,23 +691,21 @@
     input_grad = middle_grad + norm_back(first_grad, gain_first, first_hat, first_inverse)
     input_grad = share_over_head(input_grad.astype(BF), n_head).astype(F32)
 
-    small_grad = jnp.concatenate(
-        [
-            out_t_grad.astype(BF),
-            factors_w_grad.astype(BF),
-            first_gain_grad[:, None].astype(BF),
-            second_gain_grad[:, None].astype(BF),
-        ],
-        axis=1,
+    gain_cols = jnp.stack([first_gain_grad, second_gain_grad]).T
+    small_grad = jnp.concatenate([factors_w_grad, gain_cols], axis=1).astype(BF)
+    small_sum = small_grad.reshape(
+        lax.axis_size("a"), lax.axis_size("b"), 2, rows, small_grad.shape[1]
     )
-    small_sum = lax.psum_scatter(small_grad, SEQ, scatter_dimension=0, tiled=True)
+    small_sum = ordered_scatter(small_sum, "c", 2)
+    small_sum = ordered_scatter(small_sum, "b", 1)
+    small_sum = ordered_scatter(small_sum, "a", 0)
     small_sum = sum_over_head(small_sum, n_head).astype(F32)
-    out_sum = lax.dynamic_slice_in_dim(small_sum, head_at * o_cols, o_cols, 1).T
-    heads_sum = lax.dynamic_slice_in_dim(small_sum, H * DH + head_at * h_cols, h_cols, 1)
-    shared_sum = small_sum[:, H * DH + H * RA : H * DH + H * RA + RA * DH]
-    gains_sum = small_sum[:, H * DH + H * RA + RA * DH :].T
-    gate_up_sum = jnp.stack([wide_sum[:, 0], wide_sum[:, 1]])
-    down_sum = wide_sum[:, 2].T
+    heads_sum = lax.dynamic_slice_in_dim(small_sum, head_at * h_cols, h_cols, 1)
+    shared_sum = small_sum[:, H * RA : H * RA + RA * DH]
+    gains_sum = small_sum[:, H * RA + RA * DH :].T
+    out_sum = out_sum.T
+    gate_up_sum = jnp.stack([gate_sum, up_sum])
+    down_sum = down_sum.T
 
     rates = step_rates()
     heads_new = adam_update(headwise, headwise_mean, headwise_square, heads_sum, rates[0])

time: 767 us -> 1020 us (1.33)
  Pallas kernels: 112 us -> 421 us
  waiting for transfers between devices: 454 us -> 212 us
  starting transfers between devices: 14.5 us -> 167 us
  other arithmetic: 41.5 us -> 75.7 us
  local copies, waits for them, and re-layouts: 49.1 us -> 62 us
  between operations: 15.9 us -> 3.73 us
    pallas_call x0 -> x4, Pallas kernels: none -> 302 us  [place(): pl.pallas_call(place_body, grid_spec=pltpu.PrefetchScalarGridSpec(num_sca...]
    reduce_scatter x3 -> x0, waiting for transfers between devices: 256 us -> none  [the longest x1 164 us: on_device(): lax.psum_scatter(wide_grad, ('a', 'b', 'h'), scatter_dimension=0, tiled=T...]
    all_gather x3 -> x0, waiting for transfers between devices: 167 us -> none  [the longest x1 70.6 us: on_device(): wide_all = lax.all_gather(wide_part, ('a', 'b', 'h'), axis=0, tiled=True)]
    ppermute x0 -> x54, waiting for transfers between devices: none -> 107 us  [the longest x25 55 us: to_ahead(): lax.ppermute(block, axis, [(i, (i + distance) % size) for i in range(size)])]
    ppermute x7 -> x64, waiting for transfers between devices: 19.8 us -> 105 us  [swap(): return lax.ppermute(block, axis, [(0, 1), (1, 0)])]
    ppermute x0 -> x54, starting transfers between devices: none -> 77.2 us  [the longest x29 44.8 us: from_ahead(): lax.ppermute(block, axis, [((i + distance) % size, i) for i in range(size)])]
    ppermute x7 -> x64, starting transfers between devices: 5.41 us -> 62.2 us  [swap(): return lax.ppermute(block, axis, [(0, 1), (1, 0)])]
    another operation x1 -> x27, other arithmetic: 0.04 us -> 20.8 us  [the longest x8 6.29 us: bulk_gather(): t2 = jnp.stack([high, swap(high, 'h')])]
  transfers between devices with their start and end apart: 15 -> 126, of which waited for: 11 -> 58; matrix products, arithmetic and copies ran while one was open for 9% -> 16% of each run, Pallas kernels for 5% -> 42%
where the time goes in v2:
time: 1020 us; the launch traced here: 1010 us
  Pallas kernels  421 us (41%)
  waiting for transfers between devices  212 us (21%)
  starting transfers between devices  167 us (16%)
  other arithmetic  75.7 us (7%)
  matrix products  67.2 us (7%)
  local copies, waits for them, and re-layouts  62 us (6%)
    pallas_call x4, Pallas kernels, place(): pl.pallas_call(place_body, grid_spec=pltpu.PrefetchScalarGridSpec(num_sca...  302 us
    ppermute x64, waiting for transfers between devices, swap(): return lax.ppermute(block, axis, [(0, 1), (1, 0)])  105 us
    pallas_call x2, Pallas kernels, attention_backward(): pl.pallas_call(backward_body, grid=(count, H // HB), in_specs=[pl.BlockSp...  66 us
    ppermute x64, starting transfers between devices, swap(): return lax.ppermute(block, axis, [(0, 1), (1, 0)])  62.2 us
    ppermute x25, waiting for transfers between devices, to_ahead(): lax.ppermute(block, axis, [(i, (i + distance) % size) for i in range(size)])  55 us
    ppermute x29, waiting for transfers between devices, from_ahead(): lax.ppermute(block, axis, [((i + distance) % size, i) for i in range(size)])  52.1 us
    ppermute x29, starting transfers between devices, from_ahead(): lax.ppermute(block, axis, [((i + distance) % size, i) for i in range(size)])  44.8 us
    pallas_call x2, Pallas kernels, attention_forward(): pl.pallas_call(forward_body, grid=(count, H // HB), in_specs=[pl.BlockSpe...  41.2 us
  transfers between devices with their start and end apart: 126, of which 58 were waited for; matrix products, arithmetic and copies ran while one was open for 16% of the time, Pallas kernels for 42%

profile of v2, /device:TPU:1, one launch (start us, length us, event | category | flops | bytes accessed | tf_op | source)
XLA Modules:
  0.0 1008.0 jit_solution(2553368833025152027)
XLA Ops:
  3.5 4.2 collective-permute-start
  9.1 4.5 collective-permute-start.36
  26.4 3.6 collective-permute-start.62
  37.4 3.5 collective-permute-done.38
  42.1 3.7 collective-permute-done.39
  56.0 5.2 collective-permute-done.56
  61.2 3.5 collective-permute-start.47
  64.8 6.7 collective-permute-start.48
  71.4 8.3 collective-permute-done.64
  80.5 12.0 %collective-permute-start.4 = (bf16[2,4,64,402]{3,2,1,0:T(8,128)(2,1)}, bf16[2,4,64,402]{3,2,1,0:T(8,128)(2,1)}, u32[]{:S(2)}, u32[]{:S(2)}) collective-permute-start(bf16[2,4,64,402]{3,2,1,0:T(8,128)(2,1)} %pad_maximum_fusion.17), channel_id=1, source_target_pairs={{0,2},{2,0},{1,3},{3,1},{4,6},{6,4},{5,7},{7,5},{8,10},{10,8},{9,1... | collective-permute-start | bytes 1234952 | tf_op jit(solution)/shard_map/ppermute | solution.py:325
  98.2 3.0 collective-permute-done.43.r2
  103.2 33.8 %place_rows.4 = bf16[4,2,2,2,32,512]{5,4,3,2,1,0:T(8,128)(2,1)} custom-call(s32[3]{0:T(128)} %pad_add_fusion.at_ref, bf16[2,4,32,512]{3,2,1,0:T(8,128)(2,1)} %copy-done.32, bf16[2,4,32,512]{3,2,1,0:T(8,128)(2,1)} %copy-done.50, bf16[2,4,32,512]{3,2,1,0:T(8,128)(2,1)} %copy-done.31, bf16[2,4,32,512]{3,2,1,0:T(8,128)(2,1)} %copy-done.49), custom_call_target="tpu_custom_call" | custom-call | tf_op jit(solution)/shard_map/place_rows/pallas_call | solution.py:432
  146.4 5.0 collective-permute-start.44
  156.3 18.6 %collective-permute-done.5 = bf16[2,2,4,64,402]{4,3,2,1,0:T(8,128)(2,1)S(1)} collective-permute-done((bf16[2,2,4,64,402]{4,3,2,1,0:T(8,128)(2,1)S(1)}, bf16[2,2,4,64,402]{4,3,2,1,0:T(8,128)(2,1)S(1)}, u32[]{:S(2)}, u32[]{:S(2)}) %collective-permute-start.5) | collective-permute-done | bytes 823328 | tf_op jit(solution)/shard_map/ppermute | solution.py:325
  178.9 3.9 convolution_bitcast_fusion.f_ref
  182.8 4.1 factor_prologue.1
  188.0 5.2 collective-permute-start.6
  195.6 3.0 broadcast_select_fusion.1
  214.2 8.0 collective-permute-done.22
  228.9 3.7 collective-permute-done.11
  232.6 5.2 collective-permute-start.13
  245.5 3.7 collective-permute-done.25
  264.3 20.6 %attention_forward.2 = (f32[2,128,1024]{2,1,0:T(8,128)}, f32[2,4,128,4]{3,2,1,0:T(8,128)}) custom-call(bf16[2,128,1024]{2,1,0:T(8,128)(2,1)} %get-tuple-element.269.q_ref, bf16[2,320,2048]{2,1,0:T(8,128)(2,1)} %copy-done.1, bf16[2,320,2048]{2,1,0:T(8,128)(2,1)} %copy-done.1, s32[1,2048]{1,0:T(1,128)} %bitcast.457, s32[128,1]{1,0:T(8,128)} %iota_add_fusion.qpos_ref), custom_call_target="tpu_custom_call" | custom-call | tf_op jit(solution)/shard_map/attention_forward/pallas_call | solution.py:219
  289.3 20.6 %attention_forward.3 = (f32[2,128,1024]{2,1,0:T(8,128)}, f32[2,4,128,4]{3,2,1,0:T(8,128)}) custom-call(bf16[2,128,1024]{2,1,0:T(8,128)(2,1)} %get-tuple-element.270.q_ref, bf16[2,320,2048]{2,1,0:T(8,128)(2,1)} %copy-done, bf16[2,320,2048]{2,1,0:T(8,128)(2,1)} %copy-done, s32[1,2048]{1,0:T(1,128)} %bitcast.458, s32[128,1]{1,0:T(8,128)} %iota_add_fusion.qpos_ref), custom_call_target="tpu_custom_call" | custom-call | tf_op jit(solution)/shard_map/attention_forward/pallas_call | solution.py:219
  312.3 3.2 multiply_reduce_fusion.2
  324.8 89.4 %place_rows.6 = bf16[4,2,2,2,32,1408]{5,4,3,2,1,0:T(8,128)(2,1)} custom-call(s32[3]{0:T(128)} %pad_add_fusion.at_ref, bf16[2,4,32,1408]{3,2,1,0:T(8,128)(2,1)} %pad_maximum_fusion.11.t1, bf16[2,4,32,1408]{3,2,1,0:T(8,128)(2,1)} %collective-permute-done.59.r1, bf16[2,4,32,1408]{3,2,1,0:T(8,128)(2,1)} %pad_maximum_fusion.12.t2, ...), custom_call_target="tpu_custom_call" | custom-call | tf_op jit(solution)/shard_map/place_rows/pallas_call | solution.py:432
  414.2 89.4 %place_rows.7 = bf16[4,2,2,2,32,1408]{5,4,3,2,1,0:T(8,128)(2,1)} custom-call(s32[3]{0:T(128)} %pad_add_fusion.at_ref, bf16[2,4,32,1408]{3,2,1,0:T(8,128)(2,1)} %pad_maximum_fusion.13.t1, bf16[2,4,32,1408]{3,2,1,0:T(8,128)(2,1)} %collective-permute-done.67.r1, bf16[2,4,32,1408]{3,2,1,0:T(8,128)(2,1)} %pad_maximum_fusion.14.t2, ...), custom_call_target="tpu_custom_call" | custom-call | tf_op jit(solution)/shard_map/place_rows/pallas_call | solution.py:432
  503.6 89.4 %place_rows.5 = bf16[4,2,2,2,32,1408]{5,4,3,2,1,0:T(8,128)(2,1)} custom-call(s32[3]{0:T(128)} %pad_add_fusion.at_ref, bf16[2,4,32,1408]{3,2,1,0:T(8,128)(2,1)} %pad_maximum_fusion.9.t1, bf16[2,4,32,1408]{3,2,1,0:T(8,128)(2,1)} %collective-permute-done.51.r1, bf16[2,4,32,1408]{3,2,1,0:T(8,128)(2,1)} %pad_maximum_fusion.10.t2, ...), custom_call_target="tpu_custom_call" | custom-call | tf_op jit(solution)/shard_map/place_rows/pallas_call | solution.py:432
  593.1 6.0 fusion.26
  601.5 5.1 fusion.131
  606.6 9.0 multiply_convert_fusion.1
  615.6 5.3 fusion.157
  620.9 3.4 convolution_add_fusion
  624.6 3.4 fusion.156
  628.8 6.8 convolution_convert_fusion
  641.6 5.4 convolution_convert_fusion.1
  646.9 5.5 convolution_convert_fusion.2
  666.7 32.9 %attention_backward.2 = (f32[2,128,1024]{2,1,0:T(8,128)}, bf16[4,2,320,128]{3,2,1,0:T(8,128)(2,1)}, bf16[4,2,320,128]{3,2,1,0:T(8,128)(2,1)}, bf16[4,2,320,128]{3,2,1,0:T(8,128)(2,1)}, bf16[4,2,320,128]{3,2,1,0:T(8,128)(2,1)}) custom-call(bf16[2,128,1024]{2,1,0:T(8,128)(2,1)} %get-tuple-element.269.q_ref, bf16[2,128,1024]{2,1,0:T(8,128)(2,1)} %get-tuple-element.267.do_ref, ...), custom_call_target="tpu_custom_call" | custom-call | tf_op jit(solution)/shard_map/attention_backward/pallas_call | solution.py:302
  723.8 3.4 collective-permute-start.101
  732.5 33.1 %attention_backward.3 = (f32[2,128,1024]{2,1,0:T(8,128)}, bf16[4,2,320,128]{3,2,1,0:T(8,128)(2,1)}, bf16[4,2,320,128]{3,2,1,0:T(8,128)(2,1)}, bf16[4,2,320,128]{3,2,1,0:T(8,128)(2,1)}, bf16[4,2,320,128]{3,2,1,0:T(8,128)(2,1)}) custom-call(bf16[2,128,1024]{2,1,0:T(8,128)(2,1)} %get-tuple-element.270.q_ref, bf16[2,128,1024]{2,1,0:T(8,128)(2,1)} %get-tuple-element.268.do_ref, ...), custom_call_target="tpu_custom_call" | custom-call | tf_op jit(solution)/shard_map/attention_backward/pallas_call | solution.py:302
  779.0 8.3 collective-permute-done.104
  790.1 12.6 %collective-permute-done.112 = bf16[4,2,32,1408]{3,2,0,1:T(8,128)(2,1)S(1)} collective-permute-done((bf16[4,2,32,1408]{3,2,0,1:T(8,128)(2,1)S(1)}, bf16[4,2,32,1408]{3,2,0,1:T(8,128)(2,1)S(1)}, u32[]{:S(2)}, u32[]{:S(2)}) %collective-permute-start.112) | collective-permute-done | bytes 720928 | tf_op jit(solution)/shard_map/ppermute | solution.py:325
  805.6 7.5 collective-permute-done.121
  813.2 25.3 %collective-permute-done.119 = bf16[4,32,1408]{2,1,0:T(8,128)(2,1)S(1)} collective-permute-done((bf16[4,32,1408]{2,1,0:T(8,128)(2,1)S(1)}, bf16[4,32,1408]{2,1,0:T(8,128)(2,1)S(1)}, u32[]{:S(2)}, u32[]{:S(2)}) %collective-permute-start.119) | collective-permute-done | bytes 360480 | tf_op jit(solution)/shard_map/ppermute | solution.py:325
  840.3 6.0 collective-permute-done.103
  848.4 5.6 collective-permute-done.111
  855.7 7.1 collective-permute-done.123
  862.8 4.0 collective-permute-done.124
  867.6 6.8 collective-permute-start.114
  876.6 8.6 collective-permute-done.108
  888.0 4.1 collective-permute-done.115
  892.1 3.2 collective-permute-start.109
  903.9 6.8 collective-permute-done.79
  910.7 4.0 collective-permute-start.86
  915.6 3.5 factor_epilogue.2
  919.1 6.9 collective-permute-start.117
  928.1 3.6 factor_epilogue.3
  931.8 5.1 fusion.12
  939.3 3.7 copy.233
  943.0 4.5 copy.234
  947.5 3.0 fusion.16
  953.1 5.1 collective-permute-start.88
  970.9 8.2 collective-permute-done.89
  989.4 8.1 collective-permute-done.91
  (576 shorter events, 258.4 us)
Async XLA Ops:
  3.5 22.9 %collective-permute-start = (bf16[64,402]{1,0:T(8,128)(2,1)S(1)}, bf16[64,402]{1,0:T(8,128)(2,1)S(1)}, u32[]{:S(2)}, u32[]{:S(2)}) collective-permute-start(bf16[64,402]{1,0:T(8,128)(2,1)S(1)} %pad_maximum_fusion.29), channel_id=1, source_target_pairs={{8,0},{16,8},{24,16},{0,24},{9,1},{17,9},{25,17},{1,25},{10,2},{18... | collective-permute-start | bytes 154376 | tf_op jit(solution)/shard_map/ppermute | solution.py:334
  7.7 22.3 %collective-permute-start.1 = (bf16[64,402]{1,0:T(8,128)(2,1)S(1)}, bf16[64,402]{1,0:T(8,128)(2,1)S(1)}, u32[]{:S(2)}, u32[]{:S(2)}) collective-permute-start(bf16[64,402]{1,0:T(8,128)(2,1)S(1)} %pad_maximum_fusion.29), channel_id=1, source_target_pairs={{16,0},{24,8},{0,16},{8,24},{17,1},{25,9},{1,17},{9,25},{18,2},{26... | collective-permute-start | bytes 154376 | tf_op jit(solution)/shard_map/ppermute | solution.py:334
  7.7 22.4 %collective-permute-start.2 = (bf16[64,402]{1,0:T(8,128)(2,1)S(1)}, bf16[64,402]{1,0:T(8,128)(2,1)S(1)}, u32[]{:S(2)}, u32[]{:S(2)}) collective-permute-start(bf16[64,402]{1,0:T(8,128)(2,1)S(1)} %pad_maximum_fusion.29), channel_id=1, source_target_pairs={{24,0},{0,8},{8,16},{16,24},{25,1},{1,9},{9,17},{17,25},{26,2},{2,... | collective-permute-start | bytes 154376 | tf_op jit(solution)/shard_map/ppermute | solution.py:334
  9.1 23.2 %collective-permute-start.36 = (bf16[64,512]{1,0:T(8,128)(2,1)S(1)}, bf16[64,512]{1,0:T(8,128)(2,1)S(1)}, u32[]{:S(2)}, u32[]{:S(2)}) collective-permute-start(bf16[64,512]{1,0:T(8,128)(2,1)S(1)} %convert_bitcast_fusion.2), channel_id=1, source_target_pairs={{0,0},{1,2},{2,1},{3,3},{4,4},{5,6},{6,5},{7,7},{8,8},{9,10},{10,9... | collective-permute-start | bytes 196616 | tf_op jit(solution)/shard_map/ppermute | solution.py:329
  14.8 32.3 %collective-permute-start.54 = (bf16[64,1408]{1,0:T(8,128)(2,1)S(1)}, bf16[64,1408]{1,0:T(8,128)(2,1)S(1)}, u32[]{:S(2)}, u32[]{:S(2)}) collective-permute-start(bf16[64,1408]{1,0:T(8,128)(2,1)S(1)} %get-tuple-element.300), channel_id=1, source_target_pairs={{0,0},{1,2},{2,1},{3,3},{4,4},{5,6},{6,5},{7,7},{8,8},{9,10},{10,9... | collective-permute-start | bytes 540680 | tf_op jit(solution)/shard_map/ppermute | solution.py:329
  26.4 20.9 %collective-permute-start.62 = (bf16[64,1408]{1,0:T(8,128)(2,1)S(1)}, bf16[64,1408]{1,0:T(8,128)(2,1)S(1)}, u32[]{:S(2)}, u32[]{:S(2)}) collective-permute-start(bf16[64,1408]{1,0:T(8,128)(2,1)S(1)} %convert_bitcast_fusion.1), channel_id=1, source_target_pairs={{0,0},{1,2},{2,1},{3,3},{4,4},{5,6},{6,5},{7,7},{8,8},{9,10},{10,9... | collective-permute-start | bytes 540680 | tf_op jit(solution)/shard_map/ppermute | solution.py:329
  30.0 563.1 %collective-permute-start.72 = (bf16[512,1024]{1,0:T(8,128)(2,1)}, bf16[512,1024]{1,0:T(8,128)(2,1)}, u32[]{:S(2)}, u32[]{:S(2)}) collective-permute-start(bf16[512,1024]{1,0:T(8,128)(2,1)} %bitcast.101), channel_id=1, source_target_pairs={{0,2},{2,0},{1,3},{3,1},{4,6},{6,4},{5,7},{7,5},{8,10},{10,8},{9,1... | collective-permute-start | bytes 3145736 | tf_op jit(solution)/shard_map/ppermute | solution.py:325
  30.1 17.5 %collective-permute-start.46 = (bf16[64,1408]{1,0:T(8,128)(2,1)S(1)}, bf16[64,1408]{1,0:T(8,128)(2,1)S(1)}, u32[]{:S(2)}, u32[]{:S(2)}) collective-permute-start(bf16[64,1408]{1,0:T(8,128)(2,1)S(1)} %get-tuple-element.299), channel_id=1, source_target_pairs={{0,0},{1,2},{2,1},{3,3},{4,4},{5,6},{6,5},{7,7},{8,8},{9,10},{10,9... | collective-permute-start | bytes 540680 | tf_op jit(solution)/shard_map/ppermute | solution.py:329
  55.4 24.4 %collective-permute-start.64 = (bf16[64,1408]{1,0:T(8,128)(2,1)S(1)}, bf16[64,1408]{1,0:T(8,128)(2,1)S(1)}, u32[]{:S(2)}, u32[]{:S(2)}) collective-permute-start(bf16[64,1408]{1,0:T(8,128)(2,1)S(1)} %collective-permute-done.62), channel_id=1, source_target_pairs={{16,0},{24,8},{0,16},{8,24},{17,1},{25,9},{1,17},{9,25},{18,2},{26... | collective-permute-start | bytes 540680 | tf_op jit(solution)/shard_map/ppermute | solution.py:334
  61.2 19.3 %collective-permute-start.65 = (bf16[64,1408]{1,0:T(8,128)(2,1)S(1)}, bf16[64,1408]{1,0:T(8,128)(2,1)S(1)}, u32[]{:S(2)}, u32[]{:S(2)}) collective-permute-start(bf16[64,1408]{1,0:T(8,128)(2,1)S(1)} %collective-permute-done.62), channel_id=1, source_target_pairs={{24,0},{0,8},{8,16},{16,24},{25,1},{1,9},{9,17},{17,25},{26,2},{2,... | collective-permute-start | bytes 540680 | tf_op jit(solution)/shard_map/ppermute | solution.py:334
  61.2 32.1 %collective-permute-start.47 = (bf16[64,1408]{1,0:T(8,128)(2,1)S(1)}, bf16[64,1408]{1,0:T(8,128)(2,1)S(1)}, u32[]{:S(2)}, u32[]{:S(2)}) collective-permute-start(bf16[64,1408]{1,0:T(8,128)(2,1)S(1)} %collective-permute-done.46), channel_id=1, source_target_pairs={{8,0},{16,8},{24,16},{0,24},{9,1},{17,9},{25,17},{1,25},{10,2},{18... | collective-permute-start | bytes 540680 | tf_op jit(solution)/shard_map/ppermute | solution.py:334
  64.8 30.6 %collective-permute-start.48 = (bf16[64,1408]{1,0:T(8,128)(2,1)S(1)}, bf16[64,1408]{1,0:T(8,128)(2,1)S(1)}, u32[]{:S(2)}, u32[]{:S(2)}) collective-permute-start(bf16[64,1408]{1,0:T(8,128)(2,1)S(1)} %collective-permute-done.46), channel_id=1, source_target_pairs={{16,0},{24,8},{0,16},{8,24},{17,1},{25,9},{1,17},{9,25},{18,2},{26... | collective-permute-start | bytes 540680 | tf_op jit(solution)/shard_map/ppermute | solution.py:334
  79.7 16.6 %collective-permute-start.49 = (bf16[64,1408]{1,0:T(8,128)(2,1)S(1)}, bf16[64,1408]{1,0:T(8,128)(2,1)S(1)}, u32[]{:S(2)}, u32[]{:S(2)}) collective-permute-start(bf16[64,1408]{1,0:T(8,128)(2,1)S(1)} %collective-permute-done.46), channel_id=1, source_target_pairs={{24,0},{0,8},{8,16},{16,24},{25,1},{1,9},{9,17},{17,25},{26,2},{2,... | collective-permute-start | bytes 540680 | tf_op jit(solution)/shard_map/ppermute | solution.py:334
  80.5 56.5 %collective-permute-start.4 = (bf16[2,4,64,402]{3,2,1,0:T(8,128)(2,1)}, bf16[2,4,64,402]{3,2,1,0:T(8,128)(2,1)}, u32[]{:S(2)}, u32[]{:S(2)}) collective-permute-start(bf16[2,4,64,402]{3,2,1,0:T(8,128)(2,1)} %pad_maximum_fusion.17), channel_id=1, source_target_pairs={{0,2},{2,0},{1,3},{3,1},{4,6},{6,4},{5,7},{7,5},{8,10},{10,8},{9,1... | collective-permute-start | bytes 1234952 | tf_op jit(solution)/shard_map/ppermute | solution.py:325
  96.3 43.5 %collective-permute-start.58 = (bf16[4,32,1408]{2,1,0:T(8,128)(2,1)}, bf16[4,32,1408]{2,1,0:T(8,128)(2,1)}, u32[]{:S(2)}, u32[]{:S(2)}) collective-permute-start(bf16[4,32,1408]{2,1,0:T(8,128)(2,1)} %get-tuple-element.304), channel_id=1, source_target_pairs={{0,4},{4,0},{1,5},{5,1},{2,6},{6,2},{3,7},{7,3},{8,12},{12,8},{9,1... | collective-permute-start | bytes 1081352 | tf_op jit(solution)/shard_map/ppermute | solution.py:325
  101.2 40.8 %collective-permute-start.60 = (bf16[4,32,1408]{2,1,0:T(8,128)(2,1)}, bf16[4,32,1408]{2,1,0:T(8,128)(2,1)}, u32[]{:S(2)}, u32[]{:S(2)}) collective-permute-start(bf16[4,32,1408]{2,1,0:T(8,128)(2,1)} %get-tuple-element.302), channel_id=1, source_target_pairs={{0,1},{1,0},{2,3},{3,2},{4,5},{5,4},{6,7},{7,6},{8,9},{9,8},{10,11... | collective-permute-start | bytes 1081352 | tf_op jit(solution)/shard_map/ppermute | solution.py:325
  102.4 42.1 %collective-permute-start.66 = (bf16[4,32,1408]{2,1,0:T(8,128)(2,1)}, bf16[4,32,1408]{2,1,0:T(8,128)(2,1)S(1)}, u32[]{:S(2)}, u32[]{:S(2)}) collective-permute-start(bf16[4,32,1408]{2,1,0:T(8,128)(2,1)} %get-tuple-element.294), channel_id=1, source_target_pairs={{0,4},{4,0},{1,5},{5,1},{2,6},{6,2},{3,7},{7,3},{8,12},{12,8},{9,1... | collective-permute-start | bytes 1081352 | tf_op jit(solution)/shard_map/ppermute | solution.py:325
  142.1 13.3 %collective-permute-start.52 = (bf16[4,32,1408]{2,1,0:T(8,128)(2,1)S(1)}, bf16[4,32,1408]{2,1,0:T(8,128)(2,1)S(1)}, u32[]{:S(2)}, u32[]{:S(2)}) collective-permute-start(bf16[4,32,1408]{2,1,0:T(8,128)(2,1)S(1)} %copy-done.45), channel_id=1, source_target_pairs={{0,1},{1,0},{2,3},{3,2},{4,5},{5,4},{6,7},{7,6},{8,9},{9,8},{10,11... | collective-permute-start | bytes 1081352 | tf_op jit(solution)/shard_map/ppermute | solution.py:325
  144.5 30.5 %collective-permute-start.5 = (bf16[2,2,4,64,402]{4,3,2,1,0:T(8,128)(2,1)S(1)}, bf16[2,2,4,64,402]{4,3,2,1,0:T(8,128)(2,1)S(1)}, u32[]{:S(2)}, u32[]{:S(2)}) collective-permute-start(bf16[2,2,4,64,402]{4,3,2,1,0:T(8,128)(2,1)S(1)} %pad_maximum_fusion.7), channel_id=1, source_target_pairs={{0,1},{1,0},{2,3},{3,2},{4,5},{5,4},{6,7},{7,6},{8,9},{9,8},{10,11... | collective-permute-start | bytes 2469896 | tf_op jit(solution)/shard_map/ppermute | solution.py:325
  146.4 49.1 %collective-permute-start.44 = (bf16[1024,512]{1,0:T(8,128)(2,1)}, bf16[1024,512]{1,0:T(8,128)(2,1)}, u32[]{:S(2)}, u32[]{:S(2)}) collective-permute-start(bf16[1024,512]{1,0:T(8,128)(2,1)} %bitcast.54), channel_id=1, source_target_pairs={{0,2},{2,0},{1,3},{3,1},{4,6},{6,4},{5,7},{7,5},{8,10},{10,8},{9,1... | collective-permute-start | bytes 3145736 | tf_op jit(solution)/shard_map/ppermute | solution.py:325
  152.3 158.9 %collective-permute-start.59 = (bf16[2,4,32,1408]{3,2,1,0:T(8,128)(2,1)}, bf16[2,4,32,1408]{3,2,1,0:T(8,128)(2,1)}, u32[]{:S(2)}, u32[]{:S(2)}) collective-permute-start(bf16[2,4,32,1408]{3,2,1,0:T(8,128)(2,1)} %pad_maximum_fusion.11.t1), channel_id=1, source_target_pairs={{0,1},{1,0},{2,3},{3,2},{4,5},{5,4},{6,7},{7,6},{8,9},{9,8},{10,11... | collective-permute-start | bytes 2162696 | tf_op jit(solution)/shard_map/ppermute | solution.py:325
  155.4 156.9 %collective-permute-start.61 = (bf16[2,4,32,1408]{3,2,1,0:T(8,128)(2,1)}, bf16[2,4,32,1408]{3,2,1,0:T(8,128)(2,1)}, u32[]{:S(2)}, u32[]{:S(2)}) collective-permute-start(bf16[2,4,32,1408]{3,2,1,0:T(8,128)(2,1)} %pad_maximum_fusion.12.t2), channel_id=1, source_target_pairs={{0,4},{4,0},{1,5},{5,1},{2,6},{6,2},{3,7},{7,3},{8,12},{12,8},{9,1... | collective-permute-start | bytes 2162696 | tf_op jit(solution)/shard_map/ppermute | solution.py:325
  207.9 14.3 %collective-permute-start.22 = (bf16[2,320,128]{2,1,0:T(8,128)(2,1)S(1)}, bf16[2,320,128]{2,1,0:T(8,128)(2,1)S(1)}, u32[]{:S(2)}, u32[]{:S(2)}) collective-permute-start(bf16[2,320,128]{2,1,0:T(8,128)(2,1)S(1)} %get-tuple-element.308), channel_id=1, source_target_pairs={{16,0},{24,8},{0,16},{8,24},{17,1},{25,9},{1,17},{9,25},{18,2},{26... | collective-permute-start | bytes 491528 | tf_op jit(solution)/shard_map/ppermute | solution.py:334
  262.9 23.4 %collective-permute-start.35 = (bf16[2,320,128]{2,1,0:T(8,128)(2,1)S(1)}, bf16[2,320,128]{2,1,0:T(8,128)(2,1)S(1)}, u32[]{:S(2)}, u32[]{:S(2)}) collective-permute-start(bf16[2,320,128]{2,1,0:T(8,128)(2,1)S(1)} %collective-permute-done.27), channel_id=1, source_target_pairs={{0,2},{2,0},{1,3},{3,1},{4,6},{6,4},{5,7},{7,5},{8,10},{10,8},{9,1... | collective-permute-start | bytes 491528 | tf_op jit(solution)/shard_map/ppermute | solution.py:325
  263.7 53.1 %collective-permute-start.67 = (bf16[2,4,32,1408]{3,2,1,0:T(8,128)(2,1)}, bf16[2,4,32,1408]{3,2,1,0:T(8,128)(2,1)}, u32[]{:S(2)}, u32[]{:S(2)}) collective-permute-start(bf16[2,4,32,1408]{3,2,1,0:T(8,128)(2,1)} %pad_maximum_fusion.13.t1), channel_id=1, source_target_pairs={{0,1},{1,0},{2,3},{3,2},{4,5},{5,4},{6,7},{7,6},{8,9},{9,8},{10,11... | collective-permute-start | bytes 2162696 | tf_op jit(solution)/shard_map/ppermute | solution.py:325
  286.2 128.0 %collective-permute-start.69 = (bf16[2,4,32,1408]{3,2,1,0:T(8,128)(2,1)}, bf16[2,4,32,1408]{3,2,1,0:T(8,128)(2,1)}, u32[]{:S(2)}, u32[]{:S(2)}) collective-permute-start(bf16[2,4,32,1408]{3,2,1,0:T(8,128)(2,1)} %pad_maximum_fusion.14.t2), channel_id=1, source_target_pairs={{0,4},{4,0},{1,5},{5,1},{2,6},{6,2},{3,7},{7,3},{8,12},{12,8},{9,1... | collective-permute-start | bytes 2162696 | tf_op jit(solution)/shard_map/ppermute | solution.py:325
  311.2 192.4 %collective-permute-start.51 = (bf16[2,4,32,1408]{3,2,1,0:T(8,128)(2,1)}, bf16[2,4,32,1408]{3,2,1,0:T(8,128)(2,1)}, u32[]{:S(2)}, u32[]{:S(2)}) collective-permute-start(bf16[2,4,32,1408]{3,2,1,0:T(8,128)(2,1)} %pad_maximum_fusion.9.t1), channel_id=1, source_target_pairs={{0,1},{1,0},{2,3},{3,2},{4,5},{5,4},{6,7},{7,6},{8,9},{9,8},{10,11... | collective-permute-start | bytes 2162696 | tf_op jit(solution)/shard_map/ppermute | solution.py:325
  312.3 191.4 %collective-permute-start.53 = (bf16[2,4,32,1408]{3,2,1,0:T(8,128)(2,1)}, bf16[2,4,32,1408]{3,2,1,0:T(8,128)(2,1)}, u32[]{:S(2)}, u32[]{:S(2)}) collective-permute-start(bf16[2,4,32,1408]{3,2,1,0:T(8,128)(2,1)} %pad_maximum_fusion.10.t2), channel_id=1, source_target_pairs={{0,4},{4,0},{1,5},{5,1},{2,6},{6,2},{3,7},{7,3},{8,12},{12,8},{9,1... | collective-permute-start | bytes 2162696 | tf_op jit(solution)/shard_map/ppermute | solution.py:325
  316.8 283.6 %collective-permute-start.45 = (bf16[512,1024]{1,0:T(8,128)(2,1)}, bf16[512,1024]{1,0:T(8,128)(2,1)}, u32[]{:S(2)}, u32[]{:S(2)}) collective-permute-start(bf16[512,1024]{1,0:T(8,128)(2,1)} %bitcast.57), channel_id=1, source_target_pairs={{0,2},{2,0},{1,3},{3,1},{4,6},{6,4},{5,7},{7,5},{8,10},{10,8},{9,1... | collective-permute-start | bytes 3145736 | tf_op jit(solution)/shard_map/ppermute | solution.py:325
  652.5 52.6 %collective-permute-start.71 = (bf16[4,128,1024]{2,1,0:T(8,128)(2,1)}, bf16[4,128,1024]{2,1,0:T(8,128)(2,1)}, u32[]{:S(2)}, u32[]{:S(2)}) collective-permute-start(bf16[4,128,1024]{2,1,0:T(8,128)(2,1)} %get-tuple-element.238), channel_id=1, source_target_pairs={{0,1},{1,0},{2,3},{3,2},{4,5},{5,4},{6,7},{7,6},{8,9},{9,8},{10,11... | collective-permute-start | bytes 3145736 | tf_op jit(solution)/shard_map/ppermute | solution.py:325
  656.9 116.3 %collective-permute-start.120 = (bf16[4,2,32,1408]{3,2,0,1:T(8,128)(2,1)}, bf16[4,2,32,1408]{3,2,0,1:T(8,128)(2,1)}, u32[]{:S(2)}, u32[]{:S(2)}) collective-permute-start(bf16[4,2,32,1408]{3,2,0,1:T(8,128)(2,1)} %bitcast.419), channel_id=1, source_target_pairs={{0,4},{4,0},{1,5},{5,1},{2,6},{6,2},{3,7},{7,3},{8,12},{12,8},{9,1... | collective-permute-start | bytes 2162696 | tf_op jit(solution)/shard_map/ppermute | solution.py:325
  661.5 45.5 %collective-permute-start.96 = (bf16[4,2,32,512]{3,2,0,1:T(8,128)(2,1)}, bf16[4,2,32,512]{3,2,0,1:T(8,128)(2,1)}, u32[]{:S(2)}, u32[]{:S(2)}) collective-permute-start(bf16[4,2,32,512]{3,2,0,1:T(8,128)(2,1)} %bitcast.425), channel_id=1, source_target_pairs={{0,4},{4,0},{1,5},{5,1},{2,6},{6,2},{3,7},{7,3},{8,12},{12,8},{9,1... | collective-permute-start | bytes 786440 | tf_op jit(solution)/shard_map/ppermute | solution.py:325
  664.2 43.9 %collective-permute-start.94 = (bf16[4,2,32,512]{3,2,0,1:T(8,128)(2,1)}, bf16[4,2,32,512]{3,2,0,1:T(8,128)(2,1)}, u32[]{:S(2)}, u32[]{:S(2)}) collective-permute-start(bf16[4,2,32,512]{3,2,0,1:T(8,128)(2,1)} %bitcast.426), channel_id=1, source_target_pairs={{0,1},{1,0},{2,3},{3,2},{4,5},{5,4},{6,7},{7,6},{8,9},{9,8},{10,11... | collective-permute-start | bytes 786440 | tf_op jit(solution)/shard_map/ppermute | solution.py:325
  699.6 68.1 %collective-permute-start.75 = (bf16[4,2,320,128]{3,2,1,0:T(8,128)(2,1)}, bf16[4,2,320,128]{3,2,1,0:T(8,128)(2,1)}, u32[]{:S(2)}, u32[]{:S(2)}) collective-permute-start(bf16[4,2,320,128]{3,2,1,0:T(8,128)(2,1)} %get-tuple-element.49), channel_id=1, source_target_pairs={{0,2},{2,0},{1,3},{3,1},{4,6},{6,4},{5,7},{7,5},{8,10},{10,8},{9,1... | collective-permute-start | bytes 1966088 | tf_op jit(solution)/shard_map/ppermute | solution.py:325
  717.5 58.6 %collective-permute-start.118 = (bf16[4,2,32,1408]{3,2,0,1:T(8,128)(2,1)}, bf16[4,2,32,1408]{3,2,0,1:T(8,128)(2,1)}, u32[]{:S(2)}, u32[]{:S(2)}) collective-permute-start(bf16[4,2,32,1408]{3,2,0,1:T(8,128)(2,1)} %bitcast.420), channel_id=1, source_target_pairs={{0,1},{1,0},{2,3},{3,2},{4,5},{5,4},{6,7},{7,6},{8,9},{9,8},{10,11... | collective-permute-start | bytes 2162696 | tf_op jit(solution)/shard_map/ppermute | solution.py:325
  720.0 49.7 %collective-permute-start.76 = (bf16[4,2,320,128]{3,2,1,0:T(8,128)(2,1)}, bf16[4,2,320,128]{3,2,1,0:T(8,128)(2,1)}, u32[]{:S(2)}, u32[]{:S(2)}) collective-permute-start(bf16[4,2,320,128]{3,2,1,0:T(8,128)(2,1)} %get-tuple-element.51), channel_id=1, source_target_pairs={{0,2},{2,0},{1,3},{3,1},{4,6},{6,4},{5,7},{7,5},{8,10},{10,8},{9,1... | collective-permute-start | bytes 1966088 | tf_op jit(solution)/shard_map/ppermute | solution.py:325
  723.8 41.8 %collective-permute-start.101 = (bf16[64,512]{1,0:T(8,128)(2,1)}, bf16[64,512]{1,0:T(8,128)(2,1)}, u32[]{:S(2)}, u32[]{:S(2)}) collective-permute-start(bf16[64,512]{1,0:T(8,128)(2,1)} %fusion.100), channel_id=1, source_target_pairs={{0,0},{1,2},{2,1},{3,3},{4,4},{5,6},{6,5},{7,7},{8,8},{9,10},{10,9... | collective-permute-start | bytes 196616 | tf_op jit(solution)/shard_map/ppermute | solution.py:329
  769.7 17.6 %collective-permute-start.104 = (bf16[4,2,32,1408]{3,2,0,1:T(8,128)(2,1)S(1)}, bf16[4,2,32,1408]{3,2,0,1:T(8,128)(2,1)S(1)}, u32[]{:S(2)}, u32[]{:S(2)}) collective-permute-start(bf16[4,2,32,1408]{3,2,0,1:T(8,128)(2,1)S(1)} %bitcast.449), channel_id=1, source_target_pairs={{0,4},{4,0},{1,5},{5,1},{2,6},{6,2},{3,7},{7,3},{8,12},{12,8},{9,1... | collective-permute-start | bytes 2162696 | tf_op jit(solution)/shard_map/ppermute | solution.py:325
  772.6 17.3 %collective-permute-start.102 = (bf16[4,2,32,1408]{3,2,0,1:T(8,128)(2,1)S(1)}, bf16[4,2,32,1408]{3,2,0,1:T(8,128)(2,1)S(1)}, u32[]{:S(2)}, u32[]{:S(2)}) collective-permute-start(bf16[4,2,32,1408]{3,2,0,1:T(8,128)(2,1)S(1)} %bitcast.448), channel_id=1, source_target_pairs={{0,1},{1,0},{2,3},{3,2},{4,5},{5,4},{6,7},{7,6},{8,9},{9,8},{10,11... | collective-permute-start | bytes 2162696 | tf_op jit(solution)/shard_map/ppermute | solution.py:325
  772.9 29.8 %collective-permute-start.112 = (bf16[4,2,32,1408]{3,2,0,1:T(8,128)(2,1)S(1)}, bf16[4,2,32,1408]{3,2,0,1:T(8,128)(2,1)S(1)}, u32[]{:S(2)}, u32[]{:S(2)}) collective-permute-start(bf16[4,2,32,1408]{3,2,0,1:T(8,128)(2,1)S(1)} %bitcast.447), channel_id=1, source_target_pairs={{0,4},{4,0},{1,5},{5,1},{2,6},{6,2},{3,7},{7,3},{8,12},{12,8},{9,1... | collective-permute-start | bytes 2162696 | tf_op jit(solution)/shard_map/ppermute | solution.py:325
  773.2 32.2 %collective-permute-start.110 = (bf16[4,2,32,1408]{3,2,0,1:T(8,128)(2,1)S(1)}, bf16[4,2,32,1408]{3,2,0,1:T(8,128)(2,1)S(1)}, u32[]{:S(2)}, u32[]{:S(2)}) collective-permute-start(bf16[4,2,32,1408]{3,2,0,1:T(8,128)(2,1)S(1)} %bitcast.446), channel_id=1, source_target_pairs={{0,1},{1,0},{2,3},{3,2},{4,5},{5,4},{6,7},{7,6},{8,9},{9,8},{10,11... | collective-permute-start | bytes 2162696 | tf_op jit(solution)/shard_map/ppermute | solution.py:325
  776.1 121.0 %collective-permute-start.77 = (bf16[4,2,320,128]{3,2,1,0:T(8,128)(2,1)S(1)}, bf16[4,2,320,128]{3,2,1,0:T(8,128)(2,1)S(1)}, u32[]{:S(2)}, u32[]{:S(2)}) collective-permute-start(bf16[4,2,320,128]{3,2,1,0:T(8,128)(2,1)S(1)} %add_convert_fusion.3), channel_id=1, source_target_pairs={{0,4},{4,0},{1,5},{5,1},{2,6},{6,2},{3,7},{7,3},{8,12},{12,8},{9,1... | collective-permute-start | bytes 1966088 | tf_op jit(solution)/shard_map/ppermute | solution.py:339
  787.3 112.5 %collective-permute-start.83 = (bf16[4,2,320,128]{3,2,1,0:T(8,128)(2,1)S(1)}, bf16[4,2,320,128]{3,2,1,0:T(8,128)(2,1)S(1)}, u32[]{:S(2)}, u32[]{:S(2)}) collective-permute-start(bf16[4,2,320,128]{3,2,1,0:T(8,128)(2,1)S(1)} %add_convert_fusion.1), channel_id=1, source_target_pairs={{0,4},{4,0},{1,5},{5,1},{2,6},{6,2},{3,7},{7,3},{8,12},{12,8},{9,1... | collective-permute-start | bytes 1966088 | tf_op jit(solution)/shard_map/ppermute | solution.py:339
  789.9 23.2 %collective-permute-start.121 = (bf16[4,32,1408]{2,1,0:T(8,128)(2,1)S(1)}, bf16[4,32,1408]{2,1,0:T(8,128)(2,1)S(1)}, u32[]{:S(2)}, u32[]{:S(2)}) collective-permute-start(bf16[4,32,1408]{2,1,0:T(8,128)(2,1)S(1)} %dynamic-slice_bitcast_fusion), channel_id=1, source_target_pairs={{0,1},{1,0},{2,3},{3,2},{4,5},{5,4},{6,7},{7,6},{8,9},{9,8},{10,11... | collective-permute-start | bytes 1081352 | tf_op jit(solution)/shard_map/ppermute | solution.py:325
  802.7 35.8 %collective-permute-start.119 = (bf16[4,32,1408]{2,1,0:T(8,128)(2,1)S(1)}, bf16[4,32,1408]{2,1,0:T(8,128)(2,1)S(1)}, u32[]{:S(2)}, u32[]{:S(2)}) collective-permute-start(bf16[4,32,1408]{2,1,0:T(8,128)(2,1)S(1)} %dynamic-slice_bitcast_fusion.1), channel_id=1, source_target_pairs={{0,4},{4,0},{1,5},{5,1},{2,6},{6,2},{3,7},{7,3},{8,12},{12,8},{9,1... | collective-permute-start | bytes 1081352 | tf_op jit(solution)/shard_map/ppermute | solution.py:325
  805.4 33.3 %collective-permute-start.105 = (bf16[4,32,1408]{2,1,0:T(8,128)(2,1)S(1)}, bf16[4,32,1408]{2,1,0:T(8,128)(2,1)S(1)}, u32[]{:S(2)}, u32[]{:S(2)}) collective-permute-start(bf16[4,32,1408]{2,1,0:T(8,128)(2,1)S(1)} %dynamic-slice_bitcast_fusion.4), channel_id=1, source_target_pairs={{0,1},{1,0},{2,3},{3,2},{4,5},{5,4},{6,7},{7,6},{8,9},{9,8},{10,11... | collective-permute-start | bytes 1081352 | tf_op jit(solution)/shard_map/ppermute | solution.py:325
  813.1 33.2 %collective-permute-start.103 = (bf16[4,32,1408]{2,1,0:T(8,128)(2,1)S(1)}, bf16[4,32,1408]{2,1,0:T(8,128)(2,1)S(1)}, u32[]{:S(2)}, u32[]{:S(2)}) collective-permute-start(bf16[4,32,1408]{2,1,0:T(8,128)(2,1)S(1)} %dynamic-slice_bitcast_fusion.5), channel_id=1, source_target_pairs={{0,4},{4,0},{1,5},{5,1},{2,6},{6,2},{3,7},{7,3},{8,12},{12,8},{9,1... | collective-permute-start | bytes 1081352 | tf_op jit(solution)/shard_map/ppermute | solution.py:325
  838.7 15.3 %collective-permute-start.111 = (bf16[4,32,1408]{2,1,0:T(8,128)(2,1)S(1)}, bf16[4,32,1408]{2,1,0:T(8,128)(2,1)S(1)}, u32[]{:S(2)}, u32[]{:S(2)}) collective-permute-start(bf16[4,32,1408]{2,1,0:T(8,128)(2,1)S(1)} %dynamic-slice_bitcast_fusion.3), channel_id=1, source_target_pairs={{0,4},{4,0},{1,5},{5,1},{2,6},{6,2},{3,7},{7,3},{8,12},{12,8},{9,1... | collective-permute-start | bytes 1081352 | tf_op jit(solution)/shard_map/ppermute | solution.py:325
  846.9 16.0 %collective-permute-start.123 = (bf16[64,1408]{1,0:T(8,128)(2,1)S(1)}, bf16[64,1408]{1,0:T(8,128)(2,1)S(1)}, u32[]{:S(2)}, u32[]{:S(2)}) collective-permute-start(bf16[64,1408]{1,0:T(8,128)(2,1)S(1)} %get-tuple-element.277), channel_id=1, source_target_pairs={{0,16},{8,24},{16,0},{24,8},{1,17},{9,25},{17,1},{25,9},{2,18},{10... | collective-permute-start | bytes 540680 | tf_op jit(solution)/shard_map/ppermute | solution.py:339
  854.0 12.8 %collective-permute-start.124 = (bf16[64,1408]{1,0:T(8,128)(2,1)S(1)}, bf16[64,1408]{1,0:T(8,128)(2,1)S(1)}, u32[]{:S(2)}, u32[]{:S(2)}) collective-permute-start(bf16[64,1408]{1,0:T(8,128)(2,1)S(1)} %get-tuple-element.278), channel_id=1, source_target_pairs={{0,24},{8,0},{16,8},{24,16},{1,25},{9,1},{17,9},{25,17},{2,26},{10... | collective-permute-start | bytes 540680 | tf_op jit(solution)/shard_map/ppermute | solution.py:339
  862.8 13.8 %collective-permute-start.107 = (bf16[64,1408]{1,0:T(8,128)(2,1)S(1)}, bf16[64,1408]{1,0:T(8,128)(2,1)S(1)}, u32[]{:S(2)}, u32[]{:S(2)}) collective-permute-start(bf16[64,1408]{1,0:T(8,128)(2,1)S(1)} %get-tuple-element.280), channel_id=1, source_target_pairs={{0,16},{8,24},{16,0},{24,8},{1,17},{9,25},{17,1},{25,9},{2,18},{10... | collective-permute-start | bytes 540680 | tf_op jit(solution)/shard_map/ppermute | solution.py:339
  866.8 18.4 %collective-permute-start.108 = (bf16[64,1408]{1,0:T(8,128)(2,1)S(1)}, bf16[64,1408]{1,0:T(8,128)(2,1)S(1)}, u32[]{:S(2)}, u32[]{:S(2)}) collective-permute-start(bf16[64,1408]{1,0:T(8,128)(2,1)S(1)} %get-tuple-element.281), channel_id=1, source_target_pairs={{0,24},{8,0},{16,8},{24,16},{1,25},{9,1},{17,9},{25,17},{2,26},{10... | collective-permute-start | bytes 540680 | tf_op jit(solution)/shard_map/ppermute | solution.py:339
  867.6 18.4 %collective-permute-start.114 = (bf16[64,1408]{1,0:T(8,128)(2,1)S(1)}, bf16[64,1408]{1,0:T(8,128)(2,1)S(1)}, u32[]{:S(2)}, u32[]{:S(2)}) collective-permute-start(bf16[64,1408]{1,0:T(8,128)(2,1)S(1)} %get-tuple-element.282), channel_id=1, source_target_pairs={{0,8},{8,16},{16,24},{24,0},{1,9},{9,17},{17,25},{25,1},{2,10},{10... | collective-permute-start | bytes 540680 | tf_op jit(solution)/shard_map/ppermute | solution.py:339
  876.6 15.5 %collective-permute-start.115 = (bf16[64,1408]{1,0:T(8,128)(2,1)S(1)}, bf16[64,1408]{1,0:T(8,128)(2,1)S(1)}, u32[]{:S(2)}, u32[]{:S(2)}) collective-permute-start(bf16[64,1408]{1,0:T(8,128)(2,1)S(1)} %get-tuple-element.283), channel_id=1, source_target_pairs={{0,16},{8,24},{16,0},{24,8},{1,17},{9,25},{17,1},{25,9},{2,18},{10... | collective-permute-start | bytes 540680 | tf_op jit(solution)/shard_map/ppermute | solution.py:339
  886.0 82.6 %collective-permute-start.125 = (bf16[64,1408]{1,0:T(8,128)(2,1)}, bf16[64,1408]{1,0:T(8,128)(2,1)}, u32[]{:S(2)}, u32[]{:S(2)}) collective-permute-start(bf16[64,1408]{1,0:T(8,128)(2,1)} %fusion.50), channel_id=1, source_target_pairs={{0,0},{1,2},{2,1},{3,3},{4,4},{5,6},{6,5},{7,7},{8,8},{9,10},{10,9... | collective-permute-start | bytes 540680 | tf_op jit(solution)/shard_map/ppermute | solution.py:329
  892.1 66.1 %collective-permute-start.109 = (bf16[64,1408]{1,0:T(8,128)(2,1)}, bf16[64,1408]{1,0:T(8,128)(2,1)}, u32[]{:S(2)}, u32[]{:S(2)}) collective-permute-start(bf16[64,1408]{1,0:T(8,128)(2,1)} %fusion.56), channel_id=1, source_target_pairs={{0,0},{1,2},{2,1},{3,3},{4,4},{5,6},{6,5},{7,7},{8,8},{9,10},{10,9... | collective-permute-start | bytes 540680 | tf_op jit(solution)/shard_map/ppermute | solution.py:329
  897.3 13.4 %collective-permute-start.79 = (bf16[2,320,128]{2,1,0:T(8,128)(2,1)S(1)}, bf16[2,320,128]{2,1,0:T(8,128)(2,1)S(1)}, u32[]{:S(2)}, u32[]{:S(2)}) collective-permute-start(bf16[2,320,128]{2,1,0:T(8,128)(2,1)S(1)} %get-tuple-element.261), channel_id=1, source_target_pairs={{0,16},{8,24},{16,0},{24,8},{1,17},{9,25},{17,1},{25,9},{2,18},{10... | collective-permute-start | bytes 491528 | tf_op jit(solution)/shard_map/ppermute | solution.py:339
  903.9 15.2 %collective-permute-start.84 = (bf16[2,320,128]{2,1,0:T(8,128)(2,1)}, bf16[2,320,128]{2,1,0:T(8,128)(2,1)}, u32[]{:S(2)}, u32[]{:S(2)}) collective-permute-start(bf16[2,320,128]{2,1,0:T(8,128)(2,1)} %get-tuple-element.262), channel_id=1, source_target_pairs={{0,8},{8,16},{16,24},{24,0},{1,9},{9,17},{17,25},{25,1},{2,10},{10... | collective-permute-start | bytes 491528 | tf_op jit(solution)/shard_map/ppermute | solution.py:339
  910.7 15.3 %collective-permute-start.85 = (bf16[2,320,128]{2,1,0:T(8,128)(2,1)}, bf16[2,320,128]{2,1,0:T(8,128)(2,1)}, u32[]{:S(2)}, u32[]{:S(2)}) collective-permute-start(bf16[2,320,128]{2,1,0:T(8,128)(2,1)} %get-tuple-element.264), channel_id=1, source_target_pairs={{0,16},{8,24},{16,0},{24,8},{1,17},{9,25},{17,1},{25,9},{2,18},{10... | collective-permute-start | bytes 491528 | tf_op jit(solution)/shard_map/ppermute | solution.py:339
  910.7 15.3 %collective-permute-start.86 = (bf16[2,320,128]{2,1,0:T(8,128)(2,1)}, bf16[2,320,128]{2,1,0:T(8,128)(2,1)}, u32[]{:S(2)}, u32[]{:S(2)}) collective-permute-start(bf16[2,320,128]{2,1,0:T(8,128)(2,1)} %get-tuple-element.263), channel_id=1, source_target_pairs={{0,24},{8,0},{16,8},{24,16},{1,25},{9,1},{17,9},{25,17},{2,26},{10... | collective-permute-start | bytes 491528 | tf_op jit(solution)/shard_map/ppermute | solution.py:339
  919.1 39.1 %collective-permute-start.117 = (bf16[64,1408]{1,0:T(8,128)(2,1)}, bf16[64,1408]{1,0:T(8,128)(2,1)}, u32[]{:S(2)}, u32[]{:S(2)}) collective-permute-start(bf16[64,1408]{1,0:T(8,128)(2,1)} %fusion.53), channel_id=1, source_target_pairs={{0,0},{1,2},{2,1},{3,3},{4,4},{5,6},{6,5},{7,7},{8,8},{9,10},{10,9... | collective-permute-start | bytes 540680 | tf_op jit(solution)/shard_map/ppermute | solution.py:329
  962.8 24.9 %collective-permute-start.87 = (bf16[4,128,1024]{2,1,0:T(8,128)(2,1)}, bf16[4,128,1024]{2,1,0:T(8,128)(2,1)}, u32[]{:S(2)}, u32[]{:S(2)}) collective-permute-start(bf16[4,128,1024]{2,1,0:T(8,128)(2,1)} %fusion.11), channel_id=1, source_target_pairs={{0,1},{1,0},{2,3},{3,2},{4,5},{5,4},{6,7},{7,6},{8,9},{9,8},{10,11... | collective-permute-start | bytes 3145736 | tf_op jit(solution)/shard_map/ppermute | solution.py:325
  981.2 16.2 %collective-permute-start.91 = (bf16[64,802]{0,1:T(8,128)(2,1)S(1)}, bf16[64,802]{0,1:T(8,128)(2,1)S(1)}, u32[]{:S(2)}, u32[]{:S(2)}) collective-permute-start(bf16[64,802]{0,1:T(8,128)(2,1)S(1)} %get-tuple-element.275), channel_id=1, source_target_pairs={{0,16},{8,24},{16,0},{24,8},{1,17},{9,25},{17,1},{25,9},{2,18},{10... | collective-permute-start | bytes 307976 | tf_op jit(solution)/shard_map/ppermute | solution.py:339
  982.8 14.7 %collective-permute-start.92 = (bf16[64,802]{0,1:T(8,128)(2,1)S(1)}, bf16[64,802]{0,1:T(8,128)(2,1)S(1)}, u32[]{:S(2)}, u32[]{:S(2)}) collective-permute-start(bf16[64,802]{0,1:T(8,128)(2,1)S(1)} %get-tuple-element.274), channel_id=1, source_target_pairs={{0,24},{8,0},{16,8},{24,16},{1,25},{9,1},{17,9},{25,17},{2,26},{10... | collective-permute-start | bytes 307976 | tf_op jit(solution)/shard_map/ppermute | solution.py:339
  (128 other events, 1329.9 us)

commit v3 on v2

--- a/solution.py
+++ b/solution.py
@@ -152,15 +152,14 @@
                 term = f_ref[0, h * RA + r : h * RA + r + 1, :] * dq
                 sums[r] = term if sums[r] is None else sums[r] + term
             rows.append(df_ref[0, wide + h * 2 * RK : wide + (h + 1) * 2 * RK, :].astype(F32))
-    g_ref[0, :base, :] = jnp.concatenate(rows, axis=0).astype(BF)
     for r in range(RQ):
-        g_ref[0, base + r * DH : base + (r + 1) * DH, :] = unrotated(sums[r], cos_t, sin_t).astype(BF)
+        rows.append(unrotated(sums[r], cos_t, sin_t))
     for r in range(RK):
-        at = base + (RQ + r) * DH
-        part = df_ref[0, r * 2 * DH : (r + 1) * 2 * DH, :].astype(F32)
-        g_ref[0, at : at + DH, :] = unrotated(part[:DH], cos_t, sin_t).astype(BF)
-        at = base + (RQ + RK + r) * DH
-        g_ref[0, at : at + DH, :] = part[DH:].astype(BF)
+        part = df_ref[0, r * 2 * DH : r * 2 * DH + DH, :].astype(F32)
+        rows.append(unrotated(part, cos_t, sin_t))
+    for r in range(RK):
+        rows.append(df_ref[0, r * 2 * DH + DH : (r + 1) * 2 * DH, :].astype(F32))
+    g_ref[0] = jnp.transpose(jnp.concatenate(rows, axis=0)).astype(BF)
 
 
 def epilogue(query_grad, factor_grad, factors, cos_t, sin_t):
@@ -175,8 +174,8 @@
             pl.BlockSpec((DH // 2, block), lambda s: (0, 0)),
             pl.BlockSpec((DH // 2, block), lambda s: (0, 0)),
         ],
-        out_specs=pl.BlockSpec((1, width, block), lambda s: (s, 0, 0)),
-        out_shape=jax.ShapeDtypeStruct((count, width, block), BF),
+        out_specs=pl.BlockSpec((1, block, width), lambda s: (s, 0, 0)),
+        out_shape=jax.ShapeDtypeStruct((count, block, width), BF),
         name="factor_epilogue",
     )(query_grad, factor_grad, factors, cos_t, sin_t)
 
@@ -234,6 +233,11 @@
             jax.ShapeDtypeStruct((count, block, width), F32),
             jax.ShapeDtypeStruct((count, H // HB, block, HB), F32),
         ],
+        cost_estimate=pl.CostEstimate(
+            flops=4 * count * H * block * length * DH,
+            bytes_accessed=2 * count * length * FAC,
+            transcendentals=count * H * block * length,
+        ),
         name="attention_forward",
     )(query, gathered, gathered, key_pos, query_pos)
 
@@ -317,6 +321,11 @@
         out_shape=[jax.ShapeDtypeStruct((count, block, width), F32)]
         + [jax.ShapeDtypeStruct((depth, count, FAC, block), BF)] * pieces,
         scratch_shapes=[pltpu.VMEM((wide, length), F32)],
+        cost_estimate=pl.CostEstimate(
+            flops=10 * count * H * block * length * DH,
+            bytes_accessed=4 * count * length * FAC,
+            transcendentals=count * H * block * length,
+        ),
         name="attention_backward",
     )(query, heads_grad, heads_wide, lse, gathered, gathered, key_pos, query_pos)
 
@@ -365,14 +374,10 @@
 
 
 def gather_blocks(block):
-    order = {}
-    for ma in range(lax.axis_size("a")):
-        at_a = from_ahead(block, "a", ma) if ma else block
-        for mb in range(lax.axis_size("b")):
-            at_b = from_ahead(at_a, "b", mb) if mb else at_a
-            order[0, mb, ma] = at_b
-            order[1, mb, ma] = swap(at_b, "c")
-    return [order[key] for key in sorted(order)]
+    for name in ("a", "b"):
+        ahead = [from_ahead(block, name, m) for m in range(1, lax.axis_size(name))]
+        block = jnp.concatenate([block] + ahead, axis=2)
+    return jnp.concatenate([block, swap(block, "c")], axis=2)
 
 
 def blocks_ahead():
@@ -388,93 +393,19 @@
     return jnp.stack(spots)
 
 
-def scatter_blocks(pieces):
-    na, nb = lax.axis_size("a"), lax.axis_size("b")
-    after_core = []
-    for mb in range(nb):
-        other = swap(pieces[nb + mb], "c")
-        after_core.append((pieces[mb].astype(F32) + other.astype(F32)).astype(BF))
-    moved = [to_ahead(after_core[mb], "b", mb) for mb in range(1, nb)]
-    total = None
-    for ma in range(na):
-        part = after_core[0][ma].astype(F32)
-        for block in moved:
-            part = part + block[ma].astype(F32)
-        if ma:
-            part = to_ahead(part.astype(BF), "a", ma).astype(F32)
-        total = part if total is None else total + part
-    return total
-
-
-def place_body(at_ref, t1, r1, t2, r2, out_ref, sems):
-    depth = t1.shape[1]
-    copies = []
-    for m in range(depth):
-        z = lax.rem(at_ref[0] + m, depth)
-        for i in range(2):
-            for j in range(2):
-                x = lax.rem(at_ref[1] + i, 2)
-                y = lax.rem(at_ref[2] + j, 2)
-                first = (r1 if j else t1).at[i, m]
-                second = (r2 if i else t2).at[j, m]
-                copies.append((first, out_ref.at[z, x, y, 0]))
-                copies.append((second, out_ref.at[z, x, y, 1]))
-    copies = [pltpu.make_async_copy(a, b, sems.at[n]) for n, (a, b) in enumerate(copies)]
-    for copy in copies:
-        copy.start()
-    for copy in copies:
-        copy.wait()
-
-
-def place(t1, r1, t2, r2):
-    _, depth, part, cols = t1.shape
-    at = jnp.stack([lax.axis_index(name) for name in ("a", "b", "h")]).astype(jnp.int32)
-    out = pl.pallas_call(
-        place_body,
-        grid_spec=pltpu.PrefetchScalarGridSpec(
-            num_scalar_prefetch=1,
-            grid=(1,),
-            in_specs=[pl.BlockSpec(memory_space=pl.ANY)] * 4,
-            out_specs=pl.BlockSpec(memory_space=pl.ANY),
-            scratch_shapes=[pltpu.SemaphoreType.DMA((8 * depth,))],
-        ),
-        out_shape=jax.ShapeDtypeStruct((depth, 2, 2, 2, part, cols), t1.dtype),
-        name="place_rows",
-    )(at, t1, r1, t2, r2)
-    return out.reshape(depth * 8 * part, cols)
-
-
-def bulk_gather(block):
-    part = block.shape[0] // 2
-    parts = [block] + [from_ahead(block, "a", m) for m in range(1, lax.axis_size("a"))]
-    low = jnp.stack([p[:part] for p in parts])
-    high = jnp.stack([p[part:] for p in parts])
-    t1 = jnp.stack([low, swap(low, "b")])
-    t2 = jnp.stack([high, swap(high, "h")])
-    return place(t1, swap(t1, "h"), t2, swap(t2, "b"))
-
-
-def bulk_scatter(grad):
-    na = lax.axis_size("a")
-    part = grad.shape[0] // (8 * na)
-    cols = grad.shape[1]
-    a, b, h = (lax.axis_index(name) for name in ("a", "b", "h"))
-    grad = grad.reshape(na, 2, 2, 2, part, cols)
-
-    def take(block, spot, dim):
-        return lax.dynamic_index_in_dim(block, spot, dim, keepdims=False)
-
-    def fold(block, axis, spot, dim):
-        other = swap(take(block, 1 - spot, dim), axis)
-        return (take(block, spot, dim).astype(F32) + other.astype(F32)).astype(BF)
-
-    low = fold(fold(grad[:, :, :, 0], "h", h, 2), "b", b, 1)
-    high = fold(fold(grad[:, :, :, 1], "b", b, 1), "h", h, 1)
-    both = jnp.concatenate([low, high], axis=1)
-    total = take(both, a, 0).astype(F32)
-    for m in range(1, na):
-        total = total + to_ahead(take(both, jnp.mod(a + m, na), 0), "a", m).astype(F32)
-    return turn_core_head(total.astype(BF)).astype(F32)
+def scatter_core(own, theirs):
+    return (own.astype(F32) + swap(theirs, "c").astype(F32)).astype(BF)
+
+
+def scatter_chips(total):
+    for name in ("b", "a"):
+        size = lax.axis_size(name)
+        total = total.reshape(size, total.shape[0] // size, *total.shape[1:])
+        part = total[0].astype(F32)
+        for m in range(1, size):
+            part = part + to_ahead(total[m], name, m).astype(F32)
+        total = part.astype(BF)
+    return total[0]
 
 
 def sum_over_head(block, n_head):
@@ -488,14 +419,10 @@
     return jnp.concatenate([jnp.where(first, own, other), jnp.where(first, other, own)], axis=axis)
 
 
-def share_over_head(block, n_head):
+def every_head(block, n_head):
     if n_head == 2:
-        other = swap(block, "h")
-        mine = lax.axis_index("h") == 0
-        first = jnp.where(mine, block, other)
-        second = jnp.where(mine, other, block)
-        return jnp.concatenate([first, second], axis=0)
-    return lax.all_gather(block, "h", axis=0, tiled=True)
+        return ordered_gather(block, "h")
+    return lax.all_gather(block, "h", axis=0)
 
 
 def on_device(
@@ -524,7 +451,7 @@
 ):
     n_head = lax.axis_size("h")
     n_seq = lax.axis_size(SEQ)
-    paired = n_head == 2 and lax.axis_size("b") == 2
+    paired = n_head == 2
     seq_at = lax.axis_index(SEQ)
     head_at = lax.axis_index("h")
     seq_all, block_len, _ = tokens.shape
@@ -537,35 +464,30 @@
 
     shared_part = lax.dynamic_slice_in_dim(shared_factors, head_at * s_cols, s_cols, 1)
     small = jnp.concatenate([headwise, shared_part, norm_gains.T], axis=1).astype(BF)
+    if n_head == 2:
+        halves = ordered_gather(small, "h")
+    else:
+        halves = lax.all_gather(small, "h", axis=0)
+    small = jnp.concatenate(
+        [halves[k, :, :h_cols] for k in range(n_head)]
+        + [halves[k, :, h_cols : h_cols + s_cols] for k in range(n_head)]
+        + [halves[0, :, h_cols + s_cols :]],
+        axis=1,
+    )
     for name in ("a", "b", "c"):
         small = ordered_gather(small, name)
-    if paired:
-        small = ordered_gather(small, "h")
-    else:
-        small = lax.all_gather(small, "h", axis=0)
-    small = small.transpose(3, 2, 1, 4, 0, 5).reshape(D, n_head, h_cols + s_cols + 2)
-    w_heads = small[:, :, :h_cols].reshape(D, H * RA)
-    w_shared = small[:, :, h_cols : h_cols + s_cols].reshape(D, RA * DH)
-    w_factors = jnp.concatenate([w_heads, w_shared], axis=1)
-    gains_low = small[:, 0, h_cols + s_cols :].T.astype(F32)
+    small = small.transpose(2, 1, 0, 3, 4).reshape(D, H * RA + RA * DH + 2)
+    w_factors = small[:, : H * RA + RA * DH]
+    gains_low = small[:, H * RA + RA * DH :].T.astype(F32)
     gain_first = gains_low[0]
     gain_second = gains_low[1]
 
-    wide_parts = [
-        part.astype(BF) for part in (out_weight.T, gate_up[0], gate_up[1], down_weight.T)
-    ]
+    wide_parts = (gate_up[0], gate_up[1], down_weight.T, out_weight.T)
+    wide_part = jnp.concatenate([part.astype(BF) for part in wide_parts], axis=1)
     if paired:
-        wide_parts = [turn_core_head(part) for part in wide_parts]
-        own_out, w_gate, w_up, w_down_t = [bulk_gather(part) for part in wide_parts]
-        w_out_t = in_core_order(own_out, swap(own_out, "c"), 1)
+        wide_all = lax.all_gather(turn_core_head(wide_part), ("a", "b", "h"), axis=0, tiled=True)
     else:
-        wide_part = jnp.concatenate(wide_parts, axis=1)
         wide_all = lax.all_gather(wide_part, SEQ + ("h",), axis=0)
-        wide_all = wide_all.reshape(n_seq, n_head, rows, 3 * f_cols + o_cols)
-        w_out_t = wide_all[..., :o_cols].transpose(0, 2, 1, 3).reshape(D, H * DH)
-        wide_all = wide_all[..., o_cols:].reshape(n_seq, n_head, rows, 3, f_cols)
-        wide_all = wide_all.transpose(3, 0, 2, 1, 4).reshape(3, D, FF)
-        w_gate, w_up, w_down_t = wide_all[0], wide_all[1], wide_all[2]
 
     spots = jnp.arange(n_seq, dtype=jnp.int32)
     own_block = jnp.sum(jnp.where(spots == seq_at, block_order, 0))
@@ -589,11 +511,25 @@
     query, own_factors = prologue(factors, cos_t, sin_t)
     half = max(1, count // 2)
     groups = [slice(at, at + half) for at in range(0, count, half)]
-    gathered = [jnp.concatenate(gather_blocks(own_factors[g]), axis=2) for g in groups]
-    forward = [
-        attention_forward(query[g], keys, key_pos, query_pos[:, None])
-        for g, keys in zip(groups, gathered)
-    ]
+    gathered = [gather_blocks(own_factors[g]) for g in groups]
+    forward = []
+    for at, g in enumerate(groups):
+        wide, stats = attention_forward(query[g], gathered[at], key_pos, query_pos[:, None])
+        if at == 0:
+            wide, wide_all = lax.optimization_barrier((wide, wide_all))
+        forward.append((wide, stats))
+    if paired:
+        w_gate = wide_all[:, :f_cols]
+        w_up = wide_all[:, f_cols : 2 * f_cols]
+        w_down_t = wide_all[:, 2 * f_cols : 3 * f_cols]
+        own_out = wide_all[:, 3 * f_cols :]
+        w_out_t = in_core_order(own_out, swap(own_out, "c"), 1)
+    else:
+        wide_all = wide_all.reshape(n_seq, n_head, rows, 3 * f_cols + o_cols)
+        w_out_t = wide_all[..., 3 * f_cols :].transpose(0, 2, 1, 3).reshape(D, H * DH)
+        wide_all = wide_all[..., : 3 * f_cols].reshape(n_seq, n_head, rows, 3, f_cols)
+        wide_all = wide_all.transpose(3, 0, 2, 1, 4).reshape(3, D, FF)
+        w_gate, w_up, w_down_t = wide_all[0], wide_all[1], wide_all[2]
     heads_wide = jnp.concatenate([part[0] for part in forward], axis=0)
     heads_low = heads_wide.astype(BF)
     attn = jnp.einsum("sce,de->scd", heads_low, w_out_t, preferred_element_type=F32)
@@ -622,14 +558,15 @@
     silu_gate = gate * sigmoid_gate
     hidden_low = (silu_gate * up).astype(BF)
     ffn = own_sum(jnp.einsum("tf,df->td", hidden_low, w_down_t, preferred_element_type=F32))
-    layer_output = share_over_head((middle + ffn).astype(BF), n_head)
+    layer_low = (middle + ffn).astype(BF)
+    down_low = jnp.einsum("td,tf->df", y_low, hidden_low, preferred_element_type=F32).astype(BF)
+    layer_all = every_head(layer_low, n_head)
 
     hidden_grad = jnp.dot(y_low, w_down_t, preferred_element_type=F32)
     up_grad = (hidden_grad * silu_gate).astype(BF)
     gate_grad = (
         hidden_grad * up * (sigmoid_gate * (1.0 + gate * (1.0 - sigmoid_gate)))
     ).astype(BF)
-    down_t_grad = jnp.einsum("td,tf->df", y_low, hidden_low, preferred_element_type=F32)
     gate_w_grad = jnp.einsum("td,tf->df", x_low, gate_grad, preferred_element_type=F32)
     up_w_grad = jnp.einsum("td,tf->df", x_low, up_grad, preferred_element_type=F32)
     second_part = jnp.einsum("tf,df->td", gate_grad, w_gate, preferred_element_type=F32)
@@ -652,44 +589,63 @@
         out_t_grad = out_grad_of(mine) + sent.astype(F32)
     else:
         out_t_grad = out_grad_of(heads_low)
-    wide_grads = [
-        grad.astype(BF) for grad in (down_t_grad, gate_w_grad, up_w_grad, out_t_grad)
-    ]
-    wide_grads, heads_grad = lax.optimization_barrier((wide_grads, heads_grad))
     if paired:
-        down_sum, gate_sum, up_sum, out_sum = [bulk_scatter(grad) for grad in wide_grads]
+        wide_grads = (gate_w_grad, up_w_grad, down_low, out_t_grad)
+        wide_grad = jnp.concatenate([grad.astype(BF) for grad in wide_grads], axis=1)
+        wide_grad, heads_grad = lax.optimization_barrier((wide_grad, heads_grad))
+        wide_sum = lax.psum_scatter(wide_grad, ("a", "b", "h"), scatter_dimension=0, tiled=True)
+        wide_sum = turn_core_head(wide_sum).astype(F32)
+        gate_sum = wide_sum[:, :f_cols]
+        up_sum = wide_sum[:, f_cols : 2 * f_cols]
+        down_sum = wide_sum[:, 2 * f_cols : 3 * f_cols]
+        out_sum = wide_sum[:, 3 * f_cols :]
     else:
-        wide_sum = jnp.concatenate(wide_grads, axis=1)
+        wide_grads = (gate_w_grad, up_w_grad, down_low, out_t_grad)
+        wide_sum = jnp.concatenate([grad.astype(BF) for grad in wide_grads], axis=1)
         wide_sum = lax.psum_scatter(wide_sum, SEQ, scatter_dimension=0, tiled=True)
         wide_sum = lax.psum(wide_sum, "h").astype(F32)
         out_sum = lax.dynamic_slice_in_dim(wide_sum, 3 * FF + head_at * o_cols, o_cols, 1)
         wide_sum = wide_sum[:, : 3 * FF].reshape(rows, 3, n_head, f_cols)
         wide_sum = lax.dynamic_index_in_dim(wide_sum, head_at, 2, keepdims=False)
-        down_sum, gate_sum, up_sum = wide_sum[:, 0], wide_sum[:, 1], wide_sum[:, 2]
-
-    joint = []
+        gate_sum, up_sum, down_sum = wide_sum[:, 0], wide_sum[:, 1], wide_sum[:, 2]
+
+    query_grads = []
+    core_sums = []
     for at, g in enumerate(groups):
+        backed = heads_grad[g]
+        if at == 1:
+            backed, core_sums[0] = lax.optimization_barrier((backed, core_sums[0]))
         query_grad, *pieces = attention_backward(
             query[g],
-            heads_grad[g],
+            backed,
             forward[at][0],
             forward[at][1],
             gathered[at],
             key_pos,
             query_pos[:, None],
-            lax.axis_size("a"),
+            n_seq // 2,
         )
-        own_grad = scatter_blocks(pieces)
-        joint.append(epilogue(query_grad, own_grad, factors[g], cos_t, sin_t))
-    joint_grad = jnp.concatenate(joint, axis=0)
-
-    first_grad = jnp.einsum("sjc,dj->scd", joint_grad, w_factors, preferred_element_type=F32)
-    factors_w_grad = jnp.einsum(
-        "scd,sjc->dj", first_normalized, joint_grad, preferred_element_type=F32
-    )
-    first_gain_grad = jnp.sum(first_grad * first_hat, axis=(0, 1))
-    input_grad = middle_grad + norm_back(first_grad, gain_first, first_hat, first_inverse)
-    input_grad = share_over_head(input_grad.astype(BF), n_head).astype(F32)
+        query_grads.append(query_grad)
+        core_sums.append(scatter_core(*pieces))
+    layer_output = layer_all.reshape(seq_all, block_len, D)
+
+    factors_w_grad = 0.0
+    first_gain_grad = 0.0
+    input_parts = []
+    own_grads = [scatter_chips(total) for total in core_sums]
+    for at, g in enumerate(groups):
+        joint_grad = epilogue(query_grads[at], own_grads[at], factors[g], cos_t, sin_t)
+        first_grad = jnp.einsum("scj,dj->scd", joint_grad, w_factors, preferred_element_type=F32)
+        factors_w_grad = factors_w_grad + jnp.einsum(
+            "scd,scj->dj", first_normalized[g], joint_grad, preferred_element_type=F32
+        )
+        first_gain_grad = first_gain_grad + jnp.sum(first_grad * first_hat[g], axis=(0, 1))
+        part = middle_grad[g] + norm_back(first_grad, gain_first, first_hat[g], first_inverse[g])
+        part = part.astype(BF)
+        if at + 1 < len(groups):
+            part, own_grads[at + 1] = lax.optimization_barrier((part, own_grads[at + 1]))
+        input_parts.append(every_head(part, n_head))
+    input_grad = jnp.concatenate(input_parts, axis=1).reshape(seq_all, block_len, D).astype(F32)
 
     gain_cols = jnp.stack([first_gain_grad, second_gain_grad]).T
     small_grad = jnp.concatenate([factors_w_grad, gain_cols], axis=1).astype(BF)

time: 1020 us -> 605 us (0.59)
  Pallas kernels: 421 us -> 119 us
  starting transfers between devices: 167 us -> 60 us
  other arithmetic: 75.7 us -> 57 us
  between operations: 3.73 us -> 16.3 us
    pallas_call x4 -> x0, Pallas kernels: 302 us -> none  [place(): pl.pallas_call(place_body, grid_spec=pltpu.PrefetchScalarGridSpec(num_sca...]
    ppermute x64 -> x17, starting transfers between devices: 62.2 us -> 12.8 us  [swap(): return lax.ppermute(block, axis, [(0, 1), (1, 0)])]
    ppermute x64 -> x17, waiting for transfers between devices: 105 us -> 62.9 us  [swap(): return lax.ppermute(block, axis, [(0, 1), (1, 0)])]
    ppermute x29 -> x11, waiting for transfers between devices: 52.1 us -> 83.3 us  [from_ahead(): lax.ppermute(block, axis, [((i + distance) % size, i) for i in range(size)])]
    ppermute x29 -> x11, starting transfers between devices: 44.8 us -> 17.9 us  [from_ahead(): lax.ppermute(block, axis, [((i + distance) % size, i) for i in range(size)])]
    ppermute x8 -> x2, starting transfers between devices: 27.6 us -> 7.94 us  [turn_core_head(): return lax.ppermute(block, ('c', 'h'), [(0, 0), (1, 2), (2, 1), (3, 3)])]
    another operation x22 -> x5, other arithmetic: 18.5 us -> 2.63 us  [the longest x8 6.29 us: bulk_gather(): t2 = jnp.stack([high, swap(high, 'h')])]
    ppermute x25 -> x13, starting transfers between devices: 32.4 us -> 21.3 us  [to_ahead(): lax.ppermute(block, axis, [(i, (i + distance) % size) for i in range(size)])]
  transfers between devices with their start and end apart: 126 -> 45, of which waited for: 58 -> 23; matrix products, arithmetic and copies ran while one was open for 16% -> 22% of each run, Pallas kernels for 42% -> 20%
where the time goes in v3:
time: 605 us; the launch traced here: 595 us
  waiting for transfers between devices  213 us (35%)
  Pallas kernels  119 us (20%)
  matrix products  72.2 us (12%)
  starting transfers between devices  60 us (10%)
  local copies, waits for them, and re-layouts  58.3 us (10%)
  other arithmetic  57 us (9%)
  between operations  16.3 us (3%)
    ppermute x11, waiting for transfers between devices, from_ahead(): lax.ppermute(block, axis, [((i + distance) % size, i) for i in range(size)])  83.3 us
    pallas_call x2, Pallas kernels, attention_backward(): pl.pallas_call(backward_body, grid=(count, H // HB), in_specs=[pl.BlockSp...  65.9 us
    ppermute x17, waiting for transfers between devices, swap(): return lax.ppermute(block, axis, [(0, 1), (1, 0)])  62.9 us
    ppermute x13, waiting for transfers between devices, to_ahead(): lax.ppermute(block, axis, [(i, (i + distance) % size) for i in range(size)])  56 us
    pallas_call x2, Pallas kernels, attention_forward(): pl.pallas_call(forward_body, grid=(count, H // HB), in_specs=[pl.BlockSpe...  41.4 us
    unnamed x137, local copies, waits for them, and re-layouts  30 us
    ppermute x13, starting transfers between devices, to_ahead(): lax.ppermute(block, axis, [(i, (i + distance) % size) for i in range(size)])  21.3 us
    ppermute x11, starting transfers between devices, from_ahead(): lax.ppermute(block, axis, [((i + distance) % size, i) for i in range(size)])  17.9 us
  transfers between devices with their start and end apart: 45, of which 23 were waited for; matrix products, arithmetic and copies ran while one was open for 22% of the time, Pallas kernels for 20%

profile of v3, /device:TPU:1, one launch (start us, length us, event | category | flops | bytes accessed | tf_op | source)
XLA Modules:
  0.0 595.4 jit_solution(7963783198233333301)
XLA Ops:
  9.6 4.5 collective-permute-start.11
  14.1 7.7 %collective-permute-done.11 = bf16[64,4736]{1,0:T(8,128)(2,1)S(1)} collective-permute-done((bf16[64,4736]{1,0:T(8,128)(2,1)S(1)}, bf16[64,4736]{1,0:T(8,128)(2,1)S(1)}, u32[]{:S(2)}, u32[]{:S(2)}) %collective-permute-start.11) | collective-permute-done | bytes 606240 | tf_op jit(solution)/shard_map/ppermute | solution.py:338
  24.1 3.5 collective-permute-done
  28.0 3.4 collective-permute-start.1
  33.2 11.0 %collective-permute-done.2 = bf16[64,802]{1,0:T(8,128)(2,1)S(1)} collective-permute-done((bf16[64,802]{1,0:T(8,128)(2,1)S(1)}, bf16[64,802]{1,0:T(8,128)(2,1)S(1)}, u32[]{:S(2)}, u32[]{:S(2)}) %collective-permute-start.2) | collective-permute-done | bytes 102688 | tf_op jit(solution)/shard_map/ppermute | solution.py:343
  46.5 6.6 %collective-permute-done.4 = bf16[4,64,802]{2,1,0:T(8,128)(2,1)S(1)} collective-permute-done((bf16[4,64,802]{2,1,0:T(8,128)(2,1)S(1)}, bf16[4,64,802]{2,1,0:T(8,128)(2,1)S(1)}, u32[]{:S(2)}, u32[]{:S(2)}) %collective-permute-start.4) | collective-permute-done | bytes 410656 | tf_op jit(solution)/shard_map/ppermute | solution.py:334
  55.3 5.1 collective-permute-start.5
  65.3 2.6 convolution_bitcast_fusion.f_ref
  67.9 4.1 factor_prologue.1
  75.0 5.7 collective-permute-start.7
  82.2 4.4 collective-permute-done.6
  86.6 17.7 %collective-permute-done.7 = bf16[2,320,128]{2,1,0:T(8,128)(2,1)S(1)} collective-permute-done((bf16[2,320,128]{2,1,0:T(8,128)(2,1)S(1)}, bf16[2,320,128]{2,1,0:T(8,128)(2,1)S(1)}, u32[]{:S(2)}, u32[]{:S(2)}) %collective-permute-start.7) | collective-permute-done | bytes 163872 | tf_op jit(solution)/shard_map/ppermute | solution.py:343
  110.4 23.1 %collective-permute-done.9 = bf16[2,320,512]{2,1,0:T(8,128)(2,1)S(1)} collective-permute-done((bf16[2,320,512]{2,1,0:T(8,128)(2,1)S(1)}, bf16[2,320,512]{2,1,0:T(8,128)(2,1)S(1)}, u32[]{:S(2)}, u32[]{:S(2)}) %collective-permute-start.9) | collective-permute-done | bytes 655392 | tf_op jit(solution)/shard_map/ppermute | solution.py:343
  134.7 2.4 collective-permute-start.10
  137.2 2.3 collective-permute-start.15
  143.2 25.9 %collective-permute-done.15 = bf16[2,320,512]{2,1,0:T(8,128)(2,1)S(1)} collective-permute-done((bf16[2,320,512]{2,1,0:T(8,128)(2,1)S(1)}, bf16[2,320,512]{2,1,0:T(8,128)(2,1)S(1)}, u32[]{:S(2)}, u32[]{:S(2)}) %collective-permute-start.15) | collective-permute-done | bytes 655392 | tf_op jit(solution)/shard_map/ppermute | solution.py:343
  174.2 20.8 %attention_forward.2 = (f32[2,128,1024]{2,1,0:T(8,128)}, f32[2,4,128,4]{3,2,1,0:T(8,128)}) custom-call(bf16[2,128,1024]{2,1,0:T(8,128)(2,1)} %get-tuple-element.248.q_ref, bf16[2,320,2048]{2,1,0:T(8,128)(2,1)} %copy-done.44, bf16[2,320,2048]{2,1,0:T(8,128)(2,1)} %copy-done.44, s32[1,2048]{1,0:T(1,128)} %bitcast.196, s32[128,1]{1,0:T(8,128)} %iota_add_fusion.qpos_ref), custom_call_target="tpu_custom_call" | custom-call | flops 2147483648 | bytes 2621440 | tf_op jit(solution)/shard_map/attention_forward/pallas_call | solution.py:218
  195.1 2.4 slice.195
  200.9 20.6 %attention_forward.3 = (f32[2,128,1024]{2,1,0:T(8,128)}, f32[2,4,128,4]{3,2,1,0:T(8,128)}) custom-call(bf16[2,128,1024]{2,1,0:T(8,128)(2,1)} %get-tuple-element.247.q_ref, bf16[2,320,2048]{2,1,0:T(8,128)(2,1)} %constant_dynamic-update-slice_fusion.16.b_ref.a_ref, bf16[2,320,2048]{2,1,0:T(8,128)(2,1)} %constant_dynamic-update-slice_fusion.16.b_ref.a_ref, ...), custom_call_target="tpu_custom_call" | custom-call | flops 2147483648 | bytes 2621440 | tf_op jit(solution)/shard_map/attention_forward/pallas_call | solution.py:218
  228.3 6.0 %fusion.3 = f32[1024,1408]{1,0:T(8,128)S(1)} fusion(bf16[1024,4736]{1,0:T(8,128)(2,1)} %all-gather.2.cloned.1.call-done, bf16[512,1024]{1,0:T(8,128)(2,1)} %collective-permute-done.21, bf16[512,1024]{1,0:T(8,128)(2,1)} %bitcast.48), kind=kOutput, calls=%fused_computation.22 | convolution fusion | flops 2956984320 | bytes 10747904 | tf_op jit(solution)/shard_map/dot_general | solution.py:565
  234.3 8.4 %fusion.9 = f32[1024,1408]{1,0:T(8,128)} fusion(bf16[1024,4736]{1,0:T(8,128)(2,1)} %all-gather.2.cloned.1.call-done, bf16[512,1024]{1,0:T(8,128)(2,1)} %collective-permute-done.18, bf16[512,1024]{1,0:T(8,128)(2,1)} %bitcast.43), kind=kOutput, calls=%fused_computation.28 | convolution fusion | flops 2956984320 | bytes 10747904 | tf_op jit(solution)/shard_map/dot_general | solution.py:556
  242.8 10.4 %multiply_convert_fusion.1 = (bf16[1024,1408]{1,0:T(8,128)(2,1)S(1)}, bf16[1024,1408]{1,0:T(8,128)(2,1)}, bf16[1024,1408]{1,0:T(8,128)(2,1)}) fusion(f32[1024,1408]{1,0:T(8,128)S(1)} %fusion.3, f32[1024,1408]{1,0:T(8,128)} %fusion.9, bf16[1024,4736]{1,0:T(8,128)(2,1)S(1)} %bitcast.195, bf16[512,1024]{1,0:T(8,128)(2,1)} %collective-permute-done.18, ...), kind=kOutput, calls=%fused_computation.2 | convolution fusion | flops 2978611200 | bytes 25165824 | tf_op jit(solution)/shard_map/dot_general | solution.py:555
  253.2 5.3 fusion.7
  258.4 3.4 fusion.18
  262.5 3.4 fusion.5
  266.3 5.5 convolution_convert_fusion.2
  278.7 5.3 convolution_convert_fusion.1
  284.1 5.5 convolution_convert_fusion
  289.6 2.2 convolution_convert_fusion.3
  292.6 5.5 pad_maximum_fusion
  300.4 33.1 %attention_backward.2 = (f32[2,128,1024]{2,1,0:T(8,128)}, bf16[8,2,320,128]{3,2,1,0:T(8,128)(2,1)}, bf16[8,2,320,128]{3,2,1,0:T(8,128)(2,1)}) custom-call(bf16[2,128,1024]{2,1,0:T(8,128)(2,1)} %get-tuple-element.248.q_ref, bf16[2,128,1024]{2,1,0:T(8,128)(2,1)} %get-tuple-element.245.do_ref, f32[2,128,1024]{2,1,0:T(8,128)} %get-tuple-element.43.o_ref, ...), custom_call_target="tpu_custom_call" | custom-call | flops 5368709120 | bytes 5242880 | tf_op jit(solution)/shard_map/attention_backward/pallas_call | solution.py:306
  342.1 2.1 add_convert_fusion.1
  346.8 32.8 %attention_backward.3 = (f32[2,128,1024]{2,1,0:T(8,128)}, bf16[8,2,320,128]{3,2,1,0:T(8,128)(2,1)}, bf16[8,2,320,128]{3,2,1,0:T(8,128)(2,1)}) custom-call(bf16[2,128,1024]{2,1,0:T(8,128)(2,1)} %get-tuple-element.247.q_ref, bf16[2,128,1024]{2,1,0:T(8,128)(2,1)} %get-tuple-element.52.do_ref, f32[2,128,1024]{2,1,0:T(8,128)} %get-tuple-element.44.o_ref, ...), custom_call_target="tpu_custom_call" | custom-call | flops 5368709120 | bytes 5242880 | tf_op jit(solution)/shard_map/attention_backward/pallas_call | solution.py:306
  379.9 2.8 convert_multiply_fusion
  384.7 2.8 collective-permute-start.28
  389.4 5.6 collective-permute-done.26
  396.8 5.2 collective-permute-done.28
  402.8 3.9 factor_epilogue.2
  406.7 2.2 add_convert_fusion
  410.8 2.4 fusion.39
  413.2 18.1 %collective-permute-done.30 = bf16[4,2,320,128]{3,2,1,0:T(8,128)(2,1)S(1)} collective-permute-done((bf16[4,2,320,128]{3,2,1,0:T(8,128)(2,1)S(1)}, bf16[4,2,320,128]{3,2,1,0:T(8,128)(2,1)S(1)}, u32[]{:S(2)}, u32[]{:S(2)}) %collective-permute-start.30) | collective-permute-done | bytes 655392 | tf_op jit(solution)/shard_map/ppermute | solution.py:348
  431.5 4.9 collective-permute-start.31
  436.4 3.1 collective-permute-start.32
  440.8 2.8 collective-permute-done.31
  443.6 9.0 %collective-permute-done.32 = bf16[1,2,320,128]{3,2,1,0:T(8,128)(2,1)S(1)} collective-permute-done((bf16[1,2,320,128]{3,2,1,0:T(8,128)(2,1)S(1)}, bf16[1,2,320,128]{3,2,1,0:T(8,128)(2,1)S(1)}, u32[]{:S(2)}, u32[]{:S(2)}) %collective-permute-start.32) | collective-permute-done | bytes 163872 | tf_op jit(solution)/shard_map/ppermute | solution.py:348
  453.8 3.7 factor_epilogue.3
  457.5 3.7 multiply_reduce_fusion.3
  461.4 4.1 fusion.2
  465.5 3.7 copy.222
  469.2 4.5 copy.223
  473.7 2.9 fusion.21
  476.6 2.5 copy.225
  479.1 3.0 collective-permute-start.36
  493.0 28.9 %collective-permute-done.34 = bf16[2,128,1024]{2,1,0:T(8,128)(2,1)} collective-permute-done((bf16[2,128,1024]{2,1,0:T(8,128)(2,1)}, bf16[2,128,1024]{2,1,0:T(8,128)(2,1)}, u32[]{:S(2)}, u32[]{:S(2)}) %collective-permute-start.34) | collective-permute-done | bytes 524320 | tf_op jit(solution)/shard_map/ppermute | solution.py:334
  521.9 2.1 select_bitcast_fusion.7
  523.9 20.5 %collective-permute-done.35 = bf16[2,128,1024]{2,1,0:T(8,128)(2,1)} collective-permute-done((bf16[2,128,1024]{2,1,0:T(8,128)(2,1)}, bf16[2,128,1024]{2,1,0:T(8,128)(2,1)}, u32[]{:S(2)}, u32[]{:S(2)}) %collective-permute-start.35) | collective-permute-done | bytes 524320 | tf_op jit(solution)/shard_map/ppermute | solution.py:334
  544.4 2.2 select_bitcast_fusion.5
  549.7 2.2 collective-permute-start.39
  553.3 3.2 collective-permute-done.38
  556.5 9.7 %collective-permute-done.39 = bf16[64,802]{0,1:T(8,128)(2,1)S(1)} collective-permute-done((bf16[64,802]{0,1:T(8,128)(2,1)S(1)}, bf16[64,802]{0,1:T(8,128)(2,1)S(1)}, u32[]{:S(2)}, u32[]{:S(2)}) %collective-permute-start.39) | collective-permute-done | bytes 102688 | tf_op jit(solution)/shard_map/ppermute | solution.py:348
  566.6 2.6 bitcast_convert_fusion
  569.3 3.3 collective-permute-done.41
  572.7 3.4 collective-permute-start.42
  581.6 2.7 collective-permute-done.42
  (302 shorter events, 104.4 us)
Async XLA Ops:
  7.2 15.5 %copy-start.45 = (f32[2,64]{1,0:T(2,128)S(1)}, f32[2,64]{1,0:T(2,128)}, u32[]{:S(2)}) copy-start(f32[2,64]{1,0:T(2,128)} %param.41) | copy-start | bytes 1540
  7.2 15.7 %copy-start.41 = (f32[64,80]{1,0:T(8,128)S(1)}, f32[64,80]{1,0:T(8,128)}, u32[]{:S(2)}) copy-start(f32[64,80]{1,0:T(8,128)} %param.26) | copy-start | bytes 61444
  7.2 187.8 %all-gather.2.cloned.1.call-start = ((), (), s32[]{:S(2)}) async-start(), calls=%async_computation.1 | async-start | bytes 10305536 | tf_op jit(solution)/shard_map/all_gather | solution.py:488
  9.6 12.3 %collective-permute-start.11 = (bf16[64,4736]{1,0:T(8,128)(2,1)S(1)}, bf16[64,4736]{1,0:T(8,128)(2,1)S(1)}, u32[]{:S(2)}, u32[]{:S(2)}) collective-permute-start(bf16[64,4736]{1,0:T(8,128)(2,1)S(1)} %pad_maximum_fusion.12), channel_id=1, source_target_pairs={{0,0},{1,2},{2,1},{3,3},{4,4},{5,6},{6,5},{7,7},{8,8},{9,10},{10,9... | collective-permute-start | bytes 1818632 | tf_op jit(solution)/shard_map/ppermute | solution.py:338
  22.7 550.0 %reduce-scatter.2.cloned.1.call-start = ((), (), s32[]{:S(2)}) async-start(), calls=%async_computation.2 | async-start | bytes 10305536 | tf_op jit(solution)/shard_map/reduce_scatter | solution.py:596
  24.0 3.6 collective-permute-start
  28.0 5.2 collective-permute-start.1
  31.4 12.8 %collective-permute-start.2 = (bf16[64,802]{1,0:T(8,128)(2,1)S(1)}, bf16[64,802]{1,0:T(8,128)(2,1)S(1)}, u32[]{:S(2)}, u32[]{:S(2)}) collective-permute-start(bf16[64,802]{1,0:T(8,128)(2,1)S(1)} %concatenate.61), channel_id=1, source_target_pairs={{16,0},{24,8},{0,16},{8,24},{17,1},{25,9},{1,17},{9,25},{18,2},{26... | collective-permute-start | bytes 307976 | tf_op jit(solution)/shard_map/ppermute | solution.py:343
  31.5 12.7 %collective-permute-start.3 = (bf16[64,802]{1,0:T(8,128)(2,1)S(1)}, bf16[64,802]{1,0:T(8,128)(2,1)S(1)}, u32[]{:S(2)}, u32[]{:S(2)}) collective-permute-start(bf16[64,802]{1,0:T(8,128)(2,1)S(1)} %concatenate.61), channel_id=1, source_target_pairs={{24,0},{0,8},{8,16},{16,24},{25,1},{1,9},{9,17},{17,25},{26,2},{2,... | collective-permute-start | bytes 307976 | tf_op jit(solution)/shard_map/ppermute | solution.py:343
  45.2 15.2 %copy-start.49 = (s32[16]{0:T(128)S(1)}, s32[16]{0:T(128)}, u32[]{:S(2)}) copy-start(s32[16]{0:T(128)} %param.25) | copy-start | bytes 196
  45.2 16.5 %copy-start.2 = (bf16[8,128,1024]{2,1,0:T(8,128)(2,1)S(1)}, bf16[8,128,1024]{2,1,0:T(8,128)(2,1)}, u32[]{:S(2)}) copy-start(bf16[8,128,1024]{2,1,0:T(8,128)(2,1)} %param.22) | copy-start | bytes 6291460
  45.2 7.9 %collective-permute-start.4 = (bf16[4,64,802]{2,1,0:T(8,128)(2,1)S(1)}, bf16[4,64,802]{2,1,0:T(8,128)(2,1)S(1)}, u32[]{:S(2)}, u32[]{:S(2)}) collective-permute-start(bf16[4,64,802]{2,1,0:T(8,128)(2,1)S(1)} %constant_dynamic-slice_fusion.1), channel_id=1, source_target_pairs={{0,4},{4,0},{1,5},{5,1},{2,6},{6,2},{3,7},{7,3},{8,12},{12,8},{9,1... | collective-permute-start | bytes 1231880 | tf_op jit(solution)/shard_map/ppermute | solution.py:334
  55.3 7.6 %collective-permute-start.5 = (bf16[2,4,64,802]{3,2,1,0:T(8,128)(2,1)}, bf16[2,4,64,802]{3,2,1,0:T(8,128)(2,1)}, u32[]{:S(2)}, u32[]{:S(2)}) collective-permute-start(bf16[2,4,64,802]{3,2,1,0:T(8,128)(2,1)} %pad_maximum_fusion.8), channel_id=1, source_target_pairs={{0,2},{2,0},{1,3},{3,1},{4,6},{6,4},{5,7},{7,5},{8,10},{10,8},{9,1... | collective-permute-start | bytes 2463752 | tf_op jit(solution)/shard_map/ppermute | solution.py:334
  73.9 12.7 %collective-permute-start.6 = (bf16[2,320,128]{2,1,0:T(8,128)(2,1)S(1)}, bf16[2,320,128]{2,1,0:T(8,128)(2,1)S(1)}, u32[]{:S(2)}, u32[]{:S(2)}) collective-permute-start(bf16[2,320,128]{2,1,0:T(8,128)(2,1)S(1)} %get-tuple-element.271), channel_id=1, source_target_pairs={{8,0},{16,8},{24,16},{0,24},{9,1},{17,9},{25,17},{1,25},{10,2},{18... | collective-permute-start | bytes 491528 | tf_op jit(solution)/shard_map/ppermute | solution.py:343
  75.0 29.3 %collective-permute-start.7 = (bf16[2,320,128]{2,1,0:T(8,128)(2,1)S(1)}, bf16[2,320,128]{2,1,0:T(8,128)(2,1)S(1)}, u32[]{:S(2)}, u32[]{:S(2)}) collective-permute-start(bf16[2,320,128]{2,1,0:T(8,128)(2,1)S(1)} %get-tuple-element.271), channel_id=1, source_target_pairs={{16,0},{24,8},{0,16},{8,24},{17,1},{25,9},{1,17},{9,25},{18,2},{26... | collective-permute-start | bytes 491528 | tf_op jit(solution)/shard_map/ppermute | solution.py:343
  80.7 23.6 %collective-permute-start.8 = (bf16[2,320,128]{2,1,0:T(8,128)(2,1)S(1)}, bf16[2,320,128]{2,1,0:T(8,128)(2,1)S(1)}, u32[]{:S(2)}, u32[]{:S(2)}) collective-permute-start(bf16[2,320,128]{2,1,0:T(8,128)(2,1)S(1)} %get-tuple-element.271), channel_id=1, source_target_pairs={{24,0},{0,8},{8,16},{16,24},{25,1},{1,9},{9,17},{17,25},{26,2},{2,... | collective-permute-start | bytes 491528 | tf_op jit(solution)/shard_map/ppermute | solution.py:343
  104.4 29.1 %collective-permute-start.9 = (bf16[2,320,512]{2,1,0:T(8,128)(2,1)S(1)}, bf16[2,320,512]{2,1,0:T(8,128)(2,1)S(1)}, u32[]{:S(2)}, u32[]{:S(2)}) collective-permute-start(bf16[2,320,512]{2,1,0:T(8,128)(2,1)S(1)} %pad_maximum_fusion.10), channel_id=1, source_target_pairs={{4,0},{0,4},{5,1},{1,5},{6,2},{2,6},{7,3},{3,7},{12,8},{8,12},{13,... | collective-permute-start | bytes 1966088 | tf_op jit(solution)/shard_map/ppermute | solution.py:343
  106.6 30.5 %collective-permute-start.12 = (bf16[2,320,128]{2,1,0:T(8,128)(2,1)S(1)}, bf16[2,320,128]{2,1,0:T(8,128)(2,1)S(1)}, u32[]{:S(2)}, u32[]{:S(2)}) collective-permute-start(bf16[2,320,128]{2,1,0:T(8,128)(2,1)S(1)} %get-tuple-element.270), channel_id=1, source_target_pairs={{8,0},{16,8},{24,16},{0,24},{9,1},{17,9},{25,17},{1,25},{10,2},{18... | collective-permute-start | bytes 491528 | tf_op jit(solution)/shard_map/ppermute | solution.py:343
  106.7 30.5 %collective-permute-start.13 = (bf16[2,320,128]{2,1,0:T(8,128)(2,1)S(1)}, bf16[2,320,128]{2,1,0:T(8,128)(2,1)S(1)}, u32[]{:S(2)}, u32[]{:S(2)}) collective-permute-start(bf16[2,320,128]{2,1,0:T(8,128)(2,1)S(1)} %get-tuple-element.270), channel_id=1, source_target_pairs={{16,0},{24,8},{0,16},{8,24},{17,1},{25,9},{1,17},{9,25},{18,2},{26... | collective-permute-start | bytes 491528 | tf_op jit(solution)/shard_map/ppermute | solution.py:343
  106.8 30.4 %collective-permute-start.14 = (bf16[2,320,128]{2,1,0:T(8,128)(2,1)S(1)}, bf16[2,320,128]{2,1,0:T(8,128)(2,1)S(1)}, u32[]{:S(2)}, u32[]{:S(2)}) collective-permute-start(bf16[2,320,128]{2,1,0:T(8,128)(2,1)S(1)} %get-tuple-element.270), channel_id=1, source_target_pairs={{24,0},{0,8},{8,16},{16,24},{25,1},{1,9},{9,17},{17,25},{26,2},{2,... | collective-permute-start | bytes 491528 | tf_op jit(solution)/shard_map/ppermute | solution.py:343
  134.7 37.9 %collective-permute-start.10 = (bf16[2,320,1024]{2,1,0:T(8,128)(2,1)}, bf16[2,320,1024]{2,1,0:T(8,128)(2,1)S(1)}, u32[]{:S(2)}, u32[]{:S(2)}) collective-permute-start(bf16[2,320,1024]{2,1,0:T(8,128)(2,1)} %get-tuple-element.262), channel_id=1, source_target_pairs={{0,2},{2,0},{1,3},{3,1},{4,6},{6,4},{5,7},{7,5},{8,10},{10,8},{9,1... | collective-permute-start | bytes 3932168 | tf_op jit(solution)/shard_map/ppermute | solution.py:334
  137.1 34.4 %copy-start.29 = (bf16[4,128,1024]{2,1,0:T(8,128)(2,1)S(1)}, bf16[4,128,1024]{2,1,0:T(8,128)(2,1)}, u32[]{:S(2)}) copy-start(bf16[4,128,1024]{2,1,0:T(8,128)(2,1)} %get-tuple-element.40) | copy-start | bytes 3145732
  137.2 31.8 %collective-permute-start.15 = (bf16[2,320,512]{2,1,0:T(8,128)(2,1)S(1)}, bf16[2,320,512]{2,1,0:T(8,128)(2,1)S(1)}, u32[]{:S(2)}, u32[]{:S(2)}) collective-permute-start(bf16[2,320,512]{2,1,0:T(8,128)(2,1)S(1)} %pad_maximum_fusion.11), channel_id=1, source_target_pairs={{4,0},{0,4},{5,1},{1,5},{6,2},{2,6},{7,3},{3,7},{12,8},{8,12},{13,... | collective-permute-start | bytes 1966088 | tf_op jit(solution)/shard_map/ppermute | solution.py:343
  143.2 29.4 %copy-start.43 = (bf16[2,320,2048]{2,1,0:T(8,128)(2,1)S(1)}, bf16[2,320,2048]{2,1,0:T(8,128)(2,1)}, u32[]{:S(2)}) copy-start(bf16[2,320,2048]{2,1,0:T(8,128)(2,1)} %get-tuple-element.263) | copy-start | bytes 7864324
  171.2 28.5 %collective-permute-start.16 = (bf16[2,320,1024]{2,1,0:T(8,128)(2,1)}, bf16[2,320,1024]{2,1,0:T(8,128)(2,1)S(1)}, u32[]{:S(2)}, u32[]{:S(2)}) collective-permute-start(bf16[2,320,1024]{2,1,0:T(8,128)(2,1)} %copy-done.42), channel_id=1, source_target_pairs={{0,2},{2,0},{1,3},{3,1},{4,6},{6,4},{5,7},{7,5},{8,10},{10,8},{9,1... | collective-permute-start | bytes 3932168 | tf_op jit(solution)/shard_map/ppermute | solution.py:334
  197.5 25.6 %collective-permute-start.17 = (bf16[1024,512]{1,0:T(8,128)(2,1)}, bf16[1024,512]{1,0:T(8,128)(2,1)}, u32[]{:S(2)}, u32[]{:S(2)}) collective-permute-start(bf16[1024,512]{1,0:T(8,128)(2,1)} %slice.195), channel_id=1, source_target_pairs={{0,2},{2,0},{1,3},{3,1},{4,6},{6,4},{5,7},{7,5},{8,10},{10,8},{9,1... | collective-permute-start | bytes 3145736 | tf_op jit(solution)/shard_map/ppermute | solution.py:334
  199.3 29.0 %collective-permute-start.21 = (bf16[512,1024]{1,0:T(8,128)(2,1)}, bf16[512,1024]{1,0:T(8,128)(2,1)}, u32[]{:S(2)}, u32[]{:S(2)}) collective-permute-start(bf16[512,1024]{1,0:T(8,128)(2,1)} %bitcast.48), channel_id=1, source_target_pairs={{0,2},{2,0},{1,3},{3,1},{4,6},{6,4},{5,7},{7,5},{8,10},{10,8},{9,1... | collective-permute-start | bytes 3145736 | tf_op jit(solution)/shard_map/ppermute | solution.py:334
  226.7 45.6 %copy-start = (f32[4,128,1024]{2,1,0:T(8,128)}, f32[4,128,1024]{2,1,0:T(8,128)S(1)}, u32[]{:S(2)}) copy-start(f32[4,128,1024]{2,1,0:T(8,128)S(1)} %get-tuple-element.291) | copy-start | bytes 6291460
  228.1 6.2 %collective-permute-start.18 = (bf16[512,1024]{1,0:T(8,128)(2,1)}, bf16[512,1024]{1,0:T(8,128)(2,1)}, u32[]{:S(2)}, u32[]{:S(2)}) collective-permute-start(bf16[512,1024]{1,0:T(8,128)(2,1)} %bitcast.43), channel_id=1, source_target_pairs={{0,2},{2,0},{1,3},{3,1},{4,6},{6,4},{5,7},{7,5},{8,10},{10,8},{9,1... | collective-permute-start | bytes 3145736 | tf_op jit(solution)/shard_map/ppermute | solution.py:334
  228.3 14.4 %slice-start = ((s8[9699328]{0:T(1024)(128)(4,1)}), s8[4194304]{0:T(1024)(128)(4,1)S(1)}, s32[]{:S(2)}) async-start(s8[9699328]{0:T(1024)(128)(4,1)} %bitcast.194), calls=%async_computation.3 | async-start | bytes 8388608
  228.3 14.4 %slice-start.1 = ((s8[9699328]{0:T(1024)(128)(4,1)}), s8[4194304]{0:T(1024)(128)(4,1)S(1)}, s32[]{:S(2)}) async-start(s8[9699328]{0:T(1024)(128)(4,1)} %bitcast.194), calls=%async_computation.4 | async-start | bytes 8388608
  234.3 8.4 %slice-start.2 = ((s8[9699328]{0:T(1024)(128)(4,1)}), s8[1310720]{0:T(1024)(128)(4,1)S(1)}, s32[]{:S(2)}) async-start(s8[9699328]{0:T(1024)(128)(4,1)} %bitcast.194), calls=%async_computation.5 | async-start | bytes 2621440
  262.0 9.8 %collective-permute-start.22 = (bf16[512,1024]{1,0:T(8,128)(2,1)S(1)}, bf16[512,1024]{1,0:T(8,128)(2,1)S(1)}, u32[]{:S(2)}, u32[]{:S(2)}) collective-permute-start(bf16[512,1024]{1,0:T(8,128)(2,1)S(1)} %slice.344), channel_id=1, source_target_pairs={{0,2},{2,0},{1,3},{3,1},{4,6},{6,4},{5,7},{7,5},{8,10},{10,8},{9,1... | collective-permute-start | bytes 3145736 | tf_op jit(solution)/shard_map/ppermute | solution.py:334
  266.1 6.9 %collective-permute-start.19 = (bf16[512,1024]{1,0:T(8,128)(2,1)S(1)}, bf16[512,1024]{1,0:T(8,128)(2,1)S(1)}, u32[]{:S(2)}, u32[]{:S(2)}) collective-permute-start(bf16[512,1024]{1,0:T(8,128)(2,1)S(1)} %slice.345), channel_id=1, source_target_pairs={{0,2},{2,0},{1,3},{3,1},{4,6},{6,4},{5,7},{7,5},{8,10},{10,8},{9,1... | collective-permute-start | bytes 3145736 | tf_op jit(solution)/shard_map/ppermute | solution.py:334
  277.7 14.2 %collective-permute-start.23 = (bf16[1024,512]{1,0:T(8,128)(2,1)S(1)}, bf16[1024,512]{1,0:T(8,128)(2,1)S(1)}, u32[]{:S(2)}, u32[]{:S(2)}) collective-permute-start(bf16[1024,512]{1,0:T(8,128)(2,1)S(1)} %bitcast_convert_fusion.1), channel_id=1, source_target_pairs={{0,2},{2,0},{1,3},{3,1},{4,6},{6,4},{5,7},{7,5},{8,10},{10,8},{9,1... | collective-permute-start | bytes 3145736 | tf_op jit(solution)/shard_map/ppermute | solution.py:334
  333.5 7.6 %collective-permute-start.24 = (bf16[8,2,320,128]{3,2,1,0:T(8,128)(2,1)}, bf16[8,2,320,128]{3,2,1,0:T(8,128)(2,1)S(1)}, u32[]{:S(2)}, u32[]{:S(2)}) collective-permute-start(bf16[8,2,320,128]{3,2,1,0:T(8,128)(2,1)} %get-tuple-element.50), channel_id=1, source_target_pairs={{0,2},{2,0},{1,3},{3,1},{4,6},{6,4},{5,7},{7,5},{8,10},{10,8},{9,1... | collective-permute-start | bytes 3932168 | tf_op jit(solution)/shard_map/ppermute | solution.py:334
  345.1 37.7 %collective-permute-start.25 = (bf16[4,2,320,128]{3,2,1,0:T(8,128)(2,1)}, bf16[4,2,320,128]{3,2,1,0:T(8,128)(2,1)}, u32[]{:S(2)}, u32[]{:S(2)}) collective-permute-start(bf16[4,2,320,128]{3,2,1,0:T(8,128)(2,1)} %slice.209), channel_id=1, source_target_pairs={{0,4},{4,0},{1,5},{5,1},{2,6},{6,2},{3,7},{7,3},{8,12},{12,8},{9,1... | collective-permute-start | bytes 1966088 | tf_op jit(solution)/shard_map/ppermute | solution.py:348
  379.6 27.1 %collective-permute-start.29 = (bf16[8,2,320,128]{3,2,1,0:T(8,128)(2,1)}, bf16[8,2,320,128]{3,2,1,0:T(8,128)(2,1)}, u32[]{:S(2)}, u32[]{:S(2)}) collective-permute-start(bf16[8,2,320,128]{3,2,1,0:T(8,128)(2,1)} %get-tuple-element.55), channel_id=1, source_target_pairs={{0,2},{2,0},{1,3},{3,1},{4,6},{6,4},{5,7},{7,5},{8,10},{10,8},{9,1... | collective-permute-start | bytes 3932168 | tf_op jit(solution)/shard_map/ppermute | solution.py:334
  384.2 10.8 %collective-permute-start.26 = (bf16[1,2,320,128]{3,2,1,0:T(8,128)(2,1)S(1)}, bf16[1,2,320,128]{3,2,1,0:T(8,128)(2,1)S(1)}, u32[]{:S(2)}, u32[]{:S(2)}) collective-permute-start(bf16[1,2,320,128]{3,2,1,0:T(8,128)(2,1)S(1)} %get-tuple-element.257), channel_id=1, source_target_pairs={{0,8},{8,16},{16,24},{24,0},{1,9},{9,17},{17,25},{25,1},{2,10},{10... | collective-permute-start | bytes 491528 | tf_op jit(solution)/shard_map/ppermute | solution.py:348
  384.3 12.5 %collective-permute-start.27 = (bf16[1,2,320,128]{3,2,1,0:T(8,128)(2,1)S(1)}, bf16[1,2,320,128]{3,2,1,0:T(8,128)(2,1)S(1)}, u32[]{:S(2)}, u32[]{:S(2)}) collective-permute-start(bf16[1,2,320,128]{3,2,1,0:T(8,128)(2,1)S(1)} %get-tuple-element.259), channel_id=1, source_target_pairs={{0,16},{8,24},{16,0},{24,8},{1,17},{9,25},{17,1},{25,9},{2,18},{10... | collective-permute-start | bytes 491528 | tf_op jit(solution)/shard_map/ppermute | solution.py:348
  384.7 17.3 %collective-permute-start.28 = (bf16[1,2,320,128]{3,2,1,0:T(8,128)(2,1)S(1)}, bf16[1,2,320,128]{3,2,1,0:T(8,128)(2,1)S(1)}, u32[]{:S(2)}, u32[]{:S(2)}) collective-permute-start(bf16[1,2,320,128]{3,2,1,0:T(8,128)(2,1)S(1)} %get-tuple-element.258), channel_id=1, source_target_pairs={{0,24},{8,0},{16,8},{24,16},{1,25},{9,1},{17,9},{25,17},{2,26},{10... | collective-permute-start | bytes 491528 | tf_op jit(solution)/shard_map/ppermute | solution.py:348
  388.9 93.3 %collective-permute-start.20 = (bf16[4,128,1024]{2,1,0:T(8,128)(2,1)S(1)}, bf16[4,128,1024]{2,1,0:T(8,128)(2,1)}, u32[]{:S(2)}, u32[]{:S(2)}) collective-permute-start(bf16[4,128,1024]{2,1,0:T(8,128)(2,1)S(1)} %copy-done.8), channel_id=1, source_target_pairs={{0,1},{1,0},{2,3},{3,2},{4,5},{5,4},{6,7},{7,6},{8,9},{9,8},{10,11... | collective-permute-start | bytes 3145736 | tf_op jit(solution)/shard_map/ppermute | solution.py:334
  409.0 22.3 %collective-permute-start.30 = (bf16[4,2,320,128]{3,2,1,0:T(8,128)(2,1)S(1)}, bf16[4,2,320,128]{3,2,1,0:T(8,128)(2,1)S(1)}, u32[]{:S(2)}, u32[]{:S(2)}) collective-permute-start(bf16[4,2,320,128]{3,2,1,0:T(8,128)(2,1)S(1)} %slice.257), channel_id=1, source_target_pairs={{0,4},{4,0},{1,5},{5,1},{2,6},{6,2},{3,7},{7,3},{8,12},{12,8},{9,1... | collective-permute-start | bytes 1966088 | tf_op jit(solution)/shard_map/ppermute | solution.py:348
  431.5 12.1 %collective-permute-start.31 = (bf16[1,2,320,128]{3,2,1,0:T(8,128)(2,1)S(1)}, bf16[1,2,320,128]{3,2,1,0:T(8,128)(2,1)S(1)}, u32[]{:S(2)}, u32[]{:S(2)}) collective-permute-start(bf16[1,2,320,128]{3,2,1,0:T(8,128)(2,1)S(1)} %get-tuple-element.254), channel_id=1, source_target_pairs={{0,8},{8,16},{16,24},{24,0},{1,9},{9,17},{17,25},{25,1},{2,10},{10... | collective-permute-start | bytes 491528 | tf_op jit(solution)/shard_map/ppermute | solution.py:348
  436.4 16.2 %collective-permute-start.32 = (bf16[1,2,320,128]{3,2,1,0:T(8,128)(2,1)S(1)}, bf16[1,2,320,128]{3,2,1,0:T(8,128)(2,1)S(1)}, u32[]{:S(2)}, u32[]{:S(2)}) collective-permute-start(bf16[1,2,320,128]{3,2,1,0:T(8,128)(2,1)S(1)} %get-tuple-element.256), channel_id=1, source_target_pairs={{0,16},{8,24},{16,0},{24,8},{1,17},{9,25},{17,1},{25,9},{2,18},{10... | collective-permute-start | bytes 491528 | tf_op jit(solution)/shard_map/ppermute | solution.py:348
  439.5 13.5 %collective-permute-start.33 = (bf16[1,2,320,128]{3,2,1,0:T(8,128)(2,1)S(1)}, bf16[1,2,320,128]{3,2,1,0:T(8,128)(2,1)S(1)}, u32[]{:S(2)}, u32[]{:S(2)}) collective-permute-start(bf16[1,2,320,128]{3,2,1,0:T(8,128)(2,1)S(1)} %get-tuple-element.255), channel_id=1, source_target_pairs={{0,24},{8,0},{16,8},{24,16},{1,25},{9,1},{17,9},{25,17},{2,26},{10... | collective-permute-start | bytes 491528 | tf_op jit(solution)/shard_map/ppermute | solution.py:348
  479.1 8.4 %collective-permute-start.36 = (bf16[4,2,64,802]{3,2,1,0:T(8,128)(2,1)}, bf16[4,2,64,802]{3,2,1,0:T(8,128)(2,1)}, u32[]{:S(2)}, u32[]{:S(2)}) collective-permute-start(bf16[4,2,64,802]{3,2,1,0:T(8,128)(2,1)} %bitcast.193), channel_id=1, source_target_pairs={{0,2},{2,0},{1,3},{3,1},{4,6},{6,4},{5,7},{7,5},{8,10},{10,8},{9,1... | collective-permute-start | bytes 2463752 | tf_op jit(solution)/shard_map/ppermute | solution.py:348
  485.0 36.9 %collective-permute-start.34 = (bf16[2,128,1024]{2,1,0:T(8,128)(2,1)}, bf16[2,128,1024]{2,1,0:T(8,128)(2,1)}, u32[]{:S(2)}, u32[]{:S(2)}) collective-permute-start(bf16[2,128,1024]{2,1,0:T(8,128)(2,1)} %fusion.26), channel_id=1, source_target_pairs={{0,1},{1,0},{2,3},{3,2},{4,5},{5,4},{6,7},{7,6},{8,9},{9,8},{10,11... | collective-permute-start | bytes 1572872 | tf_op jit(solution)/shard_map/ppermute | solution.py:334
  487.2 57.2 %collective-permute-start.35 = (bf16[2,128,1024]{2,1,0:T(8,128)(2,1)}, bf16[2,128,1024]{2,1,0:T(8,128)(2,1)}, u32[]{:S(2)}, u32[]{:S(2)}) collective-permute-start(bf16[2,128,1024]{2,1,0:T(8,128)(2,1)} %fusion.25), channel_id=1, source_target_pairs={{0,1},{1,0},{2,3},{3,2},{4,5},{5,4},{6,7},{7,6},{8,9},{9,8},{10,11... | collective-permute-start | bytes 1572872 | tf_op jit(solution)/shard_map/ppermute | solution.py:334
  492.6 54.1 %collective-permute-start.37 = (bf16[4,64,802]{2,1,0:T(8,128)(2,1)}, bf16[4,64,802]{2,1,0:T(8,128)(2,1)}, u32[]{:S(2)}, u32[]{:S(2)}) collective-permute-start(bf16[4,64,802]{2,1,0:T(8,128)(2,1)} %bitcast.66), channel_id=1, source_target_pairs={{0,4},{4,0},{1,5},{5,1},{2,6},{6,2},{3,7},{7,3},{8,12},{12,8},{9,1... | collective-permute-start | bytes 1231880 | tf_op jit(solution)/shard_map/ppermute | solution.py:348
  548.4 8.1 %collective-permute-start.38 = (bf16[64,802]{0,1:T(8,128)(2,1)S(1)}, bf16[64,802]{0,1:T(8,128)(2,1)S(1)}, u32[]{:S(2)}, u32[]{:S(2)}) collective-permute-start(bf16[64,802]{0,1:T(8,128)(2,1)S(1)} %get-tuple-element.251), channel_id=1, source_target_pairs={{0,8},{8,16},{16,24},{24,0},{1,9},{9,17},{17,25},{25,1},{2,10},{10... | collective-permute-start | bytes 307976 | tf_op jit(solution)/shard_map/ppermute | solution.py:348
  549.7 16.5 %collective-permute-start.39 = (bf16[64,802]{0,1:T(8,128)(2,1)S(1)}, bf16[64,802]{0,1:T(8,128)(2,1)S(1)}, u32[]{:S(2)}, u32[]{:S(2)}) collective-permute-start(bf16[64,802]{0,1:T(8,128)(2,1)S(1)} %get-tuple-element.253), channel_id=1, source_target_pairs={{0,16},{8,24},{16,0},{24,8},{1,17},{9,25},{17,1},{25,9},{2,18},{10... | collective-permute-start | bytes 307976 | tf_op jit(solution)/shard_map/ppermute | solution.py:348
  551.9 14.4 %collective-permute-start.40 = (bf16[64,802]{0,1:T(8,128)(2,1)S(1)}, bf16[64,802]{0,1:T(8,128)(2,1)S(1)}, u32[]{:S(2)}, u32[]{:S(2)}) collective-permute-start(bf16[64,802]{0,1:T(8,128)(2,1)S(1)} %get-tuple-element.252), channel_id=1, source_target_pairs={{0,24},{8,0},{16,8},{24,16},{1,25},{9,1},{17,9},{25,17},{2,26},{10... | collective-permute-start | bytes 307976 | tf_op jit(solution)/shard_map/ppermute | solution.py:348
  566.4 9.7 %copy-start.20 = (f32[64,640]{0,1:T(8,128)S(1)}, f32[64,640]{0,1:T(8,128)}, u32[]{:S(2)}) copy-start(f32[64,640]{0,1:T(8,128)} %copy.235) | copy-start | bytes 491524
  566.4 9.7 %copy-start.21 = (f32[64,640]{0,1:T(8,128)S(1)}, f32[64,640]{0,1:T(8,128)}, u32[]{:S(2)}) copy-start(f32[64,640]{0,1:T(8,128)} %copy.232) | copy-start | bytes 491524
  566.4 9.7 %copy-start.22 = (f32[64,640]{0,1:T(8,128)S(1)}, f32[64,640]{0,1:T(8,128)}, u32[]{:S(2)}) copy-start(f32[64,640]{0,1:T(8,128)} %copy.233) | copy-start | bytes 491524
  566.4 6.2 %collective-permute-start.41 = (bf16[64,802]{0,1:T(8,128)(2,1)S(1)}, bf16[64,802]{0,1:T(8,128)(2,1)S(1)}, u32[]{:S(2)}, u32[]{:S(2)}) collective-permute-start(bf16[64,802]{0,1:T(8,128)(2,1)S(1)} %fusion.36), channel_id=1, source_target_pairs={{0,1},{1,0},{2,3},{3,2},{4,5},{5,4},{6,7},{7,6},{8,9},{9,8},{10,11... | collective-permute-start | bytes 307976 | tf_op jit(solution)/shard_map/ppermute | solution.py:334
  572.6 8.4 %copy-start.46 = (f32[2,64]{1,0:T(2,128)S(1)}, f32[2,64]{1,0:T(2,128)}, u32[]{:S(2)}) copy-start(f32[2,64]{1,0:T(2,128)} %param.41) | copy-start | bytes 1540
  572.6 8.4 %copy-start.47 = (f32[2,64]{1,0:T(2,128)S(1)}, f32[2,64]{1,0:T(2,128)}, u32[]{:S(2)}) copy-start(f32[2,64]{1,0:T(2,128)} %param.42) | copy-start | bytes 1540
  572.6 8.4 %copy-start.48 = (f32[2,64]{1,0:T(2,128)S(1)}, f32[2,64]{1,0:T(2,128)}, u32[]{:S(2)}) copy-start(f32[2,64]{1,0:T(2,128)} %param.43) | copy-start | bytes 1540
  572.7 11.6 %collective-permute-start.42 = (bf16[64,4736]{1,0:T(8,128)(2,1)}, bf16[64,4736]{1,0:T(8,128)(2,1)S(1)}, u32[]{:S(2)}, u32[]{:S(2)}) collective-permute-start(bf16[64,4736]{1,0:T(8,128)(2,1)} %reduce-scatter.2.cloned.1.call-done), channel_id=1, source_target_pairs={{0,0},{1,2},{2,1},{3,3},{4,4},{5,6},{6,5},{7,7},{8,8},{9,10},{10,9... | collective-permute-start | bytes 1818632 | tf_op jit(solution)/shard_map/ppermute | solution.py:338
  578.0 6.5 %copy-start.18 = (f32[1408,64]{0,1:T(8,128)S(1)}, f32[1408,64]{0,1:T(8,128)}, u32[]{:S(2)}) copy-start(f32[1408,64]{0,1:T(8,128)} %param.38) | copy-start | bytes 1081348
  578.0 6.5 %copy-start.37 = (f32[1408,64]{0,1:T(8,128)S(1)}, f32[1408,64]{0,1:T(8,128)}, u32[]{:S(2)}) copy-start(f32[1408,64]{0,1:T(8,128)} %param.39) | copy-start | bytes 1081348
  578.0 6.5 %copy-start.38 = (f32[1408,64]{0,1:T(8,128)S(1)}, f32[1408,64]{0,1:T(8,128)}, u32[]{:S(2)}) copy-start(f32[1408,64]{0,1:T(8,128)} %param.40) | copy-start | bytes 1081348
  (37 other events, 95.3 us)
Sparse Core Ops, SparseCore 0:
  22.8 165.2 all-gather.1
  298.3 240.0 reduce-scatter.1

commit v4 on v3

--- a/solution.py
+++ b/solution.py
@@ -419,10 +419,74 @@
     return jnp.concatenate([jnp.where(first, own, other), jnp.where(first, other, own)], axis=axis)
 
 
+def after(block, gate):
+    return lax.optimization_barrier((block, gate))[0]
+
+
 def every_head(block, n_head):
     if n_head == 2:
-        return ordered_gather(block, "h")
+        other = swap(block, "h")
+        mine = lax.axis_index("h") == 0
+        return jnp.stack([jnp.where(mine, block, other), jnp.where(mine, other, block)])
     return lax.all_gather(block, "h", axis=0)
+
+
+def take(block, spot, dim):
+    return lax.dynamic_index_in_dim(block, spot, dim, keepdims=False)
+
+
+def fold_send(block, axis, dim):
+    spot = lax.axis_index(axis)
+    return take(block, spot, dim), swap(take(block, 1 - spot, dim), axis)
+
+
+def fold_add(pair, gate):
+    own, other = pair
+    return (after(own, gate).astype(F32) + other.astype(F32)).astype(BF)
+
+
+def depth_send(block):
+    size = lax.axis_size("a")
+    spot = lax.axis_index("a")
+    sent = [to_ahead(take(block, jnp.mod(spot + m, size), 0), "a", m) for m in range(1, size)]
+    return take(block, spot, 0), sent
+
+
+def factor_grads_body(core_ref, x_ref, gain_ref, *refs):
+    joint_refs, own_ref, sent_ref = refs[:-2], refs[-2], refs[-1]
+    total = None
+    at = 0
+    for ref in joint_refs:
+        size = ref.shape[0]
+        part = lax.dot_general(x_ref[at : at + size, :], ref[...], TN, preferred_element_type=F32)
+        total = part if total is None else total + part
+        at += size
+    na, nb, rows, _ = own_ref.shape
+    width = total.shape[1]
+    first = core_ref[0] == 0
+    gains = jnp.transpose(gain_ref[...])[:, :2]
+    for i in range(na * nb):
+        low = slice(2 * i * rows, (2 * i + 1) * rows)
+        high = slice((2 * i + 1) * rows, (2 * i + 2) * rows)
+        for block, lanes in ((total, slice(0, width)), (gains, slice(width, width + 2))):
+            own = jnp.where(first, block[low], block[high])
+            sent = jnp.where(first, block[high], block[low])
+            own_ref[i // nb, i % nb, :, lanes] = own.astype(BF)
+            sent_ref[i // nb, i % nb, :, lanes] = sent.astype(BF)
+
+
+def factor_grads(rows_of, joints, gains):
+    na, nb = lax.axis_size("a"), lax.axis_size("b")
+    shape = (na, nb, D // (2 * na * nb), H * RA + RA * DH + 2)
+    core = lax.axis_index("c").astype(jnp.int32).reshape(1)
+    vmem = pl.BlockSpec(memory_space=pltpu.VMEM)
+    return pl.pallas_call(
+        factor_grads_body,
+        in_specs=[pl.BlockSpec(memory_space=pltpu.SMEM)] + [vmem] * (2 + len(joints)),
+        out_specs=[vmem, vmem],
+        out_shape=[jax.ShapeDtypeStruct(shape, BF)] * 2,
+        name="factor_grads",
+    )(core, rows_of, gains, *joints)
 
 
 def on_device(
@@ -560,7 +624,11 @@
     ffn = own_sum(jnp.einsum("tf,df->td", hidden_low, w_down_t, preferred_element_type=F32))
     layer_low = (middle + ffn).astype(BF)
     down_low = jnp.einsum("td,tf->df", y_low, hidden_low, preferred_element_type=F32).astype(BF)
+    y_low, down_low, layer_low = lax.optimization_barrier((y_low, down_low, layer_low))
     layer_all = every_head(layer_low, n_head)
+    if paired:
+        parts = down_low.reshape(lax.axis_size("a"), 2, 2, 2, rows // 2, f_cols)
+        down_pairs = (fold_send(parts[:, :, :, 0], "h", 2), fold_send(parts[:, :, :, 1], "b", 1))
 
     hidden_grad = jnp.dot(y_low, w_down_t, preferred_element_type=F32)
     up_grad = (hidden_grad * silu_gate).astype(BF)
@@ -590,15 +658,16 @@
     else:
         out_t_grad = out_grad_of(heads_low)
     if paired:
-        wide_grads = (gate_w_grad, up_w_grad, down_low, out_t_grad)
+        wide_grads = (gate_w_grad, up_w_grad, out_t_grad)
         wide_grad = jnp.concatenate([grad.astype(BF) for grad in wide_grads], axis=1)
-        wide_grad, heads_grad = lax.optimization_barrier((wide_grad, heads_grad))
+        wide_grad, heads_grad, layer_all = lax.optimization_barrier(
+            (wide_grad, heads_grad, layer_all)
+        )
         wide_sum = lax.psum_scatter(wide_grad, ("a", "b", "h"), scatter_dimension=0, tiled=True)
         wide_sum = turn_core_head(wide_sum).astype(F32)
         gate_sum = wide_sum[:, :f_cols]
         up_sum = wide_sum[:, f_cols : 2 * f_cols]
-        down_sum = wide_sum[:, 2 * f_cols : 3 * f_cols]
-        out_sum = wide_sum[:, 3 * f_cols :]
+        out_sum = wide_sum[:, 2 * f_cols :]
     else:
         wide_grads = (gate_w_grad, up_w_grad, down_low, out_t_grad)
         wide_sum = jnp.concatenate([grad.astype(BF) for grad in wide_grads], axis=1)
@@ -626,36 +695,49 @@
             n_seq // 2,
         )
         query_grads.append(query_grad)
+        if paired and at == 0:
+            low = fold_send(fold_add(down_pairs[0], query_grad), "b", 1)
+            high = fold_send(fold_add(down_pairs[1], query_grad), "h", 1)
         core_sums.append(scatter_core(*pieces))
     layer_output = layer_all.reshape(seq_all, block_len, D)
-
-    factors_w_grad = 0.0
+    if paired:
+        low = fold_add(low, query_grads[-1])
+        high = fold_add(high, query_grads[-1])
+        down_own, down_sent = depth_send(jnp.concatenate([low, high], axis=1))
+
     first_gain_grad = 0.0
+    joints = []
     input_parts = []
     own_grads = [scatter_chips(total) for total in core_sums]
+    if paired:
+        down_sent, own_grads[1] = lax.optimization_barrier((down_sent, own_grads[1]))
     for at, g in enumerate(groups):
         joint_grad = epilogue(query_grads[at], own_grads[at], factors[g], cos_t, sin_t)
         first_grad = jnp.einsum("scj,dj->scd", joint_grad, w_factors, preferred_element_type=F32)
-        factors_w_grad = factors_w_grad + jnp.einsum(
-            "scd,scj->dj", first_normalized[g], joint_grad, preferred_element_type=F32
-        )
+        joints.append(joint_grad.reshape(-1, joint_grad.shape[2]))
         first_gain_grad = first_gain_grad + jnp.sum(first_grad * first_hat[g], axis=(0, 1))
         part = middle_grad[g] + norm_back(first_grad, gain_first, first_hat[g], first_inverse[g])
         part = part.astype(BF)
         if at + 1 < len(groups):
             part, own_grads[at + 1] = lax.optimization_barrier((part, own_grads[at + 1]))
-        input_parts.append(every_head(part, n_head))
-    input_grad = jnp.concatenate(input_parts, axis=1).reshape(seq_all, block_len, D).astype(F32)
-
-    gain_cols = jnp.stack([first_gain_grad, second_gain_grad]).T
-    small_grad = jnp.concatenate([factors_w_grad, gain_cols], axis=1).astype(BF)
-    small_sum = small_grad.reshape(
-        lax.axis_size("a"), lax.axis_size("b"), 2, rows, small_grad.shape[1]
-    )
-    small_sum = ordered_scatter(small_sum, "c", 2)
+        input_parts.append(part)
+
+    gain_rows = jnp.stack([first_gain_grad, second_gain_grad] + [jnp.zeros(D, F32)] * 6)
+    input_parts = [every_head(part, n_head) for part in input_parts]
+    if len(groups) > 1:
+        joints[-1] = after(joints[-1], input_parts[0])
+    small_own, small_sent = factor_grads(first_normalized.reshape(-1, D), joints, gain_rows)
+    small_sum = scatter_core(small_own, small_sent)
     small_sum = ordered_scatter(small_sum, "b", 1)
     small_sum = ordered_scatter(small_sum, "a", 0)
+    small_sum = after(small_sum, input_parts[-1])
     small_sum = sum_over_head(small_sum, n_head).astype(F32)
+    input_grad = jnp.concatenate(input_parts, axis=1).reshape(seq_all, block_len, D).astype(F32)
+    if paired:
+        down_sum = down_own.astype(F32)
+        for part in down_sent:
+            down_sum = down_sum + part.astype(F32)
+        down_sum = turn_core_head(down_sum.astype(BF)).astype(F32)
     heads_sum = lax.dynamic_slice_in_dim(small_sum, head_at * h_cols, h_cols, 1)
     shared_sum = small_sum[:, H * RA : H * RA + RA * DH]
     gains_sum = small_sum[:, H * RA + RA * DH :].T

time: 605 us -> 608 us (level)
  starting transfers between devices: 60 us -> 78.8 us
  local copies, waits for them, and re-layouts: 58.3 us -> 48.3 us
  matrix products: 72.2 us -> 65.1 us
    convert_element_type x0 -> x6, other arithmetic: none -> 7.56 us  [the longest x4 5.19 us: fold_add(): return (after(own, gate).astype(F32) + other.astype(F32)).astype(BF)]
    ppermute x13 -> x15, starting transfers between devices: 21.3 us -> 28.6 us  [to_ahead(): lax.ppermute(block, axis, [(i, (i + distance) % size) for i in range(size)])]
    another operation x8 -> x4, other arithmetic: 10.8 us -> 3.64 us  [ordered_gather(): jnp.stack([jnp.where(mine, block, other), jnp.where(mine, other, block)])]
    unnamed x137 -> x173, local copies, waits for them, and re-layouts: 30 us -> 22.8 us
    ppermute x17 -> x22, waiting for transfers between devices: 62.9 us -> 55.9 us  [swap(): return lax.ppermute(block, axis, [(0, 1), (1, 0)])]
    dot_general x2 -> x0, matrix products: 6.56 us -> none  [on_device(): jnp.einsum('scd,scj->dj', first_normalized[g], joint_grad, preferred_elem...]
    ppermute x2 -> x3, starting transfers between devices: 7.94 us -> 14.4 us  [turn_core_head(): return lax.ppermute(block, ('c', 'h'), [(0, 0), (1, 2), (2, 1), (3, 3)])]
    ppermute x13 -> x15, waiting for transfers between devices: 56 us -> 62.2 us  [to_ahead(): lax.ppermute(block, axis, [(i, (i + distance) % size) for i in range(size)])]
  transfers between devices with their start and end apart: 45 -> 53, of which waited for: 23 -> 24; matrix products, arithmetic and copies ran while one was open for 22% -> 20% of each run, Pallas kernels for 20% -> 20%
where the time goes in v4:
time: 608 us; the launch traced here: 601 us
  waiting for transfers between devices  214 us (35%)
  Pallas kernels  123 us (20%)
  starting transfers between devices  78.8 us (13%)
  matrix products  65.1 us (11%)
  other arithmetic  54.9 us (9%)
  local copies, waits for them, and re-layouts  48.3 us (8%)
  between operations  16.6 us (3%)
    ppermute x11, waiting for transfers between devices, from_ahead(): lax.ppermute(block, axis, [((i + distance) % size, i) for i in range(size)])  84.2 us
    pallas_call x2, Pallas kernels, attention_backward(): pl.pallas_call(backward_body, grid=(count, H // HB), in_specs=[pl.BlockSp...  66 us
    ppermute x15, waiting for transfers between devices, to_ahead(): lax.ppermute(block, axis, [(i, (i + distance) % size) for i in range(size)])  62.2 us
    ppermute x22, waiting for transfers between devices, swap(): return lax.ppermute(block, axis, [(0, 1), (1, 0)])  55.9 us
    pallas_call x2, Pallas kernels, attention_forward(): pl.pallas_call(forward_body, grid=(count, H // HB), in_specs=[pl.BlockSpe...  41.4 us
    ppermute x15, starting transfers between devices, to_ahead(): lax.ppermute(block, axis, [(i, (i + distance) % size) for i in range(size)])  28.6 us
    unnamed x173, local copies, waits for them, and re-layouts  22.8 us
    ppermute x22, starting transfers between devices, swap(): return lax.ppermute(block, axis, [(0, 1), (1, 0)])  19 us
  transfers between devices with their start and end apart: 53, of which 24 were waited for; matrix products, arithmetic and copies ran while one was open for 20% of the time, Pallas kernels for 20%

profile of v4, /device:TPU:1, one launch (start us, length us, event | category | flops | bytes accessed | tf_op | source)
XLA Modules:
  0.0 601.1 jit_solution(11756427526639998069)
XLA Ops:
  10.4 4.5 collective-permute-start.11
  15.0 7.7 %collective-permute-done.11 = bf16[64,4736]{1,0:T(8,128)(2,1)S(1)} collective-permute-done((bf16[64,4736]{1,0:T(8,128)(2,1)S(1)}, bf16[64,4736]{1,0:T(8,128)(2,1)S(1)}, u32[]{:S(2)}, u32[]{:S(2)}) %collective-permute-start.11) | collective-permute-done | bytes 606240 | tf_op jit(solution)/shard_map/ppermute | solution.py:338
  25.0 3.5 collective-permute-done
  28.9 3.4 collective-permute-start.1
  34.1 11.0 %collective-permute-done.2 = bf16[64,802]{1,0:T(8,128)(2,1)S(1)} collective-permute-done((bf16[64,802]{1,0:T(8,128)(2,1)S(1)}, bf16[64,802]{1,0:T(8,128)(2,1)S(1)}, u32[]{:S(2)}, u32[]{:S(2)}) %collective-permute-start.2) | collective-permute-done | bytes 102688 | tf_op jit(solution)/shard_map/ppermute | solution.py:343
  47.4 6.6 %collective-permute-done.4 = bf16[4,64,802]{2,1,0:T(8,128)(2,1)S(1)} collective-permute-done((bf16[4,64,802]{2,1,0:T(8,128)(2,1)S(1)}, bf16[4,64,802]{2,1,0:T(8,128)(2,1)S(1)}, u32[]{:S(2)}, u32[]{:S(2)}) %collective-permute-start.4) | collective-permute-done | bytes 410656 | tf_op jit(solution)/shard_map/ppermute | solution.py:334
  56.1 5.1 collective-permute-start.5
  67.8 2.4 convolution_bitcast_fusion.f_ref
  70.3 4.1 factor_prologue.1
  74.4 1.9 constant_dynamic-update-slice_fusion.15
  77.4 5.7 collective-permute-start.7
  84.6 2.9 collective-permute-done.6
  87.5 19.3 %collective-permute-done.7 = bf16[2,320,128]{2,1,0:T(8,128)(2,1)S(1)} collective-permute-done((bf16[2,320,128]{2,1,0:T(8,128)(2,1)S(1)}, bf16[2,320,128]{2,1,0:T(8,128)(2,1)S(1)}, u32[]{:S(2)}, u32[]{:S(2)}) %collective-permute-start.7) | collective-permute-done | bytes 163872 | tf_op jit(solution)/shard_map/ppermute | solution.py:343
  112.3 23.9 %collective-permute-done.9 = bf16[2,320,512]{2,1,0:T(8,128)(2,1)S(1)} collective-permute-done((bf16[2,320,512]{2,1,0:T(8,128)(2,1)S(1)}, bf16[2,320,512]{2,1,0:T(8,128)(2,1)S(1)}, u32[]{:S(2)}, u32[]{:S(2)}) %collective-permute-start.9) | collective-permute-done | bytes 655392 | tf_op jit(solution)/shard_map/ppermute | solution.py:343
  137.4 2.0 collective-permute-start.10
  145.0 25.9 %collective-permute-done.15 = bf16[2,320,512]{2,1,0:T(8,128)(2,1)S(1)} collective-permute-done((bf16[2,320,512]{2,1,0:T(8,128)(2,1)S(1)}, bf16[2,320,512]{2,1,0:T(8,128)(2,1)S(1)}, u32[]{:S(2)}, u32[]{:S(2)}) %collective-permute-start.15) | collective-permute-done | bytes 655392 | tf_op jit(solution)/shard_map/ppermute | solution.py:343
  175.1 20.8 %attention_forward.2 = (f32[2,128,1024]{2,1,0:T(8,128)}, f32[2,4,128,4]{3,2,1,0:T(8,128)}) custom-call(bf16[2,128,1024]{2,1,0:T(8,128)(2,1)} %get-tuple-element.244.q_ref, bf16[2,320,2048]{2,1,0:T(8,128)(2,1)} %copy-done.54, bf16[2,320,2048]{2,1,0:T(8,128)(2,1)} %copy-done.54, s32[1,2048]{1,0:T(1,128)} %bitcast.232, s32[128,1]{1,0:T(8,128)} %iota_add_fusion.qpos_ref), custom_call_target="tpu_custom_call" | custom-call | flops 2147483648 | bytes 2621440 | tf_op jit(solution)/shard_map/attention_forward/pallas_call | solution.py:218
  196.0 2.3 slice.192
  199.6 20.6 %attention_forward.3 = (f32[2,128,1024]{2,1,0:T(8,128)}, f32[2,4,128,4]{3,2,1,0:T(8,128)}) custom-call(bf16[2,128,1024]{2,1,0:T(8,128)(2,1)} %get-tuple-element.243.q_ref, bf16[2,320,2048]{2,1,0:T(8,128)(2,1)} %constant_dynamic-update-slice_fusion.16.b_ref.a_ref, bf16[2,320,2048]{2,1,0:T(8,128)(2,1)} %constant_dynamic-update-slice_fusion.16.b_ref.a_ref, ...), custom_call_target="tpu_custom_call" | custom-call | flops 2147483648 | bytes 2621440 | tf_op jit(solution)/shard_map/attention_forward/pallas_call | solution.py:218
  221.8 1.8 broadcast_select_fusion.1
  230.0 5.8 fusion.11
  235.9 6.9 %multiply_convert_fusion.2 = (bf16[1024,1408]{1,0:T(8,128)(2,1)S(1)}, f32[1024,1408]{1,0:T(8,128)}) fusion(f32[1024,1408]{1,0:T(8,128)S(1)} %fusion.11, bf16[1024,4736]{1,0:T(8,128)(2,1)S(1)} %bitcast.227, bf16[512,1024]{1,0:T(8,128)(2,1)S(1)} %collective-permute-done.18, bf16[512,1024]{1,0:T(8,128)(2,1)S(1)} %bitcast.223), kind=kOutput, calls=%fused_computation.3 | convolution fusion | flops 2965635072 | bytes 19398656 | tf_op jit(solution)/shard_map/dot_general | solution.py:620
  242.8 3.4 fusion.3
  246.2 2.0 copy-done.11
  251.3 1.9 pad_maximum_fusion.2
  253.8 7.2 %convolution_convert_fusion.2 = bf16[1024,1408]{1,0:T(8,128)(2,1)} fusion(bf16[1024,1408]{1,0:T(8,128)(2,1)S(1)} %copy-done.69, bf16[512,1024]{1,0:T(8,128)(2,1)} %collective-permute-done.19, bf16[512,1024]{1,0:T(8,128)(2,1)} %bitcast.44), kind=kOutput, calls=%fused_computation.8 | convolution fusion | flops 2958426112 | bytes 7864320 | tf_op jit(solution)/shard_map/td,tf->df/dot_general | solution.py:626
  263.8 8.0 %multiply_convert_fusion.1 = (bf16[1024,1408]{1,0:T(8,128)(2,1)S(1)}, bf16[1024,1408]{1,0:T(8,128)(2,1)}) fusion(f32[1024,1408]{1,0:T(8,128)S(1)} %bitcast.237, f32[1024,1408]{1,0:T(8,128)} %get-tuple-element.300, bf16[1024,1024]{1,0:T(8,128)(2,1)S(1)} %pad_maximum_fusion.2, bf16[1024,4736]{1,0:T(8,128)(2,1)S(1)} %bitcast.229), kind=kOutput, calls=%fused_computation.2 | convolution fusion | flops 2971533312 | bytes 22282240 | tf_op jit(solution)/shard_map/dot_general | solution.py:633
  271.9 6.3 %fusion.5 = f32[1024,1024]{1,0:T(8,128)S(1)} fusion(bf16[1024,1408]{1,0:T(8,128)(2,1)} %get-tuple-element.220, bf16[1024,4736]{1,0:T(8,128)(2,1)S(1)} %bitcast.229), kind=kOutput, calls=%fused_computation.18 | convolution fusion | flops 2952790016 | bytes 9961472 | tf_op jit(solution)/shard_map/tf,df->td/dot_general | solution.py:641
  278.2 3.5 fusion.16
  281.7 2.0 copy-done.13
  286.7 6.1 %convolution_convert_fusion = bf16[1024,1408]{1,0:T(8,128)(2,1)S(1)} fusion(bf16[1024,1408]{1,0:T(8,128)(2,1)} %get-tuple-element.220, bf16[512,1024]{1,0:T(8,128)(2,1)} %copy-done.61, bf16[512,1024]{1,0:T(8,128)(2,1)} %bitcast.224), kind=kOutput, calls=%fused_computation.6 | convolution fusion | flops 2958426112 | bytes 7864320 | tf_op jit(solution)/shard_map/td,tf->df/dot_general | solution.py:639
  296.0 2.2 multiply_add_fusion
  300.7 3.9 convolution_convert_fusion.1
  304.6 7.0 %collective-permute-done.23 = bf16[4,128,1024]{2,1,0:T(8,128)(2,1)S(1)} collective-permute-done((bf16[4,128,1024]{2,1,0:T(8,128)(2,1)}, bf16[4,128,1024]{2,1,0:T(8,128)(2,1)S(1)}, u32[]{:S(2)}, u32[]{:S(2)}) %collective-permute-start.23) | collective-permute-done | bytes 1048608 | tf_op jit(solution)/shard_map/ppermute | solution.py:334
  314.1 2.2 convolution_convert_fusion.3
  317.1 3.3 pad_maximum_fusion
  321.0 3.0 fusion.69
  329.5 32.9 %attention_backward.2 = (f32[2,128,1024]{2,1,0:T(8,128)}, bf16[8,2,320,128]{3,2,1,0:T(8,128)(2,1)}, bf16[8,2,320,128]{3,2,1,0:T(8,128)(2,1)}) custom-call(bf16[2,128,1024]{2,1,0:T(8,128)(2,1)} %get-tuple-element.244.q_ref, bf16[2,128,1024]{2,1,0:T(8,128)(2,1)} %get-tuple-element.241.do_ref, f32[2,128,1024]{2,1,0:T(8,128)} %get-tuple-element.59.o_ref, ...), custom_call_target="tpu_custom_call" | custom-call | flops 5368709120 | bytes 5242880 | tf_op jit(solution)/shard_map/attention_backward/pallas_call | solution.py:306
  363.4 17.2 %collective-permute-done.29 = bf16[4,2,32,1408]{3,2,1,0:T(8,128)(2,1)} collective-permute-done((bf16[4,2,32,1408]{3,2,1,0:T(8,128)(2,1)}, bf16[4,2,32,1408]{3,2,1,0:T(8,128)(2,1)}, u32[]{:S(2)}, u32[]{:S(2)}) %collective-permute-start.29) | collective-permute-done | bytes 720928 | tf_op jit(solution)/shard_map/ppermute | solution.py:334
  387.9 33.1 %attention_backward.3 = (f32[2,128,1024]{2,1,0:T(8,128)}, bf16[8,2,320,128]{3,2,1,0:T(8,128)(2,1)}, bf16[8,2,320,128]{3,2,1,0:T(8,128)(2,1)}) custom-call(bf16[2,128,1024]{2,1,0:T(8,128)(2,1)} %get-tuple-element.243.q_ref, bf16[2,128,1024]{2,1,0:T(8,128)(2,1)} %get-tuple-element.73.do_ref, f32[2,128,1024]{2,1,0:T(8,128)} %get-tuple-element.60.o_ref, ...), custom_call_target="tpu_custom_call" | custom-call | flops 5368709120 | bytes 5242880 | tf_op jit(solution)/shard_map/attention_backward/pallas_call | solution.py:306
  421.0 2.8 collective-permute-start.36
  428.9 2.9 collective-permute-start.28
  434.5 14.0 %collective-permute-done.28 = bf16[1,2,320,128]{3,2,1,0:T(8,128)(2,1)S(1)} collective-permute-done((bf16[1,2,320,128]{3,2,1,0:T(8,128)(2,1)S(1)}, bf16[1,2,320,128]{3,2,1,0:T(8,128)(2,1)S(1)}, u32[]{:S(2)}, u32[]{:S(2)}) %collective-permute-start.28) | collective-permute-done | bytes 163872 | tf_op jit(solution)/shard_map/ppermute | solution.py:348
  448.6 18.0 %collective-permute-done.27 = bf16[1,2,320,128]{3,2,1,0:T(8,128)(2,1)S(1)} collective-permute-done((bf16[1,2,320,128]{3,2,1,0:T(8,128)(2,1)S(1)}, bf16[1,2,320,128]{3,2,1,0:T(8,128)(2,1)S(1)}, u32[]{:S(2)}, u32[]{:S(2)}) %collective-permute-start.27) | collective-permute-done | bytes 163872 | tf_op jit(solution)/shard_map/ppermute | solution.py:348
  467.3 3.7 factor_epilogue.2
  471.0 2.8 multiply_reduce_fusion.4
  473.8 4.5 collective-permute-done.37
  479.7 5.4 collective-permute-start.40
  485.1 10.8 %collective-permute-start.39 = (bf16[1,2,320,128]{3,2,1,0:T(8,128)(2,1)S(1)}, bf16[1,2,320,128]{3,2,1,0:T(8,128)(2,1)S(1)}, u32[]{:S(2)}, u32[]{:S(2)}) collective-permute-start(bf16[1,2,320,128]{3,2,1,0:T(8,128)(2,1)S(1)} %get-tuple-element.258), channel_id=1, source_target_pairs={{0,16},{8,24},{16,0},{24,8},{1,17},{9,25},{17,1},{25,9},{2,18},{10... | collective-permute-start | bytes 491528 | tf_op jit(solution)/shard_map/ppermute | solution.py:348
  497.5 2.1 collective-permute-start.35
  499.6 10.6 %collective-permute-done.39 = bf16[1,2,320,128]{3,2,1,0:T(8,128)(2,1)S(1)} collective-permute-done((bf16[1,2,320,128]{3,2,1,0:T(8,128)(2,1)S(1)}, bf16[1,2,320,128]{3,2,1,0:T(8,128)(2,1)S(1)}, u32[]{:S(2)}, u32[]{:S(2)}) %collective-permute-start.39) | collective-permute-done | bytes 163872 | tf_op jit(solution)/shard_map/ppermute | solution.py:348
  511.0 3.1 collective-permute-done.35
  514.1 3.7 factor_epilogue.3
  517.8 3.7 multiply_reduce_fusion.3
  522.2 4.1 factor_grads.1
  528.5 6.1 %collective-permute-start.50 = (bf16[64,1408]{1,0:T(8,128)(2,1)S(1)}, bf16[64,1408]{1,0:T(8,128)(2,1)S(1)}, u32[]{:S(2)}, u32[]{:S(2)}) collective-permute-start(bf16[64,1408]{1,0:T(8,128)(2,1)S(1)} %fusion.32), channel_id=1, source_target_pairs={{0,0},{1,2},{2,1},{3,3},{4,4},{5,6},{6,5},{7,7},{8,8},{9,10},{10,9... | collective-permute-start | bytes 540680 | tf_op jit(solution)/shard_map/ppermute | solution.py:338
  540.1 10.1 %collective-permute-done.42 = bf16[2,128,1024]{2,1,0:T(8,128)(2,1)S(1)} collective-permute-done((bf16[2,128,1024]{2,1,0:T(8,128)(2,1)S(1)}, bf16[2,128,1024]{2,1,0:T(8,128)(2,1)S(1)}, u32[]{:S(2)}, u32[]{:S(2)}) %collective-permute-start.42) | collective-permute-done | bytes 524320 | tf_op jit(solution)/shard_map/ppermute | solution.py:334
  550.3 9.7 %collective-permute-done.41 = bf16[2,128,1024]{2,1,0:T(8,128)(2,1)S(1)} collective-permute-done((bf16[2,128,1024]{2,1,0:T(8,128)(2,1)S(1)}, bf16[2,128,1024]{2,1,0:T(8,128)(2,1)S(1)}, u32[]{:S(2)}, u32[]{:S(2)}) %collective-permute-start.41) | collective-permute-done | bytes 524320 | tf_op jit(solution)/shard_map/ppermute | solution.py:334
  560.4 3.1 collective-permute-start.46
  563.7 2.0 collective-permute-done.47
  565.7 8.8 %collective-permute-done.46 = bf16[64,802]{1,0:T(8,128)(2,1)S(1)} collective-permute-done((bf16[64,802]{1,0:T(8,128)(2,1)S(1)}, bf16[64,802]{1,0:T(8,128)(2,1)S(1)}, u32[]{:S(2)}, u32[]{:S(2)}) %collective-permute-start.46) | collective-permute-done | bytes 102688 | tf_op jit(solution)/shard_map/ppermute | solution.py:348
  574.8 2.6 bitcast_convert_fusion
  581.3 3.7 collective-permute-start.49
  586.8 4.3 collective-permute-done.49
  (370 shorter events, 108.2 us)
Async XLA Ops:
  7.2 188.8 %all-gather.2.cloned.1.call-start = ((), (), s32[]{:S(2)}) async-start(), calls=%async_computation.1 | async-start | bytes 10305536 | tf_op jit(solution)/shard_map/all_gather | solution.py:552
  8.2 15.5 %copy-start.55 = (f32[2,64]{1,0:T(2,128)S(1)}, f32[2,64]{1,0:T(2,128)}, u32[]{:S(2)}) copy-start(f32[2,64]{1,0:T(2,128)} %param.41) | copy-start | bytes 1540
  8.2 15.6 %copy-start.46 = (f32[64,80]{1,0:T(8,128)S(1)}, f32[64,80]{1,0:T(8,128)}, u32[]{:S(2)}) copy-start(f32[64,80]{1,0:T(8,128)} %param.26) | copy-start | bytes 61444
  10.4 12.3 %collective-permute-start.11 = (bf16[64,4736]{1,0:T(8,128)(2,1)S(1)}, bf16[64,4736]{1,0:T(8,128)(2,1)S(1)}, u32[]{:S(2)}, u32[]{:S(2)}) collective-permute-start(bf16[64,4736]{1,0:T(8,128)(2,1)S(1)} %pad_maximum_fusion.10), channel_id=1, source_target_pairs={{0,0},{1,2},{2,1},{3,3},{4,4},{5,6},{6,5},{7,7},{8,8},{9,10},{10,9... | collective-permute-start | bytes 1818632 | tf_op jit(solution)/shard_map/ppermute | solution.py:338
  23.6 557.8 %reduce-scatter.2.cloned.1.call-start = ((), (), s32[]{:S(2)}) async-start(), calls=%async_computation.2 | async-start | bytes 7241728 | tf_op jit(solution)/shard_map/reduce_scatter | solution.py:666
  24.9 3.6 collective-permute-start
  28.9 5.2 collective-permute-start.1
  32.3 12.8 %collective-permute-start.2 = (bf16[64,802]{1,0:T(8,128)(2,1)S(1)}, bf16[64,802]{1,0:T(8,128)(2,1)S(1)}, u32[]{:S(2)}, u32[]{:S(2)}) collective-permute-start(bf16[64,802]{1,0:T(8,128)(2,1)S(1)} %concatenate.55), channel_id=1, source_target_pairs={{16,0},{24,8},{0,16},{8,24},{17,1},{25,9},{1,17},{9,25},{18,2},{26... | collective-permute-start | bytes 307976 | tf_op jit(solution)/shard_map/ppermute | solution.py:343
  32.4 12.7 %collective-permute-start.3 = (bf16[64,802]{1,0:T(8,128)(2,1)S(1)}, bf16[64,802]{1,0:T(8,128)(2,1)S(1)}, u32[]{:S(2)}, u32[]{:S(2)}) collective-permute-start(bf16[64,802]{1,0:T(8,128)(2,1)S(1)} %concatenate.55), channel_id=1, source_target_pairs={{24,0},{0,8},{8,16},{16,24},{25,1},{1,9},{9,17},{17,25},{26,2},{2,... | collective-permute-start | bytes 307976 | tf_op jit(solution)/shard_map/ppermute | solution.py:343
  46.1 15.2 %copy-start.63 = (s32[16]{0:T(128)S(1)}, s32[16]{0:T(128)}, u32[]{:S(2)}) copy-start(s32[16]{0:T(128)} %param.25) | copy-start | bytes 196
  46.1 16.5 %copy-start.15 = (bf16[8,128,1024]{2,1,0:T(8,128)(2,1)S(1)}, bf16[8,128,1024]{2,1,0:T(8,128)(2,1)}, u32[]{:S(2)}) copy-start(bf16[8,128,1024]{2,1,0:T(8,128)(2,1)} %param.22) | copy-start | bytes 6291460
  46.1 7.9 %collective-permute-start.4 = (bf16[4,64,802]{2,1,0:T(8,128)(2,1)S(1)}, bf16[4,64,802]{2,1,0:T(8,128)(2,1)S(1)}, u32[]{:S(2)}, u32[]{:S(2)}) collective-permute-start(bf16[4,64,802]{2,1,0:T(8,128)(2,1)S(1)} %constant_dynamic-slice_fusion), channel_id=1, source_target_pairs={{0,4},{4,0},{1,5},{5,1},{2,6},{6,2},{3,7},{7,3},{8,12},{12,8},{9,1... | collective-permute-start | bytes 1231880 | tf_op jit(solution)/shard_map/ppermute | solution.py:334
  56.1 7.6 %collective-permute-start.5 = (bf16[2,4,64,802]{3,2,1,0:T(8,128)(2,1)}, bf16[2,4,64,802]{3,2,1,0:T(8,128)(2,1)}, u32[]{:S(2)}, u32[]{:S(2)}) collective-permute-start(bf16[2,4,64,802]{3,2,1,0:T(8,128)(2,1)} %pad_maximum_fusion.6), channel_id=1, source_target_pairs={{0,2},{2,0},{1,3},{3,1},{4,6},{6,4},{5,7},{7,5},{8,10},{10,8},{9,1... | collective-permute-start | bytes 2463752 | tf_op jit(solution)/shard_map/ppermute | solution.py:334
  76.3 11.2 %collective-permute-start.6 = (bf16[2,320,128]{2,1,0:T(8,128)(2,1)S(1)}, bf16[2,320,128]{2,1,0:T(8,128)(2,1)S(1)}, u32[]{:S(2)}, u32[]{:S(2)}) collective-permute-start(bf16[2,320,128]{2,1,0:T(8,128)(2,1)S(1)} %get-tuple-element.276), channel_id=1, source_target_pairs={{8,0},{16,8},{24,16},{0,24},{9,1},{17,9},{25,17},{1,25},{10,2},{18... | collective-permute-start | bytes 491528 | tf_op jit(solution)/shard_map/ppermute | solution.py:343
  77.4 29.4 %collective-permute-start.7 = (bf16[2,320,128]{2,1,0:T(8,128)(2,1)S(1)}, bf16[2,320,128]{2,1,0:T(8,128)(2,1)S(1)}, u32[]{:S(2)}, u32[]{:S(2)}) collective-permute-start(bf16[2,320,128]{2,1,0:T(8,128)(2,1)S(1)} %get-tuple-element.276), channel_id=1, source_target_pairs={{16,0},{24,8},{0,16},{8,24},{17,1},{25,9},{1,17},{9,25},{18,2},{26... | collective-permute-start | bytes 491528 | tf_op jit(solution)/shard_map/ppermute | solution.py:343
  83.1 23.7 %collective-permute-start.8 = (bf16[2,320,128]{2,1,0:T(8,128)(2,1)S(1)}, bf16[2,320,128]{2,1,0:T(8,128)(2,1)S(1)}, u32[]{:S(2)}, u32[]{:S(2)}) collective-permute-start(bf16[2,320,128]{2,1,0:T(8,128)(2,1)S(1)} %get-tuple-element.276), channel_id=1, source_target_pairs={{24,0},{0,8},{8,16},{16,24},{25,1},{1,9},{9,17},{17,25},{26,2},{2,... | collective-permute-start | bytes 491528 | tf_op jit(solution)/shard_map/ppermute | solution.py:343
  106.9 29.3 %collective-permute-start.9 = (bf16[2,320,512]{2,1,0:T(8,128)(2,1)S(1)}, bf16[2,320,512]{2,1,0:T(8,128)(2,1)S(1)}, u32[]{:S(2)}, u32[]{:S(2)}) collective-permute-start(bf16[2,320,512]{2,1,0:T(8,128)(2,1)S(1)} %pad_maximum_fusion.8), channel_id=1, source_target_pairs={{4,0},{0,4},{5,1},{1,5},{6,2},{2,6},{7,3},{3,7},{12,8},{8,12},{13,... | collective-permute-start | bytes 1966088 | tf_op jit(solution)/shard_map/ppermute | solution.py:343
  108.5 30.9 %collective-permute-start.12 = (bf16[2,320,128]{2,1,0:T(8,128)(2,1)S(1)}, bf16[2,320,128]{2,1,0:T(8,128)(2,1)S(1)}, u32[]{:S(2)}, u32[]{:S(2)}) collective-permute-start(bf16[2,320,128]{2,1,0:T(8,128)(2,1)S(1)} %get-tuple-element.275), channel_id=1, source_target_pairs={{8,0},{16,8},{24,16},{0,24},{9,1},{17,9},{25,17},{1,25},{10,2},{18... | collective-permute-start | bytes 491528 | tf_op jit(solution)/shard_map/ppermute | solution.py:343
  108.6 30.9 %collective-permute-start.13 = (bf16[2,320,128]{2,1,0:T(8,128)(2,1)S(1)}, bf16[2,320,128]{2,1,0:T(8,128)(2,1)S(1)}, u32[]{:S(2)}, u32[]{:S(2)}) collective-permute-start(bf16[2,320,128]{2,1,0:T(8,128)(2,1)S(1)} %get-tuple-element.275), channel_id=1, source_target_pairs={{16,0},{24,8},{0,16},{8,24},{17,1},{25,9},{1,17},{9,25},{18,2},{26... | collective-permute-start | bytes 491528 | tf_op jit(solution)/shard_map/ppermute | solution.py:343
  108.6 30.8 %collective-permute-start.14 = (bf16[2,320,128]{2,1,0:T(8,128)(2,1)S(1)}, bf16[2,320,128]{2,1,0:T(8,128)(2,1)S(1)}, u32[]{:S(2)}, u32[]{:S(2)}) collective-permute-start(bf16[2,320,128]{2,1,0:T(8,128)(2,1)S(1)} %get-tuple-element.275), channel_id=1, source_target_pairs={{24,0},{0,8},{8,16},{16,24},{25,1},{1,9},{9,17},{17,25},{26,2},{2,... | collective-permute-start | bytes 491528 | tf_op jit(solution)/shard_map/ppermute | solution.py:343
  137.4 36.2 %collective-permute-start.10 = (bf16[2,320,1024]{2,1,0:T(8,128)(2,1)}, bf16[2,320,1024]{2,1,0:T(8,128)(2,1)S(1)}, u32[]{:S(2)}, u32[]{:S(2)}) collective-permute-start(bf16[2,320,1024]{2,1,0:T(8,128)(2,1)} %get-tuple-element.264), channel_id=1, source_target_pairs={{0,2},{2,0},{1,3},{3,1},{4,6},{6,4},{5,7},{7,5},{8,10},{10,8},{9,1... | collective-permute-start | bytes 3932168 | tf_op jit(solution)/shard_map/ppermute | solution.py:334
  139.4 33.0 %copy-start.28 = (bf16[4,128,1024]{2,1,0:T(8,128)(2,1)S(1)}, bf16[4,128,1024]{2,1,0:T(8,128)(2,1)}, u32[]{:S(2)}) copy-start(bf16[4,128,1024]{2,1,0:T(8,128)(2,1)} %get-tuple-element.56) | copy-start | bytes 3145732
  139.5 31.3 %collective-permute-start.15 = (bf16[2,320,512]{2,1,0:T(8,128)(2,1)S(1)}, bf16[2,320,512]{2,1,0:T(8,128)(2,1)S(1)}, u32[]{:S(2)}, u32[]{:S(2)}) collective-permute-start(bf16[2,320,512]{2,1,0:T(8,128)(2,1)S(1)} %pad_maximum_fusion.9), channel_id=1, source_target_pairs={{4,0},{0,4},{5,1},{1,5},{6,2},{2,6},{7,3},{3,7},{12,8},{8,12},{13,... | collective-permute-start | bytes 1966088 | tf_op jit(solution)/shard_map/ppermute | solution.py:343
  145.0 28.5 %copy-start.53 = (bf16[2,320,2048]{2,1,0:T(8,128)(2,1)S(1)}, bf16[2,320,2048]{2,1,0:T(8,128)(2,1)}, u32[]{:S(2)}) copy-start(bf16[2,320,2048]{2,1,0:T(8,128)(2,1)} %get-tuple-element.265) | copy-start | bytes 7864324
  172.1 26.3 %collective-permute-start.16 = (bf16[2,320,1024]{2,1,0:T(8,128)(2,1)}, bf16[2,320,1024]{2,1,0:T(8,128)(2,1)S(1)}, u32[]{:S(2)}, u32[]{:S(2)}) collective-permute-start(bf16[2,320,1024]{2,1,0:T(8,128)(2,1)} %get-tuple-element.262), channel_id=1, source_target_pairs={{0,2},{2,0},{1,3},{3,1},{4,6},{6,4},{5,7},{7,5},{8,10},{10,8},{9,1... | collective-permute-start | bytes 3932168 | tf_op jit(solution)/shard_map/ppermute | solution.py:334
  198.2 23.6 %collective-permute-start.17 = (bf16[1024,512]{1,0:T(8,128)(2,1)}, bf16[1024,512]{1,0:T(8,128)(2,1)}, u32[]{:S(2)}, u32[]{:S(2)}) collective-permute-start(bf16[1024,512]{1,0:T(8,128)(2,1)} %slice.192), channel_id=1, source_target_pairs={{0,2},{2,0},{1,3},{3,1},{4,6},{6,4},{5,7},{7,5},{8,10},{10,8},{9,1... | collective-permute-start | bytes 3145736 | tf_op jit(solution)/shard_map/ppermute | solution.py:334
  225.4 69.0 %copy-start = (f32[4,128,1024]{2,1,0:T(8,128)}, f32[4,128,1024]{2,1,0:T(8,128)S(1)}, u32[]{:S(2)}) copy-start(f32[4,128,1024]{2,1,0:T(8,128)S(1)} %get-tuple-element.298) | copy-start | bytes 6291460
  225.8 4.3 collective-permute-start.18
  229.6 21.7 %collective-permute-start.19 = (bf16[512,1024]{1,0:T(8,128)(2,1)}, bf16[512,1024]{1,0:T(8,128)(2,1)}, u32[]{:S(2)}, u32[]{:S(2)}) collective-permute-start(bf16[512,1024]{1,0:T(8,128)(2,1)} %bitcast.44), channel_id=1, source_target_pairs={{0,2},{2,0},{1,3},{3,1},{4,6},{6,4},{5,7},{7,5},{8,10},{10,8},{9,1... | collective-permute-start | bytes 3145736 | tf_op jit(solution)/shard_map/ppermute | solution.py:334
  249.4 11.6 %collective-permute-start.20 = (bf16[512,1024]{1,0:T(8,128)(2,1)}, bf16[512,1024]{1,0:T(8,128)(2,1)}, u32[]{:S(2)}, u32[]{:S(2)}) collective-permute-start(bf16[512,1024]{1,0:T(8,128)(2,1)} %slice.337), channel_id=1, source_target_pairs={{0,2},{2,0},{1,3},{3,1},{4,6},{6,4},{5,7},{7,5},{8,10},{10,8},{9,1... | collective-permute-start | bytes 3145736 | tf_op jit(solution)/shard_map/ppermute | solution.py:334
  284.8 8.0 %collective-permute-start.21 = (bf16[512,1024]{1,0:T(8,128)(2,1)}, bf16[512,1024]{1,0:T(8,128)(2,1)}, u32[]{:S(2)}, u32[]{:S(2)}) collective-permute-start(bf16[512,1024]{1,0:T(8,128)(2,1)} %slice.336), channel_id=1, source_target_pairs={{0,2},{2,0},{1,3},{3,1},{4,6},{6,4},{5,7},{7,5},{8,10},{10,8},{9,1... | collective-permute-start | bytes 3145736 | tf_op jit(solution)/shard_map/ppermute | solution.py:334
  286.7 24.9 %collective-permute-start.23 = (bf16[4,128,1024]{2,1,0:T(8,128)(2,1)}, bf16[4,128,1024]{2,1,0:T(8,128)(2,1)S(1)}, u32[]{:S(2)}, u32[]{:S(2)}) collective-permute-start(bf16[4,128,1024]{2,1,0:T(8,128)(2,1)} %add_convert_fusion.2), channel_id=1, source_target_pairs={{0,1},{1,0},{2,3},{3,2},{4,5},{5,4},{6,7},{7,6},{8,9},{9,8},{10,11... | collective-permute-start | bytes 3145736 | tf_op jit(solution)/shard_map/ppermute | solution.py:334
  299.0 12.6 %copy-start.2 = (bf16[4,128,1024]{2,1,0:T(8,128)(2,1)S(1)}, bf16[4,128,1024]{2,1,0:T(8,128)(2,1)}, u32[]{:S(2)}) copy-start(bf16[4,128,1024]{2,1,0:T(8,128)(2,1)} %add_convert_fusion.2) | copy-start | bytes 3145732
  299.0 17.3 %collective-permute-start.22 = (bf16[1024,512]{1,0:T(8,128)(2,1)S(1)}, bf16[1024,512]{1,0:T(8,128)(2,1)S(1)}, u32[]{:S(2)}, u32[]{:S(2)}) collective-permute-start(bf16[1024,512]{1,0:T(8,128)(2,1)S(1)} %bitcast_convert_fusion.1), channel_id=1, source_target_pairs={{0,2},{2,0},{1,3},{3,1},{4,6},{6,4},{5,7},{7,5},{8,10},{10,8},{9,1... | collective-permute-start | bytes 3145736 | tf_op jit(solution)/shard_map/ppermute | solution.py:334
  325.4 55.2 %collective-permute-start.29 = (bf16[4,2,32,1408]{3,2,1,0:T(8,128)(2,1)}, bf16[4,2,32,1408]{3,2,1,0:T(8,128)(2,1)}, u32[]{:S(2)}, u32[]{:S(2)}) collective-permute-start(bf16[4,2,32,1408]{3,2,1,0:T(8,128)(2,1)} %get-tuple-element.236), channel_id=1, source_target_pairs={{0,1},{1,0},{2,3},{3,2},{4,5},{5,4},{6,7},{7,6},{8,9},{9,8},{10,11... | collective-permute-start | bytes 2162696 | tf_op jit(solution)/shard_map/ppermute | solution.py:334
  326.7 56.2 %collective-permute-start.31 = (bf16[4,2,32,1408]{3,2,1,0:T(8,128)(2,1)}, bf16[4,2,32,1408]{3,2,1,0:T(8,128)(2,1)}, u32[]{:S(2)}, u32[]{:S(2)}) collective-permute-start(bf16[4,2,32,1408]{3,2,1,0:T(8,128)(2,1)} %get-tuple-element.234), channel_id=1, source_target_pairs={{0,4},{4,0},{1,5},{5,1},{2,6},{6,2},{3,7},{7,3},{8,12},{12,8},{9,1... | collective-permute-start | bytes 2162696 | tf_op jit(solution)/shard_map/ppermute | solution.py:334
  362.3 23.0 %collective-permute-start.24 = (bf16[8,2,320,128]{3,2,1,0:T(8,128)(2,1)}, bf16[8,2,320,128]{3,2,1,0:T(8,128)(2,1)S(1)}, u32[]{:S(2)}, u32[]{:S(2)}) collective-permute-start(bf16[8,2,320,128]{3,2,1,0:T(8,128)(2,1)} %get-tuple-element.69), channel_id=1, source_target_pairs={{0,2},{2,0},{1,3},{3,1},{4,6},{6,4},{5,7},{7,5},{8,10},{10,8},{9,1... | collective-permute-start | bytes 3932168 | tf_op jit(solution)/shard_map/ppermute | solution.py:334
  382.9 40.8 %collective-permute-start.30 = (bf16[4,32,1408]{2,1,0:T(8,128)(2,1)}, bf16[4,32,1408]{2,1,0:T(8,128)(2,1)}, u32[]{:S(2)}, u32[]{:S(2)}) collective-permute-start(bf16[4,32,1408]{2,1,0:T(8,128)(2,1)} %get-tuple-element.255), channel_id=1, source_target_pairs={{0,4},{4,0},{1,5},{5,1},{2,6},{6,2},{3,7},{7,3},{8,12},{12,8},{9,1... | collective-permute-start | bytes 1081352 | tf_op jit(solution)/shard_map/ppermute | solution.py:334
  385.3 39.7 %collective-permute-start.32 = (bf16[4,32,1408]{2,1,0:T(8,128)(2,1)}, bf16[4,32,1408]{2,1,0:T(8,128)(2,1)}, u32[]{:S(2)}, u32[]{:S(2)}) collective-permute-start(bf16[4,32,1408]{2,1,0:T(8,128)(2,1)} %get-tuple-element.253), channel_id=1, source_target_pairs={{0,1},{1,0},{2,3},{3,2},{4,5},{5,4},{6,7},{7,6},{8,9},{9,8},{10,11... | collective-permute-start | bytes 1081352 | tf_op jit(solution)/shard_map/ppermute | solution.py:334
  386.5 41.0 %collective-permute-start.25 = (bf16[4,2,320,128]{3,2,1,0:T(8,128)(2,1)}, bf16[4,2,320,128]{3,2,1,0:T(8,128)(2,1)}, u32[]{:S(2)}, u32[]{:S(2)}) collective-permute-start(bf16[4,2,320,128]{3,2,1,0:T(8,128)(2,1)} %slice.206), channel_id=1, source_target_pairs={{0,4},{4,0},{1,5},{5,1},{2,6},{6,2},{3,7},{7,3},{8,12},{12,8},{9,1... | collective-permute-start | bytes 1966088 | tf_op jit(solution)/shard_map/ppermute | solution.py:348
  421.0 12.3 %collective-permute-start.36 = (bf16[8,2,320,128]{3,2,1,0:T(8,128)(2,1)}, bf16[8,2,320,128]{3,2,1,0:T(8,128)(2,1)S(1)}, u32[]{:S(2)}, u32[]{:S(2)}) collective-permute-start(bf16[8,2,320,128]{3,2,1,0:T(8,128)(2,1)} %get-tuple-element.80), channel_id=1, source_target_pairs={{0,2},{2,0},{1,3},{3,1},{4,6},{6,4},{5,7},{7,5},{8,10},{10,8},{9,1... | collective-permute-start | bytes 3932168 | tf_op jit(solution)/shard_map/ppermute | solution.py:334
  427.2 83.8 %collective-permute-start.33 = (bf16[64,1408]{1,0:T(8,128)(2,1)}, bf16[64,1408]{1,0:T(8,128)(2,1)}, u32[]{:S(2)}, u32[]{:S(2)}) collective-permute-start(bf16[64,1408]{1,0:T(8,128)(2,1)} %get-tuple-element.250), channel_id=1, source_target_pairs={{0,8},{8,16},{16,24},{24,0},{1,9},{9,17},{17,25},{25,1},{2,10},{10... | collective-permute-start | bytes 540680 | tf_op jit(solution)/shard_map/ppermute | solution.py:348
  427.2 83.8 %collective-permute-start.34 = (bf16[64,1408]{1,0:T(8,128)(2,1)}, bf16[64,1408]{1,0:T(8,128)(2,1)}, u32[]{:S(2)}, u32[]{:S(2)}) collective-permute-start(bf16[64,1408]{1,0:T(8,128)(2,1)} %get-tuple-element.251), channel_id=1, source_target_pairs={{0,16},{8,24},{16,0},{24,8},{1,17},{9,25},{17,1},{25,9},{2,18},{10... | collective-permute-start | bytes 540680 | tf_op jit(solution)/shard_map/ppermute | solution.py:348
  428.9 19.7 %collective-permute-start.28 = (bf16[1,2,320,128]{3,2,1,0:T(8,128)(2,1)S(1)}, bf16[1,2,320,128]{3,2,1,0:T(8,128)(2,1)S(1)}, u32[]{:S(2)}, u32[]{:S(2)}) collective-permute-start(bf16[1,2,320,128]{3,2,1,0:T(8,128)(2,1)S(1)} %get-tuple-element.260), channel_id=1, source_target_pairs={{0,24},{8,0},{16,8},{24,16},{1,25},{9,1},{17,9},{25,17},{2,26},{10... | collective-permute-start | bytes 491528 | tf_op jit(solution)/shard_map/ppermute | solution.py:348
  431.8 34.7 %collective-permute-start.27 = (bf16[1,2,320,128]{3,2,1,0:T(8,128)(2,1)S(1)}, bf16[1,2,320,128]{3,2,1,0:T(8,128)(2,1)S(1)}, u32[]{:S(2)}, u32[]{:S(2)}) collective-permute-start(bf16[1,2,320,128]{3,2,1,0:T(8,128)(2,1)S(1)} %get-tuple-element.261), channel_id=1, source_target_pairs={{0,16},{8,24},{16,0},{24,8},{1,17},{9,25},{17,1},{25,9},{2,18},{10... | collective-permute-start | bytes 491528 | tf_op jit(solution)/shard_map/ppermute | solution.py:348
  433.3 33.3 %collective-permute-start.26 = (bf16[1,2,320,128]{3,2,1,0:T(8,128)(2,1)S(1)}, bf16[1,2,320,128]{3,2,1,0:T(8,128)(2,1)S(1)}, u32[]{:S(2)}, u32[]{:S(2)}) collective-permute-start(bf16[1,2,320,128]{3,2,1,0:T(8,128)(2,1)S(1)} %get-tuple-element.259), channel_id=1, source_target_pairs={{0,8},{8,16},{16,24},{24,0},{1,9},{9,17},{17,25},{25,1},{2,10},{10... | collective-permute-start | bytes 491528 | tf_op jit(solution)/shard_map/ppermute | solution.py:348
  448.5 29.8 %collective-permute-start.37 = (bf16[4,2,320,128]{3,2,1,0:T(8,128)(2,1)}, bf16[4,2,320,128]{3,2,1,0:T(8,128)(2,1)}, u32[]{:S(2)}, u32[]{:S(2)}) collective-permute-start(bf16[4,2,320,128]{3,2,1,0:T(8,128)(2,1)} %slice.255), channel_id=1, source_target_pairs={{0,4},{4,0},{1,5},{5,1},{2,6},{6,2},{3,7},{7,3},{8,12},{12,8},{9,1... | collective-permute-start | bytes 1966088 | tf_op jit(solution)/shard_map/ppermute | solution.py:348
  473.8 22.2 %copy-start.1 = (f32[4,128,1024]{2,1,0:T(8,128)S(1)}, f32[4,128,1024]{2,1,0:T(8,128)}, u32[]{:S(2)}) copy-start(f32[4,128,1024]{2,1,0:T(8,128)} %get-tuple-element.225) | copy-start | bytes 6291460
  473.8 22.2 %copy-start.56 = (f32[2,128]{1,0:T(2,128)S(1)}, f32[2,128]{1,0:T(2,128)}, u32[]{:S(2)}) copy-start(f32[2,128]{1,0:T(2,128)} %get-tuple-element.294) | copy-start | bytes 3076
  479.6 17.8 %copy-start.41 = (bf16[64,1408]{1,0:T(8,128)(2,1)S(1)}, bf16[64,1408]{1,0:T(8,128)(2,1)}, u32[]{:S(2)}) copy-start(bf16[64,1408]{1,0:T(8,128)(2,1)} %get-tuple-element.249) | copy-start | bytes 540676
  479.7 17.8 %collective-permute-start.40 = (bf16[1,2,320,128]{3,2,1,0:T(8,128)(2,1)S(1)}, bf16[1,2,320,128]{3,2,1,0:T(8,128)(2,1)S(1)}, u32[]{:S(2)}, u32[]{:S(2)}) collective-permute-start(bf16[1,2,320,128]{3,2,1,0:T(8,128)(2,1)S(1)} %get-tuple-element.257), channel_id=1, source_target_pairs={{0,24},{8,0},{16,8},{24,16},{1,25},{9,1},{17,9},{25,17},{2,26},{10... | collective-permute-start | bytes 491528 | tf_op jit(solution)/shard_map/ppermute | solution.py:348
  485.1 25.1 %collective-permute-start.39 = (bf16[1,2,320,128]{3,2,1,0:T(8,128)(2,1)S(1)}, bf16[1,2,320,128]{3,2,1,0:T(8,128)(2,1)S(1)}, u32[]{:S(2)}, u32[]{:S(2)}) collective-permute-start(bf16[1,2,320,128]{3,2,1,0:T(8,128)(2,1)S(1)} %get-tuple-element.258), channel_id=1, source_target_pairs={{0,16},{8,24},{16,0},{24,8},{1,17},{9,25},{17,1},{25,9},{2,18},{10... | collective-permute-start | bytes 491528 | tf_op jit(solution)/shard_map/ppermute | solution.py:348
  496.0 14.3 %collective-permute-start.38 = (bf16[1,2,320,128]{3,2,1,0:T(8,128)(2,1)S(1)}, bf16[1,2,320,128]{3,2,1,0:T(8,128)(2,1)S(1)}, u32[]{:S(2)}, u32[]{:S(2)}) collective-permute-start(bf16[1,2,320,128]{3,2,1,0:T(8,128)(2,1)S(1)} %get-tuple-element.256), channel_id=1, source_target_pairs={{0,8},{8,16},{16,24},{24,0},{1,9},{9,17},{17,25},{25,1},{2,10},{10... | collective-permute-start | bytes 491528 | tf_op jit(solution)/shard_map/ppermute | solution.py:348
  497.5 16.6 %collective-permute-start.35 = (bf16[64,1408]{1,0:T(8,128)(2,1)S(1)}, bf16[64,1408]{1,0:T(8,128)(2,1)S(1)}, u32[]{:S(2)}, u32[]{:S(2)}) collective-permute-start(bf16[64,1408]{1,0:T(8,128)(2,1)S(1)} %copy-done.41), channel_id=1, source_target_pairs={{0,24},{8,0},{16,8},{24,16},{1,25},{9,1},{17,9},{25,17},{2,26},{10... | collective-permute-start | bytes 540680 | tf_op jit(solution)/shard_map/ppermute | solution.py:348
  526.2 12.7 %collective-permute-start.43 = (bf16[4,2,64,802]{3,2,1,0:T(8,128)(2,1)}, bf16[4,2,64,802]{3,2,1,0:T(8,128)(2,1)S(1)}, u32[]{:S(2)}, u32[]{:S(2)}) collective-permute-start(bf16[4,2,64,802]{3,2,1,0:T(8,128)(2,1)} %get-tuple-element.86), channel_id=1, source_target_pairs={{0,2},{2,0},{1,3},{3,1},{4,6},{6,4},{5,7},{7,5},{8,10},{10,8},{9,1... | collective-permute-start | bytes 2463752 | tf_op jit(solution)/shard_map/ppermute | solution.py:334
  528.5 9.3 %collective-permute-start.50 = (bf16[64,1408]{1,0:T(8,128)(2,1)S(1)}, bf16[64,1408]{1,0:T(8,128)(2,1)S(1)}, u32[]{:S(2)}, u32[]{:S(2)}) collective-permute-start(bf16[64,1408]{1,0:T(8,128)(2,1)S(1)} %fusion.32), channel_id=1, source_target_pairs={{0,0},{1,2},{2,1},{3,3},{4,4},{5,6},{6,5},{7,7},{8,8},{9,10},{10,9... | collective-permute-start | bytes 540680 | tf_op jit(solution)/shard_map/ppermute | solution.py:338
  536.3 14.0 %collective-permute-start.42 = (bf16[2,128,1024]{2,1,0:T(8,128)(2,1)S(1)}, bf16[2,128,1024]{2,1,0:T(8,128)(2,1)S(1)}, u32[]{:S(2)}, u32[]{:S(2)}) collective-permute-start(bf16[2,128,1024]{2,1,0:T(8,128)(2,1)S(1)} %fusion.19), channel_id=1, source_target_pairs={{0,1},{1,0},{2,3},{3,2},{4,5},{5,4},{6,7},{7,6},{8,9},{9,8},{10,11... | collective-permute-start | bytes 1572872 | tf_op jit(solution)/shard_map/ppermute | solution.py:334
  536.3 23.7 %collective-permute-start.41 = (bf16[2,128,1024]{2,1,0:T(8,128)(2,1)S(1)}, bf16[2,128,1024]{2,1,0:T(8,128)(2,1)S(1)}, u32[]{:S(2)}, u32[]{:S(2)}) collective-permute-start(bf16[2,128,1024]{2,1,0:T(8,128)(2,1)S(1)} %fusion.20), channel_id=1, source_target_pairs={{0,1},{1,0},{2,3},{3,2},{4,5},{5,4},{6,7},{7,6},{8,9},{9,8},{10,11... | collective-permute-start | bytes 1572872 | tf_op jit(solution)/shard_map/ppermute | solution.py:334
  539.3 20.8 %collective-permute-start.44 = (bf16[4,64,802]{2,1,0:T(8,128)(2,1)S(1)}, bf16[4,64,802]{2,1,0:T(8,128)(2,1)S(1)}, u32[]{:S(2)}, u32[]{:S(2)}) collective-permute-start(bf16[4,64,802]{2,1,0:T(8,128)(2,1)S(1)} %dynamic-slice_bitcast_fusion.4), channel_id=1, source_target_pairs={{0,4},{4,0},{1,5},{5,1},{2,6},{6,2},{3,7},{7,3},{8,12},{12,8},{9,1... | collective-permute-start | bytes 1231880 | tf_op jit(solution)/shard_map/ppermute | solution.py:348
  560.3 5.4 collective-permute-start.47
  560.4 14.1 %collective-permute-start.46 = (bf16[64,802]{1,0:T(8,128)(2,1)S(1)}, bf16[64,802]{1,0:T(8,128)(2,1)S(1)}, u32[]{:S(2)}, u32[]{:S(2)}) collective-permute-start(bf16[64,802]{1,0:T(8,128)(2,1)S(1)} %get-tuple-element.268), channel_id=1, source_target_pairs={{0,16},{8,24},{16,0},{24,8},{1,17},{9,25},{17,1},{25,9},{2,18},{10... | collective-permute-start | bytes 307976 | tf_op jit(solution)/shard_map/ppermute | solution.py:348
  563.5 11.0 %collective-permute-start.45 = (bf16[64,802]{1,0:T(8,128)(2,1)S(1)}, bf16[64,802]{1,0:T(8,128)(2,1)S(1)}, u32[]{:S(2)}, u32[]{:S(2)}) collective-permute-start(bf16[64,802]{1,0:T(8,128)(2,1)S(1)} %get-tuple-element.266), channel_id=1, source_target_pairs={{0,8},{8,16},{16,24},{24,0},{1,9},{9,17},{17,25},{25,1},{2,10},{10... | collective-permute-start | bytes 307976 | tf_op jit(solution)/shard_map/ppermute | solution.py:348
  574.7 4.3 collective-permute-start.48
  581.3 9.8 %collective-permute-start.49 = (bf16[64,3328]{1,0:T(8,128)(2,1)}, bf16[64,3328]{1,0:T(8,128)(2,1)S(1)}, u32[]{:S(2)}, u32[]{:S(2)}) collective-permute-start(bf16[64,3328]{1,0:T(8,128)(2,1)} %reduce-scatter.2.cloned.1.call-done), channel_id=1, source_target_pairs={{0,0},{1,2},{2,1},{3,3},{4,4},{5,6},{6,5},{7,7},{8,8},{9,10},{10,9... | collective-permute-start | bytes 1277960 | tf_op jit(solution)/shard_map/ppermute | solution.py:338
  (67 other events, 367.2 us)
Sparse Core Ops, SparseCore 0:
  23.7 166.3 all-gather.1
  320.5 167.0 reduce-scatter.1

commit v5 on v4

--- a/solution.py
+++ b/solution.py
@@ -162,15 +162,16 @@
     g_ref[0] = jnp.transpose(jnp.concatenate(rows, axis=0)).astype(BF)
 
 
-def epilogue(query_grad, factor_grad, factors, cos_t, sin_t):
-    count, width, block = factors.shape
+def epilogue(query_grad, factor_grad, factors, cos_t, sin_t, first, inner):
+    count = query_grad.shape[0]
+    _, width, block = factors.shape
     return pl.pallas_call(
         epilogue_body,
         grid=(count,),
         in_specs=[
             pl.BlockSpec((1, block, H * DH), lambda s: (s, 0, 0)),
-            pl.BlockSpec((1, FAC, block), lambda s: (s, 0, 0)),
-            pl.BlockSpec((1, width, block), lambda s: (s, 0, 0)),
+            pl.BlockSpec((1, FAC, block), lambda s: (s + inner, 0, 0)),
+            pl.BlockSpec((1, width, block), lambda s: (s + first, 0, 0)),
             pl.BlockSpec((DH // 2, block), lambda s: (0, 0)),
             pl.BlockSpec((DH // 2, block), lambda s: (0, 0)),
         ],
@@ -211,15 +212,15 @@
     lse_ref[0, 0] = jnp.concatenate(stats, axis=1)
 
 
-def attention_forward(query, gathered, key_pos, query_pos):
-    count, block, width = query.shape
-    length = gathered.shape[2]
+def attention_forward(query, first, gathered, key_pos, query_pos):
+    _, block, width = query.shape
+    count, _, length = gathered.shape
     wide = RK * 2 * DH
     return pl.pallas_call(
         forward_body,
         grid=(count, H // HB),
         in_specs=[
-            pl.BlockSpec((1, block, HB * DH), lambda s, g: (s, 0, g)),
+            pl.BlockSpec((1, block, HB * DH), lambda s, g: (s + first, 0, g)),
             pl.BlockSpec((1, wide, length), lambda s, g: (s, 0, 0)),
             pl.BlockSpec((1, 4 * HB, length), lambda s, g: (s, wide // (4 * HB) + g, 0)),
             pl.BlockSpec((1, length), lambda s, g: (0, 0)),
@@ -298,8 +299,10 @@
                 ref[m, 0, :wide, :] = acc_ref[:, lanes : lanes + block].astype(BF)
 
 
-def attention_backward(query, heads_grad, heads_wide, lse, gathered, key_pos, query_pos, depth):
-    count, block, width = query.shape
+def attention_backward(
+    query, heads_grad, heads_wide, lse, gathered, key_pos, query_pos, depth, first, inner, count
+):
+    _, block, width = query.shape
     length = gathered.shape[2]
     wide = RK * 2 * DH
     pieces = length // (depth * block)
@@ -307,12 +310,12 @@
         backward_body,
         grid=(count, H // HB),
         in_specs=[
-            pl.BlockSpec((1, block, HB * DH), lambda s, g: (s, 0, g)),
-            pl.BlockSpec((1, block, HB * DH), lambda s, g: (s, 0, g)),
-            pl.BlockSpec((1, block, HB * DH), lambda s, g: (s, 0, g)),
-            pl.BlockSpec((1, 1, block, HB), lambda s, g: (s, g, 0, 0)),
-            pl.BlockSpec((1, wide, length), lambda s, g: (s, 0, 0)),
-            pl.BlockSpec((1, 4 * HB, length), lambda s, g: (s, wide // (4 * HB) + g, 0)),
+            pl.BlockSpec((1, block, HB * DH), lambda s, g: (s + first, 0, g)),
+            pl.BlockSpec((1, block, HB * DH), lambda s, g: (s + first, 0, g)),
+            pl.BlockSpec((1, block, HB * DH), lambda s, g: (s + inner, 0, g)),
+            pl.BlockSpec((1, 1, block, HB), lambda s, g: (s + inner, g, 0, 0)),
+            pl.BlockSpec((1, wide, length), lambda s, g: (s + inner, 0, 0)),
+            pl.BlockSpec((1, 4 * HB, length), lambda s, g: (s + inner, wide // (4 * HB) + g, 0)),
             pl.BlockSpec((1, length), lambda s, g: (0, 0)),
             pl.BlockSpec((block, 1), lambda s, g: (0, 0)),
         ],
@@ -397,15 +400,13 @@
     return (own.astype(F32) + swap(theirs, "c").astype(F32)).astype(BF)
 
 
-def scatter_chips(total):
-    for name in ("b", "a"):
-        size = lax.axis_size(name)
-        total = total.reshape(size, total.shape[0] // size, *total.shape[1:])
-        part = total[0].astype(F32)
-        for m in range(1, size):
-            part = part + to_ahead(total[m], name, m).astype(F32)
-        total = part.astype(BF)
-    return total[0]
+def scatter_axis(total, name):
+    size = lax.axis_size(name)
+    total = total.reshape(size, total.shape[0] // size, *total.shape[1:])
+    part = total[0].astype(F32)
+    for m in range(1, size):
+        part = part + to_ahead(total[m], name, m).astype(F32)
+    return part.astype(BF)
 
 
 def sum_over_head(block, n_head):
@@ -417,10 +418,6 @@
 def in_core_order(own, other, axis):
     first = lax.axis_index("c") == 0
     return jnp.concatenate([jnp.where(first, own, other), jnp.where(first, other, own)], axis=axis)
-
-
-def after(block, gate):
-    return lax.optimization_barrier((block, gate))[0]
 
 
 def every_head(block, n_head):
@@ -429,27 +426,6 @@
         mine = lax.axis_index("h") == 0
         return jnp.stack([jnp.where(mine, block, other), jnp.where(mine, other, block)])
     return lax.all_gather(block, "h", axis=0)
-
-
-def take(block, spot, dim):
-    return lax.dynamic_index_in_dim(block, spot, dim, keepdims=False)
-
-
-def fold_send(block, axis, dim):
-    spot = lax.axis_index(axis)
-    return take(block, spot, dim), swap(take(block, 1 - spot, dim), axis)
-
-
-def fold_add(pair, gate):
-    own, other = pair
-    return (after(own, gate).astype(F32) + other.astype(F32)).astype(BF)
-
-
-def depth_send(block):
-    size = lax.axis_size("a")
-    spot = lax.axis_index("a")
-    sent = [to_ahead(take(block, jnp.mod(spot + m, size), 0), "a", m) for m in range(1, size)]
-    return take(block, spot, 0), sent
 
 
 def factor_grads_body(core_ref, x_ref, gain_ref, *refs):
@@ -578,7 +554,7 @@
     gathered = [gather_blocks(own_factors[g]) for g in groups]
     forward = []
     for at, g in enumerate(groups):
-        wide, stats = attention_forward(query[g], gathered[at], key_pos, query_pos[:, None])
+        wide, stats = attention_forward(query, g.start, gathered[at], key_pos, query_pos[:, None])
         if at == 0:
             wide, wide_all = lax.optimization_barrier((wide, wide_all))
         forward.append((wide, stats))
@@ -624,12 +600,7 @@
     ffn = own_sum(jnp.einsum("tf,df->td", hidden_low, w_down_t, preferred_element_type=F32))
     layer_low = (middle + ffn).astype(BF)
     down_low = jnp.einsum("td,tf->df", y_low, hidden_low, preferred_element_type=F32).astype(BF)
-    y_low, down_low, layer_low = lax.optimization_barrier((y_low, down_low, layer_low))
     layer_all = every_head(layer_low, n_head)
-    if paired:
-        parts = down_low.reshape(lax.axis_size("a"), 2, 2, 2, rows // 2, f_cols)
-        down_pairs = (fold_send(parts[:, :, :, 0], "h", 2), fold_send(parts[:, :, :, 1], "b", 1))
-
     hidden_grad = jnp.dot(y_low, w_down_t, preferred_element_type=F32)
     up_grad = (hidden_grad * silu_gate).astype(BF)
     gate_grad = (
@@ -658,7 +629,7 @@
     else:
         out_t_grad = out_grad_of(heads_low)
     if paired:
-        wide_grads = (gate_w_grad, up_w_grad, out_t_grad)
+        wide_grads = (gate_w_grad, up_w_grad, down_low, out_t_grad)
         wide_grad = jnp.concatenate([grad.astype(BF) for grad in wide_grads], axis=1)
         wide_grad, heads_grad, layer_all = lax.optimization_barrier(
             (wide_grad, heads_grad, layer_all)
@@ -667,7 +638,8 @@
         wide_sum = turn_core_head(wide_sum).astype(F32)
         gate_sum = wide_sum[:, :f_cols]
         up_sum = wide_sum[:, f_cols : 2 * f_cols]
-        out_sum = wide_sum[:, 2 * f_cols :]
+        down_sum = wide_sum[:, 2 * f_cols : 3 * f_cols]
+        out_sum = wide_sum[:, 3 * f_cols :]
     else:
         wide_grads = (gate_w_grad, up_w_grad, down_low, out_t_grad)
         wide_sum = jnp.concatenate([grad.astype(BF) for grad in wide_grads], axis=1)
@@ -678,14 +650,9 @@
         wide_sum = lax.dynamic_index_in_dim(wide_sum, head_at, 2, keepdims=False)
         gate_sum, up_sum, down_sum = wide_sum[:, 0], wide_sum[:, 1], wide_sum[:, 2]
 
-    query_grads = []
-    core_sums = []
-    for at, g in enumerate(groups):
-        backed = heads_grad[g]
-        if at == 1:
-            backed, core_sums[0] = lax.optimization_barrier((backed, core_sums[0]))
+    def backward_call(at, inner, size, backed):
         query_grad, *pieces = attention_backward(
-            query[g],
+            query,
             backed,
             forward[at][0],
             forward[at][1],
@@ -693,26 +660,45 @@
             key_pos,
             query_pos[:, None],
             n_seq // 2,
+            groups[at].start + inner,
+            inner,
+            size,
         )
-        query_grads.append(query_grad)
-        if paired and at == 0:
-            low = fold_send(fold_add(down_pairs[0], query_grad), "b", 1)
-            high = fold_send(fold_add(down_pairs[1], query_grad), "h", 1)
-        core_sums.append(scatter_core(*pieces))
+        return query_grad, scatter_core(*pieces)
+
+    query_grads = []
+    own_grads = []
+    if len(groups) > 1:
+        query_grad, total = backward_call(0, 0, half, heads_grad)
+        heads_grad, total = lax.optimization_barrier((heads_grad, total))
+        query_grads.append([query_grad])
+        total = scatter_axis(total, "b")
+        own_grads.append(total)
+    last = len(groups) - 1
+    sizes = [half // 2, half - half // 2] if half > 1 else [half]
+    inner = 0
+    calls = []
+    for i, size in enumerate(sizes):
+        if i and last:
+            heads_grad, own_grads[0] = lax.optimization_barrier((heads_grad, own_grads[0]))
+        calls.append(backward_call(last, inner, size, heads_grad))
+        inner += size
+    query_grads.append([call[0] for call in calls])
+    own_grads.append(scatter_axis(jnp.concatenate([call[1] for call in calls], axis=1), "b"))
+    own_grads = [scatter_axis(total, "a")[0] for total in own_grads]
     layer_output = layer_all.reshape(seq_all, block_len, D)
-    if paired:
-        low = fold_add(low, query_grads[-1])
-        high = fold_add(high, query_grads[-1])
-        down_own, down_sent = depth_send(jnp.concatenate([low, high], axis=1))
-
     first_gain_grad = 0.0
     joints = []
     input_parts = []
-    own_grads = [scatter_chips(total) for total in core_sums]
-    if paired:
-        down_sent, own_grads[1] = lax.optimization_barrier((down_sent, own_grads[1]))
     for at, g in enumerate(groups):
-        joint_grad = epilogue(query_grads[at], own_grads[at], factors[g], cos_t, sin_t)
+        inner = 0
+        parts = []
+        for query_grad in query_grads[at]:
+            parts.append(
+                epilogue(query_grad, own_grads[at], factors, cos_t, sin_t, g.start + inner, inner)
+            )
+            inner += query_grad.shape[0]
+        joint_grad = jnp.concatenate(parts, axis=0)
         first_grad = jnp.einsum("scj,dj->scd", joint_grad, w_factors, preferred_element_type=F32)
         joints.append(joint_grad.reshape(-1, joint_grad.shape[2]))
         first_gain_grad = first_gain_grad + jnp.sum(first_grad * first_hat[g], axis=(0, 1))
@@ -725,19 +711,14 @@
     gain_rows = jnp.stack([first_gain_grad, second_gain_grad] + [jnp.zeros(D, F32)] * 6)
     input_parts = [every_head(part, n_head) for part in input_parts]
     if len(groups) > 1:
-        joints[-1] = after(joints[-1], input_parts[0])
+        joints[-1], input_parts[0] = lax.optimization_barrier((joints[-1], input_parts[0]))
     small_own, small_sent = factor_grads(first_normalized.reshape(-1, D), joints, gain_rows)
     small_sum = scatter_core(small_own, small_sent)
     small_sum = ordered_scatter(small_sum, "b", 1)
     small_sum = ordered_scatter(small_sum, "a", 0)
-    small_sum = after(small_sum, input_parts[-1])
+    small_sum, input_parts[-1] = lax.optimization_barrier((small_sum, input_parts[-1]))
     small_sum = sum_over_head(small_sum, n_head).astype(F32)
     input_grad = jnp.concatenate(input_parts, axis=1).reshape(seq_all, block_len, D).astype(F32)
-    if paired:
-        down_sum = down_own.astype(F32)
-        for part in down_sent:
-            down_sum = down_sum + part.astype(F32)
-        down_sum = turn_core_head(down_sum.astype(BF)).astype(F32)
     heads_sum = lax.dynamic_slice_in_dim(small_sum, head_at * h_cols, h_cols, 1)
     shared_sum = small_sum[:, H * RA : H * RA + RA * DH]
     gains_sum = small_sum[:, H * RA + RA * DH :].T

time: 608 us -> 590 us (0.970)
  local copies, waits for them, and re-layouts: 48.3 us -> 26.2 us
  starting transfers between devices: 78.8 us -> 63.8 us
  waiting for transfers between devices: 214 us -> 225 us
    ppermute x22 -> x19, waiting for transfers between devices: 55.9 us -> 77.7 us  [swap(): return lax.ppermute(block, axis, [(0, 1), (1, 0)])]
    ppermute x15 -> x12, waiting for transfers between devices: 62.2 us -> 49.9 us  [to_ahead(): lax.ppermute(block, axis, [(i, (i + distance) % size) for i in range(size)])]
    unnamed x173 -> x125, local copies, waits for them, and re-layouts: 22.8 us -> 15.9 us
    ppermute x3 -> x2, starting transfers between devices: 14.4 us -> 7.87 us  [turn_core_head(): return lax.ppermute(block, ('c', 'h'), [(0, 0), (1, 2), (2, 1), (3, 3)])]
    slice x8 -> x3, local copies, waits for them, and re-layouts: 7.4 us -> 0.95 us  [scatter_axis(): part = part + to_ahead(total[m], name, m).astype(F32)]
    ppermute x15 -> x12, starting transfers between devices: 28.6 us -> 22.8 us  [to_ahead(): lax.ppermute(block, axis, [(i, (i + distance) % size) for i in range(size)])]
    ppermute x22 -> x19, starting transfers between devices: 19 us -> 15.8 us  [swap(): return lax.ppermute(block, axis, [(0, 1), (1, 0)])]
    pallas_call x2 -> x3, Pallas kernels: 66 us -> 68.9 us  [attention_backward(): pl.pallas_call(backward_body, grid=(count, H // HB), in_specs=[pl.BlockSp...]
  transfers between devices with their start and end apart: 53 -> 46, of which waited for: 24 -> 26; matrix products, arithmetic and copies ran while one was open for 20% -> 17% of each run, Pallas kernels for 20% -> 22%
where the time goes in v5:
time: 590 us; the launch traced here: 581 us
  waiting for transfers between devices  225 us (38%)
  Pallas kernels  128 us (22%)
  matrix products  67.8 us (11%)
  starting transfers between devices  63.8 us (11%)
  other arithmetic  53.9 us (9%)
  local copies, waits for them, and re-layouts  26.2 us (4%)
  between operations  16.4 us (3%)
    ppermute x11, waiting for transfers between devices, from_ahead(): lax.ppermute(block, axis, [((i + distance) % size, i) for i in range(size)])  85.5 us
    ppermute x19, waiting for transfers between devices, swap(): return lax.ppermute(block, axis, [(0, 1), (1, 0)])  77.7 us
    pallas_call x3, Pallas kernels, attention_backward(): pl.pallas_call(backward_body, grid=(count, H // HB), in_specs=[pl.BlockSp...  68.9 us
    ppermute x12, waiting for transfers between devices, to_ahead(): lax.ppermute(block, axis, [(i, (i + distance) % size) for i in range(size)])  49.9 us
    pallas_call x2, Pallas kernels, attention_forward(): pl.pallas_call(forward_body, grid=(count, H // HB), in_specs=[pl.BlockSpe...  41.5 us
    ppermute x12, starting transfers between devices, to_ahead(): lax.ppermute(block, axis, [(i, (i + distance) % size) for i in range(size)])  22.8 us
    ppermute x11, starting transfers between devices, from_ahead(): lax.ppermute(block, axis, [((i + distance) % size, i) for i in range(size)])  17.2 us
    unnamed x125, local copies, waits for them, and re-layouts  15.9 us
  transfers between devices with their start and end apart: 46, of which 26 were waited for; matrix products, arithmetic and copies ran while one was open for 17% of the time, Pallas kernels for 22%

profile of v5, /device:TPU:1, one launch (start us, length us, event | category | flops | bytes accessed | tf_op | source)
XLA Modules:
  0.0 581.3 jit_solution(17110891714328255189)
XLA Ops:
  9.6 4.5 collective-permute-start.11
  14.1 7.7 %collective-permute-done.11 = bf16[64,4736]{1,0:T(8,128)(2,1)S(1)} collective-permute-done((bf16[64,4736]{1,0:T(8,128)(2,1)S(1)}, bf16[64,4736]{1,0:T(8,128)(2,1)S(1)}, u32[]{:S(2)}, u32[]{:S(2)}) %collective-permute-start.11) | collective-permute-done | bytes 606240 | tf_op jit(solution)/shard_map/ppermute | solution.py:341
  24.1 3.5 collective-permute-done
  28.0 3.4 collective-permute-start.1
  33.2 11.0 %collective-permute-done.2 = bf16[64,802]{1,0:T(8,128)(2,1)S(1)} collective-permute-done((bf16[64,802]{1,0:T(8,128)(2,1)S(1)}, bf16[64,802]{1,0:T(8,128)(2,1)S(1)}, u32[]{:S(2)}, u32[]{:S(2)}) %collective-permute-start.2) | collective-permute-done | bytes 102688 | tf_op jit(solution)/shard_map/ppermute | solution.py:346
  46.5 6.6 %collective-permute-done.4 = bf16[4,64,802]{2,1,0:T(8,128)(2,1)S(1)} collective-permute-done((bf16[4,64,802]{2,1,0:T(8,128)(2,1)S(1)}, bf16[4,64,802]{2,1,0:T(8,128)(2,1)S(1)}, u32[]{:S(2)}, u32[]{:S(2)}) %collective-permute-start.4) | collective-permute-done | bytes 410656 | tf_op jit(solution)/shard_map/ppermute | solution.py:337
  55.3 5.1 collective-permute-start.5
  66.9 2.4 convolution_bitcast_fusion.f_ref
  69.3 4.1 factor_prologue.1
  73.4 1.9 constant_dynamic-update-slice_fusion.15
  76.4 5.7 collective-permute-start.7
  83.6 3.4 collective-permute-done.6
  87.0 18.7 %collective-permute-done.7 = bf16[2,320,128]{2,1,0:T(8,128)(2,1)S(1)} collective-permute-done((bf16[2,320,128]{2,1,0:T(8,128)(2,1)S(1)}, bf16[2,320,128]{2,1,0:T(8,128)(2,1)S(1)}, u32[]{:S(2)}, u32[]{:S(2)}) %collective-permute-start.7) | collective-permute-done | bytes 163872 | tf_op jit(solution)/shard_map/ppermute | solution.py:346
  111.3 24.1 %collective-permute-done.9 = bf16[2,320,512]{2,1,0:T(8,128)(2,1)S(1)} collective-permute-done((bf16[2,320,512]{2,1,0:T(8,128)(2,1)S(1)}, bf16[2,320,512]{2,1,0:T(8,128)(2,1)S(1)}, u32[]{:S(2)}, u32[]{:S(2)}) %collective-permute-start.9) | collective-permute-done | bytes 655392 | tf_op jit(solution)/shard_map/ppermute | solution.py:346
  136.6 1.8 collective-permute-start.10
  138.5 2.0 collective-permute-start.15
  143.1 27.0 %collective-permute-done.15 = bf16[2,320,512]{2,1,0:T(8,128)(2,1)S(1)} collective-permute-done((bf16[2,320,512]{2,1,0:T(8,128)(2,1)S(1)}, bf16[2,320,512]{2,1,0:T(8,128)(2,1)S(1)}, u32[]{:S(2)}, u32[]{:S(2)}) %collective-permute-start.15) | collective-permute-done | bytes 655392 | tf_op jit(solution)/shard_map/ppermute | solution.py:346
  175.5 20.8 %attention_forward.2 = (f32[2,128,1024]{2,1,0:T(8,128)}, f32[2,4,128,4]{3,2,1,0:T(8,128)}) custom-call(bf16[4,128,1024]{2,1,0:T(8,128)(2,1)} %get-tuple-element.52.q_ref, bf16[2,320,2048]{2,1,0:T(8,128)(2,1)} %copy-done.41, bf16[2,320,2048]{2,1,0:T(8,128)(2,1)} %copy-done.41, s32[1,2048]{1,0:T(1,128)} %bitcast.187, s32[128,1]{1,0:T(8,128)} %iota_add_fusion.qpos_ref), custom_call_target="tpu_custom_call" | custom-call | flops 2147483648 | bytes 2621440 | tf_op jit(solution)/shard_map/attention_forward/pallas_call | solution.py:219
  196.3 2.4 slice.167
  202.1 20.7 %attention_forward.3 = (f32[2,128,1024]{2,1,0:T(8,128)}, f32[2,4,128,4]{3,2,1,0:T(8,128)}) custom-call(bf16[4,128,1024]{2,1,0:T(8,128)(2,1)} %get-tuple-element.52.q_ref, bf16[2,320,2048]{2,1,0:T(8,128)(2,1)} %constant_dynamic-update-slice_fusion.16.b_ref.a_ref, bf16[2,320,2048]{2,1,0:T(8,128)(2,1)} %constant_dynamic-update-slice_fusion.16.b_ref.a_ref, ...), custom_call_target="tpu_custom_call" | custom-call | flops 2147483648 | bytes 2621440 | tf_op jit(solution)/shard_map/attention_forward/pallas_call | solution.py:219
  224.4 1.8 broadcast_select_fusion.1
  229.7 6.0 %fusion.11 = f32[1024,1408]{1,0:T(8,128)S(1)} fusion(bf16[1024,4736]{1,0:T(8,128)(2,1)} %all-gather.2.cloned.1.call-done, bf16[512,1024]{1,0:T(8,128)(2,1)} %collective-permute-done.19, bf16[512,1024]{1,0:T(8,128)(2,1)} %bitcast.44), kind=kOutput, calls=%fused_computation.23 | convolution fusion | flops 2956984320 | bytes 10747904 | tf_op jit(solution)/shard_map/dot_general | solution.py:604
  235.7 8.4 %fusion.3 = f32[1024,1408]{1,0:T(8,128)} fusion(bf16[1024,4736]{1,0:T(8,128)(2,1)} %all-gather.2.cloned.1.call-done, bf16[512,1024]{1,0:T(8,128)(2,1)} %collective-permute-done.18, bf16[512,1024]{1,0:T(8,128)(2,1)} %bitcast.43), kind=kOutput, calls=%fused_computation.15 | convolution fusion | flops 2956984320 | bytes 10747904 | tf_op jit(solution)/shard_map/dot_general | solution.py:595
  244.1 10.7 %multiply_convert_fusion = (bf16[1024,1408]{1,0:T(8,128)(2,1)}, bf16[1024,1408]{1,0:T(8,128)(2,1)}, bf16[1024,1408]{1,0:T(8,128)(2,1)}) fusion(f32[1024,1408]{1,0:T(8,128)} %fusion.3, f32[1024,1408]{1,0:T(8,128)S(1)} %fusion.11, bf16[1024,4736]{1,0:T(8,128)(2,1)S(1)} %bitcast.184, bf16[512,1024]{1,0:T(8,128)(2,1)} %collective-permute-done.18, ...), kind=kOutput, calls=%fused_computation.1 | convolution fusion | flops 2978611200 | bytes 25165824 | tf_op jit(solution)/shard_map/dot_general | solution.py:596
  254.8 5.4 fusion.5
  260.2 3.4 fusion.16
  264.2 3.4 fusion.9
  268.1 5.5 convolution_convert_fusion.2
  273.6 5.5 convolution_convert_fusion.1
  285.1 5.4 convolution_convert_fusion
  290.5 2.3 convolution_convert_fusion.3.do_ref
  292.8 14.7 %collective-permute-done.23 = bf16[4,128,1024]{2,1,0:T(8,128)(2,1)S(1)} collective-permute-done((bf16[4,128,1024]{2,1,0:T(8,128)(2,1)S(1)}, bf16[4,128,1024]{2,1,0:T(8,128)(2,1)S(1)}, u32[]{:S(2)}, u32[]{:S(2)}) %collective-permute-start.23) | collective-permute-done | bytes 1048608 | tf_op jit(solution)/shard_map/ppermute | solution.py:337
  310.0 5.5 pad_maximum_fusion
  315.5 33.1 %attention_backward.3 = (f32[2,128,1024]{2,1,0:T(8,128)}, bf16[8,2,320,128]{3,2,1,0:T(8,128)(2,1)}, bf16[8,2,320,128]{3,2,1,0:T(8,128)(2,1)}) custom-call(bf16[4,128,1024]{2,1,0:T(8,128)(2,1)} %get-tuple-element.52.q_ref, bf16[4,128,1024]{2,1,0:T(8,128)(2,1)} %convolution_convert_fusion.3.do_ref, f32[2,128,1024]{2,1,0:T(8,128)} %get-tuple-element.55.o_ref, ...), custom_call_target="tpu_custom_call" | custom-call | flops 5368709120 | bytes 5242880 | tf_op jit(solution)/shard_map/attention_backward/pallas_call | solution.py:309
  349.9 2.9 collective-permute-done.24
  357.0 17.7 %attention_backward.4 = (f32[1,128,1024]{2,1,0:T(8,128)}, bf16[8,1,320,128]{3,2,1,0:T(8,128)(2,1)}, bf16[8,1,320,128]{3,2,1,0:T(8,128)(2,1)}) custom-call(bf16[4,128,1024]{2,1,0:T(8,128)(2,1)} %get-tuple-element.52.q_ref, bf16[4,128,1024]{2,1,0:T(8,128)(2,1)} %convolution_convert_fusion.3.do_ref, f32[2,128,1024]{2,1,0:T(8,128)} %get-tuple-element.56.o_ref, ...), custom_call_target="tpu_custom_call" | custom-call | flops 2684354560 | bytes 2621440 | tf_op jit(solution)/shard_map/attention_backward/pallas_call | solution.py:309
  375.5 7.9 %collective-permute-done.25 = bf16[4,2,320,128]{3,2,1,0:T(8,128)(2,1)} collective-permute-done((bf16[4,2,320,128]{3,2,1,0:T(8,128)(2,1)}, bf16[4,2,320,128]{3,2,1,0:T(8,128)(2,1)}, u32[]{:S(2)}, u32[]{:S(2)}) %collective-permute-start.25) | collective-permute-done | bytes 655392 | tf_op jit(solution)/shard_map/ppermute | solution.py:351
  383.3 2.1 add_convert_fusion.6
  385.4 18.1 %attention_backward.5 = (f32[1,128,1024]{2,1,0:T(8,128)}, bf16[8,1,320,128]{3,2,1,0:T(8,128)(2,1)}, bf16[8,1,320,128]{3,2,1,0:T(8,128)(2,1)}) custom-call(bf16[4,128,1024]{2,1,0:T(8,128)(2,1)} %get-tuple-element.52.q_ref, bf16[4,128,1024]{2,1,0:T(8,128)(2,1)} %convolution_convert_fusion.3.do_ref, f32[2,128,1024]{2,1,0:T(8,128)} %get-tuple-element.56.o_ref, ...), custom_call_target="tpu_custom_call" | custom-call | flops 2684354560 | bytes 2621440 | tf_op jit(solution)/shard_map/attention_backward/pallas_call | solution.py:309
  403.5 2.7 collective-permute-start.30
  406.5 3.2 collective-permute-start.28
  412.0 5.6 collective-permute-done.26
  417.6 4.0 collective-permute-done.27
  421.7 3.9 collective-permute-done.28
  427.2 3.7 factor_epilogue.3
  430.9 2.8 multiply_reduce_fusion.6
  433.7 7.2 %collective-permute-done.31 = bf16[4,2,320,128]{3,2,1,0:T(8,128)(2,1)} collective-permute-done((bf16[4,2,320,128]{3,2,1,0:T(8,128)(2,1)}, bf16[4,2,320,128]{3,2,1,0:T(8,128)(2,1)}, u32[]{:S(2)}, u32[]{:S(2)}) %collective-permute-start.31) | collective-permute-done | bytes 655392 | tf_op jit(solution)/shard_map/ppermute | solution.py:351
  443.5 6.3 %collective-permute-start.33 = (bf16[1,2,320,128]{3,2,1,0:T(8,128)(2,1)S(1)}, bf16[1,2,320,128]{3,2,1,0:T(8,128)(2,1)S(1)}, u32[]{:S(2)}, u32[]{:S(2)}) collective-permute-start(bf16[1,2,320,128]{3,2,1,0:T(8,128)(2,1)S(1)} %get-tuple-element.234), channel_id=1, source_target_pairs={{0,16},{8,24},{16,0},{24,8},{1,17},{9,25},{17,1},{25,9},{2,18},{10... | collective-permute-start | bytes 491528 | tf_op jit(solution)/shard_map/ppermute | solution.py:351
  450.5 5.7 collective-permute-done.32
  456.2 8.5 %collective-permute-done.33 = bf16[1,2,320,128]{3,2,1,0:T(8,128)(2,1)S(1)} collective-permute-done((bf16[1,2,320,128]{3,2,1,0:T(8,128)(2,1)S(1)}, bf16[1,2,320,128]{3,2,1,0:T(8,128)(2,1)S(1)}, u32[]{:S(2)}, u32[]{:S(2)}) %collective-permute-start.33) | collective-permute-done | bytes 163872 | tf_op jit(solution)/shard_map/ppermute | solution.py:351
  466.0 2.8 factor_epilogue.4
  468.8 2.8 factor_epilogue.5
  471.6 3.7 multiply_reduce_fusion.3
  476.8 34.8 %collective-permute-done.35 = bf16[2,128,1024]{2,1,0:T(8,128)(2,1)S(1)} collective-permute-done((bf16[2,128,1024]{2,1,0:T(8,128)(2,1)S(1)}, bf16[2,128,1024]{2,1,0:T(8,128)(2,1)S(1)}, u32[]{:S(2)}, u32[]{:S(2)}) %collective-permute-start.35) | collective-permute-done | bytes 524320 | tf_op jit(solution)/shard_map/ppermute | solution.py:337
  511.8 4.1 factor_grads.1
  516.5 2.7 fusion.19
  520.8 4.8 collective-permute-start.37
  525.7 13.9 %collective-permute-done.41 = bf16[2,128,1024]{2,1,0:T(8,128)(2,1)} collective-permute-done((bf16[2,128,1024]{2,1,0:T(8,128)(2,1)}, bf16[2,128,1024]{2,1,0:T(8,128)(2,1)}, u32[]{:S(2)}, u32[]{:S(2)}) %collective-permute-start.41) | collective-permute-done | bytes 524320 | tf_op jit(solution)/shard_map/ppermute | solution.py:337
  542.1 3.1 collective-permute-start.38
  545.4 2.0 collective-permute-start.40
  548.3 5.7 collective-permute-done.39
  554.4 2.6 bitcast_convert_fusion
  558.5 3.3 collective-permute-start.43
  565.6 4.5 collective-permute-done.43
  (296 shorter events, 83.6 us)
Async XLA Ops:
  7.2 15.5 %copy-start.42 = (f32[2,64]{1,0:T(2,128)S(1)}, f32[2,64]{1,0:T(2,128)}, u32[]{:S(2)}) copy-start(f32[2,64]{1,0:T(2,128)} %param.41) | copy-start | bytes 1540
  7.2 15.7 %copy-start.35 = (f32[64,80]{1,0:T(8,128)S(1)}, f32[64,80]{1,0:T(8,128)}, u32[]{:S(2)}) copy-start(f32[64,80]{1,0:T(8,128)} %param.26) | copy-start | bytes 61444
  7.2 189.1 %all-gather.2.cloned.1.call-start = ((), (), s32[]{:S(2)}) async-start(), calls=%async_computation.1 | async-start | bytes 10305536 | tf_op jit(solution)/shard_map/all_gather | solution.py:528
  9.6 12.3 %collective-permute-start.11 = (bf16[64,4736]{1,0:T(8,128)(2,1)S(1)}, bf16[64,4736]{1,0:T(8,128)(2,1)S(1)}, u32[]{:S(2)}, u32[]{:S(2)}) collective-permute-start(bf16[64,4736]{1,0:T(8,128)(2,1)S(1)} %pad_maximum_fusion.16), channel_id=1, source_target_pairs={{0,0},{1,2},{2,1},{3,3},{4,4},{5,6},{6,5},{7,7},{8,8},{9,10},{10,9... | collective-permute-start | bytes 1818632 | tf_op jit(solution)/shard_map/ppermute | solution.py:341
  22.7 535.8 %reduce-scatter.2.cloned.1.call-start = ((), (), s32[]{:S(2)}) async-start(), calls=%async_computation.2 | async-start | bytes 10305536 | tf_op jit(solution)/shard_map/reduce_scatter | solution.py:637
  24.0 3.6 collective-permute-start
  28.0 5.2 collective-permute-start.1
  31.4 12.8 %collective-permute-start.2 = (bf16[64,802]{1,0:T(8,128)(2,1)S(1)}, bf16[64,802]{1,0:T(8,128)(2,1)S(1)}, u32[]{:S(2)}, u32[]{:S(2)}) collective-permute-start(bf16[64,802]{1,0:T(8,128)(2,1)S(1)} %concatenate.58), channel_id=1, source_target_pairs={{16,0},{24,8},{0,16},{8,24},{17,1},{25,9},{1,17},{9,25},{18,2},{26... | collective-permute-start | bytes 307976 | tf_op jit(solution)/shard_map/ppermute | solution.py:346
  31.5 12.7 %collective-permute-start.3 = (bf16[64,802]{1,0:T(8,128)(2,1)S(1)}, bf16[64,802]{1,0:T(8,128)(2,1)S(1)}, u32[]{:S(2)}, u32[]{:S(2)}) collective-permute-start(bf16[64,802]{1,0:T(8,128)(2,1)S(1)} %concatenate.58), channel_id=1, source_target_pairs={{24,0},{0,8},{8,16},{16,24},{25,1},{1,9},{9,17},{17,25},{26,2},{2,... | collective-permute-start | bytes 307976 | tf_op jit(solution)/shard_map/ppermute | solution.py:346
  45.2 15.2 %copy-start.45 = (s32[16]{0:T(128)S(1)}, s32[16]{0:T(128)}, u32[]{:S(2)}) copy-start(s32[16]{0:T(128)} %param.25) | copy-start | bytes 196
  45.2 16.5 %copy-start.7 = (bf16[8,128,1024]{2,1,0:T(8,128)(2,1)S(1)}, bf16[8,128,1024]{2,1,0:T(8,128)(2,1)}, u32[]{:S(2)}) copy-start(bf16[8,128,1024]{2,1,0:T(8,128)(2,1)} %param.22) | copy-start | bytes 6291460
  45.2 7.9 %collective-permute-start.4 = (bf16[4,64,802]{2,1,0:T(8,128)(2,1)S(1)}, bf16[4,64,802]{2,1,0:T(8,128)(2,1)S(1)}, u32[]{:S(2)}, u32[]{:S(2)}) collective-permute-start(bf16[4,64,802]{2,1,0:T(8,128)(2,1)S(1)} %constant_dynamic-slice_fusion), channel_id=1, source_target_pairs={{0,4},{4,0},{1,5},{5,1},{2,6},{6,2},{3,7},{7,3},{8,12},{12,8},{9,1... | collective-permute-start | bytes 1231880 | tf_op jit(solution)/shard_map/ppermute | solution.py:337
  55.3 7.6 %collective-permute-start.5 = (bf16[2,4,64,802]{3,2,1,0:T(8,128)(2,1)}, bf16[2,4,64,802]{3,2,1,0:T(8,128)(2,1)}, u32[]{:S(2)}, u32[]{:S(2)}) collective-permute-start(bf16[2,4,64,802]{3,2,1,0:T(8,128)(2,1)} %pad_maximum_fusion.11), channel_id=1, source_target_pairs={{0,2},{2,0},{1,3},{3,1},{4,6},{6,4},{5,7},{7,5},{8,10},{10,8},{9,1... | collective-permute-start | bytes 2463752 | tf_op jit(solution)/shard_map/ppermute | solution.py:337
  75.3 11.7 %collective-permute-start.6 = (bf16[2,320,128]{2,1,0:T(8,128)(2,1)S(1)}, bf16[2,320,128]{2,1,0:T(8,128)(2,1)S(1)}, u32[]{:S(2)}, u32[]{:S(2)}) collective-permute-start(bf16[2,320,128]{2,1,0:T(8,128)(2,1)S(1)} %get-tuple-element.252), channel_id=1, source_target_pairs={{8,0},{16,8},{24,16},{0,24},{9,1},{17,9},{25,17},{1,25},{10,2},{18... | collective-permute-start | bytes 491528 | tf_op jit(solution)/shard_map/ppermute | solution.py:346
  76.4 29.3 %collective-permute-start.7 = (bf16[2,320,128]{2,1,0:T(8,128)(2,1)S(1)}, bf16[2,320,128]{2,1,0:T(8,128)(2,1)S(1)}, u32[]{:S(2)}, u32[]{:S(2)}) collective-permute-start(bf16[2,320,128]{2,1,0:T(8,128)(2,1)S(1)} %get-tuple-element.252), channel_id=1, source_target_pairs={{16,0},{24,8},{0,16},{8,24},{17,1},{25,9},{1,17},{9,25},{18,2},{26... | collective-permute-start | bytes 491528 | tf_op jit(solution)/shard_map/ppermute | solution.py:346
  82.1 23.6 %collective-permute-start.8 = (bf16[2,320,128]{2,1,0:T(8,128)(2,1)S(1)}, bf16[2,320,128]{2,1,0:T(8,128)(2,1)S(1)}, u32[]{:S(2)}, u32[]{:S(2)}) collective-permute-start(bf16[2,320,128]{2,1,0:T(8,128)(2,1)S(1)} %get-tuple-element.252), channel_id=1, source_target_pairs={{24,0},{0,8},{8,16},{16,24},{25,1},{1,9},{9,17},{17,25},{26,2},{2,... | collective-permute-start | bytes 491528 | tf_op jit(solution)/shard_map/ppermute | solution.py:346
  105.9 29.5 %collective-permute-start.9 = (bf16[2,320,512]{2,1,0:T(8,128)(2,1)S(1)}, bf16[2,320,512]{2,1,0:T(8,128)(2,1)S(1)}, u32[]{:S(2)}, u32[]{:S(2)}) collective-permute-start(bf16[2,320,512]{2,1,0:T(8,128)(2,1)S(1)} %pad_maximum_fusion.14), channel_id=1, source_target_pairs={{4,0},{0,4},{5,1},{1,5},{6,2},{2,6},{7,3},{3,7},{12,8},{8,12},{13,... | collective-permute-start | bytes 1966088 | tf_op jit(solution)/shard_map/ppermute | solution.py:346
  107.5 30.9 %collective-permute-start.12 = (bf16[2,320,128]{2,1,0:T(8,128)(2,1)S(1)}, bf16[2,320,128]{2,1,0:T(8,128)(2,1)S(1)}, u32[]{:S(2)}, u32[]{:S(2)}) collective-permute-start(bf16[2,320,128]{2,1,0:T(8,128)(2,1)S(1)} %get-tuple-element.251), channel_id=1, source_target_pairs={{8,0},{16,8},{24,16},{0,24},{9,1},{17,9},{25,17},{1,25},{10,2},{18... | collective-permute-start | bytes 491528 | tf_op jit(solution)/shard_map/ppermute | solution.py:346
  107.5 30.9 %collective-permute-start.13 = (bf16[2,320,128]{2,1,0:T(8,128)(2,1)S(1)}, bf16[2,320,128]{2,1,0:T(8,128)(2,1)S(1)}, u32[]{:S(2)}, u32[]{:S(2)}) collective-permute-start(bf16[2,320,128]{2,1,0:T(8,128)(2,1)S(1)} %get-tuple-element.251), channel_id=1, source_target_pairs={{16,0},{24,8},{0,16},{8,24},{17,1},{25,9},{1,17},{9,25},{18,2},{26... | collective-permute-start | bytes 491528 | tf_op jit(solution)/shard_map/ppermute | solution.py:346
  107.6 30.8 %collective-permute-start.14 = (bf16[2,320,128]{2,1,0:T(8,128)(2,1)S(1)}, bf16[2,320,128]{2,1,0:T(8,128)(2,1)S(1)}, u32[]{:S(2)}, u32[]{:S(2)}) collective-permute-start(bf16[2,320,128]{2,1,0:T(8,128)(2,1)S(1)} %get-tuple-element.251), channel_id=1, source_target_pairs={{24,0},{0,8},{8,16},{16,24},{25,1},{1,9},{9,17},{17,25},{26,2},{2,... | collective-permute-start | bytes 491528 | tf_op jit(solution)/shard_map/ppermute | solution.py:346
  136.6 37.3 %copy-start.40 = (bf16[2,320,2048]{2,1,0:T(8,128)(2,1)S(1)}, bf16[2,320,2048]{2,1,0:T(8,128)(2,1)}, u32[]{:S(2)}) copy-start(bf16[2,320,2048]{2,1,0:T(8,128)(2,1)} %get-tuple-element.241) | copy-start | bytes 7864324
  136.6 37.2 %collective-permute-start.10 = (bf16[2,320,1024]{2,1,0:T(8,128)(2,1)}, bf16[2,320,1024]{2,1,0:T(8,128)(2,1)S(1)}, u32[]{:S(2)}, u32[]{:S(2)}) collective-permute-start(bf16[2,320,1024]{2,1,0:T(8,128)(2,1)} %get-tuple-element.240), channel_id=1, source_target_pairs={{0,2},{2,0},{1,3},{3,1},{4,6},{6,4},{5,7},{7,5},{8,10},{10,8},{9,1... | collective-permute-start | bytes 3932168 | tf_op jit(solution)/shard_map/ppermute | solution.py:337
  138.5 31.5 %collective-permute-start.15 = (bf16[2,320,512]{2,1,0:T(8,128)(2,1)S(1)}, bf16[2,320,512]{2,1,0:T(8,128)(2,1)S(1)}, u32[]{:S(2)}, u32[]{:S(2)}) collective-permute-start(bf16[2,320,512]{2,1,0:T(8,128)(2,1)S(1)} %pad_maximum_fusion.15), channel_id=1, source_target_pairs={{4,0},{0,4},{5,1},{1,5},{6,2},{2,6},{7,3},{3,7},{12,8},{8,12},{13,... | collective-permute-start | bytes 1966088 | tf_op jit(solution)/shard_map/ppermute | solution.py:346
  172.1 28.8 %collective-permute-start.16 = (bf16[2,320,1024]{2,1,0:T(8,128)(2,1)}, bf16[2,320,1024]{2,1,0:T(8,128)(2,1)S(1)}, u32[]{:S(2)}, u32[]{:S(2)}) collective-permute-start(bf16[2,320,1024]{2,1,0:T(8,128)(2,1)} %copy-done.39), channel_id=1, source_target_pairs={{0,2},{2,0},{1,3},{3,1},{4,6},{6,4},{5,7},{7,5},{8,10},{10,8},{9,1... | collective-permute-start | bytes 3932168 | tf_op jit(solution)/shard_map/ppermute | solution.py:337
  198.7 25.7 %collective-permute-start.17 = (bf16[1024,512]{1,0:T(8,128)(2,1)}, bf16[1024,512]{1,0:T(8,128)(2,1)}, u32[]{:S(2)}, u32[]{:S(2)}) collective-permute-start(bf16[1024,512]{1,0:T(8,128)(2,1)} %slice.167), channel_id=1, source_target_pairs={{0,2},{2,0},{1,3},{3,1},{4,6},{6,4},{5,7},{7,5},{8,10},{10,8},{9,1... | collective-permute-start | bytes 3145736 | tf_op jit(solution)/shard_map/ppermute | solution.py:337
  200.5 29.1 %collective-permute-start.19 = (bf16[512,1024]{1,0:T(8,128)(2,1)}, bf16[512,1024]{1,0:T(8,128)(2,1)}, u32[]{:S(2)}, u32[]{:S(2)}) collective-permute-start(bf16[512,1024]{1,0:T(8,128)(2,1)} %bitcast.44), channel_id=1, source_target_pairs={{0,2},{2,0},{1,3},{3,1},{4,6},{6,4},{5,7},{7,5},{8,10},{10,8},{9,1... | collective-permute-start | bytes 3145736 | tf_op jit(solution)/shard_map/ppermute | solution.py:337
  228.0 51.6 %copy-start = (f32[4,128,1024]{2,1,0:T(8,128)}, f32[4,128,1024]{2,1,0:T(8,128)S(1)}, u32[]{:S(2)}) copy-start(f32[4,128,1024]{2,1,0:T(8,128)S(1)} %get-tuple-element.274) | copy-start | bytes 6291460
  229.5 6.2 %collective-permute-start.18 = (bf16[512,1024]{1,0:T(8,128)(2,1)}, bf16[512,1024]{1,0:T(8,128)(2,1)}, u32[]{:S(2)}, u32[]{:S(2)}) collective-permute-start(bf16[512,1024]{1,0:T(8,128)(2,1)} %bitcast.43), channel_id=1, source_target_pairs={{0,2},{2,0},{1,3},{3,1},{4,6},{6,4},{5,7},{7,5},{8,10},{10,8},{9,1... | collective-permute-start | bytes 3145736 | tf_op jit(solution)/shard_map/ppermute | solution.py:337
  229.6 14.4 %slice-start = ((s8[9699328]{0:T(1024)(128)(4,1)}), s8[4194304]{0:T(1024)(128)(4,1)S(1)}, s32[]{:S(2)}) async-start(s8[9699328]{0:T(1024)(128)(4,1)} %bitcast.183), calls=%async_computation.3 | async-start | bytes 8388608
  229.6 14.4 %slice-start.1 = ((s8[9699328]{0:T(1024)(128)(4,1)}), s8[4194304]{0:T(1024)(128)(4,1)S(1)}, s32[]{:S(2)}) async-start(s8[9699328]{0:T(1024)(128)(4,1)} %bitcast.183), calls=%async_computation.4 | async-start | bytes 8388608
  235.7 8.4 %slice-start.2 = ((s8[9699328]{0:T(1024)(128)(4,1)}), s8[1310720]{0:T(1024)(128)(4,1)S(1)}, s32[]{:S(2)}) async-start(s8[9699328]{0:T(1024)(128)(4,1)} %bitcast.183), calls=%async_computation.5 | async-start | bytes 2621440
  263.8 15.3 %collective-permute-start.20 = (bf16[512,1024]{1,0:T(8,128)(2,1)S(1)}, bf16[512,1024]{1,0:T(8,128)(2,1)S(1)}, u32[]{:S(2)}, u32[]{:S(2)}) collective-permute-start(bf16[512,1024]{1,0:T(8,128)(2,1)S(1)} %slice.312), channel_id=1, source_target_pairs={{0,2},{2,0},{1,3},{3,1},{4,6},{6,4},{5,7},{7,5},{8,10},{10,8},{9,1... | collective-permute-start | bytes 3145736 | tf_op jit(solution)/shard_map/ppermute | solution.py:337
  267.8 12.5 %collective-permute-start.22 = (bf16[512,1024]{1,0:T(8,128)(2,1)S(1)}, bf16[512,1024]{1,0:T(8,128)(2,1)S(1)}, u32[]{:S(2)}, u32[]{:S(2)}) collective-permute-start(bf16[512,1024]{1,0:T(8,128)(2,1)S(1)} %slice.311), channel_id=1, source_target_pairs={{0,2},{2,0},{1,3},{3,1},{4,6},{6,4},{5,7},{7,5},{8,10},{10,8},{9,1... | collective-permute-start | bytes 3145736 | tf_op jit(solution)/shard_map/ppermute | solution.py:337
  283.2 24.3 %collective-permute-start.23 = (bf16[4,128,1024]{2,1,0:T(8,128)(2,1)S(1)}, bf16[4,128,1024]{2,1,0:T(8,128)(2,1)S(1)}, u32[]{:S(2)}, u32[]{:S(2)}) collective-permute-start(bf16[4,128,1024]{2,1,0:T(8,128)(2,1)S(1)} %get-tuple-element.220), channel_id=1, source_target_pairs={{0,1},{1,0},{2,3},{3,2},{4,5},{5,4},{6,7},{7,6},{8,9},{9,8},{10,11... | collective-permute-start | bytes 3145736 | tf_op jit(solution)/shard_map/ppermute | solution.py:337
  284.1 25.1 %collective-permute-start.21 = (bf16[1024,512]{1,0:T(8,128)(2,1)S(1)}, bf16[1024,512]{1,0:T(8,128)(2,1)S(1)}, u32[]{:S(2)}, u32[]{:S(2)}) collective-permute-start(bf16[1024,512]{1,0:T(8,128)(2,1)S(1)} %bitcast_convert_fusion.1), channel_id=1, source_target_pairs={{0,2},{2,0},{1,3},{3,1},{4,6},{6,4},{5,7},{7,5},{8,10},{10,8},{9,1... | collective-permute-start | bytes 3145736 | tf_op jit(solution)/shard_map/ppermute | solution.py:337
  348.6 4.1 collective-permute-start.24
  355.3 28.0 %collective-permute-start.25 = (bf16[4,2,320,128]{3,2,1,0:T(8,128)(2,1)}, bf16[4,2,320,128]{3,2,1,0:T(8,128)(2,1)}, u32[]{:S(2)}, u32[]{:S(2)}) collective-permute-start(bf16[4,2,320,128]{3,2,1,0:T(8,128)(2,1)} %slice.179), channel_id=1, source_target_pairs={{0,4},{4,0},{1,5},{5,1},{2,6},{6,2},{3,7},{7,3},{8,12},{12,8},{9,1... | collective-permute-start | bytes 1966088 | tf_op jit(solution)/shard_map/ppermute | solution.py:351
  374.7 34.9 %collective-permute-start.29 = (bf16[8,1,320,128]{3,2,1,0:T(8,128)(2,1)}, bf16[8,1,320,128]{3,2,1,0:T(8,128)(2,1)}, u32[]{:S(2)}, u32[]{:S(2)}) collective-permute-start(bf16[8,1,320,128]{3,2,1,0:T(8,128)(2,1)} %get-tuple-element.70), channel_id=1, source_target_pairs={{0,2},{2,0},{1,3},{3,1},{4,6},{6,4},{5,7},{7,5},{8,10},{10,8},{9,1... | collective-permute-start | bytes 1966088 | tf_op jit(solution)/shard_map/ppermute | solution.py:337
  385.4 20.8 %copy-start.5 = (bf16[4,2,320,128]{3,2,1,0:T(8,128)(2,1)S(1)}, bf16[4,2,320,128]{3,2,1,0:T(8,128)(2,1)}, u32[]{:S(2)}) copy-start(bf16[4,2,320,128]{3,2,1,0:T(8,128)(2,1)} %add_convert_fusion.6) | copy-start | bytes 1966084
  385.4 24.2 %copy-start.23 = (bf16[8,1,320,128]{3,2,1,0:T(8,128)(2,1)S(1)}, bf16[8,1,320,128]{3,2,1,0:T(8,128)(2,1)}, u32[]{:S(2)}) copy-start(bf16[8,1,320,128]{3,2,1,0:T(8,128)(2,1)} %get-tuple-element.69) | copy-start | bytes 1966084
  403.5 7.4 %collective-permute-start.30 = (bf16[8,1,320,128]{3,2,1,0:T(8,128)(2,1)}, bf16[8,1,320,128]{3,2,1,0:T(8,128)(2,1)S(1)}, u32[]{:S(2)}, u32[]{:S(2)}) collective-permute-start(bf16[8,1,320,128]{3,2,1,0:T(8,128)(2,1)} %get-tuple-element.73), channel_id=1, source_target_pairs={{0,2},{2,0},{1,3},{3,1},{4,6},{6,4},{5,7},{7,5},{8,10},{10,8},{9,1... | collective-permute-start | bytes 1966088 | tf_op jit(solution)/shard_map/ppermute | solution.py:337
  406.3 11.3 %collective-permute-start.26 = (bf16[1,2,320,128]{3,2,1,0:T(8,128)(2,1)S(1)}, bf16[1,2,320,128]{3,2,1,0:T(8,128)(2,1)S(1)}, u32[]{:S(2)}, u32[]{:S(2)}) collective-permute-start(bf16[1,2,320,128]{3,2,1,0:T(8,128)(2,1)S(1)} %get-tuple-element.235), channel_id=1, source_target_pairs={{0,8},{8,16},{16,24},{24,0},{1,9},{9,17},{17,25},{25,1},{2,10},{10... | collective-permute-start | bytes 491528 | tf_op jit(solution)/shard_map/ppermute | solution.py:351
  406.4 15.3 %collective-permute-start.27 = (bf16[1,2,320,128]{3,2,1,0:T(8,128)(2,1)S(1)}, bf16[1,2,320,128]{3,2,1,0:T(8,128)(2,1)S(1)}, u32[]{:S(2)}, u32[]{:S(2)}) collective-permute-start(bf16[1,2,320,128]{3,2,1,0:T(8,128)(2,1)S(1)} %get-tuple-element.237), channel_id=1, source_target_pairs={{0,16},{8,24},{16,0},{24,8},{1,17},{9,25},{17,1},{25,9},{2,18},{10... | collective-permute-start | bytes 491528 | tf_op jit(solution)/shard_map/ppermute | solution.py:351
  406.5 19.1 %collective-permute-start.28 = (bf16[1,2,320,128]{3,2,1,0:T(8,128)(2,1)S(1)}, bf16[1,2,320,128]{3,2,1,0:T(8,128)(2,1)S(1)}, u32[]{:S(2)}, u32[]{:S(2)}) collective-permute-start(bf16[1,2,320,128]{3,2,1,0:T(8,128)(2,1)S(1)} %get-tuple-element.236), channel_id=1, source_target_pairs={{0,24},{8,0},{16,8},{24,16},{1,25},{9,1},{17,9},{25,17},{2,26},{10... | collective-permute-start | bytes 491528 | tf_op jit(solution)/shard_map/ppermute | solution.py:351
  412.0 29.0 %collective-permute-start.31 = (bf16[4,2,320,128]{3,2,1,0:T(8,128)(2,1)}, bf16[4,2,320,128]{3,2,1,0:T(8,128)(2,1)}, u32[]{:S(2)}, u32[]{:S(2)}) collective-permute-start(bf16[4,2,320,128]{3,2,1,0:T(8,128)(2,1)} %pad_maximum_fusion.13), channel_id=1, source_target_pairs={{0,4},{4,0},{1,5},{5,1},{2,6},{6,2},{3,7},{7,3},{8,12},{12,8},{9,1... | collective-permute-start | bytes 1966088 | tf_op jit(solution)/shard_map/ppermute | solution.py:351
  433.7 16.4 %copy-start.2 = (f32[4,128,1024]{2,1,0:T(8,128)S(1)}, f32[4,128,1024]{2,1,0:T(8,128)}, u32[]{:S(2)}) copy-start(f32[4,128,1024]{2,1,0:T(8,128)} %get-tuple-element.216) | copy-start | bytes 6291460
  442.3 13.9 %collective-permute-start.32 = (bf16[1,2,320,128]{3,2,1,0:T(8,128)(2,1)S(1)}, bf16[1,2,320,128]{3,2,1,0:T(8,128)(2,1)S(1)}, u32[]{:S(2)}, u32[]{:S(2)}) collective-permute-start(bf16[1,2,320,128]{3,2,1,0:T(8,128)(2,1)S(1)} %get-tuple-element.232), channel_id=1, source_target_pairs={{0,8},{8,16},{16,24},{24,0},{1,9},{9,17},{17,25},{25,1},{2,10},{10... | collective-permute-start | bytes 491528 | tf_op jit(solution)/shard_map/ppermute | solution.py:351
  443.5 21.2 %collective-permute-start.33 = (bf16[1,2,320,128]{3,2,1,0:T(8,128)(2,1)S(1)}, bf16[1,2,320,128]{3,2,1,0:T(8,128)(2,1)S(1)}, u32[]{:S(2)}, u32[]{:S(2)}) collective-permute-start(bf16[1,2,320,128]{3,2,1,0:T(8,128)(2,1)S(1)} %get-tuple-element.234), channel_id=1, source_target_pairs={{0,16},{8,24},{16,0},{24,8},{1,17},{9,25},{17,1},{25,9},{2,18},{10... | collective-permute-start | bytes 491528 | tf_op jit(solution)/shard_map/ppermute | solution.py:351
  449.9 15.4 %collective-permute-start.34 = (bf16[1,2,320,128]{3,2,1,0:T(8,128)(2,1)S(1)}, bf16[1,2,320,128]{3,2,1,0:T(8,128)(2,1)S(1)}, u32[]{:S(2)}, u32[]{:S(2)}) collective-permute-start(bf16[1,2,320,128]{3,2,1,0:T(8,128)(2,1)S(1)} %get-tuple-element.233), channel_id=1, source_target_pairs={{0,24},{8,0},{16,8},{24,16},{1,25},{9,1},{17,9},{25,17},{2,26},{10... | collective-permute-start | bytes 491528 | tf_op jit(solution)/shard_map/ppermute | solution.py:351
  471.6 40.0 %collective-permute-start.35 = (bf16[2,128,1024]{2,1,0:T(8,128)(2,1)S(1)}, bf16[2,128,1024]{2,1,0:T(8,128)(2,1)S(1)}, u32[]{:S(2)}, u32[]{:S(2)}) collective-permute-start(bf16[2,128,1024]{2,1,0:T(8,128)(2,1)S(1)} %fusion.20), channel_id=1, source_target_pairs={{0,1},{1,0},{2,3},{3,2},{4,5},{5,4},{6,7},{7,6},{8,9},{9,8},{10,11... | collective-permute-start | bytes 1572872 | tf_op jit(solution)/shard_map/ppermute | solution.py:337
  516.0 3.3 collective-permute-start.36
  519.2 20.4 %collective-permute-start.41 = (bf16[2,128,1024]{2,1,0:T(8,128)(2,1)}, bf16[2,128,1024]{2,1,0:T(8,128)(2,1)}, u32[]{:S(2)}, u32[]{:S(2)}) collective-permute-start(bf16[2,128,1024]{2,1,0:T(8,128)(2,1)} %fusion.19), channel_id=1, source_target_pairs={{0,1},{1,0},{2,3},{3,2},{4,5},{5,4},{6,7},{7,6},{8,9},{9,8},{10,11... | collective-permute-start | bytes 1572872 | tf_op jit(solution)/shard_map/ppermute | solution.py:337
  520.8 20.1 %collective-permute-start.37 = (bf16[4,64,802]{2,1,0:T(8,128)(2,1)S(1)}, bf16[4,64,802]{2,1,0:T(8,128)(2,1)}, u32[]{:S(2)}, u32[]{:S(2)}) collective-permute-start(bf16[4,64,802]{2,1,0:T(8,128)(2,1)S(1)} %dynamic-slice_bitcast_fusion), channel_id=1, source_target_pairs={{0,4},{4,0},{1,5},{5,1},{2,6},{6,2},{3,7},{7,3},{8,12},{12,8},{9,1... | collective-permute-start | bytes 1231880 | tf_op jit(solution)/shard_map/ppermute | solution.py:351
  542.1 6.2 %collective-permute-start.38 = (bf16[64,802]{1,0:T(8,128)(2,1)S(1)}, bf16[64,802]{1,0:T(8,128)(2,1)S(1)}, u32[]{:S(2)}, u32[]{:S(2)}) collective-permute-start(bf16[64,802]{1,0:T(8,128)(2,1)S(1)} %get-tuple-element.242), channel_id=1, source_target_pairs={{0,8},{8,16},{16,24},{24,0},{1,9},{9,17},{17,25},{25,1},{2,10},{10... | collective-permute-start | bytes 307976 | tf_op jit(solution)/shard_map/ppermute | solution.py:351
  545.2 8.8 %collective-permute-start.39 = (bf16[64,802]{1,0:T(8,128)(2,1)S(1)}, bf16[64,802]{1,0:T(8,128)(2,1)S(1)}, u32[]{:S(2)}, u32[]{:S(2)}) collective-permute-start(bf16[64,802]{1,0:T(8,128)(2,1)S(1)} %get-tuple-element.244), channel_id=1, source_target_pairs={{0,16},{8,24},{16,0},{24,8},{1,17},{9,25},{17,1},{25,9},{2,18},{10... | collective-permute-start | bytes 307976 | tf_op jit(solution)/shard_map/ppermute | solution.py:351
  545.4 8.6 %collective-permute-start.40 = (bf16[64,802]{1,0:T(8,128)(2,1)S(1)}, bf16[64,802]{1,0:T(8,128)(2,1)S(1)}, u32[]{:S(2)}, u32[]{:S(2)}) collective-permute-start(bf16[64,802]{1,0:T(8,128)(2,1)S(1)} %get-tuple-element.243), channel_id=1, source_target_pairs={{0,24},{8,0},{16,8},{24,16},{1,25},{9,1},{17,9},{25,17},{2,26},{10... | collective-permute-start | bytes 307976 | tf_op jit(solution)/shard_map/ppermute | solution.py:351
  554.0 4.2 collective-permute-start.42
  554.4 9.5 %copy-start.36 = (f32[64,80]{1,0:T(8,128)S(1)}, f32[64,80]{1,0:T(8,128)}, u32[]{:S(2)}) copy-start(f32[64,80]{1,0:T(8,128)} %param.26) | copy-start | bytes 61444
  554.4 9.5 %copy-start.37 = (f32[64,80]{1,0:T(8,128)S(1)}, f32[64,80]{1,0:T(8,128)}, u32[]{:S(2)}) copy-start(f32[64,80]{1,0:T(8,128)} %param.27) | copy-start | bytes 61444
  554.4 9.5 %copy-start.38 = (f32[64,80]{1,0:T(8,128)S(1)}, f32[64,80]{1,0:T(8,128)}, u32[]{:S(2)}) copy-start(f32[64,80]{1,0:T(8,128)} %param.28) | copy-start | bytes 61444
  554.4 10.2 %copy-start.30 = (f32[64,640]{1,0:T(8,128)S(1)}, f32[64,640]{1,0:T(8,128)}, u32[]{:S(2)}) copy-start(f32[64,640]{1,0:T(8,128)} %param.29) | copy-start | bytes 491524
  554.4 10.2 %copy-start.31 = (f32[64,640]{1,0:T(8,128)S(1)}, f32[64,640]{1,0:T(8,128)}, u32[]{:S(2)}) copy-start(f32[64,640]{1,0:T(8,128)} %param.30) | copy-start | bytes 491524
  554.4 10.2 %copy-start.32 = (f32[64,640]{1,0:T(8,128)S(1)}, f32[64,640]{1,0:T(8,128)}, u32[]{:S(2)}) copy-start(f32[64,640]{1,0:T(8,128)} %param.31) | copy-start | bytes 491524
  558.5 11.6 %collective-permute-start.43 = (bf16[64,4736]{1,0:T(8,128)(2,1)}, bf16[64,4736]{1,0:T(8,128)(2,1)S(1)}, u32[]{:S(2)}, u32[]{:S(2)}) collective-permute-start(bf16[64,4736]{1,0:T(8,128)(2,1)} %reduce-scatter.2.cloned.1.call-done), channel_id=1, source_target_pairs={{0,0},{1,2},{2,1},{3,3},{4,4},{5,6},{6,5},{7,7},{8,8},{9,10},{10,9... | collective-permute-start | bytes 1818632 | tf_op jit(solution)/shard_map/ppermute | solution.py:341
  (36 other events, 112.6 us)
Sparse Core Ops, SparseCore 0:
  22.8 166.1 all-gather.1
  315.7 213.8 reduce-scatter.1

commit v6 on v5

--- a/solution.py
+++ b/solution.py
@@ -597,10 +597,12 @@
     sigmoid_gate = jax.nn.sigmoid(gate)
     silu_gate = gate * sigmoid_gate
     hidden_low = (silu_gate * up).astype(BF)
-    ffn = own_sum(jnp.einsum("tf,df->td", hidden_low, w_down_t, preferred_element_type=F32))
+    ffn_part = jnp.einsum("tf,df->td", hidden_low, w_down_t, preferred_element_type=F32)
+    y_low, ffn_part = lax.optimization_barrier((y_low, ffn_part))
+    ffn = own_sum(ffn_part)
     layer_low = (middle + ffn).astype(BF)
     down_low = jnp.einsum("td,tf->df", y_low, hidden_low, preferred_element_type=F32).astype(BF)
-    layer_all = every_head(layer_low, n_head)
+    layer_parts = [layer_low[g] for g in groups]
     hidden_grad = jnp.dot(y_low, w_down_t, preferred_element_type=F32)
     up_grad = (hidden_grad * silu_gate).astype(BF)
     gate_grad = (
@@ -629,17 +631,16 @@
     else:
         out_t_grad = out_grad_of(heads_low)
     if paired:
-        wide_grads = (gate_w_grad, up_w_grad, down_low, out_t_grad)
+        wide_grads = (gate_w_grad, up_w_grad, down_low)
         wide_grad = jnp.concatenate([grad.astype(BF) for grad in wide_grads], axis=1)
-        wide_grad, heads_grad, layer_all = lax.optimization_barrier(
-            (wide_grad, heads_grad, layer_all)
-        )
+        wide_grad, heads_grad = lax.optimization_barrier((wide_grad, heads_grad))
+        na, nb = lax.axis_size("a"), lax.axis_size("b")
+        out_sum = out_t_grad.astype(BF).reshape(na, nb, 2, rows, o_cols)
         wide_sum = lax.psum_scatter(wide_grad, ("a", "b", "h"), scatter_dimension=0, tiled=True)
         wide_sum = turn_core_head(wide_sum).astype(F32)
         gate_sum = wide_sum[:, :f_cols]
         up_sum = wide_sum[:, f_cols : 2 * f_cols]
-        down_sum = wide_sum[:, 2 * f_cols : 3 * f_cols]
-        out_sum = wide_sum[:, 3 * f_cols :]
+        down_sum = wide_sum[:, 2 * f_cols :]
     else:
         wide_grads = (gate_w_grad, up_w_grad, down_low, out_t_grad)
         wide_sum = jnp.concatenate([grad.astype(BF) for grad in wide_grads], axis=1)
@@ -670,7 +671,11 @@
     own_grads = []
     if len(groups) > 1:
         query_grad, total = backward_call(0, 0, half, heads_grad)
-        heads_grad, total = lax.optimization_barrier((heads_grad, total))
+        heads_grad, total, out_sum, layer_parts[0] = lax.optimization_barrier(
+            (heads_grad, total, out_sum, layer_parts[0])
+        )
+        if paired:
+            out_sum = ordered_scatter(out_sum, "b", 1)
         query_grads.append([query_grad])
         total = scatter_axis(total, "b")
         own_grads.append(total)
@@ -680,13 +685,18 @@
     calls = []
     for i, size in enumerate(sizes):
         if i and last:
-            heads_grad, own_grads[0] = lax.optimization_barrier((heads_grad, own_grads[0]))
+            heads_grad, own_grads[0], out_sum, layer_parts[1] = lax.optimization_barrier(
+                (heads_grad, own_grads[0], out_sum, layer_parts[1])
+            )
         calls.append(backward_call(last, inner, size, heads_grad))
         inner += size
     query_grads.append([call[0] for call in calls])
+    layer_parts = [every_head(part, n_head) for part in layer_parts]
     own_grads.append(scatter_axis(jnp.concatenate([call[1] for call in calls], axis=1), "b"))
     own_grads = [scatter_axis(total, "a")[0] for total in own_grads]
-    layer_output = layer_all.reshape(seq_all, block_len, D)
+    if paired:
+        out_sum = ordered_scatter(ordered_scatter(out_sum, "a", 0), "h", 0)
+        out_sum = turn_core_head(out_sum).astype(F32)
     first_gain_grad = 0.0
     joints = []
     input_parts = []
@@ -699,6 +709,7 @@
             )
             inner += query_grad.shape[0]
         joint_grad = jnp.concatenate(parts, axis=0)
+        joint_grad, layer_parts[at] = lax.optimization_barrier((joint_grad, layer_parts[at]))
         first_grad = jnp.einsum("scj,dj->scd", joint_grad, w_factors, preferred_element_type=F32)
         joints.append(joint_grad.reshape(-1, joint_grad.shape[2]))
         first_gain_grad = first_gain_grad + jnp.sum(first_grad * first_hat[g], axis=(0, 1))
@@ -708,13 +719,14 @@
             part, own_grads[at + 1] = lax.optimization_barrier((part, own_grads[at + 1]))
         input_parts.append(part)
 
+    layer_output = jnp.concatenate(layer_parts, axis=1).reshape(seq_all, block_len, D)
     gain_rows = jnp.stack([first_gain_grad, second_gain_grad] + [jnp.zeros(D, F32)] * 6)
     input_parts = [every_head(part, n_head) for part in input_parts]
-    if len(groups) > 1:
-        joints[-1], input_parts[0] = lax.optimization_barrier((joints[-1], input_parts[0]))
     small_own, small_sent = factor_grads(first_normalized.reshape(-1, D), joints, gain_rows)
     small_sum = scatter_core(small_own, small_sent)
     small_sum = ordered_scatter(small_sum, "b", 1)
+    if len(groups) > 1:
+        small_sum, input_parts[0] = lax.optimization_barrier((small_sum, input_parts[0]))
     small_sum = ordered_scatter(small_sum, "a", 0)
     small_sum, input_parts[-1] = lax.optimization_barrier((small_sum, input_parts[-1]))
     small_sum = sum_over_head(small_sum, n_head).astype(F32)

time: 590 us -> 588 us (level)
  waiting for transfers between devices: 225 us -> 192 us
  starting transfers between devices: 63.8 us -> 85.5 us
  other arithmetic: 53.9 us -> 60.2 us
  local copies, waits for them, and re-layouts: 26.2 us -> 32.5 us
    ppermute x19 -> x20, waiting for transfers between devices: 77.7 us -> 30.7 us  [swap(): return lax.ppermute(block, axis, [(0, 1), (1, 0)])]
    ppermute x12 -> x17, waiting for transfers between devices: 49.9 us -> 64.2 us  [to_ahead(): lax.ppermute(block, axis, [(i, (i + distance) % size) for i in range(size)])]
    ppermute x12 -> x17, starting transfers between devices: 22.8 us -> 35.8 us  [to_ahead(): lax.ppermute(block, axis, [(i, (i + distance) % size) for i in range(size)])]
    ppermute x2 -> x3, starting transfers between devices: 7.87 us -> 15.7 us  [turn_core_head(): return lax.ppermute(block, ('c', 'h'), [(0, 0), (1, 2), (2, 1), (3, 3)])]
    ppermute x19 -> x20, starting transfers between devices: 15.8 us -> 17 us  [swap(): return lax.ppermute(block, axis, [(0, 1), (1, 0)])]
    unnamed x125 -> x137, local copies, waits for them, and re-layouts: 15.9 us -> 16.9 us
    ppermute x2 -> x3, waiting for transfers between devices: 12.2 us -> 11.2 us  [turn_core_head(): return lax.ppermute(block, ('c', 'h'), [(0, 0), (1, 2), (2, 1), (3, 3)])]
  transfers between devices with their start and end apart: 46 -> 53, of which waited for: 26 -> 24; matrix products, arithmetic and copies ran while one was open for 17% -> 17% of each run, Pallas kernels for 22% -> 22%
where the time goes in v6:
time: 588 us; the launch traced here: 580 us
  waiting for transfers between devices  192 us (33%)
  Pallas kernels  128 us (22%)
  starting transfers between devices  85.5 us (15%)
  matrix products  66.1 us (11%)
  other arithmetic  60.2 us (10%)
  local copies, waits for them, and re-layouts  32.5 us (6%)
  between operations  16.4 us (3%)
    ppermute x11, waiting for transfers between devices, from_ahead(): lax.ppermute(block, axis, [((i + distance) % size, i) for i in range(size)])  85.6 us
    pallas_call x3, Pallas kernels, attention_backward(): pl.pallas_call(backward_body, grid=(count, H // HB), in_specs=[pl.BlockSp...  68.6 us
    ppermute x17, waiting for transfers between devices, to_ahead(): lax.ppermute(block, axis, [(i, (i + distance) % size) for i in range(size)])  64.2 us
    pallas_call x2, Pallas kernels, attention_forward(): pl.pallas_call(forward_body, grid=(count, H // HB), in_specs=[pl.BlockSpe...  41.4 us
    ppermute x17, starting transfers between devices, to_ahead(): lax.ppermute(block, axis, [(i, (i + distance) % size) for i in range(size)])  35.8 us
    ppermute x20, waiting for transfers between devices, swap(): return lax.ppermute(block, axis, [(0, 1), (1, 0)])  30.7 us
    ppermute x20, starting transfers between devices, swap(): return lax.ppermute(block, axis, [(0, 1), (1, 0)])  17 us
    unnamed x137, local copies, waits for them, and re-layouts  16.9 us
  transfers between devices with their start and end apart: 53, of which 24 were waited for; matrix products, arithmetic and copies ran while one was open for 17% of the time, Pallas kernels for 22%

profile of v6, /device:TPU:1, one launch (start us, length us, event | category | flops | bytes accessed | tf_op | source)
XLA Modules:
  0.0 580.1 jit_solution(13836903070757959693)
XLA Ops:
  9.6 4.5 collective-permute-start.11
  14.1 7.7 %collective-permute-done.11 = bf16[64,4736]{1,0:T(8,128)(2,1)S(1)} collective-permute-done((bf16[64,4736]{1,0:T(8,128)(2,1)S(1)}, bf16[64,4736]{1,0:T(8,128)(2,1)S(1)}, u32[]{:S(2)}, u32[]{:S(2)}) %collective-permute-start.11) | collective-permute-done | bytes 606240 | tf_op jit(solution)/shard_map/ppermute | solution.py:341
  24.1 3.5 collective-permute-done
  28.1 3.4 collective-permute-start.1
  33.3 11.0 %collective-permute-done.2 = bf16[64,802]{1,0:T(8,128)(2,1)S(1)} collective-permute-done((bf16[64,802]{1,0:T(8,128)(2,1)S(1)}, bf16[64,802]{1,0:T(8,128)(2,1)S(1)}, u32[]{:S(2)}, u32[]{:S(2)}) %collective-permute-start.2) | collective-permute-done | bytes 102688 | tf_op jit(solution)/shard_map/ppermute | solution.py:346
  46.6 6.6 %collective-permute-done.4 = bf16[4,64,802]{2,1,0:T(8,128)(2,1)S(1)} collective-permute-done((bf16[4,64,802]{2,1,0:T(8,128)(2,1)S(1)}, bf16[4,64,802]{2,1,0:T(8,128)(2,1)S(1)}, u32[]{:S(2)}, u32[]{:S(2)}) %collective-permute-start.4) | collective-permute-done | bytes 410656 | tf_op jit(solution)/shard_map/ppermute | solution.py:337
  55.3 5.1 collective-permute-start.5
  67.0 2.4 convolution_bitcast_fusion.f_ref
  69.4 4.1 factor_prologue.1
  76.6 5.7 collective-permute-start.7
  83.8 3.2 collective-permute-done.6
  86.9 19.0 %collective-permute-done.7 = bf16[2,320,128]{2,1,0:T(8,128)(2,1)S(1)} collective-permute-done((bf16[2,320,128]{2,1,0:T(8,128)(2,1)S(1)}, bf16[2,320,128]{2,1,0:T(8,128)(2,1)S(1)}, u32[]{:S(2)}, u32[]{:S(2)}) %collective-permute-start.7) | collective-permute-done | bytes 163872 | tf_op jit(solution)/shard_map/ppermute | solution.py:346
  111.3 24.1 %collective-permute-done.9 = bf16[2,320,512]{2,1,0:T(8,128)(2,1)S(1)} collective-permute-done((bf16[2,320,512]{2,1,0:T(8,128)(2,1)S(1)}, bf16[2,320,512]{2,1,0:T(8,128)(2,1)S(1)}, u32[]{:S(2)}, u32[]{:S(2)}) %collective-permute-start.9) | collective-permute-done | bytes 655392 | tf_op jit(solution)/shard_map/ppermute | solution.py:346
  136.6 2.0 collective-permute-start.10
  143.1 27.0 %collective-permute-done.15 = bf16[2,320,512]{2,1,0:T(8,128)(2,1)S(1)} collective-permute-done((bf16[2,320,512]{2,1,0:T(8,128)(2,1)S(1)}, bf16[2,320,512]{2,1,0:T(8,128)(2,1)S(1)}, u32[]{:S(2)}, u32[]{:S(2)}) %collective-permute-start.15) | collective-permute-done | bytes 655392 | tf_op jit(solution)/shard_map/ppermute | solution.py:346
  175.5 20.8 %attention_forward.2 = (f32[2,128,1024]{2,1,0:T(8,128)}, f32[2,4,128,4]{3,2,1,0:T(8,128)}) custom-call(bf16[4,128,1024]{2,1,0:T(8,128)(2,1)} %get-tuple-element.61.q_ref, bf16[2,320,2048]{2,1,0:T(8,128)(2,1)} %copy-done.47, bf16[2,320,2048]{2,1,0:T(8,128)(2,1)} %copy-done.47, s32[1,2048]{1,0:T(1,128)} %bitcast.220, s32[128,1]{1,0:T(8,128)} %iota_add_fusion.qpos_ref), custom_call_target="tpu_custom_call" | custom-call | flops 2147483648 | bytes 2621440 | tf_op jit(solution)/shard_map/attention_forward/pallas_call | solution.py:219
  196.4 2.4 slice.170
  202.3 20.6 %attention_forward.3 = (f32[2,128,1024]{2,1,0:T(8,128)}, f32[2,4,128,4]{3,2,1,0:T(8,128)}) custom-call(bf16[4,128,1024]{2,1,0:T(8,128)(2,1)} %get-tuple-element.61.q_ref, bf16[2,320,2048]{2,1,0:T(8,128)(2,1)} %constant_dynamic-update-slice_fusion.16.b_ref.a_ref, bf16[2,320,2048]{2,1,0:T(8,128)(2,1)} %constant_dynamic-update-slice_fusion.16.b_ref.a_ref, ...), custom_call_target="tpu_custom_call" | custom-call | flops 2147483648 | bytes 2621440 | tf_op jit(solution)/shard_map/attention_forward/pallas_call | solution.py:219
  228.7 2.0 pad_maximum_fusion.2
  231.2 5.5 fusion.11
  236.7 7.3 %multiply_convert_fusion.2 = (bf16[1024,1408]{1,0:T(8,128)(2,1)}, f32[1024,1408]{1,0:T(8,128)}) fusion(f32[1024,1408]{1,0:T(8,128)S(1)} %fusion.11, bf16[1024,4736]{1,0:T(8,128)(2,1)S(1)} %bitcast.217, bf16[512,1024]{1,0:T(8,128)(2,1)S(1)} %collective-permute-done.18, bf16[512,1024]{1,0:T(8,128)(2,1)S(1)} %bitcast.213), kind=kOutput, calls=%fused_computation.3 | convolution fusion | flops 2965635072 | bytes 19398656 | tf_op jit(solution)/shard_map/dot_general | solution.py:596
  244.0 5.4 fusion.3
  249.5 3.7 convolution_convert_fusion
  253.2 9.3 %multiply_convert_fusion.1 = (bf16[1024,1408]{1,0:T(8,128)(2,1)}, bf16[1024,1408]{1,0:T(8,128)(2,1)}) fusion(f32[1024,1408]{1,0:T(8,128)} %copy-done.53, f32[1024,1408]{1,0:T(8,128)} %get-tuple-element.300, bf16[1024,1024]{1,0:T(8,128)(2,1)S(1)} %pad_maximum_fusion.2, bf16[1024,4736]{1,0:T(8,128)(2,1)S(1)} %bitcast.217), kind=kOutput, calls=%fused_computation.2 | convolution fusion | flops 2971533312 | bytes 22282240 | tf_op jit(solution)/shard_map/dot_general | solution.py:606
  262.5 5.2 fusion.5
  267.8 5.3 fusion.16
  277.0 3.8 convolution_convert_fusion.2
  280.8 3.9 convolution_convert_fusion.1
  284.7 3.8 pad_maximum_fusion
  288.4 2.2 slice_add_fusion
  296.4 2.3 convolution_convert_fusion.3.do_ref
  300.5 32.9 %attention_backward.3 = (f32[2,128,1024]{2,1,0:T(8,128)}, bf16[8,2,320,128]{3,2,1,0:T(8,128)(2,1)}, bf16[8,2,320,128]{3,2,1,0:T(8,128)(2,1)}) custom-call(bf16[4,128,1024]{2,1,0:T(8,128)(2,1)} %get-tuple-element.61.q_ref, bf16[4,128,1024]{2,1,0:T(8,128)(2,1)} %convolution_convert_fusion.3.do_ref, f32[2,128,1024]{2,1,0:T(8,128)} %get-tuple-element.64.o_ref, ...), custom_call_target="tpu_custom_call" | custom-call | flops 5368709120 | bytes 5242880 | tf_op jit(solution)/shard_map/attention_backward/pallas_call | solution.py:309
  333.9 2.2 fusion.63
  336.1 2.1 fusion.14
  338.3 2.1 add_convert_fusion
  344.4 17.9 %attention_backward.4 = (f32[1,128,1024]{2,1,0:T(8,128)}, bf16[8,1,320,128]{3,2,1,0:T(8,128)(2,1)}, bf16[8,1,320,128]{3,2,1,0:T(8,128)(2,1)}) custom-call(bf16[4,128,1024]{2,1,0:T(8,128)(2,1)} %get-tuple-element.61.q_ref, bf16[4,128,1024]{2,1,0:T(8,128)(2,1)} %convolution_convert_fusion.3.do_ref, f32[2,128,1024]{2,1,0:T(8,128)} %get-tuple-element.65.o_ref, ...), custom_call_target="tpu_custom_call" | custom-call | flops 2684354560 | bytes 2621440 | tf_op jit(solution)/shard_map/attention_backward/pallas_call | solution.py:309
  362.7 2.2 fusion.21
  367.3 11.8 %collective-permute-done.24 = bf16[4,2,320,128]{3,2,1,0:T(8,128)(2,1)} collective-permute-done((bf16[4,2,320,128]{3,2,1,0:T(8,128)(2,1)}, bf16[4,2,320,128]{3,2,1,0:T(8,128)(2,1)}, u32[]{:S(2)}, u32[]{:S(2)}) %collective-permute-start.24) | collective-permute-done | bytes 655392 | tf_op jit(solution)/shard_map/ppermute | solution.py:351
  379.0 2.1 add_convert_fusion.6
  381.2 17.8 %attention_backward.5 = (f32[1,128,1024]{2,1,0:T(8,128)}, bf16[8,1,320,128]{3,2,1,0:T(8,128)(2,1)}, bf16[8,1,320,128]{3,2,1,0:T(8,128)(2,1)}) custom-call(bf16[4,128,1024]{2,1,0:T(8,128)(2,1)} %get-tuple-element.61.q_ref, bf16[4,128,1024]{2,1,0:T(8,128)(2,1)} %convolution_convert_fusion.3.do_ref, f32[2,128,1024]{2,1,0:T(8,128)} %get-tuple-element.65.o_ref, ...), custom_call_target="tpu_custom_call" | custom-call | flops 2684354560 | bytes 2621440 | tf_op jit(solution)/shard_map/attention_backward/pallas_call | solution.py:309
  402.2 2.3 collective-permute-start.47
  406.9 4.8 collective-permute-done.46
  412.6 3.9 collective-permute-start.28
  417.8 17.9 %collective-permute-done.27 = bf16[1,2,320,128]{3,2,1,0:T(8,128)(2,1)S(1)} collective-permute-done((bf16[1,2,320,128]{3,2,1,0:T(8,128)(2,1)S(1)}, bf16[1,2,320,128]{3,2,1,0:T(8,128)(2,1)S(1)}, u32[]{:S(2)}, u32[]{:S(2)}) %collective-permute-start.27) | collective-permute-done | bytes 163872 | tf_op jit(solution)/shard_map/ppermute | solution.py:351
  436.4 4.0 factor_epilogue.3
  440.4 2.9 multiply_reduce_fusion.5
  444.8 7.2 %collective-permute-start.32 = (bf16[4,2,320,128]{3,2,1,0:T(8,128)(2,1)S(1)}, bf16[4,2,320,128]{3,2,1,0:T(8,128)(2,1)S(1)}, u32[]{:S(2)}, u32[]{:S(2)}) collective-permute-start(bf16[4,2,320,128]{3,2,1,0:T(8,128)(2,1)S(1)} %pad_maximum_fusion.13), channel_id=1, source_target_pairs={{0,4},{4,0},{1,5},{5,1},{2,6},{6,2},{3,7},{7,3},{8,12},{12,8},{9,1... | collective-permute-start | bytes 1966088 | tf_op jit(solution)/shard_map/ppermute | solution.py:351
  453.8 6.8 %collective-permute-start.49 = (bf16[64,512]{1,0:T(8,128)(2,1)}, bf16[64,512]{1,0:T(8,128)(2,1)}, u32[]{:S(2)}, u32[]{:S(2)}) collective-permute-start(bf16[64,512]{1,0:T(8,128)(2,1)} %fusion.42), channel_id=1, source_target_pairs={{0,0},{1,2},{2,1},{3,3},{4,4},{5,6},{6,5},{7,7},{8,8},{9,10},{10,9... | collective-permute-start | bytes 196616 | tf_op jit(solution)/shard_map/ppermute | solution.py:341
  460.6 3.9 collective-permute-done.32
  464.7 4.8 collective-permute-start.33
  473.7 16.3 %collective-permute-done.34 = bf16[1,2,320,128]{3,2,1,0:T(8,128)(2,1)S(1)} collective-permute-done((bf16[1,2,320,128]{3,2,1,0:T(8,128)(2,1)S(1)}, bf16[1,2,320,128]{3,2,1,0:T(8,128)(2,1)S(1)}, u32[]{:S(2)}, u32[]{:S(2)}) %collective-permute-start.34) | collective-permute-done | bytes 163872 | tf_op jit(solution)/shard_map/ppermute | solution.py:351
  490.7 2.8 factor_epilogue.4
  493.5 2.8 factor_epilogue.5
  497.4 3.7 multiply_reduce_fusion.3
  501.8 4.0 factor_grads.1
  505.9 2.2 collective-permute-start.37
  516.4 8.7 %collective-permute-done.43 = bf16[2,128,1024]{2,1,0:T(8,128)(2,1)S(1)} collective-permute-done((bf16[2,128,1024]{2,1,0:T(8,128)(2,1)S(1)}, bf16[2,128,1024]{2,1,0:T(8,128)(2,1)S(1)}, u32[]{:S(2)}, u32[]{:S(2)}) %collective-permute-start.43) | collective-permute-done | bytes 524320 | tf_op jit(solution)/shard_map/ppermute | solution.py:337
  525.1 11.2 %collective-permute-done.39 = bf16[2,128,1024]{2,1,0:T(8,128)(2,1)S(1)} collective-permute-done((bf16[2,128,1024]{2,1,0:T(8,128)(2,1)S(1)}, bf16[2,128,1024]{2,1,0:T(8,128)(2,1)S(1)}, u32[]{:S(2)}, u32[]{:S(2)}) %collective-permute-start.39) | collective-permute-done | bytes 524320 | tf_op jit(solution)/shard_map/ppermute | solution.py:337
  536.8 6.0 %collective-permute-start.40 = (bf16[64,802]{1,0:T(8,128)(2,1)S(1)}, bf16[64,802]{1,0:T(8,128)(2,1)S(1)}, u32[]{:S(2)}, u32[]{:S(2)}) collective-permute-start(bf16[64,802]{1,0:T(8,128)(2,1)S(1)} %get-tuple-element.266), channel_id=1, source_target_pairs={{0,8},{8,16},{16,24},{24,0},{1,9},{9,17},{17,25},{25,1},{2,10},{10... | collective-permute-start | bytes 307976 | tf_op jit(solution)/shard_map/ppermute | solution.py:351
  545.1 2.1 collective-permute-done.40
  547.2 5.7 collective-permute-done.41
  554.5 2.6 bitcast_convert_fusion
  557.4 4.4 collective-permute-start.50
  565.6 3.5 collective-permute-done.50
  (334 shorter events, 105.0 us)
Async XLA Ops:
  7.2 15.5 %copy-start.48 = (f32[2,64]{1,0:T(2,128)S(1)}, f32[2,64]{1,0:T(2,128)}, u32[]{:S(2)}) copy-start(f32[2,64]{1,0:T(2,128)} %param.41) | copy-start | bytes 1540
  7.2 15.7 %copy-start.40 = (f32[64,80]{1,0:T(8,128)S(1)}, f32[64,80]{1,0:T(8,128)}, u32[]{:S(2)}) copy-start(f32[64,80]{1,0:T(8,128)} %param.26) | copy-start | bytes 61444
  7.2 189.1 %all-gather.2.cloned.1.call-start = ((), (), s32[]{:S(2)}) async-start(), calls=%async_computation.1 | async-start | bytes 10305536 | tf_op jit(solution)/shard_map/all_gather | solution.py:528
  9.6 12.3 %collective-permute-start.11 = (bf16[64,4736]{1,0:T(8,128)(2,1)S(1)}, bf16[64,4736]{1,0:T(8,128)(2,1)S(1)}, u32[]{:S(2)}, u32[]{:S(2)}) collective-permute-start(bf16[64,4736]{1,0:T(8,128)(2,1)S(1)} %pad_maximum_fusion.16), channel_id=1, source_target_pairs={{0,0},{1,2},{2,1},{3,3},{4,4},{5,6},{6,5},{7,7},{8,8},{9,10},{10,9... | collective-permute-start | bytes 1818632 | tf_op jit(solution)/shard_map/ppermute | solution.py:341
  22.7 534.7 %reduce-scatter.2.cloned.1.call-start = ((), (), s32[]{:S(2)}) async-start(), calls=%async_computation.2 | async-start | bytes 9191424 | tf_op jit(solution)/shard_map/reduce_scatter | solution.py:639
  24.0 3.6 collective-permute-start
  28.1 5.2 collective-permute-start.1
  31.5 12.8 %collective-permute-start.2 = (bf16[64,802]{1,0:T(8,128)(2,1)S(1)}, bf16[64,802]{1,0:T(8,128)(2,1)S(1)}, u32[]{:S(2)}, u32[]{:S(2)}) collective-permute-start(bf16[64,802]{1,0:T(8,128)(2,1)S(1)} %concatenate.61), channel_id=1, source_target_pairs={{16,0},{24,8},{0,16},{8,24},{17,1},{25,9},{1,17},{9,25},{18,2},{26... | collective-permute-start | bytes 307976 | tf_op jit(solution)/shard_map/ppermute | solution.py:346
  31.6 12.7 %collective-permute-start.3 = (bf16[64,802]{1,0:T(8,128)(2,1)S(1)}, bf16[64,802]{1,0:T(8,128)(2,1)S(1)}, u32[]{:S(2)}, u32[]{:S(2)}) collective-permute-start(bf16[64,802]{1,0:T(8,128)(2,1)S(1)} %concatenate.61), channel_id=1, source_target_pairs={{24,0},{0,8},{8,16},{16,24},{25,1},{1,9},{9,17},{17,25},{26,2},{2,... | collective-permute-start | bytes 307976 | tf_op jit(solution)/shard_map/ppermute | solution.py:346
  45.3 15.2 %copy-start.51 = (s32[16]{0:T(128)S(1)}, s32[16]{0:T(128)}, u32[]{:S(2)}) copy-start(s32[16]{0:T(128)} %param.25) | copy-start | bytes 196
  45.3 16.5 %copy-start.12 = (bf16[8,128,1024]{2,1,0:T(8,128)(2,1)S(1)}, bf16[8,128,1024]{2,1,0:T(8,128)(2,1)}, u32[]{:S(2)}) copy-start(bf16[8,128,1024]{2,1,0:T(8,128)(2,1)} %param.22) | copy-start | bytes 6291460
  45.3 7.9 %collective-permute-start.4 = (bf16[4,64,802]{2,1,0:T(8,128)(2,1)S(1)}, bf16[4,64,802]{2,1,0:T(8,128)(2,1)S(1)}, u32[]{:S(2)}, u32[]{:S(2)}) collective-permute-start(bf16[4,64,802]{2,1,0:T(8,128)(2,1)S(1)} %constant_dynamic-slice_fusion), channel_id=1, source_target_pairs={{0,4},{4,0},{1,5},{5,1},{2,6},{6,2},{3,7},{7,3},{8,12},{12,8},{9,1... | collective-permute-start | bytes 1231880 | tf_op jit(solution)/shard_map/ppermute | solution.py:337
  55.3 7.6 %collective-permute-start.5 = (bf16[2,4,64,802]{3,2,1,0:T(8,128)(2,1)}, bf16[2,4,64,802]{3,2,1,0:T(8,128)(2,1)}, u32[]{:S(2)}, u32[]{:S(2)}) collective-permute-start(bf16[2,4,64,802]{3,2,1,0:T(8,128)(2,1)} %pad_maximum_fusion.11), channel_id=1, source_target_pairs={{0,2},{2,0},{1,3},{3,1},{4,6},{6,4},{5,7},{7,5},{8,10},{10,8},{9,1... | collective-permute-start | bytes 2463752 | tf_op jit(solution)/shard_map/ppermute | solution.py:337
  75.5 11.5 %collective-permute-start.6 = (bf16[2,320,128]{2,1,0:T(8,128)(2,1)S(1)}, bf16[2,320,128]{2,1,0:T(8,128)(2,1)S(1)}, u32[]{:S(2)}, u32[]{:S(2)}) collective-permute-start(bf16[2,320,128]{2,1,0:T(8,128)(2,1)S(1)} %get-tuple-element.276), channel_id=1, source_target_pairs={{8,0},{16,8},{24,16},{0,24},{9,1},{17,9},{25,17},{1,25},{10,2},{18... | collective-permute-start | bytes 491528 | tf_op jit(solution)/shard_map/ppermute | solution.py:346
  76.6 29.4 %collective-permute-start.7 = (bf16[2,320,128]{2,1,0:T(8,128)(2,1)S(1)}, bf16[2,320,128]{2,1,0:T(8,128)(2,1)S(1)}, u32[]{:S(2)}, u32[]{:S(2)}) collective-permute-start(bf16[2,320,128]{2,1,0:T(8,128)(2,1)S(1)} %get-tuple-element.276), channel_id=1, source_target_pairs={{16,0},{24,8},{0,16},{8,24},{17,1},{25,9},{1,17},{9,25},{18,2},{26... | collective-permute-start | bytes 491528 | tf_op jit(solution)/shard_map/ppermute | solution.py:346
  82.3 23.7 %collective-permute-start.8 = (bf16[2,320,128]{2,1,0:T(8,128)(2,1)S(1)}, bf16[2,320,128]{2,1,0:T(8,128)(2,1)S(1)}, u32[]{:S(2)}, u32[]{:S(2)}) collective-permute-start(bf16[2,320,128]{2,1,0:T(8,128)(2,1)S(1)} %get-tuple-element.276), channel_id=1, source_target_pairs={{24,0},{0,8},{8,16},{16,24},{25,1},{1,9},{9,17},{17,25},{26,2},{2,... | collective-permute-start | bytes 491528 | tf_op jit(solution)/shard_map/ppermute | solution.py:346
  106.0 29.4 %collective-permute-start.9 = (bf16[2,320,512]{2,1,0:T(8,128)(2,1)S(1)}, bf16[2,320,512]{2,1,0:T(8,128)(2,1)S(1)}, u32[]{:S(2)}, u32[]{:S(2)}) collective-permute-start(bf16[2,320,512]{2,1,0:T(8,128)(2,1)S(1)} %pad_maximum_fusion.14), channel_id=1, source_target_pairs={{4,0},{0,4},{5,1},{1,5},{6,2},{2,6},{7,3},{3,7},{12,8},{8,12},{13,... | collective-permute-start | bytes 1966088 | tf_op jit(solution)/shard_map/ppermute | solution.py:346
  107.5 31.1 %collective-permute-start.12 = (bf16[2,320,128]{2,1,0:T(8,128)(2,1)S(1)}, bf16[2,320,128]{2,1,0:T(8,128)(2,1)S(1)}, u32[]{:S(2)}, u32[]{:S(2)}) collective-permute-start(bf16[2,320,128]{2,1,0:T(8,128)(2,1)S(1)} %get-tuple-element.275), channel_id=1, source_target_pairs={{8,0},{16,8},{24,16},{0,24},{9,1},{17,9},{25,17},{1,25},{10,2},{18... | collective-permute-start | bytes 491528 | tf_op jit(solution)/shard_map/ppermute | solution.py:346
  107.6 31.0 %collective-permute-start.13 = (bf16[2,320,128]{2,1,0:T(8,128)(2,1)S(1)}, bf16[2,320,128]{2,1,0:T(8,128)(2,1)S(1)}, u32[]{:S(2)}, u32[]{:S(2)}) collective-permute-start(bf16[2,320,128]{2,1,0:T(8,128)(2,1)S(1)} %get-tuple-element.275), channel_id=1, source_target_pairs={{16,0},{24,8},{0,16},{8,24},{17,1},{25,9},{1,17},{9,25},{18,2},{26... | collective-permute-start | bytes 491528 | tf_op jit(solution)/shard_map/ppermute | solution.py:346
  107.7 30.9 %collective-permute-start.14 = (bf16[2,320,128]{2,1,0:T(8,128)(2,1)S(1)}, bf16[2,320,128]{2,1,0:T(8,128)(2,1)S(1)}, u32[]{:S(2)}, u32[]{:S(2)}) collective-permute-start(bf16[2,320,128]{2,1,0:T(8,128)(2,1)S(1)} %get-tuple-element.275), channel_id=1, source_target_pairs={{24,0},{0,8},{8,16},{16,24},{25,1},{1,9},{9,17},{17,25},{26,2},{2,... | collective-permute-start | bytes 491528 | tf_op jit(solution)/shard_map/ppermute | solution.py:346
  136.6 37.3 %copy-start.46 = (bf16[2,320,2048]{2,1,0:T(8,128)(2,1)S(1)}, bf16[2,320,2048]{2,1,0:T(8,128)(2,1)}, u32[]{:S(2)}) copy-start(bf16[2,320,2048]{2,1,0:T(8,128)(2,1)} %get-tuple-element.262) | copy-start | bytes 7864324
  136.6 37.3 %collective-permute-start.10 = (bf16[2,320,1024]{2,1,0:T(8,128)(2,1)}, bf16[2,320,1024]{2,1,0:T(8,128)(2,1)S(1)}, u32[]{:S(2)}, u32[]{:S(2)}) collective-permute-start(bf16[2,320,1024]{2,1,0:T(8,128)(2,1)} %get-tuple-element.261), channel_id=1, source_target_pairs={{0,2},{2,0},{1,3},{3,1},{4,6},{6,4},{5,7},{7,5},{8,10},{10,8},{9,1... | collective-permute-start | bytes 3932168 | tf_op jit(solution)/shard_map/ppermute | solution.py:337
  138.7 31.4 %collective-permute-start.15 = (bf16[2,320,512]{2,1,0:T(8,128)(2,1)S(1)}, bf16[2,320,512]{2,1,0:T(8,128)(2,1)S(1)}, u32[]{:S(2)}, u32[]{:S(2)}) collective-permute-start(bf16[2,320,512]{2,1,0:T(8,128)(2,1)S(1)} %pad_maximum_fusion.15), channel_id=1, source_target_pairs={{4,0},{0,4},{5,1},{1,5},{6,2},{2,6},{7,3},{3,7},{12,8},{8,12},{13,... | collective-permute-start | bytes 1966088 | tf_op jit(solution)/shard_map/ppermute | solution.py:346
  172.3 28.7 %collective-permute-start.16 = (bf16[2,320,1024]{2,1,0:T(8,128)(2,1)}, bf16[2,320,1024]{2,1,0:T(8,128)(2,1)S(1)}, u32[]{:S(2)}, u32[]{:S(2)}) collective-permute-start(bf16[2,320,1024]{2,1,0:T(8,128)(2,1)} %copy-done.45), channel_id=1, source_target_pairs={{0,2},{2,0},{1,3},{3,1},{4,6},{6,4},{5,7},{7,5},{8,10},{10,8},{9,1... | collective-permute-start | bytes 3932168 | tf_op jit(solution)/shard_map/ppermute | solution.py:337
  198.8 25.8 %collective-permute-start.17 = (bf16[1024,512]{1,0:T(8,128)(2,1)}, bf16[1024,512]{1,0:T(8,128)(2,1)}, u32[]{:S(2)}, u32[]{:S(2)}) collective-permute-start(bf16[1024,512]{1,0:T(8,128)(2,1)} %slice.170), channel_id=1, source_target_pairs={{0,2},{2,0},{1,3},{3,1},{4,6},{6,4},{5,7},{7,5},{8,10},{10,8},{9,1... | collective-permute-start | bytes 3145736 | tf_op jit(solution)/shard_map/ppermute | solution.py:337
  200.6 28.0 %collective-permute-start.19 = (bf16[512,1024]{1,0:T(8,128)(2,1)}, bf16[512,1024]{1,0:T(8,128)(2,1)}, u32[]{:S(2)}, u32[]{:S(2)}) collective-permute-start(bf16[512,1024]{1,0:T(8,128)(2,1)} %bitcast.44), channel_id=1, source_target_pairs={{0,2},{2,0},{1,3},{3,1},{4,6},{6,4},{5,7},{7,5},{8,10},{10,8},{9,1... | collective-permute-start | bytes 3145736 | tf_op jit(solution)/shard_map/ppermute | solution.py:337
  228.2 62.4 %copy-start = (f32[4,128,1024]{2,1,0:T(8,128)}, f32[4,128,1024]{2,1,0:T(8,128)S(1)}, u32[]{:S(2)}) copy-start(f32[4,128,1024]{2,1,0:T(8,128)S(1)} %get-tuple-element.298) | copy-start | bytes 6291460
  228.4 2.7 collective-permute-start.18
  249.5 24.8 %copy-start.9 = (f32[1024,1024]{1,0:T(8,128)}, f32[1024,1024]{1,0:T(8,128)S(1)}, u32[]{:S(2)}) copy-start(f32[1024,1024]{1,0:T(8,128)S(1)} %fusion.3) | copy-start | bytes 12582916
  274.2 14.2 %collective-permute-start.20 = (bf16[512,1024]{1,0:T(8,128)(2,1)}, bf16[512,1024]{1,0:T(8,128)(2,1)}, u32[]{:S(2)}, u32[]{:S(2)}) collective-permute-start(bf16[512,1024]{1,0:T(8,128)(2,1)} %slice.311), channel_id=1, source_target_pairs={{0,2},{2,0},{1,3},{3,1},{4,6},{6,4},{5,7},{7,5},{8,10},{10,8},{9,1... | collective-permute-start | bytes 3145736 | tf_op jit(solution)/shard_map/ppermute | solution.py:337
  275.4 15.9 %collective-permute-start.23 = (bf16[512,1024]{1,0:T(8,128)(2,1)}, bf16[512,1024]{1,0:T(8,128)(2,1)}, u32[]{:S(2)}, u32[]{:S(2)}) collective-permute-start(bf16[512,1024]{1,0:T(8,128)(2,1)} %slice.310), channel_id=1, source_target_pairs={{0,2},{2,0},{1,3},{3,1},{4,6},{6,4},{5,7},{7,5},{8,10},{10,8},{9,1... | collective-permute-start | bytes 3145736 | tf_op jit(solution)/shard_map/ppermute | solution.py:337
  300.5 35.6 %collective-permute-start.22 = (bf16[1024,512]{1,0:T(8,128)(2,1)}, bf16[1024,512]{1,0:T(8,128)(2,1)}, u32[]{:S(2)}, u32[]{:S(2)}) collective-permute-start(bf16[1024,512]{1,0:T(8,128)(2,1)} %bitcast_convert_fusion.1), channel_id=1, source_target_pairs={{0,2},{2,0},{1,3},{3,1},{4,6},{6,4},{5,7},{7,5},{8,10},{10,8},{9,1... | collective-permute-start | bytes 3145736 | tf_op jit(solution)/shard_map/ppermute | solution.py:337
  333.4 4.9 collective-permute-start.21
  341.2 21.5 %collective-permute-start.25 = (bf16[4,2,64,512]{3,2,1,0:T(8,128)(2,1)}, bf16[4,2,64,512]{3,2,1,0:T(8,128)(2,1)}, u32[]{:S(2)}, u32[]{:S(2)}) collective-permute-start(bf16[4,2,64,512]{3,2,1,0:T(8,128)(2,1)} %dynamic-slice_bitcast_fusion), channel_id=1, source_target_pairs={{0,4},{4,0},{1,5},{5,1},{2,6},{6,2},{3,7},{7,3},{8,12},{12,8},{9,1... | collective-permute-start | bytes 1572872 | tf_op jit(solution)/shard_map/ppermute | solution.py:351
  342.9 22.0 %collective-permute-start.29 = (bf16[2,128,1024]{2,1,0:T(8,128)(2,1)}, bf16[2,128,1024]{2,1,0:T(8,128)(2,1)}, u32[]{:S(2)}, u32[]{:S(2)}) collective-permute-start(bf16[2,128,1024]{2,1,0:T(8,128)(2,1)} %get-tuple-element.78), channel_id=1, source_target_pairs={{0,1},{1,0},{2,3},{3,2},{4,5},{5,4},{6,7},{7,6},{8,9},{9,8},{10,11... | collective-permute-start | bytes 1572872 | tf_op jit(solution)/shard_map/ppermute | solution.py:337
  344.3 34.8 %collective-permute-start.24 = (bf16[4,2,320,128]{3,2,1,0:T(8,128)(2,1)}, bf16[4,2,320,128]{3,2,1,0:T(8,128)(2,1)}, u32[]{:S(2)}, u32[]{:S(2)}) collective-permute-start(bf16[4,2,320,128]{3,2,1,0:T(8,128)(2,1)} %slice.181), channel_id=1, source_target_pairs={{0,4},{4,0},{1,5},{5,1},{2,6},{6,2},{3,7},{7,3},{8,12},{12,8},{9,1... | collective-permute-start | bytes 1966088 | tf_op jit(solution)/shard_map/ppermute | solution.py:351
  362.3 39.9 %collective-permute-start.30 = (bf16[8,1,320,128]{3,2,1,0:T(8,128)(2,1)}, bf16[8,1,320,128]{3,2,1,0:T(8,128)(2,1)}, u32[]{:S(2)}, u32[]{:S(2)}) collective-permute-start(bf16[8,1,320,128]{3,2,1,0:T(8,128)(2,1)} %get-tuple-element.84), channel_id=1, source_target_pairs={{0,2},{2,0},{1,3},{3,1},{4,6},{6,4},{5,7},{7,5},{8,10},{10,8},{9,1... | collective-permute-start | bytes 1966088 | tf_op jit(solution)/shard_map/ppermute | solution.py:337
  381.2 18.8 %copy-start.17 = (bf16[4,2,64,512]{3,2,1,0:T(8,128)(2,1)S(1)}, bf16[4,2,64,512]{3,2,1,0:T(8,128)(2,1)}, u32[]{:S(2)}) copy-start(bf16[4,2,64,512]{3,2,1,0:T(8,128)(2,1)} %fusion.21) | copy-start | bytes 1572868
  381.2 90.5 %collective-permute-start.36 = (bf16[2,128,1024]{2,1,0:T(8,128)(2,1)}, bf16[2,128,1024]{2,1,0:T(8,128)(2,1)}, u32[]{:S(2)}, u32[]{:S(2)}) collective-permute-start(bf16[2,128,1024]{2,1,0:T(8,128)(2,1)} %get-tuple-element.90), channel_id=1, source_target_pairs={{0,1},{1,0},{2,3},{3,2},{4,5},{5,4},{6,7},{7,6},{8,9},{9,8},{10,11... | collective-permute-start | bytes 1572872 | tf_op jit(solution)/shard_map/ppermute | solution.py:337
  399.0 44.4 %collective-permute-start.31 = (bf16[8,1,320,128]{3,2,1,0:T(8,128)(2,1)}, bf16[8,1,320,128]{3,2,1,0:T(8,128)(2,1)}, u32[]{:S(2)}, u32[]{:S(2)}) collective-permute-start(bf16[8,1,320,128]{3,2,1,0:T(8,128)(2,1)} %get-tuple-element.87), channel_id=1, source_target_pairs={{0,2},{2,0},{1,3},{3,1},{4,6},{6,4},{5,7},{7,5},{8,10},{10,8},{9,1... | collective-permute-start | bytes 1966088 | tf_op jit(solution)/shard_map/ppermute | solution.py:337
  400.0 6.9 %collective-permute-start.45 = (bf16[2,64,512]{2,1,0:T(8,128)(2,1)S(1)}, bf16[2,64,512]{2,1,0:T(8,128)(2,1)S(1)}, u32[]{:S(2)}, u32[]{:S(2)}) collective-permute-start(bf16[2,64,512]{2,1,0:T(8,128)(2,1)S(1)} %get-tuple-element.263), channel_id=1, source_target_pairs={{0,8},{8,16},{16,24},{24,0},{1,9},{9,17},{17,25},{25,1},{2,10},{10... | collective-permute-start | bytes 393224 | tf_op jit(solution)/shard_map/ppermute | solution.py:351
  400.4 11.4 %collective-permute-start.46 = (bf16[2,64,512]{2,1,0:T(8,128)(2,1)S(1)}, bf16[2,64,512]{2,1,0:T(8,128)(2,1)S(1)}, u32[]{:S(2)}, u32[]{:S(2)}) collective-permute-start(bf16[2,64,512]{2,1,0:T(8,128)(2,1)S(1)} %get-tuple-element.265), channel_id=1, source_target_pairs={{0,16},{8,24},{16,0},{24,8},{1,17},{9,25},{17,1},{25,9},{2,18},{10... | collective-permute-start | bytes 393224 | tf_op jit(solution)/shard_map/ppermute | solution.py:351
  402.2 10.4 %collective-permute-start.47 = (bf16[2,64,512]{2,1,0:T(8,128)(2,1)S(1)}, bf16[2,64,512]{2,1,0:T(8,128)(2,1)S(1)}, u32[]{:S(2)}, u32[]{:S(2)}) collective-permute-start(bf16[2,64,512]{2,1,0:T(8,128)(2,1)S(1)} %get-tuple-element.264), channel_id=1, source_target_pairs={{0,24},{8,0},{16,8},{24,16},{1,25},{9,1},{17,9},{25,17},{2,26},{10... | collective-permute-start | bytes 393224 | tf_op jit(solution)/shard_map/ppermute | solution.py:351
  406.9 9.7 %collective-permute-start.26 = (bf16[1,2,320,128]{3,2,1,0:T(8,128)(2,1)S(1)}, bf16[1,2,320,128]{3,2,1,0:T(8,128)(2,1)S(1)}, u32[]{:S(2)}, u32[]{:S(2)}) collective-permute-start(bf16[1,2,320,128]{3,2,1,0:T(8,128)(2,1)S(1)} %get-tuple-element.256), channel_id=1, source_target_pairs={{0,8},{8,16},{16,24},{24,0},{1,9},{9,17},{17,25},{25,1},{2,10},{10... | collective-permute-start | bytes 491528 | tf_op jit(solution)/shard_map/ppermute | solution.py:351
  411.8 23.9 %collective-permute-start.27 = (bf16[1,2,320,128]{3,2,1,0:T(8,128)(2,1)S(1)}, bf16[1,2,320,128]{3,2,1,0:T(8,128)(2,1)S(1)}, u32[]{:S(2)}, u32[]{:S(2)}) collective-permute-start(bf16[1,2,320,128]{3,2,1,0:T(8,128)(2,1)S(1)} %get-tuple-element.258), channel_id=1, source_target_pairs={{0,16},{8,24},{16,0},{24,8},{1,17},{9,25},{17,1},{25,9},{2,18},{10... | collective-permute-start | bytes 491528 | tf_op jit(solution)/shard_map/ppermute | solution.py:351
  412.6 23.1 %collective-permute-start.28 = (bf16[1,2,320,128]{3,2,1,0:T(8,128)(2,1)S(1)}, bf16[1,2,320,128]{3,2,1,0:T(8,128)(2,1)S(1)}, u32[]{:S(2)}, u32[]{:S(2)}) collective-permute-start(bf16[1,2,320,128]{3,2,1,0:T(8,128)(2,1)S(1)} %get-tuple-element.257), channel_id=1, source_target_pairs={{0,24},{8,0},{16,8},{24,16},{1,25},{9,1},{17,9},{25,17},{2,26},{10... | collective-permute-start | bytes 491528 | tf_op jit(solution)/shard_map/ppermute | solution.py:351
  416.6 36.5 %collective-permute-start.48 = (bf16[64,512]{1,0:T(8,128)(2,1)S(1)}, bf16[64,512]{1,0:T(8,128)(2,1)S(1)}, u32[]{:S(2)}, u32[]{:S(2)}) collective-permute-start(bf16[64,512]{1,0:T(8,128)(2,1)S(1)} %dynamic-slice_bitcast_fusion.8), channel_id=1, source_target_pairs={{0,1},{1,0},{2,3},{3,2},{4,5},{5,4},{6,7},{7,6},{8,9},{9,8},{10,11... | collective-permute-start | bytes 196616 | tf_op jit(solution)/shard_map/ppermute | solution.py:351
  444.8 19.6 %collective-permute-start.32 = (bf16[4,2,320,128]{3,2,1,0:T(8,128)(2,1)S(1)}, bf16[4,2,320,128]{3,2,1,0:T(8,128)(2,1)S(1)}, u32[]{:S(2)}, u32[]{:S(2)}) collective-permute-start(bf16[4,2,320,128]{3,2,1,0:T(8,128)(2,1)S(1)} %pad_maximum_fusion.13), channel_id=1, source_target_pairs={{0,4},{4,0},{1,5},{5,1},{2,6},{6,2},{3,7},{7,3},{8,12},{12,8},{9,1... | collective-permute-start | bytes 1966088 | tf_op jit(solution)/shard_map/ppermute | solution.py:351
  453.8 54.3 %collective-permute-start.49 = (bf16[64,512]{1,0:T(8,128)(2,1)}, bf16[64,512]{1,0:T(8,128)(2,1)}, u32[]{:S(2)}, u32[]{:S(2)}) collective-permute-start(bf16[64,512]{1,0:T(8,128)(2,1)} %fusion.42), channel_id=1, source_target_pairs={{0,0},{1,2},{2,1},{3,3},{4,4},{5,6},{6,5},{7,7},{8,8},{9,10},{10,9... | collective-permute-start | bytes 196616 | tf_op jit(solution)/shard_map/ppermute | solution.py:341
  464.7 9.0 %collective-permute-start.33 = (bf16[1,2,320,128]{3,2,1,0:T(8,128)(2,1)S(1)}, bf16[1,2,320,128]{3,2,1,0:T(8,128)(2,1)S(1)}, u32[]{:S(2)}, u32[]{:S(2)}) collective-permute-start(bf16[1,2,320,128]{3,2,1,0:T(8,128)(2,1)S(1)} %get-tuple-element.253), channel_id=1, source_target_pairs={{0,8},{8,16},{16,24},{24,0},{1,9},{9,17},{17,25},{25,1},{2,10},{10... | collective-permute-start | bytes 491528 | tf_op jit(solution)/shard_map/ppermute | solution.py:351
  469.5 20.5 %collective-permute-start.34 = (bf16[1,2,320,128]{3,2,1,0:T(8,128)(2,1)S(1)}, bf16[1,2,320,128]{3,2,1,0:T(8,128)(2,1)S(1)}, u32[]{:S(2)}, u32[]{:S(2)}) collective-permute-start(bf16[1,2,320,128]{3,2,1,0:T(8,128)(2,1)S(1)} %get-tuple-element.255), channel_id=1, source_target_pairs={{0,16},{8,24},{16,0},{24,8},{1,17},{9,25},{17,1},{25,9},{2,18},{10... | collective-permute-start | bytes 491528 | tf_op jit(solution)/shard_map/ppermute | solution.py:351
  470.9 19.1 %collective-permute-start.35 = (bf16[1,2,320,128]{3,2,1,0:T(8,128)(2,1)S(1)}, bf16[1,2,320,128]{3,2,1,0:T(8,128)(2,1)S(1)}, u32[]{:S(2)}, u32[]{:S(2)}) collective-permute-start(bf16[1,2,320,128]{3,2,1,0:T(8,128)(2,1)S(1)} %get-tuple-element.254), channel_id=1, source_target_pairs={{0,24},{8,0},{16,8},{24,16},{1,25},{9,1},{17,9},{25,17},{2,26},{10... | collective-permute-start | bytes 491528 | tf_op jit(solution)/shard_map/ppermute | solution.py:351
  505.9 8.8 %collective-permute-start.37 = (bf16[4,2,64,802]{3,2,1,0:T(8,128)(2,1)}, bf16[4,2,64,802]{3,2,1,0:T(8,128)(2,1)S(1)}, u32[]{:S(2)}, u32[]{:S(2)}) collective-permute-start(bf16[4,2,64,802]{3,2,1,0:T(8,128)(2,1)} %get-tuple-element.94), channel_id=1, source_target_pairs={{0,2},{2,0},{1,3},{3,1},{4,6},{6,4},{5,7},{7,5},{8,10},{10,8},{9,1... | collective-permute-start | bytes 2463752 | tf_op jit(solution)/shard_map/ppermute | solution.py:337
  511.7 13.4 %collective-permute-start.43 = (bf16[2,128,1024]{2,1,0:T(8,128)(2,1)S(1)}, bf16[2,128,1024]{2,1,0:T(8,128)(2,1)S(1)}, u32[]{:S(2)}, u32[]{:S(2)}) collective-permute-start(bf16[2,128,1024]{2,1,0:T(8,128)(2,1)S(1)} %fusion.19), channel_id=1, source_target_pairs={{0,1},{1,0},{2,3},{3,2},{4,5},{5,4},{6,7},{7,6},{8,9},{9,8},{10,11... | collective-permute-start | bytes 1572872 | tf_op jit(solution)/shard_map/ppermute | solution.py:337
  513.1 23.3 %collective-permute-start.39 = (bf16[2,128,1024]{2,1,0:T(8,128)(2,1)S(1)}, bf16[2,128,1024]{2,1,0:T(8,128)(2,1)S(1)}, u32[]{:S(2)}, u32[]{:S(2)}) collective-permute-start(bf16[2,128,1024]{2,1,0:T(8,128)(2,1)S(1)} %copy-done.16), channel_id=1, source_target_pairs={{0,1},{1,0},{2,3},{3,2},{4,5},{5,4},{6,7},{7,6},{8,9},{9,8},{10,11... | collective-permute-start | bytes 1572872 | tf_op jit(solution)/shard_map/ppermute | solution.py:337
  515.0 21.6 %collective-permute-start.38 = (bf16[4,64,802]{2,1,0:T(8,128)(2,1)S(1)}, bf16[4,64,802]{2,1,0:T(8,128)(2,1)S(1)}, u32[]{:S(2)}, u32[]{:S(2)}) collective-permute-start(bf16[4,64,802]{2,1,0:T(8,128)(2,1)S(1)} %dynamic-slice_bitcast_fusion.1), channel_id=1, source_target_pairs={{0,4},{4,0},{1,5},{5,1},{2,6},{6,2},{3,7},{7,3},{8,12},{12,8},{9,1... | collective-permute-start | bytes 1231880 | tf_op jit(solution)/shard_map/ppermute | solution.py:351
  536.8 10.4 %collective-permute-start.40 = (bf16[64,802]{1,0:T(8,128)(2,1)S(1)}, bf16[64,802]{1,0:T(8,128)(2,1)S(1)}, u32[]{:S(2)}, u32[]{:S(2)}) collective-permute-start(bf16[64,802]{1,0:T(8,128)(2,1)S(1)} %get-tuple-element.266), channel_id=1, source_target_pairs={{0,8},{8,16},{16,24},{24,0},{1,9},{9,17},{17,25},{25,1},{2,10},{10... | collective-permute-start | bytes 307976 | tf_op jit(solution)/shard_map/ppermute | solution.py:351
  542.8 10.1 %collective-permute-start.41 = (bf16[64,802]{1,0:T(8,128)(2,1)S(1)}, bf16[64,802]{1,0:T(8,128)(2,1)S(1)}, u32[]{:S(2)}, u32[]{:S(2)}) collective-permute-start(bf16[64,802]{1,0:T(8,128)(2,1)S(1)} %get-tuple-element.268), channel_id=1, source_target_pairs={{0,16},{8,24},{16,0},{24,8},{1,17},{9,25},{17,1},{25,9},{2,18},{10... | collective-permute-start | bytes 307976 | tf_op jit(solution)/shard_map/ppermute | solution.py:351
  544.6 8.2 %collective-permute-start.42 = (bf16[64,802]{1,0:T(8,128)(2,1)S(1)}, bf16[64,802]{1,0:T(8,128)(2,1)S(1)}, u32[]{:S(2)}, u32[]{:S(2)}) collective-permute-start(bf16[64,802]{1,0:T(8,128)(2,1)S(1)} %get-tuple-element.267), channel_id=1, source_target_pairs={{0,24},{8,0},{16,8},{24,16},{1,25},{9,1},{17,9},{25,17},{2,26},{10... | collective-permute-start | bytes 307976 | tf_op jit(solution)/shard_map/ppermute | solution.py:351
  553.0 4.2 collective-permute-start.44
  554.4 10.2 %copy-start.37 = (f32[64,640]{1,0:T(8,128)S(1)}, f32[64,640]{1,0:T(8,128)}, u32[]{:S(2)}) copy-start(f32[64,640]{1,0:T(8,128)} %param.29) | copy-start | bytes 491524
  554.4 10.2 %copy-start.38 = (f32[64,640]{1,0:T(8,128)S(1)}, f32[64,640]{1,0:T(8,128)}, u32[]{:S(2)}) copy-start(f32[64,640]{1,0:T(8,128)} %param.30) | copy-start | bytes 491524
  554.4 10.2 %copy-start.39 = (f32[64,640]{1,0:T(8,128)S(1)}, f32[64,640]{1,0:T(8,128)}, u32[]{:S(2)}) copy-start(f32[64,640]{1,0:T(8,128)} %param.31) | copy-start | bytes 491524
  557.4 11.7 %collective-permute-start.50 = (bf16[64,4224]{1,0:T(8,128)(2,1)}, bf16[64,4224]{1,0:T(8,128)(2,1)S(1)}, u32[]{:S(2)}, u32[]{:S(2)}) collective-permute-start(bf16[64,4224]{1,0:T(8,128)(2,1)} %reduce-scatter.2.cloned.1.call-done), channel_id=1, source_target_pairs={{0,0},{1,2},{2,1},{3,3},{4,4},{5,6},{6,5},{7,7},{8,8},{9,10},{10,9... | collective-permute-start | bytes 1622024 | tf_op jit(solution)/shard_map/ppermute | solution.py:341
  (49 other events, 200.1 us)
Sparse Core Ops, SparseCore 0:
  22.8 166.2 all-gather.1
  298.8 198.4 reduce-scatter.1

commit v7 on v6

--- a/solution.py
+++ b/solution.py
@@ -631,16 +631,15 @@
     else:
         out_t_grad = out_grad_of(heads_low)
     if paired:
-        wide_grads = (gate_w_grad, up_w_grad, down_low)
+        wide_grads = (gate_w_grad, up_w_grad, down_low, out_t_grad)
         wide_grad = jnp.concatenate([grad.astype(BF) for grad in wide_grads], axis=1)
         wide_grad, heads_grad = lax.optimization_barrier((wide_grad, heads_grad))
-        na, nb = lax.axis_size("a"), lax.axis_size("b")
-        out_sum = out_t_grad.astype(BF).reshape(na, nb, 2, rows, o_cols)
         wide_sum = lax.psum_scatter(wide_grad, ("a", "b", "h"), scatter_dimension=0, tiled=True)
         wide_sum = turn_core_head(wide_sum).astype(F32)
         gate_sum = wide_sum[:, :f_cols]
         up_sum = wide_sum[:, f_cols : 2 * f_cols]
-        down_sum = wide_sum[:, 2 * f_cols :]
+        down_sum = wide_sum[:, 2 * f_cols : 3 * f_cols]
+        out_sum = wide_sum[:, 3 * f_cols :]
     else:
         wide_grads = (gate_w_grad, up_w_grad, down_low, out_t_grad)
         wide_sum = jnp.concatenate([grad.astype(BF) for grad in wide_grads], axis=1)
@@ -671,11 +670,9 @@
     own_grads = []
     if len(groups) > 1:
         query_grad, total = backward_call(0, 0, half, heads_grad)
-        heads_grad, total, out_sum, layer_parts[0] = lax.optimization_barrier(
-            (heads_grad, total, out_sum, layer_parts[0])
+        heads_grad, total, layer_parts[0] = lax.optimization_barrier(
+            (heads_grad, total, layer_parts[0])
         )
-        if paired:
-            out_sum = ordered_scatter(out_sum, "b", 1)
         query_grads.append([query_grad])
         total = scatter_axis(total, "b")
         own_grads.append(total)
@@ -685,8 +682,8 @@
     calls = []
     for i, size in enumerate(sizes):
         if i and last:
-            heads_grad, own_grads[0], out_sum, layer_parts[1] = lax.optimization_barrier(
-                (heads_grad, own_grads[0], out_sum, layer_parts[1])
+            heads_grad, own_grads[0], layer_parts[1] = lax.optimization_barrier(
+                (heads_grad, own_grads[0], layer_parts[1])
             )
         calls.append(backward_call(last, inner, size, heads_grad))
         inner += size
@@ -694,9 +691,6 @@
     layer_parts = [every_head(part, n_head) for part in layer_parts]
     own_grads.append(scatter_axis(jnp.concatenate([call[1] for call in calls], axis=1), "b"))
     own_grads = [scatter_axis(total, "a")[0] for total in own_grads]
-    if paired:
-        out_sum = ordered_scatter(ordered_scatter(out_sum, "a", 0), "h", 0)
-        out_sum = turn_core_head(out_sum).astype(F32)
     first_gain_grad = 0.0
     joints = []
     input_parts = []

time: 588 us -> 595 us (1.012)
  waiting for transfers between devices: 192 us -> 228 us
  starting transfers between devices: 85.5 us -> 64.8 us
    ppermute x20, waiting for transfers between devices: 30.7 us -> 73.5 us  [swap(): return lax.ppermute(block, axis, [(0, 1), (1, 0)])]
    ppermute x17 -> x12, starting transfers between devices: 35.8 us -> 18.3 us  [to_ahead(): lax.ppermute(block, axis, [(i, (i + distance) % size) for i in range(size)])]
    ppermute x3 -> x2, starting transfers between devices: 15.7 us -> 9 us  [turn_core_head(): return lax.ppermute(block, ('c', 'h'), [(0, 0), (1, 2), (2, 1), (3, 3)])]
    ppermute x17 -> x12, waiting for transfers between devices: 64.2 us -> 57.5 us  [to_ahead(): lax.ppermute(block, axis, [(i, (i + distance) % size) for i in range(size)])]
    unnamed x137 -> x127, local copies, waits for them, and re-layouts: 16.9 us -> 16.6 us
  transfers between devices with their start and end apart: 53 -> 47, of which waited for: 24 -> 24; matrix products, arithmetic and copies ran while one was open for 17% -> 18% of each run, Pallas kernels for 22% -> 22%
where the time goes in v7:
time: 595 us; the launch traced here: 589 us
  waiting for transfers between devices  228 us (38%)
  Pallas kernels  127 us (21%)
  matrix products  66.6 us (11%)
  starting transfers between devices  64.8 us (11%)
  other arithmetic  56.9 us (10%)
  local copies, waits for them, and re-layouts  28.2 us (5%)
  between operations  16.2 us (3%)
    ppermute x11, waiting for transfers between devices, from_ahead(): lax.ppermute(block, axis, [((i + distance) % size, i) for i in range(size)])  85.5 us
    ppermute x20, waiting for transfers between devices, swap(): return lax.ppermute(block, axis, [(0, 1), (1, 0)])  73.5 us
    pallas_call x3, Pallas kernels, attention_backward(): pl.pallas_call(backward_body, grid=(count, H // HB), in_specs=[pl.BlockSp...  68.6 us
    ppermute x12, waiting for transfers between devices, to_ahead(): lax.ppermute(block, axis, [(i, (i + distance) % size) for i in range(size)])  57.5 us
    pallas_call x2, Pallas kernels, attention_forward(): pl.pallas_call(forward_body, grid=(count, H // HB), in_specs=[pl.BlockSpe...  41.4 us
    ppermute x20, starting transfers between devices, swap(): return lax.ppermute(block, axis, [(0, 1), (1, 0)])  21.3 us
    ppermute x12, starting transfers between devices, to_ahead(): lax.ppermute(block, axis, [(i, (i + distance) % size) for i in range(size)])  18.3 us
    unnamed x127, local copies, waits for them, and re-layouts  16.6 us
  transfers between devices with their start and end apart: 47, of which 24 were waited for; matrix products, arithmetic and copies ran while one was open for 18% of the time, Pallas kernels for 22%

profile of v7, /device:TPU:1, one launch (start us, length us, event | category | flops | bytes accessed | tf_op | source)
XLA Modules:
  0.0 588.5 jit_solution(13953166396742249642)
XLA Ops:
  10.4 4.5 collective-permute-start.11
  15.0 7.7 %collective-permute-done.11 = bf16[64,4736]{1,0:T(8,128)(2,1)S(1)} collective-permute-done((bf16[64,4736]{1,0:T(8,128)(2,1)S(1)}, bf16[64,4736]{1,0:T(8,128)(2,1)S(1)}, u32[]{:S(2)}, u32[]{:S(2)}) %collective-permute-start.11) | collective-permute-done | bytes 606240 | tf_op jit(solution)/shard_map/ppermute | solution.py:341
  25.0 3.5 collective-permute-done
  29.0 3.4 collective-permute-start.1
  34.2 11.0 %collective-permute-done.2 = bf16[64,802]{1,0:T(8,128)(2,1)S(1)} collective-permute-done((bf16[64,802]{1,0:T(8,128)(2,1)S(1)}, bf16[64,802]{1,0:T(8,128)(2,1)S(1)}, u32[]{:S(2)}, u32[]{:S(2)}) %collective-permute-start.2) | collective-permute-done | bytes 102688 | tf_op jit(solution)/shard_map/ppermute | solution.py:346
  46.6 6.6 %collective-permute-done.4 = bf16[4,64,802]{2,1,0:T(8,128)(2,1)S(1)} collective-permute-done((bf16[4,64,802]{2,1,0:T(8,128)(2,1)S(1)}, bf16[4,64,802]{2,1,0:T(8,128)(2,1)S(1)}, u32[]{:S(2)}, u32[]{:S(2)}) %collective-permute-start.4) | collective-permute-done | bytes 410656 | tf_op jit(solution)/shard_map/ppermute | solution.py:337
  53.4 5.2 collective-permute-start.5
  66.2 1.6 convert_multiply_fusion
  67.8 2.4 convolution_bitcast_fusion.f_ref
  70.2 4.1 factor_prologue.1
  74.3 1.9 constant_dynamic-update-slice_fusion.15
  77.1 5.8 collective-permute-start.7
  84.4 4.9 collective-permute-done.6
  89.4 17.3 %collective-permute-done.7 = bf16[2,320,128]{2,1,0:T(8,128)(2,1)S(1)} collective-permute-done((bf16[2,320,128]{2,1,0:T(8,128)(2,1)S(1)}, bf16[2,320,128]{2,1,0:T(8,128)(2,1)S(1)}, u32[]{:S(2)}, u32[]{:S(2)}) %collective-permute-start.7) | collective-permute-done | bytes 163872 | tf_op jit(solution)/shard_map/ppermute | solution.py:346
  111.7 24.1 %collective-permute-done.9 = bf16[2,320,512]{2,1,0:T(8,128)(2,1)S(1)} collective-permute-done((bf16[2,320,512]{2,1,0:T(8,128)(2,1)S(1)}, bf16[2,320,512]{2,1,0:T(8,128)(2,1)S(1)}, u32[]{:S(2)}, u32[]{:S(2)}) %collective-permute-start.9) | collective-permute-done | bytes 655392 | tf_op jit(solution)/shard_map/ppermute | solution.py:346
  137.0 2.2 collective-permute-start.10
  143.3 27.0 %collective-permute-done.15 = bf16[2,320,512]{2,1,0:T(8,128)(2,1)S(1)} collective-permute-done((bf16[2,320,512]{2,1,0:T(8,128)(2,1)S(1)}, bf16[2,320,512]{2,1,0:T(8,128)(2,1)S(1)}, u32[]{:S(2)}, u32[]{:S(2)}) %collective-permute-start.15) | collective-permute-done | bytes 655392 | tf_op jit(solution)/shard_map/ppermute | solution.py:346
  175.0 20.6 %attention_forward.2 = (f32[2,128,1024]{2,1,0:T(8,128)}, f32[2,4,128,4]{3,2,1,0:T(8,128)}) custom-call(bf16[4,128,1024]{2,1,0:T(8,128)(2,1)} %get-tuple-element.59.q_ref, bf16[2,320,2048]{2,1,0:T(8,128)(2,1)} %copy-done.42, bf16[2,320,2048]{2,1,0:T(8,128)(2,1)} %copy-done.42, s32[1,2048]{1,0:T(1,128)} %bitcast.194, s32[128,1]{1,0:T(8,128)} %iota_add_fusion.qpos_ref), custom_call_target="tpu_custom_call" | custom-call | flops 2147483648 | bytes 2621440 | tf_op jit(solution)/shard_map/attention_forward/pallas_call | solution.py:219
  195.7 2.4 slice.173
  201.5 20.8 %attention_forward.3 = (f32[2,128,1024]{2,1,0:T(8,128)}, f32[2,4,128,4]{3,2,1,0:T(8,128)}) custom-call(bf16[4,128,1024]{2,1,0:T(8,128)(2,1)} %get-tuple-element.59.q_ref, bf16[2,320,2048]{2,1,0:T(8,128)(2,1)} %constant_dynamic-update-slice_fusion.16.b_ref.a_ref, bf16[2,320,2048]{2,1,0:T(8,128)(2,1)} %constant_dynamic-update-slice_fusion.16.b_ref.a_ref, ...), custom_call_target="tpu_custom_call" | custom-call | flops 2147483648 | bytes 2621440 | tf_op jit(solution)/shard_map/attention_forward/pallas_call | solution.py:219
  224.0 1.8 broadcast_select_fusion.1
  229.1 1.9 pad_maximum_fusion.2
  232.0 6.3 %fusion.11 = f32[1024,1408]{1,0:T(8,128)S(1)} fusion(bf16[1024,4736]{1,0:T(8,128)(2,1)} %all-gather.2.cloned.1.call-done, bf16[512,1024]{1,0:T(8,128)(2,1)} %collective-permute-done.18, bf16[512,1024]{1,0:T(8,128)(2,1)} %bitcast.43), kind=kOutput, calls=%fused_computation.23 | convolution fusion | flops 2956984320 | bytes 10747904 | tf_op jit(solution)/shard_map/dot_general | solution.py:595
  238.4 9.1 %multiply_convert_fusion.2 = (bf16[1024,1408]{1,0:T(8,128)(2,1)S(1)}, f32[1024,1408]{1,0:T(8,128)}) fusion(f32[1024,1408]{1,0:T(8,128)S(1)} %fusion.11, bf16[1024,4736]{1,0:T(8,128)(2,1)S(1)} %bitcast.191, bf16[512,1024]{1,0:T(8,128)(2,1)} %collective-permute-done.18, bf16[512,1024]{1,0:T(8,128)(2,1)} %bitcast.43), kind=kOutput, calls=%fused_computation.3 | convolution fusion | flops 2965635072 | bytes 19398656 | tf_op jit(solution)/shard_map/dot_general | solution.py:596
  247.6 3.4 fusion.3
  251.3 9.2 %multiply_convert_fusion.1 = (bf16[1024,1408]{1,0:T(8,128)(2,1)S(1)}, bf16[1024,1408]{1,0:T(8,128)(2,1)}) fusion(f32[1024,1408]{1,0:T(8,128)} %copy-done.48, f32[1024,1408]{1,0:T(8,128)} %get-tuple-element.293, bf16[1024,1024]{1,0:T(8,128)(2,1)S(1)} %pad_maximum_fusion.2, bf16[1024,4736]{1,0:T(8,128)(2,1)S(1)} %bitcast.191), kind=kOutput, calls=%fused_computation.2 | convolution fusion | flops 2971533312 | bytes 22282240 | tf_op jit(solution)/shard_map/dot_general | solution.py:606
  260.5 5.3 fusion.5
  265.7 5.4 fusion.16
  271.9 5.3 convolution_convert_fusion.1
  277.2 5.3 convolution_convert_fusion.2
  285.8 1.7 add_convert_fusion.1
  289.4 3.9 convolution_convert_fusion
  293.3 2.3 convolution_convert_fusion.3.do_ref
  296.4 5.5 pad_maximum_fusion
  301.9 32.9 %attention_backward.3 = (f32[2,128,1024]{2,1,0:T(8,128)}, bf16[8,2,320,128]{3,2,1,0:T(8,128)(2,1)}, bf16[8,2,320,128]{3,2,1,0:T(8,128)(2,1)}) custom-call(bf16[4,128,1024]{2,1,0:T(8,128)(2,1)} %get-tuple-element.59.q_ref, bf16[4,128,1024]{2,1,0:T(8,128)(2,1)} %convolution_convert_fusion.3.do_ref, f32[2,128,1024]{2,1,0:T(8,128)} %get-tuple-element.62.o_ref, ...), custom_call_target="tpu_custom_call" | custom-call | flops 5368709120 | bytes 5242880 | tf_op jit(solution)/shard_map/attention_backward/pallas_call | solution.py:309
  336.0 2.2 collective-permute-done.22
  341.2 17.7 %attention_backward.4 = (f32[1,128,1024]{2,1,0:T(8,128)}, bf16[8,1,320,128]{3,2,1,0:T(8,128)(2,1)}, bf16[8,1,320,128]{3,2,1,0:T(8,128)(2,1)}) custom-call(bf16[4,128,1024]{2,1,0:T(8,128)(2,1)} %get-tuple-element.59.q_ref, bf16[4,128,1024]{2,1,0:T(8,128)(2,1)} %convolution_convert_fusion.3.do_ref, f32[2,128,1024]{2,1,0:T(8,128)} %get-tuple-element.63.o_ref, ...), custom_call_target="tpu_custom_call" | custom-call | flops 2684354560 | bytes 2621440 | tf_op jit(solution)/shard_map/attention_backward/pallas_call | solution.py:309
  359.4 19.3 %collective-permute-done.28 = bf16[2,128,1024]{2,1,0:T(8,128)(2,1)} collective-permute-done((bf16[2,128,1024]{2,1,0:T(8,128)(2,1)}, bf16[2,128,1024]{2,1,0:T(8,128)(2,1)}, u32[]{:S(2)}, u32[]{:S(2)}) %collective-permute-start.28) | collective-permute-done | bytes 524320 | tf_op jit(solution)/shard_map/ppermute | solution.py:337
  381.0 2.1 add_convert_fusion.6
  383.1 18.0 %attention_backward.5 = (f32[1,128,1024]{2,1,0:T(8,128)}, bf16[8,1,320,128]{3,2,1,0:T(8,128)(2,1)}, bf16[8,1,320,128]{3,2,1,0:T(8,128)(2,1)}) custom-call(bf16[4,128,1024]{2,1,0:T(8,128)(2,1)} %get-tuple-element.59.q_ref, bf16[4,128,1024]{2,1,0:T(8,128)(2,1)} %convolution_convert_fusion.3.do_ref, f32[2,128,1024]{2,1,0:T(8,128)} %get-tuple-element.63.o_ref, ...), custom_call_target="tpu_custom_call" | custom-call | flops 2684354560 | bytes 2621440 | tf_op jit(solution)/shard_map/attention_backward/pallas_call | solution.py:309
  405.0 5.8 collective-permute-done.27
  410.7 10.3 %collective-permute-done.26 = bf16[1,2,320,128]{3,2,1,0:T(8,128)(2,1)S(1)} collective-permute-done((bf16[1,2,320,128]{3,2,1,0:T(8,128)(2,1)S(1)}, bf16[1,2,320,128]{3,2,1,0:T(8,128)(2,1)S(1)}, u32[]{:S(2)}, u32[]{:S(2)}) %collective-permute-start.26) | collective-permute-done | bytes 163872 | tf_op jit(solution)/shard_map/ppermute | solution.py:351
  421.8 3.7 factor_epilogue.3
  428.0 1.9 multiply_reduce_fusion.5
  431.0 20.4 %collective-permute-done.31 = bf16[4,2,320,128]{3,2,1,0:T(8,128)(2,1)S(1)} collective-permute-done((bf16[4,2,320,128]{3,2,1,0:T(8,128)(2,1)S(1)}, bf16[4,2,320,128]{3,2,1,0:T(8,128)(2,1)S(1)}, u32[]{:S(2)}, u32[]{:S(2)}) %collective-permute-start.31) | collective-permute-done | bytes 655392 | tf_op jit(solution)/shard_map/ppermute | solution.py:351
  451.6 4.0 collective-permute-start.34
  455.6 5.1 collective-permute-start.33
  460.7 1.6 collective-permute-start.32
  465.6 6.9 %collective-permute-done.33 = bf16[1,2,320,128]{3,2,1,0:T(8,128)(2,1)S(1)} collective-permute-done((bf16[1,2,320,128]{3,2,1,0:T(8,128)(2,1)S(1)}, bf16[1,2,320,128]{3,2,1,0:T(8,128)(2,1)S(1)}, u32[]{:S(2)}, u32[]{:S(2)}) %collective-permute-start.33) | collective-permute-done | bytes 163872 | tf_op jit(solution)/shard_map/ppermute | solution.py:351
  472.5 3.8 collective-permute-done.32
  477.1 2.8 factor_epilogue.5
  479.9 2.8 factor_epilogue.4
  483.7 3.8 multiply_reduce_fusion.3
  488.2 4.1 factor_grads.1
  492.2 7.0 %collective-permute-start.36 = (bf16[4,2,64,802]{3,2,1,0:T(8,128)(2,1)}, bf16[4,2,64,802]{3,2,1,0:T(8,128)(2,1)}, u32[]{:S(2)}, u32[]{:S(2)}) collective-permute-start(bf16[4,2,64,802]{3,2,1,0:T(8,128)(2,1)} %get-tuple-element.91), channel_id=1, source_target_pairs={{0,2},{2,0},{1,3},{3,1},{4,6},{6,4},{5,7},{7,5},{8,10},{10,8},{9,1... | collective-permute-start | bytes 2463752 | tf_op jit(solution)/shard_map/ppermute | solution.py:337
  499.4 1.9 fusion.19
  506.9 27.3 %collective-permute-done.42 = bf16[2,128,1024]{2,1,0:T(8,128)(2,1)S(1)} collective-permute-done((bf16[2,128,1024]{2,1,0:T(8,128)(2,1)S(1)}, bf16[2,128,1024]{2,1,0:T(8,128)(2,1)S(1)}, u32[]{:S(2)}, u32[]{:S(2)}) %collective-permute-start.42) | collective-permute-done | bytes 524320 | tf_op jit(solution)/shard_map/ppermute | solution.py:337
  534.1 13.3 %collective-permute-done.38 = bf16[2,128,1024]{2,1,0:T(8,128)(2,1)S(1)} collective-permute-done((bf16[2,128,1024]{2,1,0:T(8,128)(2,1)S(1)}, bf16[2,128,1024]{2,1,0:T(8,128)(2,1)S(1)}, u32[]{:S(2)}, u32[]{:S(2)}) %collective-permute-start.38) | collective-permute-done | bytes 524320 | tf_op jit(solution)/shard_map/ppermute | solution.py:337
  547.9 3.1 collective-permute-start.41
  553.0 8.1 %collective-permute-done.40 = bf16[64,802]{1,0:T(8,128)(2,1)S(1)} collective-permute-done((bf16[64,802]{1,0:T(8,128)(2,1)S(1)}, bf16[64,802]{1,0:T(8,128)(2,1)S(1)}, u32[]{:S(2)}, u32[]{:S(2)}) %collective-permute-start.40) | collective-permute-done | bytes 102688 | tf_op jit(solution)/shard_map/ppermute | solution.py:351
  562.0 2.6 bitcast_convert_fusion
  565.1 4.5 collective-permute-start.44
  573.4 4.2 collective-permute-done.44
  579.7 1.7 multiply_subtract_fusion
  (306 shorter events, 86.0 us)
Async XLA Ops:
  7.2 188.5 %all-gather.2.cloned.1.call-start = ((), (), s32[]{:S(2)}) async-start(), calls=%async_computation.1 | async-start | bytes 10305536 | tf_op jit(solution)/shard_map/all_gather | solution.py:528
  8.2 15.5 %copy-start.43 = (f32[2,64]{1,0:T(2,128)S(1)}, f32[2,64]{1,0:T(2,128)}, u32[]{:S(2)}) copy-start(f32[2,64]{1,0:T(2,128)} %param.41) | copy-start | bytes 1540
  8.2 15.6 %copy-start.37 = (f32[64,80]{1,0:T(8,128)S(1)}, f32[64,80]{1,0:T(8,128)}, u32[]{:S(2)}) copy-start(f32[64,80]{1,0:T(8,128)} %param.26) | copy-start | bytes 61444
  10.4 12.3 %collective-permute-start.11 = (bf16[64,4736]{1,0:T(8,128)(2,1)S(1)}, bf16[64,4736]{1,0:T(8,128)(2,1)S(1)}, u32[]{:S(2)}, u32[]{:S(2)}) collective-permute-start(bf16[64,4736]{1,0:T(8,128)(2,1)S(1)} %pad_maximum_fusion.16), channel_id=1, source_target_pairs={{0,0},{1,2},{2,1},{3,3},{4,4},{5,6},{6,5},{7,7},{8,8},{9,10},{10,9... | collective-permute-start | bytes 1818632 | tf_op jit(solution)/shard_map/ppermute | solution.py:341
  23.6 541.6 %reduce-scatter.2.cloned.1.call-start = ((), (), s32[]{:S(2)}) async-start(), calls=%async_computation.2 | async-start | bytes 10305536 | tf_op jit(solution)/shard_map/reduce_scatter | solution.py:637
  24.9 3.6 collective-permute-start
  29.0 5.2 collective-permute-start.1
  32.4 12.8 %collective-permute-start.2 = (bf16[64,802]{1,0:T(8,128)(2,1)S(1)}, bf16[64,802]{1,0:T(8,128)(2,1)S(1)}, u32[]{:S(2)}, u32[]{:S(2)}) collective-permute-start(bf16[64,802]{1,0:T(8,128)(2,1)S(1)} %concatenate.61), channel_id=1, source_target_pairs={{16,0},{24,8},{0,16},{8,24},{17,1},{25,9},{1,17},{9,25},{18,2},{26... | collective-permute-start | bytes 307976 | tf_op jit(solution)/shard_map/ppermute | solution.py:346
  32.5 12.7 %collective-permute-start.3 = (bf16[64,802]{1,0:T(8,128)(2,1)S(1)}, bf16[64,802]{1,0:T(8,128)(2,1)S(1)}, u32[]{:S(2)}, u32[]{:S(2)}) collective-permute-start(bf16[64,802]{1,0:T(8,128)(2,1)S(1)} %concatenate.61), channel_id=1, source_target_pairs={{24,0},{0,8},{8,16},{16,24},{25,1},{1,9},{9,17},{17,25},{26,2},{2,... | collective-permute-start | bytes 307976 | tf_op jit(solution)/shard_map/ppermute | solution.py:346
  45.2 13.4 %copy-start.46 = (s32[16]{0:T(128)S(1)}, s32[16]{0:T(128)}, u32[]{:S(2)}) copy-start(s32[16]{0:T(128)} %param.25) | copy-start | bytes 196
  45.3 7.9 %collective-permute-start.4 = (bf16[4,64,802]{2,1,0:T(8,128)(2,1)S(1)}, bf16[4,64,802]{2,1,0:T(8,128)(2,1)S(1)}, u32[]{:S(2)}, u32[]{:S(2)}) collective-permute-start(bf16[4,64,802]{2,1,0:T(8,128)(2,1)S(1)} %constant_dynamic-slice_fusion), channel_id=1, source_target_pairs={{0,4},{4,0},{1,5},{5,1},{2,6},{6,2},{3,7},{7,3},{8,12},{12,8},{9,1... | collective-permute-start | bytes 1231880 | tf_op jit(solution)/shard_map/ppermute | solution.py:337
  53.4 8.8 %collective-permute-start.5 = (bf16[2,4,64,802]{3,2,1,0:T(8,128)(2,1)S(1)}, bf16[2,4,64,802]{3,2,1,0:T(8,128)(2,1)}, u32[]{:S(2)}, u32[]{:S(2)}) collective-permute-start(bf16[2,4,64,802]{3,2,1,0:T(8,128)(2,1)S(1)} %pad_maximum_fusion.11), channel_id=1, source_target_pairs={{0,2},{2,0},{1,3},{3,1},{4,6},{6,4},{5,7},{7,5},{8,10},{10,8},{9,1... | collective-permute-start | bytes 2463752 | tf_op jit(solution)/shard_map/ppermute | solution.py:337
  76.2 13.2 %collective-permute-start.6 = (bf16[2,320,128]{2,1,0:T(8,128)(2,1)S(1)}, bf16[2,320,128]{2,1,0:T(8,128)(2,1)S(1)}, u32[]{:S(2)}, u32[]{:S(2)}) collective-permute-start(bf16[2,320,128]{2,1,0:T(8,128)(2,1)S(1)} %get-tuple-element.269), channel_id=1, source_target_pairs={{8,0},{16,8},{24,16},{0,24},{9,1},{17,9},{25,17},{1,25},{10,2},{18... | collective-permute-start | bytes 491528 | tf_op jit(solution)/shard_map/ppermute | solution.py:346
  77.1 29.6 %collective-permute-start.7 = (bf16[2,320,128]{2,1,0:T(8,128)(2,1)S(1)}, bf16[2,320,128]{2,1,0:T(8,128)(2,1)S(1)}, u32[]{:S(2)}, u32[]{:S(2)}) collective-permute-start(bf16[2,320,128]{2,1,0:T(8,128)(2,1)S(1)} %get-tuple-element.269), channel_id=1, source_target_pairs={{16,0},{24,8},{0,16},{8,24},{17,1},{25,9},{1,17},{9,25},{18,2},{26... | collective-permute-start | bytes 491528 | tf_op jit(solution)/shard_map/ppermute | solution.py:346
  83.0 23.7 %collective-permute-start.8 = (bf16[2,320,128]{2,1,0:T(8,128)(2,1)S(1)}, bf16[2,320,128]{2,1,0:T(8,128)(2,1)S(1)}, u32[]{:S(2)}, u32[]{:S(2)}) collective-permute-start(bf16[2,320,128]{2,1,0:T(8,128)(2,1)S(1)} %get-tuple-element.269), channel_id=1, source_target_pairs={{24,0},{0,8},{8,16},{16,24},{25,1},{1,9},{9,17},{17,25},{26,2},{2,... | collective-permute-start | bytes 491528 | tf_op jit(solution)/shard_map/ppermute | solution.py:346
  106.8 29.0 %collective-permute-start.9 = (bf16[2,320,512]{2,1,0:T(8,128)(2,1)S(1)}, bf16[2,320,512]{2,1,0:T(8,128)(2,1)S(1)}, u32[]{:S(2)}, u32[]{:S(2)}) collective-permute-start(bf16[2,320,512]{2,1,0:T(8,128)(2,1)S(1)} %pad_maximum_fusion.14), channel_id=1, source_target_pairs={{4,0},{0,4},{5,1},{1,5},{6,2},{2,6},{7,3},{3,7},{12,8},{8,12},{13,... | collective-permute-start | bytes 1966088 | tf_op jit(solution)/shard_map/ppermute | solution.py:346
  107.8 31.4 %collective-permute-start.12 = (bf16[2,320,128]{2,1,0:T(8,128)(2,1)S(1)}, bf16[2,320,128]{2,1,0:T(8,128)(2,1)S(1)}, u32[]{:S(2)}, u32[]{:S(2)}) collective-permute-start(bf16[2,320,128]{2,1,0:T(8,128)(2,1)S(1)} %get-tuple-element.268), channel_id=1, source_target_pairs={{8,0},{16,8},{24,16},{0,24},{9,1},{17,9},{25,17},{1,25},{10,2},{18... | collective-permute-start | bytes 491528 | tf_op jit(solution)/shard_map/ppermute | solution.py:346
  107.8 31.3 %collective-permute-start.13 = (bf16[2,320,128]{2,1,0:T(8,128)(2,1)S(1)}, bf16[2,320,128]{2,1,0:T(8,128)(2,1)S(1)}, u32[]{:S(2)}, u32[]{:S(2)}) collective-permute-start(bf16[2,320,128]{2,1,0:T(8,128)(2,1)S(1)} %get-tuple-element.268), channel_id=1, source_target_pairs={{16,0},{24,8},{0,16},{8,24},{17,1},{25,9},{1,17},{9,25},{18,2},{26... | collective-permute-start | bytes 491528 | tf_op jit(solution)/shard_map/ppermute | solution.py:346
  107.9 31.2 %collective-permute-start.14 = (bf16[2,320,128]{2,1,0:T(8,128)(2,1)S(1)}, bf16[2,320,128]{2,1,0:T(8,128)(2,1)S(1)}, u32[]{:S(2)}, u32[]{:S(2)}) collective-permute-start(bf16[2,320,128]{2,1,0:T(8,128)(2,1)S(1)} %get-tuple-element.268), channel_id=1, source_target_pairs={{24,0},{0,8},{8,16},{16,24},{25,1},{1,9},{9,17},{17,25},{26,2},{2,... | collective-permute-start | bytes 491528 | tf_op jit(solution)/shard_map/ppermute | solution.py:346
  137.0 36.4 %copy-start.41 = (bf16[2,320,2048]{2,1,0:T(8,128)(2,1)S(1)}, bf16[2,320,2048]{2,1,0:T(8,128)(2,1)}, u32[]{:S(2)}) copy-start(bf16[2,320,2048]{2,1,0:T(8,128)(2,1)} %get-tuple-element.258) | copy-start | bytes 7864324
  137.0 36.4 %collective-permute-start.10 = (bf16[2,320,1024]{2,1,0:T(8,128)(2,1)}, bf16[2,320,1024]{2,1,0:T(8,128)(2,1)S(1)}, u32[]{:S(2)}, u32[]{:S(2)}) collective-permute-start(bf16[2,320,1024]{2,1,0:T(8,128)(2,1)} %get-tuple-element.257), channel_id=1, source_target_pairs={{0,2},{2,0},{1,3},{3,1},{4,6},{6,4},{5,7},{7,5},{8,10},{10,8},{9,1... | collective-permute-start | bytes 3932168 | tf_op jit(solution)/shard_map/ppermute | solution.py:337
  139.3 31.0 %collective-permute-start.15 = (bf16[2,320,512]{2,1,0:T(8,128)(2,1)S(1)}, bf16[2,320,512]{2,1,0:T(8,128)(2,1)S(1)}, u32[]{:S(2)}, u32[]{:S(2)}) collective-permute-start(bf16[2,320,512]{2,1,0:T(8,128)(2,1)S(1)} %pad_maximum_fusion.15), channel_id=1, source_target_pairs={{4,0},{0,4},{5,1},{1,5},{6,2},{2,6},{7,3},{3,7},{12,8},{8,12},{13,... | collective-permute-start | bytes 1966088 | tf_op jit(solution)/shard_map/ppermute | solution.py:346
  171.4 28.8 %collective-permute-start.16 = (bf16[2,320,1024]{2,1,0:T(8,128)(2,1)}, bf16[2,320,1024]{2,1,0:T(8,128)(2,1)S(1)}, u32[]{:S(2)}, u32[]{:S(2)}) collective-permute-start(bf16[2,320,1024]{2,1,0:T(8,128)(2,1)} %get-tuple-element.255), channel_id=1, source_target_pairs={{0,2},{2,0},{1,3},{3,1},{4,6},{6,4},{5,7},{7,5},{8,10},{10,8},{9,1... | collective-permute-start | bytes 3932168 | tf_op jit(solution)/shard_map/ppermute | solution.py:337
  198.1 25.9 %collective-permute-start.17 = (bf16[1024,512]{1,0:T(8,128)(2,1)}, bf16[1024,512]{1,0:T(8,128)(2,1)}, u32[]{:S(2)}, u32[]{:S(2)}) collective-permute-start(bf16[1024,512]{1,0:T(8,128)(2,1)} %slice.173), channel_id=1, source_target_pairs={{0,2},{2,0},{1,3},{3,1},{4,6},{6,4},{5,7},{7,5},{8,10},{10,8},{9,1... | collective-permute-start | bytes 3145736 | tf_op jit(solution)/shard_map/ppermute | solution.py:337
  199.8 29.3 %collective-permute-start.19 = (bf16[512,1024]{1,0:T(8,128)(2,1)}, bf16[512,1024]{1,0:T(8,128)(2,1)}, u32[]{:S(2)}, u32[]{:S(2)}) collective-permute-start(bf16[512,1024]{1,0:T(8,128)(2,1)} %bitcast.44), channel_id=1, source_target_pairs={{0,2},{2,0},{1,3},{3,1},{4,6},{6,4},{5,7},{7,5},{8,10},{10,8},{9,1... | collective-permute-start | bytes 3145736 | tf_op jit(solution)/shard_map/ppermute | solution.py:337
  227.6 55.3 %copy-start = (f32[4,128,1024]{2,1,0:T(8,128)}, f32[4,128,1024]{2,1,0:T(8,128)S(1)}, u32[]{:S(2)}) copy-start(f32[4,128,1024]{2,1,0:T(8,128)S(1)} %get-tuple-element.291) | copy-start | bytes 6291460
  229.0 3.0 collective-permute-start.18
  229.1 9.3 %slice-start = ((s8[9699328]{0:T(1024)(128)(4,1)}), s8[4194304]{0:T(1024)(128)(4,1)S(1)}, s32[]{:S(2)}) async-start(s8[9699328]{0:T(1024)(128)(4,1)} %bitcast.190), calls=%async_computation.3 | async-start | bytes 8388608
  238.4 9.2 %copy-start.48 = (f32[1024,1408]{1,0:T(8,128)}, f32[1024,1408]{1,0:T(8,128)S(1)}, u32[]{:S(2)}) copy-start(f32[1024,1408]{1,0:T(8,128)S(1)} %fusion.11) | copy-start | bytes 17301508
  251.2 32.4 %collective-permute-start.23 = (bf16[512,1024]{1,0:T(8,128)(2,1)S(1)}, bf16[512,1024]{1,0:T(8,128)(2,1)S(1)}, u32[]{:S(2)}, u32[]{:S(2)}) collective-permute-start(bf16[512,1024]{1,0:T(8,128)(2,1)S(1)} %slice.320), channel_id=1, source_target_pairs={{0,2},{2,0},{1,3},{3,1},{4,6},{6,4},{5,7},{7,5},{8,10},{10,8},{9,1... | collective-permute-start | bytes 3145736 | tf_op jit(solution)/shard_map/ppermute | solution.py:337
  271.3 11.2 %collective-permute-start.20 = (bf16[512,1024]{1,0:T(8,128)(2,1)S(1)}, bf16[512,1024]{1,0:T(8,128)(2,1)S(1)}, u32[]{:S(2)}, u32[]{:S(2)}) collective-permute-start(bf16[512,1024]{1,0:T(8,128)(2,1)S(1)} %slice.321), channel_id=1, source_target_pairs={{0,2},{2,0},{1,3},{3,1},{4,6},{6,4},{5,7},{7,5},{8,10},{10,8},{9,1... | collective-permute-start | bytes 3145736 | tf_op jit(solution)/shard_map/ppermute | solution.py:337
  288.3 7.3 %collective-permute-start.21 = (bf16[1024,512]{1,0:T(8,128)(2,1)S(1)}, bf16[1024,512]{1,0:T(8,128)(2,1)S(1)}, u32[]{:S(2)}, u32[]{:S(2)}) collective-permute-start(bf16[1024,512]{1,0:T(8,128)(2,1)S(1)} %bitcast_convert_fusion.1), channel_id=1, source_target_pairs={{0,2},{2,0},{1,3},{3,1},{4,6},{6,4},{5,7},{7,5},{8,10},{10,8},{9,1... | collective-permute-start | bytes 3145736 | tf_op jit(solution)/shard_map/ppermute | solution.py:337
  301.9 33.0 %copy-start.4 = (bf16[4,128,1024]{2,1,0:T(8,128)(2,1)S(1)}, bf16[4,128,1024]{2,1,0:T(8,128)(2,1)}, u32[]{:S(2)}) copy-start(bf16[4,128,1024]{2,1,0:T(8,128)(2,1)} %get-tuple-element.231) | copy-start | bytes 3145732
  334.8 3.3 collective-permute-start.22
  338.5 40.2 %collective-permute-start.28 = (bf16[2,128,1024]{2,1,0:T(8,128)(2,1)}, bf16[2,128,1024]{2,1,0:T(8,128)(2,1)}, u32[]{:S(2)}, u32[]{:S(2)}) collective-permute-start(bf16[2,128,1024]{2,1,0:T(8,128)(2,1)} %get-tuple-element.75), channel_id=1, source_target_pairs={{0,1},{1,0},{2,3},{3,2},{4,5},{5,4},{6,7},{7,6},{8,9},{9,8},{10,11... | collective-permute-start | bytes 1572872 | tf_op jit(solution)/shard_map/ppermute | solution.py:337
  339.9 41.1 %collective-permute-start.24 = (bf16[4,2,320,128]{3,2,1,0:T(8,128)(2,1)}, bf16[4,2,320,128]{3,2,1,0:T(8,128)(2,1)}, u32[]{:S(2)}, u32[]{:S(2)}) collective-permute-start(bf16[4,2,320,128]{3,2,1,0:T(8,128)(2,1)} %slice.184), channel_id=1, source_target_pairs={{0,4},{4,0},{1,5},{5,1},{2,6},{6,2},{3,7},{7,3},{8,12},{12,8},{9,1... | collective-permute-start | bytes 1966088 | tf_op jit(solution)/shard_map/ppermute | solution.py:351
  358.9 44.6 %collective-permute-start.29 = (bf16[8,1,320,128]{3,2,1,0:T(8,128)(2,1)}, bf16[8,1,320,128]{3,2,1,0:T(8,128)(2,1)}, u32[]{:S(2)}, u32[]{:S(2)}) collective-permute-start(bf16[8,1,320,128]{3,2,1,0:T(8,128)(2,1)} %get-tuple-element.81), channel_id=1, source_target_pairs={{0,2},{2,0},{1,3},{3,1},{4,6},{6,4},{5,7},{7,5},{8,10},{10,8},{9,1... | collective-permute-start | bytes 1966088 | tf_op jit(solution)/shard_map/ppermute | solution.py:337
  383.1 18.8 %copy-start.8 = (bf16[4,2,320,128]{3,2,1,0:T(8,128)(2,1)S(1)}, bf16[4,2,320,128]{3,2,1,0:T(8,128)(2,1)}, u32[]{:S(2)}) copy-start(bf16[4,2,320,128]{3,2,1,0:T(8,128)(2,1)} %add_convert_fusion.6) | copy-start | bytes 1966084
  401.1 24.4 %collective-permute-start.30 = (bf16[8,1,320,128]{3,2,1,0:T(8,128)(2,1)}, bf16[8,1,320,128]{3,2,1,0:T(8,128)(2,1)}, u32[]{:S(2)}, u32[]{:S(2)}) collective-permute-start(bf16[8,1,320,128]{3,2,1,0:T(8,128)(2,1)} %get-tuple-element.84), channel_id=1, source_target_pairs={{0,2},{2,0},{1,3},{3,1},{4,6},{6,4},{5,7},{7,5},{8,10},{10,8},{9,1... | collective-permute-start | bytes 1966088 | tf_op jit(solution)/shard_map/ppermute | solution.py:337
  402.0 8.8 %collective-permute-start.27 = (bf16[1,2,320,128]{3,2,1,0:T(8,128)(2,1)S(1)}, bf16[1,2,320,128]{3,2,1,0:T(8,128)(2,1)S(1)}, u32[]{:S(2)}, u32[]{:S(2)}) collective-permute-start(bf16[1,2,320,128]{3,2,1,0:T(8,128)(2,1)S(1)} %get-tuple-element.253), channel_id=1, source_target_pairs={{0,24},{8,0},{16,8},{24,16},{1,25},{9,1},{17,9},{25,17},{2,26},{10... | collective-permute-start | bytes 491528 | tf_op jit(solution)/shard_map/ppermute | solution.py:351
  402.0 18.9 %collective-permute-start.26 = (bf16[1,2,320,128]{3,2,1,0:T(8,128)(2,1)S(1)}, bf16[1,2,320,128]{3,2,1,0:T(8,128)(2,1)S(1)}, u32[]{:S(2)}, u32[]{:S(2)}) collective-permute-start(bf16[1,2,320,128]{3,2,1,0:T(8,128)(2,1)S(1)} %get-tuple-element.254), channel_id=1, source_target_pairs={{0,16},{8,24},{16,0},{24,8},{1,17},{9,25},{17,1},{25,9},{2,18},{10... | collective-permute-start | bytes 491528 | tf_op jit(solution)/shard_map/ppermute | solution.py:351
  402.1 18.9 %collective-permute-start.25 = (bf16[1,2,320,128]{3,2,1,0:T(8,128)(2,1)S(1)}, bf16[1,2,320,128]{3,2,1,0:T(8,128)(2,1)S(1)}, u32[]{:S(2)}, u32[]{:S(2)}) collective-permute-start(bf16[1,2,320,128]{3,2,1,0:T(8,128)(2,1)S(1)} %get-tuple-element.252), channel_id=1, source_target_pairs={{0,8},{8,16},{16,24},{24,0},{1,9},{9,17},{17,25},{25,1},{2,10},{10... | collective-permute-start | bytes 491528 | tf_op jit(solution)/shard_map/ppermute | solution.py:351
  403.5 58.8 %collective-permute-start.35 = (bf16[2,128,1024]{2,1,0:T(8,128)(2,1)}, bf16[2,128,1024]{2,1,0:T(8,128)(2,1)}, u32[]{:S(2)}, u32[]{:S(2)}) collective-permute-start(bf16[2,128,1024]{2,1,0:T(8,128)(2,1)} %get-tuple-element.87), channel_id=1, source_target_pairs={{0,1},{1,0},{2,3},{3,2},{4,5},{5,4},{6,7},{7,6},{8,9},{9,8},{10,11... | collective-permute-start | bytes 1572872 | tf_op jit(solution)/shard_map/ppermute | solution.py:337
  427.1 24.3 %collective-permute-start.31 = (bf16[4,2,320,128]{3,2,1,0:T(8,128)(2,1)S(1)}, bf16[4,2,320,128]{3,2,1,0:T(8,128)(2,1)S(1)}, u32[]{:S(2)}, u32[]{:S(2)}) collective-permute-start(bf16[4,2,320,128]{3,2,1,0:T(8,128)(2,1)S(1)} %pad_maximum_fusion.13), channel_id=1, source_target_pairs={{0,4},{4,0},{1,5},{5,1},{2,6},{6,2},{3,7},{7,3},{8,12},{12,8},{9,1... | collective-permute-start | bytes 1966088 | tf_op jit(solution)/shard_map/ppermute | solution.py:351
  451.6 14.0 %collective-permute-start.34 = (bf16[1,2,320,128]{3,2,1,0:T(8,128)(2,1)S(1)}, bf16[1,2,320,128]{3,2,1,0:T(8,128)(2,1)S(1)}, u32[]{:S(2)}, u32[]{:S(2)}) collective-permute-start(bf16[1,2,320,128]{3,2,1,0:T(8,128)(2,1)S(1)} %get-tuple-element.250), channel_id=1, source_target_pairs={{0,24},{8,0},{16,8},{24,16},{1,25},{9,1},{17,9},{25,17},{2,26},{10... | collective-permute-start | bytes 491528 | tf_op jit(solution)/shard_map/ppermute | solution.py:351
  455.6 16.9 %collective-permute-start.33 = (bf16[1,2,320,128]{3,2,1,0:T(8,128)(2,1)S(1)}, bf16[1,2,320,128]{3,2,1,0:T(8,128)(2,1)S(1)}, u32[]{:S(2)}, u32[]{:S(2)}) collective-permute-start(bf16[1,2,320,128]{3,2,1,0:T(8,128)(2,1)S(1)} %get-tuple-element.251), channel_id=1, source_target_pairs={{0,16},{8,24},{16,0},{24,8},{1,17},{9,25},{17,1},{25,9},{2,18},{10... | collective-permute-start | bytes 491528 | tf_op jit(solution)/shard_map/ppermute | solution.py:351
  460.7 15.6 %collective-permute-start.32 = (bf16[1,2,320,128]{3,2,1,0:T(8,128)(2,1)S(1)}, bf16[1,2,320,128]{3,2,1,0:T(8,128)(2,1)S(1)}, u32[]{:S(2)}, u32[]{:S(2)}) collective-permute-start(bf16[1,2,320,128]{3,2,1,0:T(8,128)(2,1)S(1)} %get-tuple-element.249), channel_id=1, source_target_pairs={{0,8},{8,16},{16,24},{24,0},{1,9},{9,17},{17,25},{25,1},{2,10},{10... | collective-permute-start | bytes 491528 | tf_op jit(solution)/shard_map/ppermute | solution.py:351
  483.7 15.6 %copy-start.45 = (f32[2,64]{1,0:T(2,128)S(1)}, f32[2,64]{1,0:T(2,128)}, u32[]{:S(2)}) copy-start(f32[2,64]{1,0:T(2,128)} %param.42) | copy-start | bytes 1540
  492.2 10.6 %copy-start.5 = (bf16[2,2,128,1024]{3,2,1,0:T(8,128)(2,1)S(1)}, bf16[2,2,128,1024]{3,2,1,0:T(8,128)(2,1)}, u32[]{:S(2)}) copy-start(bf16[2,2,128,1024]{3,2,1,0:T(8,128)(2,1)} %pad_maximum_fusion.7) | copy-start | bytes 3145732
  492.2 12.1 %collective-permute-start.36 = (bf16[4,2,64,802]{3,2,1,0:T(8,128)(2,1)}, bf16[4,2,64,802]{3,2,1,0:T(8,128)(2,1)}, u32[]{:S(2)}, u32[]{:S(2)}) collective-permute-start(bf16[4,2,64,802]{3,2,1,0:T(8,128)(2,1)} %get-tuple-element.91), channel_id=1, source_target_pairs={{0,2},{2,0},{1,3},{3,1},{4,6},{6,4},{5,7},{7,5},{8,10},{10,8},{9,1... | collective-permute-start | bytes 2463752 | tf_op jit(solution)/shard_map/ppermute | solution.py:337
  501.4 32.8 %collective-permute-start.42 = (bf16[2,128,1024]{2,1,0:T(8,128)(2,1)S(1)}, bf16[2,128,1024]{2,1,0:T(8,128)(2,1)S(1)}, u32[]{:S(2)}, u32[]{:S(2)}) collective-permute-start(bf16[2,128,1024]{2,1,0:T(8,128)(2,1)S(1)} %fusion.19), channel_id=1, source_target_pairs={{0,1},{1,0},{2,3},{3,2},{4,5},{5,4},{6,7},{7,6},{8,9},{9,8},{10,11... | collective-permute-start | bytes 1572872 | tf_op jit(solution)/shard_map/ppermute | solution.py:337
  501.4 46.0 %collective-permute-start.38 = (bf16[2,128,1024]{2,1,0:T(8,128)(2,1)S(1)}, bf16[2,128,1024]{2,1,0:T(8,128)(2,1)S(1)}, u32[]{:S(2)}, u32[]{:S(2)}) collective-permute-start(bf16[2,128,1024]{2,1,0:T(8,128)(2,1)S(1)} %copy-done.15), channel_id=1, source_target_pairs={{0,1},{1,0},{2,3},{3,2},{4,5},{5,4},{6,7},{7,6},{8,9},{9,8},{10,11... | collective-permute-start | bytes 1572872 | tf_op jit(solution)/shard_map/ppermute | solution.py:337
  505.9 41.8 %collective-permute-start.37 = (bf16[4,64,802]{2,1,0:T(8,128)(2,1)S(1)}, bf16[4,64,802]{2,1,0:T(8,128)(2,1)S(1)}, u32[]{:S(2)}, u32[]{:S(2)}) collective-permute-start(bf16[4,64,802]{2,1,0:T(8,128)(2,1)S(1)} %dynamic-slice_bitcast_fusion), channel_id=1, source_target_pairs={{0,4},{4,0},{1,5},{5,1},{2,6},{6,2},{3,7},{7,3},{8,12},{12,8},{9,1... | collective-permute-start | bytes 1231880 | tf_op jit(solution)/shard_map/ppermute | solution.py:351
  547.9 5.1 collective-permute-start.41
  551.0 10.1 %collective-permute-start.40 = (bf16[64,802]{1,0:T(8,128)(2,1)S(1)}, bf16[64,802]{1,0:T(8,128)(2,1)S(1)}, u32[]{:S(2)}, u32[]{:S(2)}) collective-permute-start(bf16[64,802]{1,0:T(8,128)(2,1)S(1)} %get-tuple-element.261), channel_id=1, source_target_pairs={{0,16},{8,24},{16,0},{24,8},{1,17},{9,25},{17,1},{25,9},{2,18},{10... | collective-permute-start | bytes 307976 | tf_op jit(solution)/shard_map/ppermute | solution.py:351
  551.0 10.1 %collective-permute-start.39 = (bf16[64,802]{1,0:T(8,128)(2,1)S(1)}, bf16[64,802]{1,0:T(8,128)(2,1)S(1)}, u32[]{:S(2)}, u32[]{:S(2)}) collective-permute-start(bf16[64,802]{1,0:T(8,128)(2,1)S(1)} %get-tuple-element.259), channel_id=1, source_target_pairs={{0,8},{8,16},{16,24},{24,0},{1,9},{9,17},{17,25},{25,1},{2,10},{10... | collective-permute-start | bytes 307976 | tf_op jit(solution)/shard_map/ppermute | solution.py:351
  561.2 3.7 collective-permute-start.43
  561.9 9.7 %copy-start.38 = (f32[64,80]{1,0:T(8,128)S(1)}, f32[64,80]{1,0:T(8,128)}, u32[]{:S(2)}) copy-start(f32[64,80]{1,0:T(8,128)} %param.26) | copy-start | bytes 61444
  562.0 9.7 %copy-start.39 = (f32[64,80]{1,0:T(8,128)S(1)}, f32[64,80]{1,0:T(8,128)}, u32[]{:S(2)}) copy-start(f32[64,80]{1,0:T(8,128)} %param.27) | copy-start | bytes 61444
  562.0 9.7 %copy-start.40 = (f32[64,80]{1,0:T(8,128)S(1)}, f32[64,80]{1,0:T(8,128)}, u32[]{:S(2)}) copy-start(f32[64,80]{1,0:T(8,128)} %param.28) | copy-start | bytes 61444
  562.0 10.4 %copy-start.32 = (f32[64,640]{1,0:T(8,128)S(1)}, f32[64,640]{1,0:T(8,128)}, u32[]{:S(2)}) copy-start(f32[64,640]{1,0:T(8,128)} %param.29) | copy-start | bytes 491524
  562.0 10.4 %copy-start.33 = (f32[64,640]{1,0:T(8,128)S(1)}, f32[64,640]{1,0:T(8,128)}, u32[]{:S(2)}) copy-start(f32[64,640]{1,0:T(8,128)} %param.30) | copy-start | bytes 491524
  562.0 10.4 %copy-start.34 = (f32[64,640]{1,0:T(8,128)S(1)}, f32[64,640]{1,0:T(8,128)}, u32[]{:S(2)}) copy-start(f32[64,640]{1,0:T(8,128)} %param.31) | copy-start | bytes 491524
  565.1 12.4 %collective-permute-start.44 = (bf16[64,4736]{1,0:T(8,128)(2,1)}, bf16[64,4736]{1,0:T(8,128)(2,1)S(1)}, u32[]{:S(2)}, u32[]{:S(2)}) collective-permute-start(bf16[64,4736]{1,0:T(8,128)(2,1)} %reduce-scatter.2.cloned.1.call-done), channel_id=1, source_target_pairs={{0,0},{1,2},{2,1},{3,3},{4,4},{5,6},{6,5},{7,7},{8,8},{9,10},{10,9... | collective-permute-start | bytes 1818632 | tf_op jit(solution)/shard_map/ppermute | solution.py:341
  (38 other events, 126.6 us)
Sparse Core Ops, SparseCore 0:
  23.7 166.2 all-gather.1
  302.0 236.6 reduce-scatter.1
